TPU v7x, 32 devices: a whole 2x2x4 slice. The times are simulated.
32 devices in a mesh: section: 4 (over z), expert: 8 (over y, x, core).
Axes of the slice: x: 2, y: 2, z: 4, core: 2. Of those that a mesh axis runs over, the one named last changes fastest.
Arguments:
- tokens: bfloat16 [48, 4096], P('expert'), may hold values from -6 to 6
- expert_ids: int32 [4, 48, 1], P('section', 'expert'), may hold values from 0 to 3; in each aligned block of 6 rows (0 to 5, 6 to 11, ..., all dimensions but the last counted through in order) at most 2 rows name the same one
- gate_scale: float32 [4, 48], P('section', 'expert'), may hold values from 0.3 to 1
- norm_gain: float32 [4, 4096], P('section'), may hold values from 0.5 to 1.5
- w_gate: bfloat16 [4, 4096, 4096], P('section', None, 'expert'), may hold values from -0.09375 to 0.09375
- w_up: bfloat16 [4, 4096, 4096], P('section', None, 'expert'), may hold values from -0.09375 to 0.09375
- w_down: bfloat16 [4, 4096, 4096], P('section', 'expert'), may hold values from -0.1875 to 0.1875
Outputs:
- section_out: bfloat16 [4, 48, 4096], P('section', 'expert')
Inputs may be any that keep to these rules, and one draw needn't show every extreme that they name: `expert_ids`: within each layer, the 6 tokens of one index of expert choose any one expert at most 2 times.
All inputs are finite; a program needn't handle non-finite values.
Results may differ from a plain program's by a relative error of at most 0.035.
Values may be sent and summed in bfloat16 or wider, within the bound.
No kernel may reach another device: no remote copies, remote signals or barrier semaphores. Data moves between devices by JAX's collectives and lax.ppermute only.
A program may use at most 64 MiB of HBM per device.

v0:
```python
import functools

import jax
import jax.numpy as jnp
from jax import lax
from jax.experimental import pallas as pl
from jax.experimental.pallas import tpu as pltpu
from jax.sharding import PartitionSpec as P


EXPERTS = 4
CAP = 2
LANES = 128
BLOCKS = 4
START_FLOPS = 10_000_000_000
F32 = jnp.float32
BF16 = jnp.bfloat16
VMEM = pl.BlockSpec(memory_space=pltpu.VMEM)


def call(kernel, outs, args, limit=2 << 20, scratch=(), flops=1000, specs=None, moved=None):
    if moved is None:
        moved = sum(a.size * a.dtype.itemsize for a in args)
    return pl.pallas_call(
        kernel,
        out_shape=outs,
        in_specs=specs or [VMEM] * len(args),
        out_specs=jax.tree.map(lambda _: VMEM, outs),
        scratch_shapes=scratch,
        compiler_params=pltpu.CompilerParams(vmem_limit_bytes=limit),
        cost_estimate=pl.CostEstimate(flops=flops, bytes_accessed=moved, transcendentals=0),
    )(*args)


def shape(dims, kind=BF16):
    return jax.ShapeDtypeStruct(dims, kind)


def place(group):
    index = lax.axis_index("expert")
    return index // group, lax.rem(index, group)


def iota(dims, axis):
    return lax.broadcasted_iota(jnp.int32, dims, axis)


def rank_kernel(ids, out):
    rows = ids.shape[1]
    ids_row = ids[...]
    ids_full = jnp.broadcast_to(ids_row, (rows, rows))
    diagonal = iota((rows, rows), 0) == iota((rows, rows), 1)
    ids_column = jnp.sum(jnp.where(diagonal, ids_full, 0), axis=1, keepdims=True)
    earlier = iota((rows, rows), 0) < iota((rows, rows), 1)
    rank = jnp.sum(jnp.where((ids_full == ids_column) & earlier, 1, 0), axis=0, keepdims=True)
    out[...] = jnp.full(out.shape, -1.0, F32)
    out[:, 0:rows] = jnp.broadcast_to((ids_row * CAP + rank).astype(F32), (out.shape[0], rows))


def slot_kernel(group, position, tokens, scale, *outs):
    expert, _ = place(group)
    rows = tokens.shape[0]
    width = tokens.shape[1]
    codes = position[...]
    index = iota(codes.shape, 0)
    wanted = (expert ^ (index // CAP)) * CAP + lax.rem(index, CAP)
    chosen = jnp.where(codes == wanted.astype(F32), 1.0, 0.0)[:, 0:rows].astype(BF16)
    body = jnp.dot(chosen, tokens[...], preferred_element_type=F32)
    value = scale[...]
    first = value.astype(BF16).astype(F32)
    second = (value - first).astype(BF16).astype(F32)
    third = value - first - second
    for i in range(EXPERTS):
        outs[i][:, 0:width] = body[i * CAP : (i + 1) * CAP, :].astype(BF16)
        outs[i][:, width : width + LANES] = codes[0:CAP, :].astype(BF16)
        outs[i][:, width + LANES :] = jnp.zeros((CAP, (BLOCKS - 1) * LANES), BF16)
        for n, piece in enumerate((first, second, third)):
            at = width + (n + 1) * LANES
            outs[i][:, at : at + rows] = jnp.broadcast_to(piece, (CAP, rows)).astype(BF16)


def expert_math(values, gain, w_gate, w_up, w_down, parts):
    inverse = lax.rsqrt(jnp.mean(values * values, axis=-1, keepdims=True) + 1e-06)
    normed = (values * inverse * gain[...]).astype(BF16)
    gate = jnp.dot(normed, w_gate[0], preferred_element_type=F32)
    upward = jnp.dot(normed, w_up[0], preferred_element_type=F32)
    hidden = (gate / (1.0 + jnp.exp(-gate)) * upward).astype(BF16)
    step = 512
    for at in range(0, values.shape[1], step):
        parts[:, at : at + step] = jnp.dot(
            hidden, w_down[0, :, at : at + step], preferred_element_type=F32
        )


def deal(parts, chunks, own, group):
    width = chunks[0].shape[1]
    for m in range(group):
        at = pl.multiple_of((own ^ m) * width, width)
        chunks[m][...] = parts[:, pl.ds(at, width)].astype(BF16)


def deal_rows(source, blocks, own):
    slots = blocks[0].shape[0]
    for m in range(len(blocks)):
        at = pl.multiple_of((own ^ m) * slots, slots)
        blocks[m][...] = source[pl.ds(at, slots), :].astype(BF16)


def join_kernel(group, width, *refs):
    count = group * EXPERTS
    whole, half, table, position = refs[count : count + 4]
    block, rows = refs[count + 4 :]
    _, own = place(group)
    slots = EXPERTS * CAP
    for m in range(group):
        for i in range(EXPERTS):
            block[i * CAP : (i + 1) * CAP, :] = refs[m * EXPERTS + i][...].astype(F32)
        at = pl.multiple_of((own ^ m) * slots, slots)
        rows[pl.ds(at, slots), :] = block[...]
    table[...] = rows[:, width:].astype(BF16)
    position[...] = rows[:, width : width + LANES].astype(BF16)
    at = pl.multiple_of(own * half.shape[1], half.shape[1])
    half[...] = rows[:, pl.ds(at, half.shape[1])].astype(BF16)
    whole[...] = rows[:, 0:width].astype(BF16)


def expert_kernel(group, tick, count, last, *refs):
    pieces = refs[:count]
    gain, w_gate, w_up, w_down = refs[count : count + 4]
    outs = refs[count + 4 : count + 4 + group]
    rows, parts = refs[-2:]
    _, own = place(group)

    @pl.when(lax.axis_index("section") == tick)
    def _():
        width = pieces[0].shape[1]
        for m in range(count):
            at = pl.multiple_of((own ^ m) * width, width) if count > 1 else 0
            rows[:, pl.ds(at, width)] = pieces[m][...].astype(F32)
        expert_math(rows[...], gain, w_gate, w_up, w_down, parts)
        if last:
            deal_rows(parts, outs, own)
            deal_rows(rows, refs[count + 4 + group : count + 5 + group], own)
        else:
            deal(parts, outs, own, group)


def slot_codes(expert, dims):
    return expert * CAP + lax.rem(iota(dims, 0), CAP)


def scales(expert, table):
    rows = table.shape[0]
    position = table[:, 0:LANES].astype(F32)
    mine = position == slot_codes(expert, (rows, LANES)).astype(F32)
    scale = sum(table[:, n * LANES : (n + 1) * LANES].astype(F32) for n in range(1, BLOCKS))
    return jnp.sum(jnp.where(mine, scale, 0.0), axis=1, keepdims=True)


def updated(pieces, before, scale):
    total = pieces[0][...].astype(F32)
    for piece in pieces[1:]:
        total = total + piece[...].astype(F32)
    return before[...].astype(F32) + scale * total


def update_kernel(group, *refs):
    half, table, out = refs[group], refs[group + 1], refs[-1]
    expert, _ = place(group)
    out[...] = updated(refs[:group], half, scales(expert, table)).astype(BF16)


def keep_kernel(group, saved, *refs):
    outs, buffer = refs[saved : saved + group], refs[-1]
    section = lax.axis_index("section")
    _, own = place(group)
    for n in range(saved):

        @pl.when(section == n)
        def _(n=n):
            buffer[...] = refs[n][...].astype(F32)

    deal_rows(buffer, outs, own)


def leave_kernel(group, *refs):
    before, table = refs[group : group + 2]
    kept = refs[group + 2 : 2 * group + 2]
    outs = refs[2 * group + 2 : 2 * group + 2 + EXPERTS]
    column, rows = refs[-2:]
    slots = EXPERTS * CAP
    final = lax.axis_size("section") - 1
    section = lax.axis_index("section")
    expert, own = place(group)

    @pl.when(section == final)
    def _():
        column[...] = jnp.broadcast_to(scales(expert, table), column.shape)
        at = pl.multiple_of(own * slots, slots)
        scale = column[pl.ds(at, slots), :][:, 0:1]
        rows[...] = updated(refs[:group], before, scale)

    @pl.when(section != final)
    def _():
        width = kept[0].shape[1]
        for m in range(group):
            at = pl.multiple_of((own ^ m) * width, width)
            rows[:, pl.ds(at, width)] = kept[m][...].astype(F32)

    for i in range(EXPERTS):
        outs[i][...] = rows[i * CAP : (i + 1) * CAP, :].astype(BF16)


def choice_kernel(group, current, before, out):
    expert, _ = place(group)
    rows = current.shape[0]
    span = EXPERTS * CAP
    here = current[...].astype(F32)
    there = before[...].astype(F32)
    mine = jnp.where(here == slot_codes(expert, here.shape).astype(F32), 1.0, 0.0).astype(BF16)
    a, b = iota((rows, rows), 0), iota((rows, rows), 1)
    for i in range(EXPERTS):
        codes = slot_codes(expert ^ i, there.shape).astype(F32)
        theirs = jnp.where(there == codes, 1.0, 0.0).astype(BF16)
        both = lax.dot_general(
            mine, theirs, (((1,), (1,)), ((), ())), preferred_element_type=F32
        )
        both = jnp.where(a // CAP == b // CAP, both, 0.0).astype(BF16)
        moved = (a // span) * span + (((lax.rem(a, span) // CAP) ^ i) * CAP) + lax.rem(a, CAP)
        order = jnp.where(moved == b, 1.0, 0.0).astype(BF16)
        out[i] = jnp.dot(both, order, preferred_element_type=F32).astype(BF16)


def pick_kernel(*refs):
    choice, out = refs[EXPERTS], refs[-1]
    total = jnp.dot(choice[0], refs[0][...], preferred_element_type=F32)
    for i in range(1, EXPERTS):
        total = total + jnp.dot(choice[i], refs[i][...], preferred_element_type=F32)
    out[...] = total.astype(BF16)


def home_kernel(group, *refs):
    table, out, block = refs[EXPERTS:]
    expert, _ = place(group)
    slots = EXPERTS * CAP
    count = out.shape[1]
    for i in range(EXPERTS):
        block[i * CAP : (i + 1) * CAP, :] = refs[i][...].astype(F32)
    lanes = -(-count // 16) * 16
    position = jnp.broadcast_to(table[0:1, 0:lanes].astype(F32), (slots, lanes))
    index = iota((slots, lanes), 0)
    wanted = (expert ^ (index // CAP)) * CAP + lax.rem(index, CAP)
    chosen = jnp.where(position == wanted.astype(F32), 1.0, 0.0).astype(BF16)
    full = lax.dot_general(
        chosen, block[...].astype(BF16), (((0,), (0,)), ((), ())), preferred_element_type=F32
    )
    out[0] = full[0:count, :].astype(BF16)


def local(tokens, expert_ids, gate_scale, norm_gain, w_gate, w_up, w_down):
    peers = lax.axis_size("expert")
    sections = lax.axis_size("section")
    count, width = tokens.shape
    group = peers // EXPERTS
    chunk = width // group
    rows = peers * CAP
    slots = EXPERTS * CAP
    wide = width + BLOCKS * LANES
    weights = (norm_gain, w_gate, w_up, w_down)

    def across(value, i):
        pairs = [(d, (d // group ^ i) * group + d % group) for d in range(peers)]
        if i == 0:
            return value
        return lax.ppermute(value, "expert", pairs)

    def within(value, m):
        return lax.ppermute(value, "expert", [(d, d ^ m) for d in range(peers)])

    def onward(value, hops, i):
        pairs = [
            (s * peers + d, hops[s] * peers + (d // group ^ i) * group + d % group)
            for s in range(sections)
            for d in range(peers)
        ]
        return lax.ppermute(value, ("section", "expert"), pairs)

    def cycle(tick, turn):
        hops = list(range(sections))
        others = [(tick + n) % sections for n in range(2, sections)]
        ring = [tick, tick + 1] + (others[turn : turn + 1] if turn < 2 else [])
        for n, s in enumerate(ring):
            hops[s] = ring[(n + 1) % len(ring)]
        return hops

    position = call(
        rank_kernel, shape((slots, LANES), F32), (expert_ids.reshape(1, count),), flops=START_FLOPS
    )
    sent = call(
        functools.partial(slot_kernel, group),
        [shape((CAP, wide))] * EXPERTS,
        (position, tokens, gate_scale),
    )
    arrived = [across(sent[i], i) for i in range(EXPERTS)]
    pieces = list(arrived)
    for m in range(1, group):
        pieces += [within(piece, m) for piece in arrived]
    flops = 6 * rows * width * w_gate.shape[2]
    whole, half, table, position = call(
        functools.partial(join_kernel, group, width),
        [shape((rows, width)), shape((rows, chunk)), shape((rows, BLOCKS * LANES)), shape((rows, LANES))],
        tuple(pieces),
        scratch=[pltpu.VMEM((slots, wide), F32), pltpu.VMEM((rows, wide), F32)],
    )
    before = onward(position, [(s + 1) % sections for s in range(sections)], 0)
    choice = call(
        functools.partial(choice_kernel, group), shape((EXPERTS, rows, rows)), (position, before)
    )
    saved = []
    pieces = [whole]
    for tick in range(sections):
        last = tick == sections - 1
        if tick:
            gathered = [
                onward(saved[-1], cycle(tick - 1, EXPERTS - 1 - i), i) for i in range(EXPERTS)
            ]
            kept = []
            if last:
                kept = call(
                    functools.partial(keep_kernel, group, len(saved)),
                    [shape((slots, chunk))] * group,
                    tuple(saved),
                    scratch=[pltpu.VMEM((rows, chunk), F32)],
                )
                kept = [kept[0]] + [within(kept[m], m) for m in range(1, group)]
            half = call(pick_kernel, shape((rows, chunk)), (*gathered, choice, *kept))
            pieces = [half] + [within(half, m) for m in range(1, group)]
        parts = call(
            functools.partial(expert_kernel, group, tick, len(pieces), last),
            [shape((slots, width))] * (group + 1) if last else [shape((rows, chunk))] * group,
            (*pieces, *weights),
            limit=4 << 20,
            scratch=[pltpu.VMEM((rows, width), F32), pltpu.VMEM((rows, width), F32)],
            flops=flops,
        )
        terms = [parts[0]] + [within(parts[m], m) for m in range(1, group)]
        if not last:
            saved.append(
                call(
                    functools.partial(update_kernel, group),
                    shape((rows, chunk)),
                    (*terms, half, table),
                )
            )
    leaving = call(
        functools.partial(leave_kernel, group),
        [shape((CAP, width))] * EXPERTS,
        (*terms, parts[group], table, *kept),
        scratch=[pltpu.VMEM((rows, LANES), F32), pltpu.VMEM((slots, width), F32)],
    )
    back = [across(leaving[i], i) for i in range(EXPERTS)]
    return call(
        functools.partial(home_kernel, group),
        shape((1, count, width)),
        (*back, sent[0][:, width : width + LANES]),
        scratch=[pltpu.VMEM((slots, width), F32)],
    )


def solution(mesh):
    return jax.shard_map(
        local,
        mesh=mesh,
        in_specs=(
            P("expert", None),
            P("section", "expert", None),
            P("section", "expert"),
            P("section", None),
            P("section", None, "expert"),
            P("section", None, "expert"),
            P("section", "expert", None),
        ),
        out_specs=P("section", "expert", None),
        check_vma=False,
    )
```

profile of v0, /device:TPU:24, one launch (start us, length us, event | category | flops | bytes accessed | tf_op | source)
XLA Modules:
  0.0 64.3 jit_solution(8315232542564947970)
XLA Ops:
  1.7 1.6 %collective-permute-start = (bf16[2,4608]{1,0:T(2,128)(2,1)S(1)}, bf16[2,4608]{1,0:T(2,128)(2,1)S(1)}, u32[]{:S(2)}, u32[]{:S(2)}) collective-permute-start(bf16[2,4608]{1,0:T(2,128)(2,1)S(1)} %get-tuple-element.29), channel_id=1, source_target_pairs={{0,2},{1,3},{2,0},{3,1},{4,6},{5,7},{6,4},{7,5},{8,10},{9,11},{10,... | collective-permute-start | bytes 55304 | tf_op jit(solution)/shard_map/ppermute | solution.py:275
  3.2 1.5 %collective-permute-start.1 = (bf16[2,4608]{1,0:T(2,128)(2,1)S(1)}, bf16[2,4608]{1,0:T(2,128)(2,1)S(1)}, u32[]{:S(2)}, u32[]{:S(2)}) collective-permute-start(bf16[2,4608]{1,0:T(2,128)(2,1)S(1)} %get-tuple-element.30), channel_id=1, source_target_pairs={{0,4},{1,5},{2,6},{3,7},{4,0},{5,1},{6,2},{7,3},{8,12},{9,13},{10,... | collective-permute-start | bytes 55304 | tf_op jit(solution)/shard_map/ppermute | solution.py:275
  5.7 1.2 %collective-permute-done.1.refs_2_ = bf16[2,4608]{1,0:T(2,128)(2,1)S(1)} collective-permute-done((bf16[2,4608]{1,0:T(2,128)(2,1)S(1)}, bf16[2,4608]{1,0:T(2,128)(2,1)S(1)}, u32[]{:S(2)}, u32[]{:S(2)}) %collective-permute-start.1) | collective-permute-done | bytes 18464 | tf_op jit(solution)/shard_map/ppermute | solution.py:275
  7.0 2.4 %collective-permute-done.2.refs_3_ = bf16[2,4608]{1,0:T(2,128)(2,1)S(1)} collective-permute-done((bf16[2,4608]{1,0:T(2,128)(2,1)S(1)}, bf16[2,4608]{1,0:T(2,128)(2,1)S(1)}, u32[]{:S(2)}, u32[]{:S(2)}) %collective-permute-start.2) | collective-permute-done | bytes 18464 | tf_op jit(solution)/shard_map/ppermute | solution.py:275
  9.4 1.2 %collective-permute-done.6.refs_7_ = bf16[2,4608]{1,0:T(2,128)(2,1)S(1)} collective-permute-done((bf16[2,4608]{1,0:T(2,128)(2,1)S(1)}, bf16[2,4608]{1,0:T(2,128)(2,1)S(1)}, u32[]{:S(2)}, u32[]{:S(2)}) %collective-permute-start.6) | collective-permute-done | bytes 18464 | tf_op jit(solution)/shard_map/ppermute | solution.py:278
  12.8 2.2 %collective-permute-start.10 = (bf16[16,2048]{1,0:T(8,128)(2,1)S(1)}, bf16[16,2048]{1,0:T(8,128)(2,1)S(1)}, u32[]{:S(2)}, u32[]{:S(2)}) collective-permute-start(bf16[16,2048]{1,0:T(8,128)(2,1)S(1)} %shard_map.77.refs_0_), channel_id=1, source_target_pairs={{0,12},{1,13},{2,14},{3,15},{4,8},{5,9},{6,10},{7,11},{8,28},{9,29... | collective-permute-start | bytes 196616 | tf_op jit(solution)/shard_map/ppermute | solution.py:286
  15.0 1.5 %collective-permute-start.9 = (bf16[16,2048]{1,0:T(8,128)(2,1)S(1)}, bf16[16,2048]{1,0:T(8,128)(2,1)S(1)}, u32[]{:S(2)}, u32[]{:S(2)}) collective-permute-start(bf16[16,2048]{1,0:T(8,128)(2,1)S(1)} %shard_map.77.refs_0_), channel_id=1, source_target_pairs={{0,10},{1,11},{2,8},{3,9},{4,14},{5,15},{6,12},{7,13},{8,2},{9,3},... | collective-permute-start | bytes 196616 | tf_op jit(solution)/shard_map/ppermute | solution.py:286
  17.1 4.3 %collective-permute-start.12 = (bf16[16,128]{1,0:T(8,128)(2,1)S(1)}, bf16[16,128]{1,0:T(8,128)(2,1)S(1)}, u32[]{:S(2)}, u32[]{:S(2)}) collective-permute-start(bf16[16,128]{1,0:T(8,128)(2,1)S(1)} %get-tuple-element.37.current), channel_id=1, source_target_pairs={{0,8},{1,9},{2,10},{3,11},{4,12},{5,13},{6,14},{7,15},{8,16},{9,17... | collective-permute-start | bytes 12296 | tf_op jit(solution)/shard_map/ppermute | solution.py:286
  21.4 1.3 %collective-permute-done.12.before = bf16[16,128]{1,0:T(8,128)(2,1)S(1)} collective-permute-done((bf16[16,128]{1,0:T(8,128)(2,1)S(1)}, bf16[16,128]{1,0:T(8,128)(2,1)S(1)}, u32[]{:S(2)}, u32[]{:S(2)}) %collective-permute-start.12) | collective-permute-done | bytes 4128 | tf_op jit(solution)/shard_map/ppermute | solution.py:286
  23.5 1.2 %collective-permute-done.13.refs_1_ = bf16[16,2048]{1,0:T(8,128)(2,1)S(1)} collective-permute-done((bf16[16,2048]{1,0:T(8,128)(2,1)S(1)}, bf16[16,2048]{1,0:T(8,128)(2,1)S(1)}, u32[]{:S(2)}, u32[]{:S(2)}) %collective-permute-start.13) | collective-permute-done | bytes 65568 | tf_op jit(solution)/shard_map/ppermute | solution.py:278
  24.9 1.1 %collective-permute-done.14.refs_1_ = bf16[16,2048]{1,0:T(8,128)(2,1)S(1)} collective-permute-done((bf16[16,2048]{1,0:T(8,128)(2,1)S(1)}, bf16[16,2048]{1,0:T(8,128)(2,1)S(1)}, u32[]{:S(2)}, u32[]{:S(2)}) %collective-permute-start.14) | collective-permute-done | bytes 65568 | tf_op jit(solution)/shard_map/ppermute | solution.py:278
  26.1 4.4 %collective-permute-start.18 = (bf16[16,2048]{1,0:T(8,128)(2,1)S(1)}, bf16[16,2048]{1,0:T(8,128)(2,1)S(1)}, u32[]{:S(2)}, u32[]{:S(2)}) collective-permute-start(bf16[16,2048]{1,0:T(8,128)(2,1)S(1)} %shard_map.81.refs_1_), channel_id=1, source_target_pairs={{0,6},{1,7},{2,4},{3,5},{4,2},{5,3},{6,0},{7,1},{8,22},{9,23},{10,... | collective-permute-start | bytes 196616 | tf_op jit(solution)/shard_map/ppermute | solution.py:286
  30.4 1.5 %collective-permute-start.17 = (bf16[16,2048]{1,0:T(8,128)(2,1)S(1)}, bf16[16,2048]{1,0:T(8,128)(2,1)S(1)}, u32[]{:S(2)}, u32[]{:S(2)}) collective-permute-start(bf16[16,2048]{1,0:T(8,128)(2,1)S(1)} %shard_map.81.refs_1_), channel_id=1, source_target_pairs={{0,12},{1,13},{2,14},{3,15},{4,8},{5,9},{6,10},{7,11},{8,20},{9,21... | collective-permute-start | bytes 196616 | tf_op jit(solution)/shard_map/ppermute | solution.py:286
  32.0 1.5 %collective-permute-start.16 = (bf16[16,2048]{1,0:T(8,128)(2,1)S(1)}, bf16[16,2048]{1,0:T(8,128)(2,1)S(1)}, u32[]{:S(2)}, u32[]{:S(2)}) collective-permute-start(bf16[16,2048]{1,0:T(8,128)(2,1)S(1)} %shard_map.81.refs_1_), channel_id=1, source_target_pairs={{0,2},{1,3},{2,0},{3,1},{4,6},{5,7},{6,4},{7,5},{8,18},{9,19},{10,... | collective-permute-start | bytes 196616 | tf_op jit(solution)/shard_map/ppermute | solution.py:286
  34.7 1.5 %collective-permute-done.16.refs_1_ = bf16[16,2048]{1,0:T(8,128)(2,1)S(1)} collective-permute-done((bf16[16,2048]{1,0:T(8,128)(2,1)S(1)}, bf16[16,2048]{1,0:T(8,128)(2,1)S(1)}, u32[]{:S(2)}, u32[]{:S(2)}) %collective-permute-start.16) | collective-permute-done | bytes 65568 | tf_op jit(solution)/shard_map/ppermute | solution.py:286
  36.5 1.2 %collective-permute-done.19.refs_1_ = bf16[16,2048]{1,0:T(8,128)(2,1)S(1)} collective-permute-done((bf16[16,2048]{1,0:T(8,128)(2,1)S(1)}, bf16[16,2048]{1,0:T(8,128)(2,1)S(1)}, u32[]{:S(2)}, u32[]{:S(2)}) %collective-permute-start.19) | collective-permute-done | bytes 65568 | tf_op jit(solution)/shard_map/ppermute | solution.py:278
  39.1 3.6 %collective-permute-start.24 = (bf16[16,2048]{1,0:T(8,128)(2,1)S(1)}, bf16[16,2048]{1,0:T(8,128)(2,1)S(1)}, u32[]{:S(2)}, u32[]{:S(2)}) collective-permute-start(bf16[16,2048]{1,0:T(8,128)(2,1)S(1)} %shard_map.84.refs_2_), channel_id=1, source_target_pairs={{0,22},{1,23},{2,20},{3,21},{4,18},{5,19},{6,16},{7,17},{8,14},{9,... | collective-permute-start | bytes 196616 | tf_op jit(solution)/shard_map/ppermute | solution.py:286
  42.7 2.4 %collective-permute-start.23 = (bf16[16,2048]{1,0:T(8,128)(2,1)S(1)}, bf16[16,2048]{1,0:T(8,128)(2,1)S(1)}, u32[]{:S(2)}, u32[]{:S(2)}) collective-permute-start(bf16[16,2048]{1,0:T(8,128)(2,1)S(1)} %shard_map.84.refs_2_), channel_id=1, source_target_pairs={{0,4},{1,5},{2,6},{3,7},{4,0},{5,1},{6,2},{7,3},{8,20},{9,21},{10,... | collective-permute-start | bytes 196616 | tf_op jit(solution)/shard_map/ppermute | solution.py:286
  45.2 4.7 %collective-permute-start.21 = (bf16[16,2048]{1,0:T(8,128)(2,1)S(1)}, bf16[16,2048]{1,0:T(8,128)(2,1)S(1)}, u32[]{:S(2)}, u32[]{:S(2)}) collective-permute-start(bf16[16,2048]{1,0:T(8,128)(2,1)S(1)} %shard_map.84.refs_2_), channel_id=1, source_target_pairs={{0,0},{1,1},{2,2},{3,3},{4,4},{5,5},{6,6},{7,7},{8,8},{9,9},{10,10... | collective-permute-start | bytes 196616 | tf_op jit(solution)/shard_map/ppermute | solution.py:286
  50.1 1.2 %collective-permute-done.25.refs_6_.refs_5_ = bf16[8,2048]{1,0:T(8,128)(2,1)S(1)} collective-permute-done((bf16[8,2048]{1,0:T(8,128)(2,1)S(1)}, bf16[8,2048]{1,0:T(8,128)(2,1)S(1)}, u32[]{:S(2)}, u32[]{:S(2)}) %collective-permute-start.25) | collective-permute-done | bytes 32800 | tf_op jit(solution)/shard_map/ppermute | solution.py:278
  52.5 1.2 %collective-permute-done.26.refs_1_ = bf16[16,2048]{1,0:T(8,128)(2,1)S(1)} collective-permute-done((bf16[16,2048]{1,0:T(8,128)(2,1)S(1)}, bf16[16,2048]{1,0:T(8,128)(2,1)S(1)}, u32[]{:S(2)}, u32[]{:S(2)}) %collective-permute-start.26) | collective-permute-done | bytes 65568 | tf_op jit(solution)/shard_map/ppermute | solution.py:278
  53.7 1.9 %shard_map.87 = (bf16[8,4096]{1,0:T(8,128)(2,1)S(1)}, bf16[8,4096]{1,0:T(8,128)(2,1)S(1)}, bf16[8,4096]{1,0:T(8,128)(2,1)S(1)}) custom-call(bf16[16,2048]{1,0:T(8,128)(2,1)S(1)} %shard_map.86.refs_0_, bf16[16,2048]{1,0:T(8,128)(2,1)S(1)} %collective-permute-done.26.refs_1_, f32[1,4096]{1,0:T(1,128)S(1)} %copy-done.3, bf16[1,4096,512]{2,1,0:T(8,128)(2,1)S(1)} %copy-done, ...), custom_call_target="tpu_custom_call" | custom-call | flops 201326592 | bytes 12730368 | tf_op jit(solution)/shard_map/pallas_call | solution.py:24
  58.8 1.9 %collective-permute-start.30 = (bf16[2,4096]{1,0:T(2,128)(2,1)S(1)}, bf16[2,4096]{1,0:T(2,128)(2,1)S(1)}, u32[]{:S(2)}, u32[]{:S(2)}) collective-permute-start(bf16[2,4096]{1,0:T(2,128)(2,1)S(1)} %get-tuple-element.50), channel_id=1, source_target_pairs={{0,6},{1,7},{2,4},{3,5},{4,2},{5,3},{6,0},{7,1},{8,14},{9,15},{10,... | collective-permute-start | bytes 49160 | tf_op jit(solution)/shard_map/ppermute | solution.py:275
  61.9 1.6 %collective-permute-done.30.refs_3_ = bf16[2,4096]{1,0:T(2,128)(2,1)S(1)} collective-permute-done((bf16[2,4096]{1,0:T(2,128)(2,1)S(1)}, bf16[2,4096]{1,0:T(2,128)(2,1)S(1)}, u32[]{:S(2)}, u32[]{:S(2)}) %collective-permute-start.30) | collective-permute-done | bytes 16416 | tf_op jit(solution)/shard_map/ppermute | solution.py:275
  (70 shorter events, 15.7 us)
Async XLA Ops:
  1.7 3.8 %collective-permute-start = (bf16[2,4608]{1,0:T(2,128)(2,1)S(1)}, bf16[2,4608]{1,0:T(2,128)(2,1)S(1)}, u32[]{:S(2)}, u32[]{:S(2)}) collective-permute-start(bf16[2,4608]{1,0:T(2,128)(2,1)S(1)} %get-tuple-element.29), channel_id=1, source_target_pairs={{0,2},{1,3},{2,0},{3,1},{4,6},{5,7},{6,4},{7,5},{8,10},{9,11},{10,... | collective-permute-start | bytes 55304 | tf_op jit(solution)/shard_map/ppermute | solution.py:275
  3.2 3.8 %collective-permute-start.1 = (bf16[2,4608]{1,0:T(2,128)(2,1)S(1)}, bf16[2,4608]{1,0:T(2,128)(2,1)S(1)}, u32[]{:S(2)}, u32[]{:S(2)}) collective-permute-start(bf16[2,4608]{1,0:T(2,128)(2,1)S(1)} %get-tuple-element.30), channel_id=1, source_target_pairs={{0,4},{1,5},{2,6},{3,7},{4,0},{5,1},{6,2},{7,3},{8,12},{9,13},{10,... | collective-permute-start | bytes 55304 | tf_op jit(solution)/shard_map/ppermute | solution.py:275
  4.8 4.7 %collective-permute-start.2 = (bf16[2,4608]{1,0:T(2,128)(2,1)S(1)}, bf16[2,4608]{1,0:T(2,128)(2,1)S(1)}, u32[]{:S(2)}, u32[]{:S(2)}) collective-permute-start(bf16[2,4608]{1,0:T(2,128)(2,1)S(1)} %get-tuple-element.31), channel_id=1, source_target_pairs={{0,6},{1,7},{2,4},{3,5},{4,2},{5,3},{6,0},{7,1},{8,14},{9,15},{10,... | collective-permute-start | bytes 55304 | tf_op jit(solution)/shard_map/ppermute | solution.py:275
  5.2 4.2 %collective-permute-start.3 = (bf16[2,4608]{1,0:T(2,128)(2,1)S(1)}, bf16[2,4608]{1,0:T(2,128)(2,1)S(1)}, u32[]{:S(2)}, u32[]{:S(2)}) collective-permute-start(bf16[2,4608]{1,0:T(2,128)(2,1)S(1)} %get-tuple-element.28.refs_0_), channel_id=1, source_target_pairs={{0,1},{1,0},{2,3},{3,2},{4,5},{5,4},{6,7},{7,6},{8,9},{9,8},{10,11... | collective-permute-start | bytes 55304 | tf_op jit(solution)/shard_map/ppermute | solution.py:278
  5.5 3.9 %collective-permute-start.4 = (bf16[2,4608]{1,0:T(2,128)(2,1)S(1)}, bf16[2,4608]{1,0:T(2,128)(2,1)S(1)}, u32[]{:S(2)}, u32[]{:S(2)}) collective-permute-start(bf16[2,4608]{1,0:T(2,128)(2,1)S(1)} %collective-permute-done.refs_1_), channel_id=1, source_target_pairs={{0,1},{1,0},{2,3},{3,2},{4,5},{5,4},{6,7},{7,6},{8,9},{9,8},{10,11... | collective-permute-start | bytes 55304 | tf_op jit(solution)/shard_map/ppermute | solution.py:278
  7.0 2.4 %collective-permute-start.5 = (bf16[2,4608]{1,0:T(2,128)(2,1)S(1)}, bf16[2,4608]{1,0:T(2,128)(2,1)S(1)}, u32[]{:S(2)}, u32[]{:S(2)}) collective-permute-start(bf16[2,4608]{1,0:T(2,128)(2,1)S(1)} %collective-permute-done.1.refs_2_), channel_id=1, source_target_pairs={{0,1},{1,0},{2,3},{3,2},{4,5},{5,4},{6,7},{7,6},{8,9},{9,8},{10,11... | collective-permute-start | bytes 55304 | tf_op jit(solution)/shard_map/ppermute | solution.py:278
  10.8 1.3 %collective-permute-start.7 = (bf16[16,2048]{1,0:T(8,128)(2,1)S(1)}, bf16[16,2048]{1,0:T(8,128)(2,1)S(1)}, u32[]{:S(2)}, u32[]{:S(2)}) collective-permute-start(bf16[16,2048]{1,0:T(8,128)(2,1)S(1)} %get-tuple-element.34), channel_id=1, source_target_pairs={{0,1},{1,0},{2,3},{3,2},{4,5},{5,4},{6,7},{7,6},{8,9},{9,8},{10,11... | collective-permute-start | bytes 196616 | tf_op jit(solution)/shard_map/ppermute | solution.py:278
  12.2 10.9 %collective-permute-start.11 = (bf16[16,2048]{1,0:T(8,128)(2,1)S(1)}, bf16[16,2048]{1,0:T(8,128)(2,1)S(1)}, u32[]{:S(2)}, u32[]{:S(2)}) collective-permute-start(bf16[16,2048]{1,0:T(8,128)(2,1)S(1)} %shard_map.77.refs_0_), channel_id=1, source_target_pairs={{0,14},{1,15},{2,12},{3,13},{4,10},{5,11},{6,8},{7,9},{8,22},{9,23... | collective-permute-start | bytes 196616 | tf_op jit(solution)/shard_map/ppermute | solution.py:286
  12.8 10.4 %collective-permute-start.10 = (bf16[16,2048]{1,0:T(8,128)(2,1)S(1)}, bf16[16,2048]{1,0:T(8,128)(2,1)S(1)}, u32[]{:S(2)}, u32[]{:S(2)}) collective-permute-start(bf16[16,2048]{1,0:T(8,128)(2,1)S(1)} %shard_map.77.refs_0_), channel_id=1, source_target_pairs={{0,12},{1,13},{2,14},{3,15},{4,8},{5,9},{6,10},{7,11},{8,28},{9,29... | collective-permute-start | bytes 196616 | tf_op jit(solution)/shard_map/ppermute | solution.py:286
  15.0 8.2 %collective-permute-start.9 = (bf16[16,2048]{1,0:T(8,128)(2,1)S(1)}, bf16[16,2048]{1,0:T(8,128)(2,1)S(1)}, u32[]{:S(2)}, u32[]{:S(2)}) collective-permute-start(bf16[16,2048]{1,0:T(8,128)(2,1)S(1)} %shard_map.77.refs_0_), channel_id=1, source_target_pairs={{0,10},{1,11},{2,8},{3,9},{4,14},{5,15},{6,12},{7,13},{8,2},{9,3},... | collective-permute-start | bytes 196616 | tf_op jit(solution)/shard_map/ppermute | solution.py:286
  16.4 6.7 %collective-permute-start.8 = (bf16[16,2048]{1,0:T(8,128)(2,1)S(1)}, bf16[16,2048]{1,0:T(8,128)(2,1)S(1)}, u32[]{:S(2)}, u32[]{:S(2)}) collective-permute-start(bf16[16,2048]{1,0:T(8,128)(2,1)S(1)} %shard_map.77.refs_0_), channel_id=1, source_target_pairs={{0,8},{1,9},{2,10},{3,11},{4,12},{5,13},{6,14},{7,15},{8,0},{9,1},... | collective-permute-start | bytes 196616 | tf_op jit(solution)/shard_map/ppermute | solution.py:286
  17.1 5.7 %collective-permute-start.12 = (bf16[16,128]{1,0:T(8,128)(2,1)S(1)}, bf16[16,128]{1,0:T(8,128)(2,1)S(1)}, u32[]{:S(2)}, u32[]{:S(2)}) collective-permute-start(bf16[16,128]{1,0:T(8,128)(2,1)S(1)} %get-tuple-element.37.current), channel_id=1, source_target_pairs={{0,8},{1,9},{2,10},{3,11},{4,12},{5,13},{6,14},{7,15},{8,16},{9,17... | collective-permute-start | bytes 12296 | tf_op jit(solution)/shard_map/ppermute | solution.py:286
  23.4 1.3 %collective-permute-start.13 = (bf16[16,2048]{1,0:T(8,128)(2,1)S(1)}, bf16[16,2048]{1,0:T(8,128)(2,1)S(1)}, u32[]{:S(2)}, u32[]{:S(2)}) collective-permute-start(bf16[16,2048]{1,0:T(8,128)(2,1)S(1)} %shard_map.79.refs_0_.refs_2_), channel_id=1, source_target_pairs={{0,1},{1,0},{2,3},{3,2},{4,5},{5,4},{6,7},{7,6},{8,9},{9,8},{10,11... | collective-permute-start | bytes 196616 | tf_op jit(solution)/shard_map/ppermute | solution.py:278
  26.1 8.0 %collective-permute-start.18 = (bf16[16,2048]{1,0:T(8,128)(2,1)S(1)}, bf16[16,2048]{1,0:T(8,128)(2,1)S(1)}, u32[]{:S(2)}, u32[]{:S(2)}) collective-permute-start(bf16[16,2048]{1,0:T(8,128)(2,1)S(1)} %shard_map.81.refs_1_), channel_id=1, source_target_pairs={{0,6},{1,7},{2,4},{3,5},{4,2},{5,3},{6,0},{7,1},{8,22},{9,23},{10,... | collective-permute-start | bytes 196616 | tf_op jit(solution)/shard_map/ppermute | solution.py:286
  30.4 4.3 %collective-permute-start.17 = (bf16[16,2048]{1,0:T(8,128)(2,1)S(1)}, bf16[16,2048]{1,0:T(8,128)(2,1)S(1)}, u32[]{:S(2)}, u32[]{:S(2)}) collective-permute-start(bf16[16,2048]{1,0:T(8,128)(2,1)S(1)} %shard_map.81.refs_1_), channel_id=1, source_target_pairs={{0,12},{1,13},{2,14},{3,15},{4,8},{5,9},{6,10},{7,11},{8,20},{9,21... | collective-permute-start | bytes 196616 | tf_op jit(solution)/shard_map/ppermute | solution.py:286
  32.0 4.3 %collective-permute-start.16 = (bf16[16,2048]{1,0:T(8,128)(2,1)S(1)}, bf16[16,2048]{1,0:T(8,128)(2,1)S(1)}, u32[]{:S(2)}, u32[]{:S(2)}) collective-permute-start(bf16[16,2048]{1,0:T(8,128)(2,1)S(1)} %shard_map.81.refs_1_), channel_id=1, source_target_pairs={{0,2},{1,3},{2,0},{3,1},{4,6},{5,7},{6,4},{7,5},{8,18},{9,19},{10,... | collective-permute-start | bytes 196616 | tf_op jit(solution)/shard_map/ppermute | solution.py:286
  33.4 2.8 %collective-permute-start.15 = (bf16[16,2048]{1,0:T(8,128)(2,1)S(1)}, bf16[16,2048]{1,0:T(8,128)(2,1)S(1)}, u32[]{:S(2)}, u32[]{:S(2)}) collective-permute-start(bf16[16,2048]{1,0:T(8,128)(2,1)S(1)} %shard_map.81.refs_1_), channel_id=1, source_target_pairs={{0,0},{1,1},{2,2},{3,3},{4,4},{5,5},{6,6},{7,7},{8,16},{9,17},{10,... | collective-permute-start | bytes 196616 | tf_op jit(solution)/shard_map/ppermute | solution.py:286
  39.1 12.2 %collective-permute-start.24 = (bf16[16,2048]{1,0:T(8,128)(2,1)S(1)}, bf16[16,2048]{1,0:T(8,128)(2,1)S(1)}, u32[]{:S(2)}, u32[]{:S(2)}) collective-permute-start(bf16[16,2048]{1,0:T(8,128)(2,1)S(1)} %shard_map.84.refs_2_), channel_id=1, source_target_pairs={{0,22},{1,23},{2,20},{3,21},{4,18},{5,19},{6,16},{7,17},{8,14},{9,... | collective-permute-start | bytes 196616 | tf_op jit(solution)/shard_map/ppermute | solution.py:286
  42.7 8.6 %collective-permute-start.23 = (bf16[16,2048]{1,0:T(8,128)(2,1)S(1)}, bf16[16,2048]{1,0:T(8,128)(2,1)S(1)}, u32[]{:S(2)}, u32[]{:S(2)}) collective-permute-start(bf16[16,2048]{1,0:T(8,128)(2,1)S(1)} %shard_map.84.refs_2_), channel_id=1, source_target_pairs={{0,4},{1,5},{2,6},{3,7},{4,0},{5,1},{6,2},{7,3},{8,20},{9,21},{10,... | collective-permute-start | bytes 196616 | tf_op jit(solution)/shard_map/ppermute | solution.py:286
  45.1 6.2 %collective-permute-start.22 = (bf16[16,2048]{1,0:T(8,128)(2,1)S(1)}, bf16[16,2048]{1,0:T(8,128)(2,1)S(1)}, u32[]{:S(2)}, u32[]{:S(2)}) collective-permute-start(bf16[16,2048]{1,0:T(8,128)(2,1)S(1)} %shard_map.84.refs_2_), channel_id=1, source_target_pairs={{0,2},{1,3},{2,0},{3,1},{4,6},{5,7},{6,4},{7,5},{8,10},{9,11},{10,... | collective-permute-start | bytes 196616 | tf_op jit(solution)/shard_map/ppermute | solution.py:286
  45.2 7.0 %collective-permute-start.21 = (bf16[16,2048]{1,0:T(8,128)(2,1)S(1)}, bf16[16,2048]{1,0:T(8,128)(2,1)S(1)}, u32[]{:S(2)}, u32[]{:S(2)}) collective-permute-start(bf16[16,2048]{1,0:T(8,128)(2,1)S(1)} %shard_map.84.refs_2_), channel_id=1, source_target_pairs={{0,0},{1,1},{2,2},{3,3},{4,4},{5,5},{6,6},{7,7},{8,8},{9,9},{10,10... | collective-permute-start | bytes 196616 | tf_op jit(solution)/shard_map/ppermute | solution.py:286
  57.2 3.8 %collective-permute-start.28 = (bf16[2,4096]{1,0:T(2,128)(2,1)S(1)}, bf16[2,4096]{1,0:T(2,128)(2,1)S(1)}, u32[]{:S(2)}, u32[]{:S(2)}) collective-permute-start(bf16[2,4096]{1,0:T(2,128)(2,1)S(1)} %get-tuple-element.48), channel_id=1, source_target_pairs={{0,2},{1,3},{2,0},{3,1},{4,6},{5,7},{6,4},{7,5},{8,10},{9,11},{10,... | collective-permute-start | bytes 49160 | tf_op jit(solution)/shard_map/ppermute | solution.py:275
  58.1 3.7 %collective-permute-start.29 = (bf16[2,4096]{1,0:T(2,128)(2,1)S(1)}, bf16[2,4096]{1,0:T(2,128)(2,1)S(1)}, u32[]{:S(2)}, u32[]{:S(2)}) collective-permute-start(bf16[2,4096]{1,0:T(2,128)(2,1)S(1)} %get-tuple-element.49), channel_id=1, source_target_pairs={{0,4},{1,5},{2,6},{3,7},{4,0},{5,1},{6,2},{7,3},{8,12},{9,13},{10,... | collective-permute-start | bytes 49160 | tf_op jit(solution)/shard_map/ppermute | solution.py:275
  58.8 4.6 %collective-permute-start.30 = (bf16[2,4096]{1,0:T(2,128)(2,1)S(1)}, bf16[2,4096]{1,0:T(2,128)(2,1)S(1)}, u32[]{:S(2)}, u32[]{:S(2)}) collective-permute-start(bf16[2,4096]{1,0:T(2,128)(2,1)S(1)} %get-tuple-element.50), channel_id=1, source_target_pairs={{0,6},{1,7},{2,4},{3,5},{4,2},{5,3},{6,0},{7,1},{8,14},{9,15},{10,... | collective-permute-start | bytes 49160 | tf_op jit(solution)/shard_map/ppermute | solution.py:275
  (14 other events, 51.6 us)
where the time goes:
time: 64.5 us; the launch traced here: 64.3 us
  starting transfers between devices  36.5 us (57%)
  waiting for transfers between devices  21.5 us (33%)
  Pallas kernels  4.74 us (7%)
  local copies, waits for them, and re-layouts  1.39 us (2%)
    ppermute x13, starting transfers between devices, onward(): return lax.ppermute(value, ('section', 'expert'), pairs)  28.1 us
    ppermute x12, waiting for transfers between devices, within(): return lax.ppermute(value, 'expert', [(d, d ^ m) for d in range(peers)])  10.5 us
    ppermute x6, starting transfers between devices, across(): return lax.ppermute(value, 'expert', pairs)  7.11 us
    ppermute x6, waiting for transfers between devices, across(): return lax.ppermute(value, 'expert', pairs)  6.65 us
    pallas_call x17, Pallas kernels, call(): pl.pallas_call(kernel, out_shape=outs, in_specs=specs or [VMEM] * len(arg...  4.74 us
    ppermute x13, waiting for transfers between devices, onward(): return lax.ppermute(value, ('section', 'expert'), pairs)  4.36 us
    unnamed x14, local copies, waits for them, and re-layouts  1.39 us
    ppermute x12, starting transfers between devices, within(): return lax.ppermute(value, 'expert', [(d, d ^ m) for d in range(peers)])  1.31 us
  transfers between devices with their start and end apart: 31, of which 19 were waited for; matrix products, arithmetic and copies ran while one was open for 0% of the time, Pallas kernels for 1%

commit v1 on v0

--- a/solution.py
+++ b/solution.py
@@ -18,7 +18,7 @@
 VMEM = pl.BlockSpec(memory_space=pltpu.VMEM)
 
 
-def call(kernel, outs, args, limit=2 << 20, scratch=(), flops=1000, specs=None, moved=None):
+def call(kernel, outs, args, limit=4 << 20, scratch=(), flops=1000, specs=None, moved=None):
     if moved is None:
         moved = sum(a.size * a.dtype.itemsize for a in args)
     return pl.pallas_call(
@@ -79,24 +79,21 @@
             outs[i][:, at : at + rows] = jnp.broadcast_to(piece, (CAP, rows)).astype(BF16)
 
 
-def expert_math(values, gain, w_gate, w_up, w_down, parts):
-    inverse = lax.rsqrt(jnp.mean(values * values, axis=-1, keepdims=True) + 1e-06)
-    normed = (values * inverse * gain[...]).astype(BF16)
-    gate = jnp.dot(normed, w_gate[0], preferred_element_type=F32)
-    upward = jnp.dot(normed, w_up[0], preferred_element_type=F32)
-    hidden = (gate / (1.0 + jnp.exp(-gate)) * upward).astype(BF16)
-    step = 512
-    for at in range(0, values.shape[1], step):
-        parts[:, at : at + step] = jnp.dot(
-            hidden, w_down[0, :, at : at + step], preferred_element_type=F32
-        )
-
-
-def deal(parts, chunks, own, group):
-    width = chunks[0].shape[1]
-    for m in range(group):
-        at = pl.multiple_of((own ^ m) * width, width)
-        chunks[m][...] = parts[:, pl.ds(at, width)].astype(BF16)
+def hidden_of(gate, upward):
+    return (gate / (1.0 + jnp.exp(-gate)) * upward).astype(BF16)
+
+
+def down(hidden, w_down, first, out):
+    step = min(512, out.shape[1])
+    for n in range(0, out.shape[1], step):
+        at = first + n if isinstance(first, int) else pl.multiple_of(first + n, step)
+        out[:, n : n + step] = jnp.dot(
+            hidden, w_down[0, :, pl.ds(at, step)], preferred_element_type=F32
+        ).astype(out.dtype)
+
+
+def active(tick):
+    return pl.when(lax.axis_index("section") == tick)
 
 
 def deal_rows(source, blocks, own):
@@ -124,25 +121,81 @@
     whole[...] = rows[:, 0:width].astype(BF16)
 
 
-def expert_kernel(group, tick, count, last, *refs):
-    pieces = refs[:count]
-    gain, w_gate, w_up, w_down = refs[count : count + 4]
-    outs = refs[count + 4 : count + 4 + group]
-    rows, parts = refs[-2:]
-    _, own = place(group)
-
-    @pl.when(lax.axis_index("section") == tick)
-    def _():
-        width = pieces[0].shape[1]
-        for m in range(count):
-            at = pl.multiple_of((own ^ m) * width, width) if count > 1 else 0
-            rows[:, pl.ds(at, width)] = pieces[m][...].astype(F32)
-        expert_math(rows[...], gain, w_gate, w_up, w_down, parts)
+def whole_kernel(group, tick, rows, gain, w_gate, w_up, w_down, *outs):
+    _, own = place(group)
+
+    @active(tick)
+    def _():
+        values = rows[...].astype(F32)
+        inverse = lax.rsqrt(jnp.mean(values * values, axis=-1, keepdims=True) + 1e-06)
+        normed = (values * inverse * gain[...]).astype(BF16)
+        gate = jnp.dot(normed, w_gate[0], preferred_element_type=F32)
+        upward = jnp.dot(normed, w_up[0], preferred_element_type=F32)
+        hidden = hidden_of(gate, upward)
+        outs[0][...] = hidden
+        width = outs[1].shape[1]
+        for m in range(1, group):
+            down(hidden, w_down, pl.multiple_of((own ^ m) * width, width), outs[m])
+
+
+def products(half, at, gain, w_gate, w_up):
+    width = half.shape[1]
+    values = half[...].astype(F32)
+    scaled = (values * gain[:, pl.ds(at, width)]).astype(BF16)
+    gate = jnp.dot(scaled, w_gate[0, pl.ds(at, width), :], preferred_element_type=F32)
+    upward = jnp.dot(scaled, w_up[0, pl.ds(at, width), :], preferred_element_type=F32)
+    return gate, upward, jnp.sum(values * values, axis=-1, keepdims=True)
+
+
+def half_kernel(group, tick, half, gain, w_gate, w_up, gate_out, up_out, square_out):
+    _, own = place(group)
+
+    @active(tick)
+    def _():
+        width = half.shape[1]
+        at = pl.multiple_of(own * width, width)
+        gate, upward, square = products(half, at, gain, w_gate, w_up)
+        gate_out[...] = gate
+        up_out[...] = upward
+        square_out[...] = jnp.broadcast_to(square, square_out.shape)
+
+
+def rest_kernel(group, tick, last, *refs):
+    halves = refs[:group]
+    gate_in, up_in, square_in, gain, w_gate, w_up, w_down = refs[group : group + 7]
+    outs = refs[group + 7 :]
+    _, own = place(group)
+
+    @active(tick)
+    def _():
+        gate, upward, square = gate_in[...], up_in[...], square_in[:, 0:1]
+        width = halves[0].shape[1]
+        for m in range(1, group):
+            at = pl.multiple_of((own ^ m) * width, width)
+            more = products(halves[m], at, gain, w_gate, w_up)
+            gate, upward, square = gate + more[0], upward + more[1], square + more[2]
+        inverse = lax.rsqrt(square / gain.shape[1] + 1e-06)
+        hidden = hidden_of(gate * inverse, upward * inverse)
         if last:
-            deal_rows(parts, outs, own)
-            deal_rows(rows, refs[count + 4 + group : count + 5 + group], own)
+            rows, parts = outs[-2:]
+            for m in range(group):
+                at = pl.multiple_of((own ^ m) * width, width)
+                rows[:, pl.ds(at, width)] = halves[m][...].astype(F32)
+            down(hidden, w_down, 0, parts)
+            deal_rows(parts, outs[:group], own)
+            deal_rows(rows, outs[group : group + 1], own)
         else:
-            deal(parts, outs, own, group)
+            outs[0][...] = hidden
+            for m in range(1, group):
+                down(hidden, w_down, pl.multiple_of((own ^ m) * width, width), outs[m])
+
+
+def own_kernel(group, tick, hidden, w_down, out):
+    _, own = place(group)
+
+    @active(tick)
+    def _():
+        down(hidden[...], w_down, pl.multiple_of(own * out.shape[1], out.shape[1]), out)
 
 
 def slot_codes(expert, dims):
@@ -277,13 +330,20 @@
     def within(value, m):
         return lax.ppermute(value, "expert", [(d, d ^ m) for d in range(peers)])
 
-    def onward(value, hops, i):
+    def onward(value, hops, moves):
         pairs = [
-            (s * peers + d, hops[s] * peers + (d // group ^ i) * group + d % group)
+            (s * peers + d, hops[s] * peers + (d // group ^ moves[s]) * group + d % group)
             for s in range(sections)
             for d in range(peers)
         ]
         return lax.ppermute(value, ("section", "expert"), pairs)
+
+    def gather(value, tick):
+        outs = []
+        for i in range(EXPERTS):
+            moves = [i if s == tick else 0 for s in range(sections)]
+            outs.append(onward(value, cycle(tick, EXPERTS - 1 - i), moves))
+        return outs
 
     def cycle(tick, turn):
         hops = list(range(sections))
@@ -312,18 +372,16 @@
         tuple(pieces),
         scratch=[pltpu.VMEM((slots, wide), F32), pltpu.VMEM((rows, wide), F32)],
     )
-    before = onward(position, [(s + 1) % sections for s in range(sections)], 0)
+    before = onward(position, [(s + 1) % sections for s in range(sections)], [0] * sections)
     choice = call(
         functools.partial(choice_kernel, group), shape((EXPERTS, rows, rows)), (position, before)
     )
     saved = []
-    pieces = [whole]
+    inner = w_gate.shape[2]
     for tick in range(sections):
         last = tick == sections - 1
         if tick:
-            gathered = [
-                onward(saved[-1], cycle(tick - 1, EXPERTS - 1 - i), i) for i in range(EXPERTS)
-            ]
+            gathered = gather(saved[-1], tick - 1)
             kept = []
             if last:
                 kept = call(
@@ -334,16 +392,43 @@
                 )
                 kept = [kept[0]] + [within(kept[m], m) for m in range(1, group)]
             half = call(pick_kernel, shape((rows, chunk)), (*gathered, choice, *kept))
-            pieces = [half] + [within(half, m) for m in range(1, group)]
-        parts = call(
-            functools.partial(expert_kernel, group, tick, len(pieces), last),
-            [shape((slots, width))] * (group + 1) if last else [shape((rows, chunk))] * group,
-            (*pieces, *weights),
-            limit=4 << 20,
-            scratch=[pltpu.VMEM((rows, width), F32), pltpu.VMEM((rows, width), F32)],
-            flops=flops,
-        )
-        terms = [parts[0]] + [within(parts[m], m) for m in range(1, group)]
+            halves = [half] + [within(half, m) for m in range(1, group)]
+            begun = call(
+                functools.partial(half_kernel, group, tick),
+                [shape((rows, inner), F32)] * 2 + [shape((rows, LANES), F32)],
+                (half, *weights[:3]),
+                flops=flops // (3 * group) * 2,
+            )
+            outs = [shape((rows, inner))] + [shape((rows, chunk))] * (group - 1)
+            scratch = []
+            if last:
+                outs = [shape((slots, width))] * (group + 1)
+                scratch = [pltpu.VMEM((rows, width), F32)] * 2
+            outs = call(
+                functools.partial(rest_kernel, group, tick, last),
+                outs,
+                (*halves, *begun, *weights),
+                scratch=scratch,
+                flops=flops // 2,
+            )
+        else:
+            outs = call(
+                functools.partial(whole_kernel, group, tick),
+                [shape((rows, inner))] + [shape((rows, chunk))] * (group - 1),
+                (whole, *weights),
+                flops=flops * 5 // 6,
+            )
+        terms = [within(outs[m], m) for m in range(1, group)]
+        if last:
+            terms = [outs[0]] + terms
+        else:
+            own = call(
+                functools.partial(own_kernel, group, tick),
+                shape((rows, chunk)),
+                (outs[0], w_down),
+                flops=flops // 6,
+            )
+            terms = [own] + terms
         if not last:
             saved.append(
                 call(
@@ -355,7 +440,7 @@
     leaving = call(
         functools.partial(leave_kernel, group),
         [shape((CAP, width))] * EXPERTS,
-        (*terms, parts[group], table, *kept),
+        (*terms, outs[group], table, *kept),
         scratch=[pltpu.VMEM((rows, LANES), F32), pltpu.VMEM((slots, width), F32)],
     )
     back = [across(leaving[i], i) for i in range(EXPERTS)]

time: 64.5 us -> 74.4 us (1.15)
  starting transfers between devices: 36.5 us -> 47.5 us
  waiting for transfers between devices: 21.5 us -> 20 us
    ppermute x13, starting transfers between devices: 28.1 us -> 39 us  [onward(): return lax.ppermute(value, ('section', 'expert'), pairs)]
    pallas_call x17 -> x23, Pallas kernels: 4.74 us -> 4.8 us  [call(): pl.pallas_call(kernel, out_shape=outs, in_specs=specs or [VMEM] * len(arg...]
  transfers between devices with their start and end apart: 31 -> 31, of which waited for: 19 -> 17; matrix products, arithmetic and copies ran while one was open for 0% -> 0% of each run, Pallas kernels for 1% -> 1%
where the time goes in v1:
time: 74.4 us; the launch traced here: 74 us
  starting transfers between devices  47.5 us (64%)
  waiting for transfers between devices  20 us (27%)
  Pallas kernels  4.8 us (6%)
  local copies, waits for them, and re-layouts  1.39 us (2%)
    ppermute x13, starting transfers between devices, onward(): return lax.ppermute(value, ('section', 'expert'), pairs)  39 us
    ppermute x12, waiting for transfers between devices, within(): return lax.ppermute(value, 'expert', [(d, d ^ m) for d in range(peers)])  9.75 us
    ppermute x6, starting transfers between devices, across(): return lax.ppermute(value, 'expert', pairs)  7.11 us
    ppermute x6, waiting for transfers between devices, across(): return lax.ppermute(value, 'expert', pairs)  6.46 us
    pallas_call x23, Pallas kernels, call(): pl.pallas_call(kernel, out_shape=outs, in_specs=specs or [VMEM] * len(arg...  4.8 us
    ppermute x13, waiting for transfers between devices, onward(): return lax.ppermute(value, ('section', 'expert'), pairs)  3.78 us
  transfers between devices with their start and end apart: 31, of which 17 were waited for; matrix products, arithmetic and copies ran while one was open for 0% of the time, Pallas kernels for 1%

profile of v1, /device:TPU:24, one launch (start us, length us, event | category | flops | bytes accessed | tf_op | source)
XLA Modules:
  0.0 74.0 jit_solution(5767795523083636536)
XLA Ops:
  1.7 1.6 %collective-permute-start = (bf16[2,4608]{1,0:T(2,128)(2,1)S(1)}, bf16[2,4608]{1,0:T(2,128)(2,1)S(1)}, u32[]{:S(2)}, u32[]{:S(2)}) collective-permute-start(bf16[2,4608]{1,0:T(2,128)(2,1)S(1)} %get-tuple-element.38), channel_id=1, source_target_pairs={{0,2},{1,3},{2,0},{3,1},{4,6},{5,7},{6,4},{7,5},{8,10},{9,11},{10,... | collective-permute-start | bytes 55304 | tf_op jit(solution)/shard_map/ppermute | solution.py:328
  3.2 1.5 %collective-permute-start.1 = (bf16[2,4608]{1,0:T(2,128)(2,1)S(1)}, bf16[2,4608]{1,0:T(2,128)(2,1)S(1)}, u32[]{:S(2)}, u32[]{:S(2)}) collective-permute-start(bf16[2,4608]{1,0:T(2,128)(2,1)S(1)} %get-tuple-element.39), channel_id=1, source_target_pairs={{0,4},{1,5},{2,6},{3,7},{4,0},{5,1},{6,2},{7,3},{8,12},{9,13},{10,... | collective-permute-start | bytes 55304 | tf_op jit(solution)/shard_map/ppermute | solution.py:328
  5.7 1.2 %collective-permute-done.1.refs_2_ = bf16[2,4608]{1,0:T(2,128)(2,1)S(1)} collective-permute-done((bf16[2,4608]{1,0:T(2,128)(2,1)S(1)}, bf16[2,4608]{1,0:T(2,128)(2,1)S(1)}, u32[]{:S(2)}, u32[]{:S(2)}) %collective-permute-start.1) | collective-permute-done | bytes 18464 | tf_op jit(solution)/shard_map/ppermute | solution.py:328
  7.0 2.4 %collective-permute-done.2.refs_3_ = bf16[2,4608]{1,0:T(2,128)(2,1)S(1)} collective-permute-done((bf16[2,4608]{1,0:T(2,128)(2,1)S(1)}, bf16[2,4608]{1,0:T(2,128)(2,1)S(1)}, u32[]{:S(2)}, u32[]{:S(2)}) %collective-permute-start.2) | collective-permute-done | bytes 18464 | tf_op jit(solution)/shard_map/ppermute | solution.py:328
  9.4 1.2 %collective-permute-done.6.refs_7_ = bf16[2,4608]{1,0:T(2,128)(2,1)S(1)} collective-permute-done((bf16[2,4608]{1,0:T(2,128)(2,1)S(1)}, bf16[2,4608]{1,0:T(2,128)(2,1)S(1)}, u32[]{:S(2)}, u32[]{:S(2)}) %collective-permute-start.6) | collective-permute-done | bytes 18464 | tf_op jit(solution)/shard_map/ppermute | solution.py:331
  11.0 1.1 %collective-permute-done.7.refs_1_ = bf16[16,2048]{1,0:T(8,128)(2,1)S(1)} collective-permute-done((bf16[16,2048]{1,0:T(8,128)(2,1)S(1)}, bf16[16,2048]{1,0:T(8,128)(2,1)S(1)}, u32[]{:S(2)}, u32[]{:S(2)}) %collective-permute-start.7) | collective-permute-done | bytes 65568 | tf_op jit(solution)/shard_map/ppermute | solution.py:331
  12.9 5.0 %collective-permute-start.10 = (bf16[16,2048]{1,0:T(8,128)(2,1)S(1)}, bf16[16,2048]{1,0:T(8,128)(2,1)S(1)}, u32[]{:S(2)}, u32[]{:S(2)}) collective-permute-start(bf16[16,2048]{1,0:T(8,128)(2,1)S(1)} %shard_map.78.refs_0_), channel_id=1, source_target_pairs={{0,12},{1,13},{2,14},{3,15},{4,8},{5,9},{6,10},{7,11},{8,24},{9,25... | collective-permute-start | bytes 196616 | tf_op jit(solution)/shard_map/ppermute | solution.py:339
  19.2 6.1 %collective-permute-start.12 = (bf16[16,128]{1,0:T(8,128)(2,1)S(1)}, bf16[16,128]{1,0:T(8,128)(2,1)S(1)}, u32[]{:S(2)}, u32[]{:S(2)}) collective-permute-start(bf16[16,128]{1,0:T(8,128)(2,1)S(1)} %get-tuple-element.46.current), channel_id=1, source_target_pairs={{0,8},{1,9},{2,10},{3,11},{4,12},{5,13},{6,14},{7,15},{8,16},{9,17... | collective-permute-start | bytes 12296 | tf_op jit(solution)/shard_map/ppermute | solution.py:339
  25.3 1.3 %collective-permute-done.12.before = bf16[16,128]{1,0:T(8,128)(2,1)S(1)} collective-permute-done((bf16[16,128]{1,0:T(8,128)(2,1)S(1)}, bf16[16,128]{1,0:T(8,128)(2,1)S(1)}, u32[]{:S(2)}, u32[]{:S(2)}) %collective-permute-start.12) | collective-permute-done | bytes 4128 | tf_op jit(solution)/shard_map/ppermute | solution.py:339
  27.4 1.2 %collective-permute-done.13.refs_1_ = bf16[16,2048]{1,0:T(8,128)(2,1)S(1)} collective-permute-done((bf16[16,2048]{1,0:T(8,128)(2,1)S(1)}, bf16[16,2048]{1,0:T(8,128)(2,1)S(1)}, u32[]{:S(2)}, u32[]{:S(2)}) %collective-permute-start.13) | collective-permute-done | bytes 65568 | tf_op jit(solution)/shard_map/ppermute | solution.py:331
  28.7 1.1 %collective-permute-done.14.refs_1_ = bf16[16,2048]{1,0:T(8,128)(2,1)S(1)} collective-permute-done((bf16[16,2048]{1,0:T(8,128)(2,1)S(1)}, bf16[16,2048]{1,0:T(8,128)(2,1)S(1)}, u32[]{:S(2)}, u32[]{:S(2)}) %collective-permute-start.14) | collective-permute-done | bytes 65568 | tf_op jit(solution)/shard_map/ppermute | solution.py:331
  29.9 4.4 %collective-permute-start.18 = (bf16[16,2048]{1,0:T(8,128)(2,1)S(1)}, bf16[16,2048]{1,0:T(8,128)(2,1)S(1)}, u32[]{:S(2)}, u32[]{:S(2)}) collective-permute-start(bf16[16,2048]{1,0:T(8,128)(2,1)S(1)} %shard_map.84.refs_1_), channel_id=1, source_target_pairs={{0,0},{1,1},{2,2},{3,3},{4,4},{5,5},{6,6},{7,7},{8,22},{9,23},{10,... | collective-permute-start | bytes 196616 | tf_op jit(solution)/shard_map/ppermute | solution.py:339
  36.7 1.2 %collective-permute-done.19.refs_1_ = bf16[16,2048]{1,0:T(8,128)(2,1)S(1)} collective-permute-done((bf16[16,2048]{1,0:T(8,128)(2,1)S(1)}, bf16[16,2048]{1,0:T(8,128)(2,1)S(1)}, u32[]{:S(2)}, u32[]{:S(2)}) %collective-permute-start.19) | collective-permute-done | bytes 65568 | tf_op jit(solution)/shard_map/ppermute | solution.py:331
  38.0 1.1 %collective-permute-done.20.refs_1_ = bf16[16,2048]{1,0:T(8,128)(2,1)S(1)} collective-permute-done((bf16[16,2048]{1,0:T(8,128)(2,1)S(1)}, bf16[16,2048]{1,0:T(8,128)(2,1)S(1)}, u32[]{:S(2)}, u32[]{:S(2)}) %collective-permute-start.20) | collective-permute-done | bytes 65568 | tf_op jit(solution)/shard_map/ppermute | solution.py:331
  39.2 7.3 %collective-permute-start.24 = (bf16[16,2048]{1,0:T(8,128)(2,1)S(1)}, bf16[16,2048]{1,0:T(8,128)(2,1)S(1)}, u32[]{:S(2)}, u32[]{:S(2)}) collective-permute-start(bf16[16,2048]{1,0:T(8,128)(2,1)S(1)} %shard_map.89.refs_2_), channel_id=1, source_target_pairs={{0,16},{1,17},{2,18},{3,19},{4,20},{5,21},{6,22},{7,23},{8,8},{9,9... | collective-permute-start | bytes 196616 | tf_op jit(solution)/shard_map/ppermute | solution.py:339
  46.6 5.6 %collective-permute-start.23 = (bf16[16,2048]{1,0:T(8,128)(2,1)S(1)}, bf16[16,2048]{1,0:T(8,128)(2,1)S(1)}, u32[]{:S(2)}, u32[]{:S(2)}) collective-permute-start(bf16[16,2048]{1,0:T(8,128)(2,1)S(1)} %shard_map.89.refs_2_), channel_id=1, source_target_pairs={{0,0},{1,1},{2,2},{3,3},{4,4},{5,5},{6,6},{7,7},{8,16},{9,17},{10,... | collective-permute-start | bytes 196616 | tf_op jit(solution)/shard_map/ppermute | solution.py:339
  52.1 4.4 %collective-permute-start.22 = (bf16[16,2048]{1,0:T(8,128)(2,1)S(1)}, bf16[16,2048]{1,0:T(8,128)(2,1)S(1)}, u32[]{:S(2)}, u32[]{:S(2)}) collective-permute-start(bf16[16,2048]{1,0:T(8,128)(2,1)S(1)} %shard_map.89.refs_2_), channel_id=1, source_target_pairs={{0,0},{1,1},{2,2},{3,3},{4,4},{5,5},{6,6},{7,7},{8,8},{9,9},{10,10... | collective-permute-start | bytes 196616 | tf_op jit(solution)/shard_map/ppermute | solution.py:339
  56.5 2.4 %collective-permute-start.21 = (bf16[16,2048]{1,0:T(8,128)(2,1)S(1)}, bf16[16,2048]{1,0:T(8,128)(2,1)S(1)}, u32[]{:S(2)}, u32[]{:S(2)}) collective-permute-start(bf16[16,2048]{1,0:T(8,128)(2,1)S(1)} %shard_map.89.refs_2_), channel_id=1, source_target_pairs={{0,0},{1,1},{2,2},{3,3},{4,4},{5,5},{6,6},{7,7},{8,8},{9,9},{10,10... | collective-permute-start | bytes 196616 | tf_op jit(solution)/shard_map/ppermute | solution.py:339
  59.0 1.2 %collective-permute-done.25.refs_6_.refs_5_ = bf16[8,2048]{1,0:T(8,128)(2,1)S(1)} collective-permute-done((bf16[8,2048]{1,0:T(8,128)(2,1)S(1)}, bf16[8,2048]{1,0:T(8,128)(2,1)S(1)}, u32[]{:S(2)}, u32[]{:S(2)}) %collective-permute-start.25) | collective-permute-done | bytes 32800 | tf_op jit(solution)/shard_map/ppermute | solution.py:331
  60.3 2.4 %collective-permute-done.21.refs_0_ = bf16[16,2048]{1,0:T(8,128)(2,1)S(1)} collective-permute-done((bf16[16,2048]{1,0:T(8,128)(2,1)S(1)}, bf16[16,2048]{1,0:T(8,128)(2,1)S(1)}, u32[]{:S(2)}, u32[]{:S(2)}) %collective-permute-start.21) | collective-permute-done | bytes 65568 | tf_op jit(solution)/shard_map/ppermute | solution.py:339
  64.2 1.3 %shard_map.93 = (bf16[8,4096]{1,0:T(8,128)(2,1)S(1)}, bf16[8,4096]{1,0:T(8,128)(2,1)S(1)}, bf16[8,4096]{1,0:T(8,128)(2,1)S(1)}) custom-call(bf16[16,2048]{1,0:T(8,128)(2,1)S(1)} %shard_map.91.half.refs_0_, bf16[16,2048]{1,0:T(8,128)(2,1)S(1)} %collective-permute-done.26.refs_1_, f32[16,512]{1,0:T(8,128)S(1)} %get-tuple-element.59.refs_2_, ...), custom_call_target="tpu_custom_call" | custom-call | flops 100663296 | bytes 12804096 | tf_op jit(solution)/shard_map/pallas_call | solution.py:24
  65.7 1.1 %collective-permute-done.27.refs_1_ = bf16[8,4096]{1,0:T(8,128)(2,1)S(1)} collective-permute-done((bf16[8,4096]{1,0:T(8,128)(2,1)S(1)}, bf16[8,4096]{1,0:T(8,128)(2,1)S(1)}, u32[]{:S(2)}, u32[]{:S(2)}) %collective-permute-start.27) | collective-permute-done | bytes 65568 | tf_op jit(solution)/shard_map/ppermute | solution.py:331
  68.5 2.1 %collective-permute-start.30 = (bf16[2,4096]{1,0:T(2,128)(2,1)S(1)}, bf16[2,4096]{1,0:T(2,128)(2,1)S(1)}, u32[]{:S(2)}, u32[]{:S(2)}) collective-permute-start(bf16[2,4096]{1,0:T(2,128)(2,1)S(1)} %get-tuple-element.68), channel_id=1, source_target_pairs={{0,6},{1,7},{2,4},{3,5},{4,2},{5,3},{6,0},{7,1},{8,14},{9,15},{10,... | collective-permute-start | bytes 49160 | tf_op jit(solution)/shard_map/ppermute | solution.py:328
  71.4 1.7 %collective-permute-done.30.refs_3_ = bf16[2,4096]{1,0:T(2,128)(2,1)S(1)} collective-permute-done((bf16[2,4096]{1,0:T(2,128)(2,1)S(1)}, bf16[2,4096]{1,0:T(2,128)(2,1)S(1)}, u32[]{:S(2)}, u32[]{:S(2)}) %collective-permute-start.30) | collective-permute-done | bytes 16416 | tf_op jit(solution)/shard_map/ppermute | solution.py:328
  (76 shorter events, 13.8 us)
Async XLA Ops:
  1.7 3.8 %collective-permute-start = (bf16[2,4608]{1,0:T(2,128)(2,1)S(1)}, bf16[2,4608]{1,0:T(2,128)(2,1)S(1)}, u32[]{:S(2)}, u32[]{:S(2)}) collective-permute-start(bf16[2,4608]{1,0:T(2,128)(2,1)S(1)} %get-tuple-element.38), channel_id=1, source_target_pairs={{0,2},{1,3},{2,0},{3,1},{4,6},{5,7},{6,4},{7,5},{8,10},{9,11},{10,... | collective-permute-start | bytes 55304 | tf_op jit(solution)/shard_map/ppermute | solution.py:328
  3.2 3.8 %collective-permute-start.1 = (bf16[2,4608]{1,0:T(2,128)(2,1)S(1)}, bf16[2,4608]{1,0:T(2,128)(2,1)S(1)}, u32[]{:S(2)}, u32[]{:S(2)}) collective-permute-start(bf16[2,4608]{1,0:T(2,128)(2,1)S(1)} %get-tuple-element.39), channel_id=1, source_target_pairs={{0,4},{1,5},{2,6},{3,7},{4,0},{5,1},{6,2},{7,3},{8,12},{9,13},{10,... | collective-permute-start | bytes 55304 | tf_op jit(solution)/shard_map/ppermute | solution.py:328
  4.8 4.7 %collective-permute-start.2 = (bf16[2,4608]{1,0:T(2,128)(2,1)S(1)}, bf16[2,4608]{1,0:T(2,128)(2,1)S(1)}, u32[]{:S(2)}, u32[]{:S(2)}) collective-permute-start(bf16[2,4608]{1,0:T(2,128)(2,1)S(1)} %get-tuple-element.40), channel_id=1, source_target_pairs={{0,6},{1,7},{2,4},{3,5},{4,2},{5,3},{6,0},{7,1},{8,14},{9,15},{10,... | collective-permute-start | bytes 55304 | tf_op jit(solution)/shard_map/ppermute | solution.py:328
  5.2 4.2 %collective-permute-start.3 = (bf16[2,4608]{1,0:T(2,128)(2,1)S(1)}, bf16[2,4608]{1,0:T(2,128)(2,1)S(1)}, u32[]{:S(2)}, u32[]{:S(2)}) collective-permute-start(bf16[2,4608]{1,0:T(2,128)(2,1)S(1)} %get-tuple-element.37.refs_0_), channel_id=1, source_target_pairs={{0,1},{1,0},{2,3},{3,2},{4,5},{5,4},{6,7},{7,6},{8,9},{9,8},{10,11... | collective-permute-start | bytes 55304 | tf_op jit(solution)/shard_map/ppermute | solution.py:331
  5.5 3.9 %collective-permute-start.4 = (bf16[2,4608]{1,0:T(2,128)(2,1)S(1)}, bf16[2,4608]{1,0:T(2,128)(2,1)S(1)}, u32[]{:S(2)}, u32[]{:S(2)}) collective-permute-start(bf16[2,4608]{1,0:T(2,128)(2,1)S(1)} %collective-permute-done.refs_1_), channel_id=1, source_target_pairs={{0,1},{1,0},{2,3},{3,2},{4,5},{5,4},{6,7},{7,6},{8,9},{9,8},{10,11... | collective-permute-start | bytes 55304 | tf_op jit(solution)/shard_map/ppermute | solution.py:331
  7.0 2.4 %collective-permute-start.5 = (bf16[2,4608]{1,0:T(2,128)(2,1)S(1)}, bf16[2,4608]{1,0:T(2,128)(2,1)S(1)}, u32[]{:S(2)}, u32[]{:S(2)}) collective-permute-start(bf16[2,4608]{1,0:T(2,128)(2,1)S(1)} %collective-permute-done.1.refs_2_), channel_id=1, source_target_pairs={{0,1},{1,0},{2,3},{3,2},{4,5},{5,4},{6,7},{7,6},{8,9},{9,8},{10,11... | collective-permute-start | bytes 55304 | tf_op jit(solution)/shard_map/ppermute | solution.py:331
  10.8 1.3 %collective-permute-start.7 = (bf16[16,2048]{1,0:T(8,128)(2,1)S(1)}, bf16[16,2048]{1,0:T(8,128)(2,1)S(1)}, u32[]{:S(2)}, u32[]{:S(2)}) collective-permute-start(bf16[16,2048]{1,0:T(8,128)(2,1)S(1)} %get-tuple-element.43), channel_id=1, source_target_pairs={{0,1},{1,0},{2,3},{3,2},{4,5},{5,4},{6,7},{7,6},{8,9},{9,8},{10,11... | collective-permute-start | bytes 196616 | tf_op jit(solution)/shard_map/ppermute | solution.py:331
  12.2 14.8 %collective-permute-start.11 = (bf16[16,2048]{1,0:T(8,128)(2,1)S(1)}, bf16[16,2048]{1,0:T(8,128)(2,1)S(1)}, u32[]{:S(2)}, u32[]{:S(2)}) collective-permute-start(bf16[16,2048]{1,0:T(8,128)(2,1)S(1)} %shard_map.78.refs_0_), channel_id=1, source_target_pairs={{0,14},{1,15},{2,12},{3,13},{4,10},{5,11},{6,8},{7,9},{8,16},{9,17... | collective-permute-start | bytes 196616 | tf_op jit(solution)/shard_map/ppermute | solution.py:339
  12.9 14.1 %collective-permute-start.10 = (bf16[16,2048]{1,0:T(8,128)(2,1)S(1)}, bf16[16,2048]{1,0:T(8,128)(2,1)S(1)}, u32[]{:S(2)}, u32[]{:S(2)}) collective-permute-start(bf16[16,2048]{1,0:T(8,128)(2,1)S(1)} %shard_map.78.refs_0_), channel_id=1, source_target_pairs={{0,12},{1,13},{2,14},{3,15},{4,8},{5,9},{6,10},{7,11},{8,24},{9,25... | collective-permute-start | bytes 196616 | tf_op jit(solution)/shard_map/ppermute | solution.py:339
  17.9 9.2 %collective-permute-start.9 = (bf16[16,2048]{1,0:T(8,128)(2,1)S(1)}, bf16[16,2048]{1,0:T(8,128)(2,1)S(1)}, u32[]{:S(2)}, u32[]{:S(2)}) collective-permute-start(bf16[16,2048]{1,0:T(8,128)(2,1)S(1)} %shard_map.78.refs_0_), channel_id=1, source_target_pairs={{0,10},{1,11},{2,8},{3,9},{4,14},{5,15},{6,12},{7,13},{8,0},{9,1},... | collective-permute-start | bytes 196616 | tf_op jit(solution)/shard_map/ppermute | solution.py:339
  18.5 8.5 %collective-permute-start.8 = (bf16[16,2048]{1,0:T(8,128)(2,1)S(1)}, bf16[16,2048]{1,0:T(8,128)(2,1)S(1)}, u32[]{:S(2)}, u32[]{:S(2)}) collective-permute-start(bf16[16,2048]{1,0:T(8,128)(2,1)S(1)} %shard_map.78.refs_0_), channel_id=1, source_target_pairs={{0,8},{1,9},{2,10},{3,11},{4,12},{5,13},{6,14},{7,15},{8,0},{9,1},... | collective-permute-start | bytes 196616 | tf_op jit(solution)/shard_map/ppermute | solution.py:339
  19.2 7.4 %collective-permute-start.12 = (bf16[16,128]{1,0:T(8,128)(2,1)S(1)}, bf16[16,128]{1,0:T(8,128)(2,1)S(1)}, u32[]{:S(2)}, u32[]{:S(2)}) collective-permute-start(bf16[16,128]{1,0:T(8,128)(2,1)S(1)} %get-tuple-element.46.current), channel_id=1, source_target_pairs={{0,8},{1,9},{2,10},{3,11},{4,12},{5,13},{6,14},{7,15},{8,16},{9,17... | collective-permute-start | bytes 12296 | tf_op jit(solution)/shard_map/ppermute | solution.py:339
  27.2 1.3 %collective-permute-start.13 = (bf16[16,2048]{1,0:T(8,128)(2,1)S(1)}, bf16[16,2048]{1,0:T(8,128)(2,1)S(1)}, u32[]{:S(2)}, u32[]{:S(2)}) collective-permute-start(bf16[16,2048]{1,0:T(8,128)(2,1)S(1)} %shard_map.80.half.refs_0_.refs_2_), channel_id=1, source_target_pairs={{0,1},{1,0},{2,3},{3,2},{4,5},{5,4},{6,7},{7,6},{8,9},{9,8},{10,11... | collective-permute-start | bytes 196616 | tf_op jit(solution)/shard_map/ppermute | solution.py:331
  29.9 6.4 %collective-permute-start.18 = (bf16[16,2048]{1,0:T(8,128)(2,1)S(1)}, bf16[16,2048]{1,0:T(8,128)(2,1)S(1)}, u32[]{:S(2)}, u32[]{:S(2)}) collective-permute-start(bf16[16,2048]{1,0:T(8,128)(2,1)S(1)} %shard_map.84.refs_1_), channel_id=1, source_target_pairs={{0,0},{1,1},{2,2},{3,3},{4,4},{5,5},{6,6},{7,7},{8,22},{9,23},{10,... | collective-permute-start | bytes 196616 | tf_op jit(solution)/shard_map/ppermute | solution.py:339
  34.3 2.0 %collective-permute-start.17 = (bf16[16,2048]{1,0:T(8,128)(2,1)S(1)}, bf16[16,2048]{1,0:T(8,128)(2,1)S(1)}, u32[]{:S(2)}, u32[]{:S(2)}) collective-permute-start(bf16[16,2048]{1,0:T(8,128)(2,1)S(1)} %shard_map.84.refs_1_), channel_id=1, source_target_pairs={{0,8},{1,9},{2,10},{3,11},{4,12},{5,13},{6,14},{7,15},{8,20},{9,21... | collective-permute-start | bytes 196616 | tf_op jit(solution)/shard_map/ppermute | solution.py:339
  35.0 1.4 %collective-permute-start.16 = (bf16[16,2048]{1,0:T(8,128)(2,1)S(1)}, bf16[16,2048]{1,0:T(8,128)(2,1)S(1)}, u32[]{:S(2)}, u32[]{:S(2)}) collective-permute-start(bf16[16,2048]{1,0:T(8,128)(2,1)S(1)} %shard_map.84.refs_1_), channel_id=1, source_target_pairs={{0,0},{1,1},{2,2},{3,3},{4,4},{5,5},{6,6},{7,7},{8,18},{9,19},{10,... | collective-permute-start | bytes 196616 | tf_op jit(solution)/shard_map/ppermute | solution.py:339
  36.6 1.3 %collective-permute-start.19 = (bf16[16,2048]{1,0:T(8,128)(2,1)S(1)}, bf16[16,2048]{1,0:T(8,128)(2,1)S(1)}, u32[]{:S(2)}, u32[]{:S(2)}) collective-permute-start(bf16[16,2048]{1,0:T(8,128)(2,1)S(1)} %shard_map.85.half.refs_0_.refs_2_), channel_id=1, source_target_pairs={{0,1},{1,0},{2,3},{3,2},{4,5},{5,4},{6,7},{7,6},{8,9},{9,8},{10,11... | collective-permute-start | bytes 196616 | tf_op jit(solution)/shard_map/ppermute | solution.py:331
  39.2 21.0 %collective-permute-start.24 = (bf16[16,2048]{1,0:T(8,128)(2,1)S(1)}, bf16[16,2048]{1,0:T(8,128)(2,1)S(1)}, u32[]{:S(2)}, u32[]{:S(2)}) collective-permute-start(bf16[16,2048]{1,0:T(8,128)(2,1)S(1)} %shard_map.89.refs_2_), channel_id=1, source_target_pairs={{0,16},{1,17},{2,18},{3,19},{4,20},{5,21},{6,22},{7,23},{8,8},{9,9... | collective-permute-start | bytes 196616 | tf_op jit(solution)/shard_map/ppermute | solution.py:339
  46.6 13.7 %collective-permute-start.23 = (bf16[16,2048]{1,0:T(8,128)(2,1)S(1)}, bf16[16,2048]{1,0:T(8,128)(2,1)S(1)}, u32[]{:S(2)}, u32[]{:S(2)}) collective-permute-start(bf16[16,2048]{1,0:T(8,128)(2,1)S(1)} %shard_map.89.refs_2_), channel_id=1, source_target_pairs={{0,0},{1,1},{2,2},{3,3},{4,4},{5,5},{6,6},{7,7},{8,16},{9,17},{10,... | collective-permute-start | bytes 196616 | tf_op jit(solution)/shard_map/ppermute | solution.py:339
  52.1 8.1 %collective-permute-start.22 = (bf16[16,2048]{1,0:T(8,128)(2,1)S(1)}, bf16[16,2048]{1,0:T(8,128)(2,1)S(1)}, u32[]{:S(2)}, u32[]{:S(2)}) collective-permute-start(bf16[16,2048]{1,0:T(8,128)(2,1)S(1)} %shard_map.89.refs_2_), channel_id=1, source_target_pairs={{0,0},{1,1},{2,2},{3,3},{4,4},{5,5},{6,6},{7,7},{8,8},{9,9},{10,10... | collective-permute-start | bytes 196616 | tf_op jit(solution)/shard_map/ppermute | solution.py:339
  56.5 6.2 %collective-permute-start.21 = (bf16[16,2048]{1,0:T(8,128)(2,1)S(1)}, bf16[16,2048]{1,0:T(8,128)(2,1)S(1)}, u32[]{:S(2)}, u32[]{:S(2)}) collective-permute-start(bf16[16,2048]{1,0:T(8,128)(2,1)S(1)} %shard_map.89.refs_2_), channel_id=1, source_target_pairs={{0,0},{1,1},{2,2},{3,3},{4,4},{5,5},{6,6},{7,7},{8,8},{9,9},{10,10... | collective-permute-start | bytes 196616 | tf_op jit(solution)/shard_map/ppermute | solution.py:339
  67.1 3.8 %collective-permute-start.28 = (bf16[2,4096]{1,0:T(2,128)(2,1)S(1)}, bf16[2,4096]{1,0:T(2,128)(2,1)S(1)}, u32[]{:S(2)}, u32[]{:S(2)}) collective-permute-start(bf16[2,4096]{1,0:T(2,128)(2,1)S(1)} %get-tuple-element.66), channel_id=1, source_target_pairs={{0,2},{1,3},{2,0},{3,1},{4,6},{5,7},{6,4},{7,5},{8,10},{9,11},{10,... | collective-permute-start | bytes 49160 | tf_op jit(solution)/shard_map/ppermute | solution.py:328
  67.7 3.7 %collective-permute-start.29 = (bf16[2,4096]{1,0:T(2,128)(2,1)S(1)}, bf16[2,4096]{1,0:T(2,128)(2,1)S(1)}, u32[]{:S(2)}, u32[]{:S(2)}) collective-permute-start(bf16[2,4096]{1,0:T(2,128)(2,1)S(1)} %get-tuple-element.67), channel_id=1, source_target_pairs={{0,4},{1,5},{2,6},{3,7},{4,0},{5,1},{6,2},{7,3},{8,12},{9,13},{10,... | collective-permute-start | bytes 49160 | tf_op jit(solution)/shard_map/ppermute | solution.py:328
  68.5 4.6 %collective-permute-start.30 = (bf16[2,4096]{1,0:T(2,128)(2,1)S(1)}, bf16[2,4096]{1,0:T(2,128)(2,1)S(1)}, u32[]{:S(2)}, u32[]{:S(2)}) collective-permute-start(bf16[2,4096]{1,0:T(2,128)(2,1)S(1)} %get-tuple-element.68), channel_id=1, source_target_pairs={{0,6},{1,7},{2,4},{3,5},{4,2},{5,3},{6,0},{7,1},{8,14},{9,15},{10,... | collective-permute-start | bytes 49160 | tf_op jit(solution)/shard_map/ppermute | solution.py:328
  (14 other events, 51.0 us)

commit v2 on v1

--- a/solution.py
+++ b/solution.py
@@ -330,20 +330,16 @@
     def within(value, m):
         return lax.ppermute(value, "expert", [(d, d ^ m) for d in range(peers)])
 
-    def onward(value, hops, moves):
+    def onward(value, hops, i):
         pairs = [
-            (s * peers + d, hops[s] * peers + (d // group ^ moves[s]) * group + d % group)
+            (s * peers + d, hops[s] * peers + (d // group ^ i) * group + d % group)
             for s in range(sections)
             for d in range(peers)
         ]
         return lax.ppermute(value, ("section", "expert"), pairs)
 
     def gather(value, tick):
-        outs = []
-        for i in range(EXPERTS):
-            moves = [i if s == tick else 0 for s in range(sections)]
-            outs.append(onward(value, cycle(tick, EXPERTS - 1 - i), moves))
-        return outs
+        return [onward(value, cycle(tick, EXPERTS - 1 - i), i) for i in range(EXPERTS)]
 
     def cycle(tick, turn):
         hops = list(range(sections))
@@ -372,7 +368,7 @@
         tuple(pieces),
         scratch=[pltpu.VMEM((slots, wide), F32), pltpu.VMEM((rows, wide), F32)],
     )
-    before = onward(position, [(s + 1) % sections for s in range(sections)], [0] * sections)
+    before = onward(position, [(s + 1) % sections for s in range(sections)], 0)
     choice = call(
         functools.partial(choice_kernel, group), shape((EXPERTS, rows, rows)), (position, before)
     )

time: 74.4 us -> 63.5 us (0.85)
  starting transfers between devices: 47.5 us -> 36.5 us
    ppermute x13, starting transfers between devices: 39 us -> 28.1 us  [onward(): return lax.ppermute(value, ('section', 'expert'), pairs)]
  transfers between devices with their start and end apart: 31 -> 31, of which waited for: 17 -> 19; matrix products, arithmetic and copies ran while one was open for 0% -> 0% of each run, Pallas kernels for 1% -> 2%
where the time goes in v2:
time: 63.5 us; the launch traced here: 63.3 us
  starting transfers between devices  36.5 us (57%)
  waiting for transfers between devices  20.4 us (32%)
  Pallas kernels  4.79 us (8%)
  local copies, waits for them, and re-layouts  1.39 us (2%)
    ppermute x13, starting transfers between devices, onward(): return lax.ppermute(value, ('section', 'expert'), pairs)  28.1 us
    ppermute x12, waiting for transfers between devices, within(): return lax.ppermute(value, 'expert', [(d, d ^ m) for d in range(peers)])  9.75 us
    ppermute x6, starting transfers between devices, across(): return lax.ppermute(value, 'expert', pairs)  7.11 us
    ppermute x6, waiting for transfers between devices, across(): return lax.ppermute(value, 'expert', pairs)  6.26 us
    pallas_call x23, Pallas kernels, call(): pl.pallas_call(kernel, out_shape=outs, in_specs=specs or [VMEM] * len(arg...  4.79 us
    ppermute x13, waiting for transfers between devices, onward(): return lax.ppermute(value, ('section', 'expert'), pairs)  4.35 us
    unnamed x14, local copies, waits for them, and re-layouts  1.39 us
    ppermute x12, starting transfers between devices, within(): return lax.ppermute(value, 'expert', [(d, d ^ m) for d in range(peers)])  1.31 us
  transfers between devices with their start and end apart: 31, of which 19 were waited for; matrix products, arithmetic and copies ran while one was open for 0% of the time, Pallas kernels for 2%

profile of v2, /device:TPU:24, one launch (start us, length us, event | category | flops | bytes accessed | tf_op | source)
XLA Modules:
  0.0 63.3 jit_solution(8593140749652812486)
XLA Ops:
  1.7 1.6 %collective-permute-start = (bf16[2,4608]{1,0:T(2,128)(2,1)S(1)}, bf16[2,4608]{1,0:T(2,128)(2,1)S(1)}, u32[]{:S(2)}, u32[]{:S(2)}) collective-permute-start(bf16[2,4608]{1,0:T(2,128)(2,1)S(1)} %get-tuple-element.38), channel_id=1, source_target_pairs={{0,2},{1,3},{2,0},{3,1},{4,6},{5,7},{6,4},{7,5},{8,10},{9,11},{10,... | collective-permute-start | bytes 55304 | tf_op jit(solution)/shard_map/ppermute | solution.py:328
  3.2 1.5 %collective-permute-start.1 = (bf16[2,4608]{1,0:T(2,128)(2,1)S(1)}, bf16[2,4608]{1,0:T(2,128)(2,1)S(1)}, u32[]{:S(2)}, u32[]{:S(2)}) collective-permute-start(bf16[2,4608]{1,0:T(2,128)(2,1)S(1)} %get-tuple-element.39), channel_id=1, source_target_pairs={{0,4},{1,5},{2,6},{3,7},{4,0},{5,1},{6,2},{7,3},{8,12},{9,13},{10,... | collective-permute-start | bytes 55304 | tf_op jit(solution)/shard_map/ppermute | solution.py:328
  5.7 1.2 %collective-permute-done.1.refs_2_ = bf16[2,4608]{1,0:T(2,128)(2,1)S(1)} collective-permute-done((bf16[2,4608]{1,0:T(2,128)(2,1)S(1)}, bf16[2,4608]{1,0:T(2,128)(2,1)S(1)}, u32[]{:S(2)}, u32[]{:S(2)}) %collective-permute-start.1) | collective-permute-done | bytes 18464 | tf_op jit(solution)/shard_map/ppermute | solution.py:328
  7.0 2.4 %collective-permute-done.2.refs_3_ = bf16[2,4608]{1,0:T(2,128)(2,1)S(1)} collective-permute-done((bf16[2,4608]{1,0:T(2,128)(2,1)S(1)}, bf16[2,4608]{1,0:T(2,128)(2,1)S(1)}, u32[]{:S(2)}, u32[]{:S(2)}) %collective-permute-start.2) | collective-permute-done | bytes 18464 | tf_op jit(solution)/shard_map/ppermute | solution.py:328
  9.4 1.2 %collective-permute-done.6.refs_7_ = bf16[2,4608]{1,0:T(2,128)(2,1)S(1)} collective-permute-done((bf16[2,4608]{1,0:T(2,128)(2,1)S(1)}, bf16[2,4608]{1,0:T(2,128)(2,1)S(1)}, u32[]{:S(2)}, u32[]{:S(2)}) %collective-permute-start.6) | collective-permute-done | bytes 18464 | tf_op jit(solution)/shard_map/ppermute | solution.py:331
  12.8 2.2 %collective-permute-start.10 = (bf16[16,2048]{1,0:T(8,128)(2,1)S(1)}, bf16[16,2048]{1,0:T(8,128)(2,1)S(1)}, u32[]{:S(2)}, u32[]{:S(2)}) collective-permute-start(bf16[16,2048]{1,0:T(8,128)(2,1)S(1)} %shard_map.78.refs_0_), channel_id=1, source_target_pairs={{0,12},{1,13},{2,14},{3,15},{4,8},{5,9},{6,10},{7,11},{8,28},{9,29... | collective-permute-start | bytes 196616 | tf_op jit(solution)/shard_map/ppermute | solution.py:339
  15.0 1.5 %collective-permute-start.9 = (bf16[16,2048]{1,0:T(8,128)(2,1)S(1)}, bf16[16,2048]{1,0:T(8,128)(2,1)S(1)}, u32[]{:S(2)}, u32[]{:S(2)}) collective-permute-start(bf16[16,2048]{1,0:T(8,128)(2,1)S(1)} %shard_map.78.refs_0_), channel_id=1, source_target_pairs={{0,10},{1,11},{2,8},{3,9},{4,14},{5,15},{6,12},{7,13},{8,2},{9,3},... | collective-permute-start | bytes 196616 | tf_op jit(solution)/shard_map/ppermute | solution.py:339
  17.1 4.3 %collective-permute-start.12 = (bf16[16,128]{1,0:T(8,128)(2,1)S(1)}, bf16[16,128]{1,0:T(8,128)(2,1)S(1)}, u32[]{:S(2)}, u32[]{:S(2)}) collective-permute-start(bf16[16,128]{1,0:T(8,128)(2,1)S(1)} %get-tuple-element.46.current), channel_id=1, source_target_pairs={{0,8},{1,9},{2,10},{3,11},{4,12},{5,13},{6,14},{7,15},{8,16},{9,17... | collective-permute-start | bytes 12296 | tf_op jit(solution)/shard_map/ppermute | solution.py:339
  21.4 1.3 %collective-permute-done.12.before = bf16[16,128]{1,0:T(8,128)(2,1)S(1)} collective-permute-done((bf16[16,128]{1,0:T(8,128)(2,1)S(1)}, bf16[16,128]{1,0:T(8,128)(2,1)S(1)}, u32[]{:S(2)}, u32[]{:S(2)}) %collective-permute-start.12) | collective-permute-done | bytes 4128 | tf_op jit(solution)/shard_map/ppermute | solution.py:339
  23.5 1.2 %collective-permute-done.13.refs_1_ = bf16[16,2048]{1,0:T(8,128)(2,1)S(1)} collective-permute-done((bf16[16,2048]{1,0:T(8,128)(2,1)S(1)}, bf16[16,2048]{1,0:T(8,128)(2,1)S(1)}, u32[]{:S(2)}, u32[]{:S(2)}) %collective-permute-start.13) | collective-permute-done | bytes 65568 | tf_op jit(solution)/shard_map/ppermute | solution.py:331
  24.9 1.1 %collective-permute-done.14.refs_1_ = bf16[16,2048]{1,0:T(8,128)(2,1)S(1)} collective-permute-done((bf16[16,2048]{1,0:T(8,128)(2,1)S(1)}, bf16[16,2048]{1,0:T(8,128)(2,1)S(1)}, u32[]{:S(2)}, u32[]{:S(2)}) %collective-permute-start.14) | collective-permute-done | bytes 65568 | tf_op jit(solution)/shard_map/ppermute | solution.py:331
  26.1 3.4 %collective-permute-start.18 = (bf16[16,2048]{1,0:T(8,128)(2,1)S(1)}, bf16[16,2048]{1,0:T(8,128)(2,1)S(1)}, u32[]{:S(2)}, u32[]{:S(2)}) collective-permute-start(bf16[16,2048]{1,0:T(8,128)(2,1)S(1)} %shard_map.84.refs_1_), channel_id=1, source_target_pairs={{0,6},{1,7},{2,4},{3,5},{4,2},{5,3},{6,0},{7,1},{8,22},{9,23},{10,... | collective-permute-start | bytes 196616 | tf_op jit(solution)/shard_map/ppermute | solution.py:339
  29.4 1.5 %collective-permute-start.17 = (bf16[16,2048]{1,0:T(8,128)(2,1)S(1)}, bf16[16,2048]{1,0:T(8,128)(2,1)S(1)}, u32[]{:S(2)}, u32[]{:S(2)}) collective-permute-start(bf16[16,2048]{1,0:T(8,128)(2,1)S(1)} %shard_map.84.refs_1_), channel_id=1, source_target_pairs={{0,12},{1,13},{2,14},{3,15},{4,8},{5,9},{6,10},{7,11},{8,20},{9,21... | collective-permute-start | bytes 196616 | tf_op jit(solution)/shard_map/ppermute | solution.py:339
  31.0 1.5 %collective-permute-start.16 = (bf16[16,2048]{1,0:T(8,128)(2,1)S(1)}, bf16[16,2048]{1,0:T(8,128)(2,1)S(1)}, u32[]{:S(2)}, u32[]{:S(2)}) collective-permute-start(bf16[16,2048]{1,0:T(8,128)(2,1)S(1)} %shard_map.84.refs_1_), channel_id=1, source_target_pairs={{0,2},{1,3},{2,0},{3,1},{4,6},{5,7},{6,4},{7,5},{8,18},{9,19},{10,... | collective-permute-start | bytes 196616 | tf_op jit(solution)/shard_map/ppermute | solution.py:339
  33.7 1.5 %collective-permute-done.16.refs_1_ = bf16[16,2048]{1,0:T(8,128)(2,1)S(1)} collective-permute-done((bf16[16,2048]{1,0:T(8,128)(2,1)S(1)}, bf16[16,2048]{1,0:T(8,128)(2,1)S(1)}, u32[]{:S(2)}, u32[]{:S(2)}) %collective-permute-start.16) | collective-permute-done | bytes 65568 | tf_op jit(solution)/shard_map/ppermute | solution.py:339
  35.5 1.2 %collective-permute-done.19.refs_1_ = bf16[16,2048]{1,0:T(8,128)(2,1)S(1)} collective-permute-done((bf16[16,2048]{1,0:T(8,128)(2,1)S(1)}, bf16[16,2048]{1,0:T(8,128)(2,1)S(1)}, u32[]{:S(2)}, u32[]{:S(2)}) %collective-permute-start.19) | collective-permute-done | bytes 65568 | tf_op jit(solution)/shard_map/ppermute | solution.py:331
  36.9 1.1 %collective-permute-done.20.refs_1_ = bf16[16,2048]{1,0:T(8,128)(2,1)S(1)} collective-permute-done((bf16[16,2048]{1,0:T(8,128)(2,1)S(1)}, bf16[16,2048]{1,0:T(8,128)(2,1)S(1)}, u32[]{:S(2)}, u32[]{:S(2)}) %collective-permute-start.20) | collective-permute-done | bytes 65568 | tf_op jit(solution)/shard_map/ppermute | solution.py:331
  38.1 4.2 %collective-permute-start.24 = (bf16[16,2048]{1,0:T(8,128)(2,1)S(1)}, bf16[16,2048]{1,0:T(8,128)(2,1)S(1)}, u32[]{:S(2)}, u32[]{:S(2)}) collective-permute-start(bf16[16,2048]{1,0:T(8,128)(2,1)S(1)} %shard_map.89.refs_2_), channel_id=1, source_target_pairs={{0,22},{1,23},{2,20},{3,21},{4,18},{5,19},{6,16},{7,17},{8,14},{9,... | collective-permute-start | bytes 196616 | tf_op jit(solution)/shard_map/ppermute | solution.py:339
  42.3 2.8 %collective-permute-start.23 = (bf16[16,2048]{1,0:T(8,128)(2,1)S(1)}, bf16[16,2048]{1,0:T(8,128)(2,1)S(1)}, u32[]{:S(2)}, u32[]{:S(2)}) collective-permute-start(bf16[16,2048]{1,0:T(8,128)(2,1)S(1)} %shard_map.89.refs_2_), channel_id=1, source_target_pairs={{0,4},{1,5},{2,6},{3,7},{4,0},{5,1},{6,2},{7,3},{8,20},{9,21},{10,... | collective-permute-start | bytes 196616 | tf_op jit(solution)/shard_map/ppermute | solution.py:339
  45.1 4.8 %collective-permute-start.21 = (bf16[16,2048]{1,0:T(8,128)(2,1)S(1)}, bf16[16,2048]{1,0:T(8,128)(2,1)S(1)}, u32[]{:S(2)}, u32[]{:S(2)}) collective-permute-start(bf16[16,2048]{1,0:T(8,128)(2,1)S(1)} %shard_map.89.refs_2_), channel_id=1, source_target_pairs={{0,0},{1,1},{2,2},{3,3},{4,4},{5,5},{6,6},{7,7},{8,8},{9,9},{10,10... | collective-permute-start | bytes 196616 | tf_op jit(solution)/shard_map/ppermute | solution.py:339
  50.1 1.2 %collective-permute-done.25.refs_6_.refs_5_ = bf16[8,2048]{1,0:T(8,128)(2,1)S(1)} collective-permute-done((bf16[8,2048]{1,0:T(8,128)(2,1)S(1)}, bf16[8,2048]{1,0:T(8,128)(2,1)S(1)}, u32[]{:S(2)}, u32[]{:S(2)}) %collective-permute-start.25) | collective-permute-done | bytes 32800 | tf_op jit(solution)/shard_map/ppermute | solution.py:331
  53.7 1.3 %shard_map.93 = (bf16[8,4096]{1,0:T(8,128)(2,1)S(1)}, bf16[8,4096]{1,0:T(8,128)(2,1)S(1)}, bf16[8,4096]{1,0:T(8,128)(2,1)S(1)}) custom-call(bf16[16,2048]{1,0:T(8,128)(2,1)S(1)} %shard_map.91.half.refs_0_, bf16[16,2048]{1,0:T(8,128)(2,1)S(1)} %collective-permute-done.26.refs_1_, f32[16,512]{1,0:T(8,128)S(1)} %get-tuple-element.59.refs_2_, ...), custom_call_target="tpu_custom_call" | custom-call | flops 100663296 | bytes 12804096 | tf_op jit(solution)/shard_map/pallas_call | solution.py:24
  57.8 2.3 %collective-permute-start.30 = (bf16[2,4096]{1,0:T(2,128)(2,1)S(1)}, bf16[2,4096]{1,0:T(2,128)(2,1)S(1)}, u32[]{:S(2)}, u32[]{:S(2)}) collective-permute-start(bf16[2,4096]{1,0:T(2,128)(2,1)S(1)} %get-tuple-element.68), channel_id=1, source_target_pairs={{0,6},{1,7},{2,4},{3,5},{4,2},{5,3},{6,0},{7,1},{8,14},{9,15},{10,... | collective-permute-start | bytes 49160 | tf_op jit(solution)/shard_map/ppermute | solution.py:328
  60.9 1.5 %collective-permute-done.30.refs_3_ = bf16[2,4096]{1,0:T(2,128)(2,1)S(1)} collective-permute-done((bf16[2,4096]{1,0:T(2,128)(2,1)S(1)}, bf16[2,4096]{1,0:T(2,128)(2,1)S(1)}, u32[]{:S(2)}, u32[]{:S(2)}) %collective-permute-start.30) | collective-permute-done | bytes 16416 | tf_op jit(solution)/shard_map/ppermute | solution.py:328
  (76 shorter events, 15.1 us)
Async XLA Ops:
  1.7 3.8 %collective-permute-start = (bf16[2,4608]{1,0:T(2,128)(2,1)S(1)}, bf16[2,4608]{1,0:T(2,128)(2,1)S(1)}, u32[]{:S(2)}, u32[]{:S(2)}) collective-permute-start(bf16[2,4608]{1,0:T(2,128)(2,1)S(1)} %get-tuple-element.38), channel_id=1, source_target_pairs={{0,2},{1,3},{2,0},{3,1},{4,6},{5,7},{6,4},{7,5},{8,10},{9,11},{10,... | collective-permute-start | bytes 55304 | tf_op jit(solution)/shard_map/ppermute | solution.py:328
  3.2 3.8 %collective-permute-start.1 = (bf16[2,4608]{1,0:T(2,128)(2,1)S(1)}, bf16[2,4608]{1,0:T(2,128)(2,1)S(1)}, u32[]{:S(2)}, u32[]{:S(2)}) collective-permute-start(bf16[2,4608]{1,0:T(2,128)(2,1)S(1)} %get-tuple-element.39), channel_id=1, source_target_pairs={{0,4},{1,5},{2,6},{3,7},{4,0},{5,1},{6,2},{7,3},{8,12},{9,13},{10,... | collective-permute-start | bytes 55304 | tf_op jit(solution)/shard_map/ppermute | solution.py:328
  4.8 4.7 %collective-permute-start.2 = (bf16[2,4608]{1,0:T(2,128)(2,1)S(1)}, bf16[2,4608]{1,0:T(2,128)(2,1)S(1)}, u32[]{:S(2)}, u32[]{:S(2)}) collective-permute-start(bf16[2,4608]{1,0:T(2,128)(2,1)S(1)} %get-tuple-element.40), channel_id=1, source_target_pairs={{0,6},{1,7},{2,4},{3,5},{4,2},{5,3},{6,0},{7,1},{8,14},{9,15},{10,... | collective-permute-start | bytes 55304 | tf_op jit(solution)/shard_map/ppermute | solution.py:328
  5.2 4.2 %collective-permute-start.3 = (bf16[2,4608]{1,0:T(2,128)(2,1)S(1)}, bf16[2,4608]{1,0:T(2,128)(2,1)S(1)}, u32[]{:S(2)}, u32[]{:S(2)}) collective-permute-start(bf16[2,4608]{1,0:T(2,128)(2,1)S(1)} %get-tuple-element.37.refs_0_), channel_id=1, source_target_pairs={{0,1},{1,0},{2,3},{3,2},{4,5},{5,4},{6,7},{7,6},{8,9},{9,8},{10,11... | collective-permute-start | bytes 55304 | tf_op jit(solution)/shard_map/ppermute | solution.py:331
  5.5 3.9 %collective-permute-start.4 = (bf16[2,4608]{1,0:T(2,128)(2,1)S(1)}, bf16[2,4608]{1,0:T(2,128)(2,1)S(1)}, u32[]{:S(2)}, u32[]{:S(2)}) collective-permute-start(bf16[2,4608]{1,0:T(2,128)(2,1)S(1)} %collective-permute-done.refs_1_), channel_id=1, source_target_pairs={{0,1},{1,0},{2,3},{3,2},{4,5},{5,4},{6,7},{7,6},{8,9},{9,8},{10,11... | collective-permute-start | bytes 55304 | tf_op jit(solution)/shard_map/ppermute | solution.py:331
  7.0 2.4 %collective-permute-start.5 = (bf16[2,4608]{1,0:T(2,128)(2,1)S(1)}, bf16[2,4608]{1,0:T(2,128)(2,1)S(1)}, u32[]{:S(2)}, u32[]{:S(2)}) collective-permute-start(bf16[2,4608]{1,0:T(2,128)(2,1)S(1)} %collective-permute-done.1.refs_2_), channel_id=1, source_target_pairs={{0,1},{1,0},{2,3},{3,2},{4,5},{5,4},{6,7},{7,6},{8,9},{9,8},{10,11... | collective-permute-start | bytes 55304 | tf_op jit(solution)/shard_map/ppermute | solution.py:331
  10.8 1.3 %collective-permute-start.7 = (bf16[16,2048]{1,0:T(8,128)(2,1)S(1)}, bf16[16,2048]{1,0:T(8,128)(2,1)S(1)}, u32[]{:S(2)}, u32[]{:S(2)}) collective-permute-start(bf16[16,2048]{1,0:T(8,128)(2,1)S(1)} %get-tuple-element.43), channel_id=1, source_target_pairs={{0,1},{1,0},{2,3},{3,2},{4,5},{5,4},{6,7},{7,6},{8,9},{9,8},{10,11... | collective-permute-start | bytes 196616 | tf_op jit(solution)/shard_map/ppermute | solution.py:331
  12.2 10.9 %collective-permute-start.11 = (bf16[16,2048]{1,0:T(8,128)(2,1)S(1)}, bf16[16,2048]{1,0:T(8,128)(2,1)S(1)}, u32[]{:S(2)}, u32[]{:S(2)}) collective-permute-start(bf16[16,2048]{1,0:T(8,128)(2,1)S(1)} %shard_map.78.refs_0_), channel_id=1, source_target_pairs={{0,14},{1,15},{2,12},{3,13},{4,10},{5,11},{6,8},{7,9},{8,22},{9,23... | collective-permute-start | bytes 196616 | tf_op jit(solution)/shard_map/ppermute | solution.py:339
  12.8 10.4 %collective-permute-start.10 = (bf16[16,2048]{1,0:T(8,128)(2,1)S(1)}, bf16[16,2048]{1,0:T(8,128)(2,1)S(1)}, u32[]{:S(2)}, u32[]{:S(2)}) collective-permute-start(bf16[16,2048]{1,0:T(8,128)(2,1)S(1)} %shard_map.78.refs_0_), channel_id=1, source_target_pairs={{0,12},{1,13},{2,14},{3,15},{4,8},{5,9},{6,10},{7,11},{8,28},{9,29... | collective-permute-start | bytes 196616 | tf_op jit(solution)/shard_map/ppermute | solution.py:339
  15.0 8.2 %collective-permute-start.9 = (bf16[16,2048]{1,0:T(8,128)(2,1)S(1)}, bf16[16,2048]{1,0:T(8,128)(2,1)S(1)}, u32[]{:S(2)}, u32[]{:S(2)}) collective-permute-start(bf16[16,2048]{1,0:T(8,128)(2,1)S(1)} %shard_map.78.refs_0_), channel_id=1, source_target_pairs={{0,10},{1,11},{2,8},{3,9},{4,14},{5,15},{6,12},{7,13},{8,2},{9,3},... | collective-permute-start | bytes 196616 | tf_op jit(solution)/shard_map/ppermute | solution.py:339
  16.4 6.7 %collective-permute-start.8 = (bf16[16,2048]{1,0:T(8,128)(2,1)S(1)}, bf16[16,2048]{1,0:T(8,128)(2,1)S(1)}, u32[]{:S(2)}, u32[]{:S(2)}) collective-permute-start(bf16[16,2048]{1,0:T(8,128)(2,1)S(1)} %shard_map.78.refs_0_), channel_id=1, source_target_pairs={{0,8},{1,9},{2,10},{3,11},{4,12},{5,13},{6,14},{7,15},{8,0},{9,1},... | collective-permute-start | bytes 196616 | tf_op jit(solution)/shard_map/ppermute | solution.py:339
  17.1 5.7 %collective-permute-start.12 = (bf16[16,128]{1,0:T(8,128)(2,1)S(1)}, bf16[16,128]{1,0:T(8,128)(2,1)S(1)}, u32[]{:S(2)}, u32[]{:S(2)}) collective-permute-start(bf16[16,128]{1,0:T(8,128)(2,1)S(1)} %get-tuple-element.46.current), channel_id=1, source_target_pairs={{0,8},{1,9},{2,10},{3,11},{4,12},{5,13},{6,14},{7,15},{8,16},{9,17... | collective-permute-start | bytes 12296 | tf_op jit(solution)/shard_map/ppermute | solution.py:339
  23.4 1.3 %collective-permute-start.13 = (bf16[16,2048]{1,0:T(8,128)(2,1)S(1)}, bf16[16,2048]{1,0:T(8,128)(2,1)S(1)}, u32[]{:S(2)}, u32[]{:S(2)}) collective-permute-start(bf16[16,2048]{1,0:T(8,128)(2,1)S(1)} %shard_map.80.half.refs_0_.refs_2_), channel_id=1, source_target_pairs={{0,1},{1,0},{2,3},{3,2},{4,5},{5,4},{6,7},{7,6},{8,9},{9,8},{10,11... | collective-permute-start | bytes 196616 | tf_op jit(solution)/shard_map/ppermute | solution.py:331
  26.1 7.0 %collective-permute-start.18 = (bf16[16,2048]{1,0:T(8,128)(2,1)S(1)}, bf16[16,2048]{1,0:T(8,128)(2,1)S(1)}, u32[]{:S(2)}, u32[]{:S(2)}) collective-permute-start(bf16[16,2048]{1,0:T(8,128)(2,1)S(1)} %shard_map.84.refs_1_), channel_id=1, source_target_pairs={{0,6},{1,7},{2,4},{3,5},{4,2},{5,3},{6,0},{7,1},{8,22},{9,23},{10,... | collective-permute-start | bytes 196616 | tf_op jit(solution)/shard_map/ppermute | solution.py:339
  29.4 4.3 %collective-permute-start.17 = (bf16[16,2048]{1,0:T(8,128)(2,1)S(1)}, bf16[16,2048]{1,0:T(8,128)(2,1)S(1)}, u32[]{:S(2)}, u32[]{:S(2)}) collective-permute-start(bf16[16,2048]{1,0:T(8,128)(2,1)S(1)} %shard_map.84.refs_1_), channel_id=1, source_target_pairs={{0,12},{1,13},{2,14},{3,15},{4,8},{5,9},{6,10},{7,11},{8,20},{9,21... | collective-permute-start | bytes 196616 | tf_op jit(solution)/shard_map/ppermute | solution.py:339
  31.0 4.3 %collective-permute-start.16 = (bf16[16,2048]{1,0:T(8,128)(2,1)S(1)}, bf16[16,2048]{1,0:T(8,128)(2,1)S(1)}, u32[]{:S(2)}, u32[]{:S(2)}) collective-permute-start(bf16[16,2048]{1,0:T(8,128)(2,1)S(1)} %shard_map.84.refs_1_), channel_id=1, source_target_pairs={{0,2},{1,3},{2,0},{3,1},{4,6},{5,7},{6,4},{7,5},{8,18},{9,19},{10,... | collective-permute-start | bytes 196616 | tf_op jit(solution)/shard_map/ppermute | solution.py:339
  32.5 2.8 %collective-permute-start.15 = (bf16[16,2048]{1,0:T(8,128)(2,1)S(1)}, bf16[16,2048]{1,0:T(8,128)(2,1)S(1)}, u32[]{:S(2)}, u32[]{:S(2)}) collective-permute-start(bf16[16,2048]{1,0:T(8,128)(2,1)S(1)} %shard_map.84.refs_1_), channel_id=1, source_target_pairs={{0,0},{1,1},{2,2},{3,3},{4,4},{5,5},{6,6},{7,7},{8,16},{9,17},{10,... | collective-permute-start | bytes 196616 | tf_op jit(solution)/shard_map/ppermute | solution.py:339
  38.1 13.2 %collective-permute-start.24 = (bf16[16,2048]{1,0:T(8,128)(2,1)S(1)}, bf16[16,2048]{1,0:T(8,128)(2,1)S(1)}, u32[]{:S(2)}, u32[]{:S(2)}) collective-permute-start(bf16[16,2048]{1,0:T(8,128)(2,1)S(1)} %shard_map.89.refs_2_), channel_id=1, source_target_pairs={{0,22},{1,23},{2,20},{3,21},{4,18},{5,19},{6,16},{7,17},{8,14},{9,... | collective-permute-start | bytes 196616 | tf_op jit(solution)/shard_map/ppermute | solution.py:339
  42.3 9.0 %collective-permute-start.23 = (bf16[16,2048]{1,0:T(8,128)(2,1)S(1)}, bf16[16,2048]{1,0:T(8,128)(2,1)S(1)}, u32[]{:S(2)}, u32[]{:S(2)}) collective-permute-start(bf16[16,2048]{1,0:T(8,128)(2,1)S(1)} %shard_map.89.refs_2_), channel_id=1, source_target_pairs={{0,4},{1,5},{2,6},{3,7},{4,0},{5,1},{6,2},{7,3},{8,20},{9,21},{10,... | collective-permute-start | bytes 196616 | tf_op jit(solution)/shard_map/ppermute | solution.py:339
  45.1 6.2 %collective-permute-start.22 = (bf16[16,2048]{1,0:T(8,128)(2,1)S(1)}, bf16[16,2048]{1,0:T(8,128)(2,1)S(1)}, u32[]{:S(2)}, u32[]{:S(2)}) collective-permute-start(bf16[16,2048]{1,0:T(8,128)(2,1)S(1)} %shard_map.89.refs_2_), channel_id=1, source_target_pairs={{0,2},{1,3},{2,0},{3,1},{4,6},{5,7},{6,4},{7,5},{8,10},{9,11},{10,... | collective-permute-start | bytes 196616 | tf_op jit(solution)/shard_map/ppermute | solution.py:339
  45.1 7.1 %collective-permute-start.21 = (bf16[16,2048]{1,0:T(8,128)(2,1)S(1)}, bf16[16,2048]{1,0:T(8,128)(2,1)S(1)}, u32[]{:S(2)}, u32[]{:S(2)}) collective-permute-start(bf16[16,2048]{1,0:T(8,128)(2,1)S(1)} %shard_map.89.refs_2_), channel_id=1, source_target_pairs={{0,0},{1,1},{2,2},{3,3},{4,4},{5,5},{6,6},{7,7},{8,8},{9,9},{10,10... | collective-permute-start | bytes 196616 | tf_op jit(solution)/shard_map/ppermute | solution.py:339
  56.6 3.8 %collective-permute-start.28 = (bf16[2,4096]{1,0:T(2,128)(2,1)S(1)}, bf16[2,4096]{1,0:T(2,128)(2,1)S(1)}, u32[]{:S(2)}, u32[]{:S(2)}) collective-permute-start(bf16[2,4096]{1,0:T(2,128)(2,1)S(1)} %get-tuple-element.66), channel_id=1, source_target_pairs={{0,2},{1,3},{2,0},{3,1},{4,6},{5,7},{6,4},{7,5},{8,10},{9,11},{10,... | collective-permute-start | bytes 49160 | tf_op jit(solution)/shard_map/ppermute | solution.py:328
  57.2 3.8 %collective-permute-start.29 = (bf16[2,4096]{1,0:T(2,128)(2,1)S(1)}, bf16[2,4096]{1,0:T(2,128)(2,1)S(1)}, u32[]{:S(2)}, u32[]{:S(2)}) collective-permute-start(bf16[2,4096]{1,0:T(2,128)(2,1)S(1)} %get-tuple-element.67), channel_id=1, source_target_pairs={{0,4},{1,5},{2,6},{3,7},{4,0},{5,1},{6,2},{7,3},{8,12},{9,13},{10,... | collective-permute-start | bytes 49160 | tf_op jit(solution)/shard_map/ppermute | solution.py:328
  57.8 4.6 %collective-permute-start.30 = (bf16[2,4096]{1,0:T(2,128)(2,1)S(1)}, bf16[2,4096]{1,0:T(2,128)(2,1)S(1)}, u32[]{:S(2)}, u32[]{:S(2)}) collective-permute-start(bf16[2,4096]{1,0:T(2,128)(2,1)S(1)} %get-tuple-element.68), channel_id=1, source_target_pairs={{0,6},{1,7},{2,4},{3,5},{4,2},{5,3},{6,0},{7,1},{8,14},{9,15},{10,... | collective-permute-start | bytes 49160 | tf_op jit(solution)/shard_map/ppermute | solution.py:328
  (14 other events, 51.6 us)

commit v3 on v2

--- a/solution.py
+++ b/solution.py
@@ -105,8 +105,8 @@
 
 def join_kernel(group, width, *refs):
     count = group * EXPERTS
-    whole, half, table, position = refs[count : count + 4]
-    block, rows = refs[count + 4 :]
+    whole, half, table = refs[count : count + 3]
+    block, rows = refs[count + 3 :]
     _, own = place(group)
     slots = EXPERTS * CAP
     for m in range(group):
@@ -115,7 +115,6 @@
         at = pl.multiple_of((own ^ m) * slots, slots)
         rows[pl.ds(at, slots), :] = block[...]
     table[...] = rows[:, width:].astype(BF16)
-    position[...] = rows[:, width : width + LANES].astype(BF16)
     at = pl.multiple_of(own * half.shape[1], half.shape[1])
     half[...] = rows[:, pl.ds(at, half.shape[1])].astype(BF16)
     whole[...] = rows[:, 0:width].astype(BF16)
@@ -218,9 +217,13 @@
 
 
 def update_kernel(group, *refs):
-    half, table, out = refs[group], refs[group + 1], refs[-1]
+    half, table, out, marked = refs[group : group + 4]
     expert, _ = place(group)
-    out[...] = updated(refs[:group], half, scales(expert, table)).astype(BF16)
+    width = out.shape[1]
+    result = updated(refs[:group], half, scales(expert, table)).astype(BF16)
+    out[...] = result
+    marked[:, 0:width] = result
+    marked[:, width:] = table[:, 0:LANES]
 
 
 def keep_kernel(group, saved, *refs):
@@ -268,8 +271,8 @@
     expert, _ = place(group)
     rows = current.shape[0]
     span = EXPERTS * CAP
-    here = current[...].astype(F32)
-    there = before[...].astype(F32)
+    here = current[:, 0:LANES].astype(F32)
+    there = before[:, before.shape[1] - LANES :].astype(F32)
     mine = jnp.where(here == slot_codes(expert, here.shape).astype(F32), 1.0, 0.0).astype(BF16)
     a, b = iota((rows, rows), 0), iota((rows, rows), 1)
     for i in range(EXPERTS):
@@ -286,7 +289,8 @@
 
 def pick_kernel(*refs):
     choice, out = refs[EXPERTS], refs[-1]
-    total = jnp.dot(choice[0], refs[0][...], preferred_element_type=F32)
+    width = out.shape[1]
+    total = jnp.dot(choice[0], refs[0][:, 0:width], preferred_element_type=F32)
     for i in range(1, EXPERTS):
         total = total + jnp.dot(choice[i], refs[i][...], preferred_element_type=F32)
     out[...] = total.astype(BF16)
@@ -338,16 +342,16 @@
         ]
         return lax.ppermute(value, ("section", "expert"), pairs)
 
-    def gather(value, tick):
-        return [onward(value, cycle(tick, EXPERTS - 1 - i), i) for i in range(EXPERTS)]
-
-    def cycle(tick, turn):
-        hops = list(range(sections))
-        others = [(tick + n) % sections for n in range(2, sections)]
-        ring = [tick, tick + 1] + (others[turn : turn + 1] if turn < 2 else [])
-        for n, s in enumerate(ring):
-            hops[s] = ring[(n + 1) % len(ring)]
-        return hops
+    def gather(value, marked, tick):
+        outs = []
+        for i in range(EXPERTS):
+            hops = list(range(sections))
+            third = [tick + 2 if tick + 2 < sections else 0] if i == EXPERTS - 1 else []
+            ring = [tick, tick + 1] + third
+            for n, s in enumerate(ring):
+                hops[s] = ring[(n + 1) % len(ring)]
+            outs.append(onward(value if i else marked, hops, i))
+        return outs
 
     position = call(
         rank_kernel, shape((slots, LANES), F32), (expert_ids.reshape(1, count),), flops=START_FLOPS
@@ -362,22 +366,23 @@
     for m in range(1, group):
         pieces += [within(piece, m) for piece in arrived]
     flops = 6 * rows * width * w_gate.shape[2]
-    whole, half, table, position = call(
+    whole, half, table = call(
         functools.partial(join_kernel, group, width),
-        [shape((rows, width)), shape((rows, chunk)), shape((rows, BLOCKS * LANES)), shape((rows, LANES))],
+        [shape((rows, width)), shape((rows, chunk)), shape((rows, BLOCKS * LANES))],
         tuple(pieces),
         scratch=[pltpu.VMEM((slots, wide), F32), pltpu.VMEM((rows, wide), F32)],
-    )
-    before = onward(position, [(s + 1) % sections for s in range(sections)], 0)
-    choice = call(
-        functools.partial(choice_kernel, group), shape((EXPERTS, rows, rows)), (position, before)
     )
     saved = []
     inner = w_gate.shape[2]
     for tick in range(sections):
         last = tick == sections - 1
         if tick:
-            gathered = gather(saved[-1], tick - 1)
+            gathered = gather(saved[-1], marked, tick - 1)
+            choice = call(
+                functools.partial(choice_kernel, group),
+                shape((EXPERTS, rows, rows)),
+                (table, gathered[0]),
+            )
             kept = []
             if last:
                 kept = call(
@@ -426,13 +431,12 @@
             )
             terms = [own] + terms
         if not last:
-            saved.append(
-                call(
-                    functools.partial(update_kernel, group),
-                    shape((rows, chunk)),
-                    (*terms, half, table),
-                )
-            )
+            latest, marked = call(
+                functools.partial(update_kernel, group),
+                [shape((rows, chunk)), shape((rows, chunk + LANES))],
+                (*terms, half, table),
+            )
+            saved.append(latest)
     leaving = call(
         functools.partial(leave_kernel, group),
         [shape((CAP, width))] * EXPERTS,

time: 63.5 us -> 66.6 us (1.049)
  waiting for transfers between devices: 20.4 us -> 26.1 us
  starting transfers between devices: 36.5 us -> 32.7 us
  Pallas kernels: 4.79 us -> 5.54 us
    ppermute x13 -> x12, waiting for transfers between devices: 4.35 us -> 9.62 us  [onward(): return lax.ppermute(value, ('section', 'expert'), pairs)]
    ppermute x13 -> x12, starting transfers between devices: 28.1 us -> 24.3 us  [onward(): return lax.ppermute(value, ('section', 'expert'), pairs)]
    ppermute x6, waiting for transfers between devices: 6.26 us -> 7.08 us  [across(): return lax.ppermute(value, 'expert', pairs)]
    pallas_call x23 -> x25, Pallas kernels: 4.79 us -> 5.54 us  [call(): pl.pallas_call(kernel, out_shape=outs, in_specs=specs or [VMEM] * len(arg...]
  transfers between devices with their start and end apart: 31 -> 30, of which waited for: 19 -> 22; matrix products, arithmetic and copies ran while one was open for 0% -> 0% of each run, Pallas kernels for 2% -> 3%
where the time goes in v3:
time: 66.6 us; the launch traced here: 66 us
  starting transfers between devices  32.7 us (49%)
  waiting for transfers between devices  26.1 us (39%)
  Pallas kernels  5.54 us (8%)
  local copies, waits for them, and re-layouts  1.39 us (2%)
    ppermute x12, starting transfers between devices, onward(): return lax.ppermute(value, ('section', 'expert'), pairs)  24.3 us
    ppermute x12, waiting for transfers between devices, onward(): return lax.ppermute(value, ('section', 'expert'), pairs)  9.62 us
    ppermute x12, waiting for transfers between devices, within(): return lax.ppermute(value, 'expert', [(d, d ^ m) for d in range(peers)])  9.36 us
    ppermute x6, starting transfers between devices, across(): return lax.ppermute(value, 'expert', pairs)  7.11 us
    ppermute x6, waiting for transfers between devices, across(): return lax.ppermute(value, 'expert', pairs)  7.08 us
    pallas_call x25, Pallas kernels, call(): pl.pallas_call(kernel, out_shape=outs, in_specs=specs or [VMEM] * len(arg...  5.54 us
    unnamed x14, local copies, waits for them, and re-layouts  1.39 us
  transfers between devices with their start and end apart: 30, of which 22 were waited for; matrix products, arithmetic and copies ran while one was open for 0% of the time, Pallas kernels for 3%

profile of v3, /device:TPU:24, one launch (start us, length us, event | category | flops | bytes accessed | tf_op | source)
XLA Modules:
  0.0 66.0 jit_solution(1993134373948302702)
XLA Ops:
  1.7 1.6 %collective-permute-start = (bf16[2,4608]{1,0:T(2,128)(2,1)S(1)}, bf16[2,4608]{1,0:T(2,128)(2,1)S(1)}, u32[]{:S(2)}, u32[]{:S(2)}) collective-permute-start(bf16[2,4608]{1,0:T(2,128)(2,1)S(1)} %get-tuple-element.43), channel_id=1, source_target_pairs={{0,2},{1,3},{2,0},{3,1},{4,6},{5,7},{6,4},{7,5},{8,10},{9,11},{10,... | collective-permute-start | bytes 55304 | tf_op jit(solution)/shard_map/ppermute | solution.py:332
  3.2 1.5 %collective-permute-start.1 = (bf16[2,4608]{1,0:T(2,128)(2,1)S(1)}, bf16[2,4608]{1,0:T(2,128)(2,1)S(1)}, u32[]{:S(2)}, u32[]{:S(2)}) collective-permute-start(bf16[2,4608]{1,0:T(2,128)(2,1)S(1)} %get-tuple-element.44), channel_id=1, source_target_pairs={{0,4},{1,5},{2,6},{3,7},{4,0},{5,1},{6,2},{7,3},{8,12},{9,13},{10,... | collective-permute-start | bytes 55304 | tf_op jit(solution)/shard_map/ppermute | solution.py:332
  5.7 1.2 %collective-permute-done.1.refs_2_ = bf16[2,4608]{1,0:T(2,128)(2,1)S(1)} collective-permute-done((bf16[2,4608]{1,0:T(2,128)(2,1)S(1)}, bf16[2,4608]{1,0:T(2,128)(2,1)S(1)}, u32[]{:S(2)}, u32[]{:S(2)}) %collective-permute-start.1) | collective-permute-done | bytes 18464 | tf_op jit(solution)/shard_map/ppermute | solution.py:332
  7.0 2.4 %collective-permute-done.2.refs_3_ = bf16[2,4608]{1,0:T(2,128)(2,1)S(1)} collective-permute-done((bf16[2,4608]{1,0:T(2,128)(2,1)S(1)}, bf16[2,4608]{1,0:T(2,128)(2,1)S(1)}, u32[]{:S(2)}, u32[]{:S(2)}) %collective-permute-start.2) | collective-permute-done | bytes 18464 | tf_op jit(solution)/shard_map/ppermute | solution.py:332
  9.4 1.2 %collective-permute-done.6.refs_7_ = bf16[2,4608]{1,0:T(2,128)(2,1)S(1)} collective-permute-done((bf16[2,4608]{1,0:T(2,128)(2,1)S(1)}, bf16[2,4608]{1,0:T(2,128)(2,1)S(1)}, u32[]{:S(2)}, u32[]{:S(2)}) %collective-permute-start.6) | collective-permute-done | bytes 18464 | tf_op jit(solution)/shard_map/ppermute | solution.py:335
  13.4 1.5 %collective-permute-start.10 = (bf16[16,2048]{1,0:T(8,128)(2,1)S(1)}, bf16[16,2048]{1,0:T(8,128)(2,1)S(1)}, u32[]{:S(2)}, u32[]{:S(2)}) collective-permute-start(bf16[16,2048]{1,0:T(8,128)(2,1)S(1)} %get-tuple-element.52.refs_0_), channel_id=1, source_target_pairs={{0,12},{1,13},{2,14},{3,15},{4,8},{5,9},{6,10},{7,11},{8,4},{9,5},... | collective-permute-start | bytes 196616 | tf_op jit(solution)/shard_map/ppermute | solution.py:343
  15.0 1.5 %collective-permute-start.9 = (bf16[16,2048]{1,0:T(8,128)(2,1)S(1)}, bf16[16,2048]{1,0:T(8,128)(2,1)S(1)}, u32[]{:S(2)}, u32[]{:S(2)}) collective-permute-start(bf16[16,2048]{1,0:T(8,128)(2,1)S(1)} %get-tuple-element.52.refs_0_), channel_id=1, source_target_pairs={{0,10},{1,11},{2,8},{3,9},{4,14},{5,15},{6,12},{7,13},{8,2},{9,3},... | collective-permute-start | bytes 196616 | tf_op jit(solution)/shard_map/ppermute | solution.py:343
  16.8 1.9 %collective-permute-done.11.refs_3_ = bf16[16,2048]{1,0:T(8,128)(2,1)S(1)} collective-permute-done((bf16[16,2048]{1,0:T(8,128)(2,1)S(1)}, bf16[16,2048]{1,0:T(8,128)(2,1)S(1)}, u32[]{:S(2)}, u32[]{:S(2)}) %collective-permute-start.11) | collective-permute-done | bytes 65568 | tf_op jit(solution)/shard_map/ppermute | solution.py:343
  19.5 1.2 %collective-permute-done.12.refs_1_ = bf16[16,2048]{1,0:T(8,128)(2,1)S(1)} collective-permute-done((bf16[16,2048]{1,0:T(8,128)(2,1)S(1)}, bf16[16,2048]{1,0:T(8,128)(2,1)S(1)}, u32[]{:S(2)}, u32[]{:S(2)}) %collective-permute-start.12) | collective-permute-done | bytes 65568 | tf_op jit(solution)/shard_map/ppermute | solution.py:335
  20.9 1.1 %collective-permute-done.13.refs_1_ = bf16[16,2048]{1,0:T(8,128)(2,1)S(1)} collective-permute-done((bf16[16,2048]{1,0:T(8,128)(2,1)S(1)}, bf16[16,2048]{1,0:T(8,128)(2,1)S(1)}, u32[]{:S(2)}, u32[]{:S(2)}) %collective-permute-start.13) | collective-permute-done | bytes 65568 | tf_op jit(solution)/shard_map/ppermute | solution.py:335
  22.8 8.6 %collective-permute-start.17 = (bf16[16,2048]{1,0:T(8,128)(2,1)S(1)}, bf16[16,2048]{1,0:T(8,128)(2,1)S(1)}, u32[]{:S(2)}, u32[]{:S(2)}) collective-permute-start(bf16[16,2048]{1,0:T(8,128)(2,1)S(1)} %get-tuple-element.59.refs_1_), channel_id=1, source_target_pairs={{0,6},{1,7},{2,4},{3,5},{4,2},{5,3},{6,0},{7,1},{8,22},{9,23},{10,... | collective-permute-start | bytes 196616 | tf_op jit(solution)/shard_map/ppermute | solution.py:343
  31.4 1.5 %collective-permute-start.16 = (bf16[16,2048]{1,0:T(8,128)(2,1)S(1)}, bf16[16,2048]{1,0:T(8,128)(2,1)S(1)}, u32[]{:S(2)}, u32[]{:S(2)}) collective-permute-start(bf16[16,2048]{1,0:T(8,128)(2,1)S(1)} %get-tuple-element.59.refs_1_), channel_id=1, source_target_pairs={{0,4},{1,5},{2,6},{3,7},{4,0},{5,1},{6,2},{7,3},{8,20},{9,21},{10,... | collective-permute-start | bytes 196616 | tf_op jit(solution)/shard_map/ppermute | solution.py:343
  34.2 1.4 %collective-permute-done.16.refs_2_ = bf16[16,2048]{1,0:T(8,128)(2,1)S(1)} collective-permute-done((bf16[16,2048]{1,0:T(8,128)(2,1)S(1)}, bf16[16,2048]{1,0:T(8,128)(2,1)S(1)}, u32[]{:S(2)}, u32[]{:S(2)}) %collective-permute-start.16) | collective-permute-done | bytes 65568 | tf_op jit(solution)/shard_map/ppermute | solution.py:343
  35.6 1.5 %collective-permute-done.15.refs_1_ = bf16[16,2048]{1,0:T(8,128)(2,1)S(1)} collective-permute-done((bf16[16,2048]{1,0:T(8,128)(2,1)S(1)}, bf16[16,2048]{1,0:T(8,128)(2,1)S(1)}, u32[]{:S(2)}, u32[]{:S(2)}) %collective-permute-start.15) | collective-permute-done | bytes 65568 | tf_op jit(solution)/shard_map/ppermute | solution.py:343
  37.5 1.2 %collective-permute-done.18.refs_1_ = bf16[16,2048]{1,0:T(8,128)(2,1)S(1)} collective-permute-done((bf16[16,2048]{1,0:T(8,128)(2,1)S(1)}, bf16[16,2048]{1,0:T(8,128)(2,1)S(1)}, u32[]{:S(2)}, u32[]{:S(2)}) %collective-permute-start.18) | collective-permute-done | bytes 65568 | tf_op jit(solution)/shard_map/ppermute | solution.py:335
  40.0 5.8 %collective-permute-start.20 = (bf16[16,2176]{1,0:T(8,128)(2,1)S(1)}, bf16[16,2176]{1,0:T(8,128)(2,1)S(1)}, u32[]{:S(2)}, u32[]{:S(2)}) collective-permute-start(bf16[16,2176]{1,0:T(8,128)(2,1)S(1)} %get-tuple-element.65), channel_id=1, source_target_pairs={{0,0},{1,1},{2,2},{3,3},{4,4},{5,5},{6,6},{7,7},{8,8},{9,9},{10,10... | collective-permute-start | bytes 208904 | tf_op jit(solution)/shard_map/ppermute | solution.py:343
  46.0 2.9 %collective-permute-start.22 = (bf16[16,2048]{1,0:T(8,128)(2,1)S(1)}, bf16[16,2048]{1,0:T(8,128)(2,1)S(1)}, u32[]{:S(2)}, u32[]{:S(2)}) collective-permute-start(bf16[16,2048]{1,0:T(8,128)(2,1)S(1)} %get-tuple-element.66.refs_2_), channel_id=1, source_target_pairs={{0,4},{1,5},{2,6},{3,7},{4,0},{5,1},{6,2},{7,3},{8,12},{9,13},{10,... | collective-permute-start | bytes 196616 | tf_op jit(solution)/shard_map/ppermute | solution.py:343
  50.1 2.7 %collective-permute-done.23.refs_3_ = bf16[16,2048]{1,0:T(8,128)(2,1)S(1)} collective-permute-done((bf16[16,2048]{1,0:T(8,128)(2,1)S(1)}, bf16[16,2048]{1,0:T(8,128)(2,1)S(1)}, u32[]{:S(2)}, u32[]{:S(2)}) %collective-permute-start.23) | collective-permute-done | bytes 65568 | tf_op jit(solution)/shard_map/ppermute | solution.py:343
  52.8 1.2 %collective-permute-done.21.refs_1_ = bf16[16,2048]{1,0:T(8,128)(2,1)S(1)} collective-permute-done((bf16[16,2048]{1,0:T(8,128)(2,1)S(1)}, bf16[16,2048]{1,0:T(8,128)(2,1)S(1)}, u32[]{:S(2)}, u32[]{:S(2)}) %collective-permute-start.21) | collective-permute-done | bytes 65568 | tf_op jit(solution)/shard_map/ppermute | solution.py:343
  55.6 1.3 %shard_map.95 = (bf16[8,4096]{1,0:T(8,128)(2,1)S(1)}, bf16[8,4096]{1,0:T(8,128)(2,1)S(1)}, bf16[8,4096]{1,0:T(8,128)(2,1)S(1)}) custom-call(bf16[16,2048]{1,0:T(8,128)(2,1)S(1)} %shard_map.93.half.refs_0_, bf16[16,2048]{1,0:T(8,128)(2,1)S(1)} %collective-permute-done.25.refs_1_, f32[16,512]{1,0:T(8,128)S(1)} %get-tuple-element.69.refs_2_, ...), custom_call_target="tpu_custom_call" | custom-call | flops 100663296 | bytes 12804096 | tf_op jit(solution)/shard_map/pallas_call | solution.py:24
  58.4 1.5 %collective-permute-start.27 = (bf16[2,4096]{1,0:T(2,128)(2,1)S(1)}, bf16[2,4096]{1,0:T(2,128)(2,1)S(1)}, u32[]{:S(2)}, u32[]{:S(2)}) collective-permute-start(bf16[2,4096]{1,0:T(2,128)(2,1)S(1)} %get-tuple-element.76), channel_id=1, source_target_pairs={{0,2},{1,3},{2,0},{3,1},{4,6},{5,7},{6,4},{7,5},{8,10},{9,11},{10,... | collective-permute-start | bytes 49160 | tf_op jit(solution)/shard_map/ppermute | solution.py:332
  60.5 1.5 %collective-permute-start.29 = (bf16[2,4096]{1,0:T(2,128)(2,1)S(1)}, bf16[2,4096]{1,0:T(2,128)(2,1)S(1)}, u32[]{:S(2)}, u32[]{:S(2)}) collective-permute-start(bf16[2,4096]{1,0:T(2,128)(2,1)S(1)} %get-tuple-element.78), channel_id=1, source_target_pairs={{0,6},{1,7},{2,4},{3,5},{4,2},{5,3},{6,0},{7,1},{8,14},{9,15},{10,... | collective-permute-start | bytes 49160 | tf_op jit(solution)/shard_map/ppermute | solution.py:332
  62.2 1.7 %collective-permute-done.28.refs_2_ = bf16[2,4096]{1,0:T(2,128)(2,1)S(1)} collective-permute-done((bf16[2,4096]{1,0:T(2,128)(2,1)S(1)}, bf16[2,4096]{1,0:T(2,128)(2,1)S(1)}, u32[]{:S(2)}, u32[]{:S(2)}) %collective-permute-start.28) | collective-permute-done | bytes 16416 | tf_op jit(solution)/shard_map/ppermute | solution.py:332
  63.9 1.2 %collective-permute-done.29.refs_3_ = bf16[2,4096]{1,0:T(2,128)(2,1)S(1)} collective-permute-done((bf16[2,4096]{1,0:T(2,128)(2,1)S(1)}, bf16[2,4096]{1,0:T(2,128)(2,1)S(1)}, u32[]{:S(2)}, u32[]{:S(2)}) %collective-permute-start.29) | collective-permute-done | bytes 16416 | tf_op jit(solution)/shard_map/ppermute | solution.py:332
  (76 shorter events, 16.5 us)
Async XLA Ops:
  1.7 3.8 %collective-permute-start = (bf16[2,4608]{1,0:T(2,128)(2,1)S(1)}, bf16[2,4608]{1,0:T(2,128)(2,1)S(1)}, u32[]{:S(2)}, u32[]{:S(2)}) collective-permute-start(bf16[2,4608]{1,0:T(2,128)(2,1)S(1)} %get-tuple-element.43), channel_id=1, source_target_pairs={{0,2},{1,3},{2,0},{3,1},{4,6},{5,7},{6,4},{7,5},{8,10},{9,11},{10,... | collective-permute-start | bytes 55304 | tf_op jit(solution)/shard_map/ppermute | solution.py:332
  3.2 3.8 %collective-permute-start.1 = (bf16[2,4608]{1,0:T(2,128)(2,1)S(1)}, bf16[2,4608]{1,0:T(2,128)(2,1)S(1)}, u32[]{:S(2)}, u32[]{:S(2)}) collective-permute-start(bf16[2,4608]{1,0:T(2,128)(2,1)S(1)} %get-tuple-element.44), channel_id=1, source_target_pairs={{0,4},{1,5},{2,6},{3,7},{4,0},{5,1},{6,2},{7,3},{8,12},{9,13},{10,... | collective-permute-start | bytes 55304 | tf_op jit(solution)/shard_map/ppermute | solution.py:332
  4.8 4.7 %collective-permute-start.2 = (bf16[2,4608]{1,0:T(2,128)(2,1)S(1)}, bf16[2,4608]{1,0:T(2,128)(2,1)S(1)}, u32[]{:S(2)}, u32[]{:S(2)}) collective-permute-start(bf16[2,4608]{1,0:T(2,128)(2,1)S(1)} %get-tuple-element.45), channel_id=1, source_target_pairs={{0,6},{1,7},{2,4},{3,5},{4,2},{5,3},{6,0},{7,1},{8,14},{9,15},{10,... | collective-permute-start | bytes 55304 | tf_op jit(solution)/shard_map/ppermute | solution.py:332
  5.2 4.2 %collective-permute-start.3 = (bf16[2,4608]{1,0:T(2,128)(2,1)S(1)}, bf16[2,4608]{1,0:T(2,128)(2,1)S(1)}, u32[]{:S(2)}, u32[]{:S(2)}) collective-permute-start(bf16[2,4608]{1,0:T(2,128)(2,1)S(1)} %get-tuple-element.42.refs_0_), channel_id=1, source_target_pairs={{0,1},{1,0},{2,3},{3,2},{4,5},{5,4},{6,7},{7,6},{8,9},{9,8},{10,11... | collective-permute-start | bytes 55304 | tf_op jit(solution)/shard_map/ppermute | solution.py:335
  5.5 3.9 %collective-permute-start.4 = (bf16[2,4608]{1,0:T(2,128)(2,1)S(1)}, bf16[2,4608]{1,0:T(2,128)(2,1)S(1)}, u32[]{:S(2)}, u32[]{:S(2)}) collective-permute-start(bf16[2,4608]{1,0:T(2,128)(2,1)S(1)} %collective-permute-done.refs_1_), channel_id=1, source_target_pairs={{0,1},{1,0},{2,3},{3,2},{4,5},{5,4},{6,7},{7,6},{8,9},{9,8},{10,11... | collective-permute-start | bytes 55304 | tf_op jit(solution)/shard_map/ppermute | solution.py:335
  7.0 2.4 %collective-permute-start.5 = (bf16[2,4608]{1,0:T(2,128)(2,1)S(1)}, bf16[2,4608]{1,0:T(2,128)(2,1)S(1)}, u32[]{:S(2)}, u32[]{:S(2)}) collective-permute-start(bf16[2,4608]{1,0:T(2,128)(2,1)S(1)} %collective-permute-done.1.refs_2_), channel_id=1, source_target_pairs={{0,1},{1,0},{2,3},{3,2},{4,5},{5,4},{6,7},{7,6},{8,9},{9,8},{10,11... | collective-permute-start | bytes 55304 | tf_op jit(solution)/shard_map/ppermute | solution.py:335
  10.8 1.3 %collective-permute-start.7 = (bf16[16,2048]{1,0:T(8,128)(2,1)S(1)}, bf16[16,2048]{1,0:T(8,128)(2,1)S(1)}, u32[]{:S(2)}, u32[]{:S(2)}) collective-permute-start(bf16[16,2048]{1,0:T(8,128)(2,1)S(1)} %get-tuple-element.48), channel_id=1, source_target_pairs={{0,1},{1,0},{2,3},{3,2},{4,5},{5,4},{6,7},{7,6},{8,9},{9,8},{10,11... | collective-permute-start | bytes 196616 | tf_op jit(solution)/shard_map/ppermute | solution.py:335
  12.2 4.2 %collective-permute-start.8 = (bf16[16,2176]{1,0:T(8,128)(2,1)S(1)}, bf16[16,2176]{1,0:T(8,128)(2,1)S(1)}, u32[]{:S(2)}, u32[]{:S(2)}) collective-permute-start(bf16[16,2176]{1,0:T(8,128)(2,1)S(1)} %get-tuple-element.51), channel_id=1, source_target_pairs={{0,8},{1,9},{2,10},{3,11},{4,12},{5,13},{6,14},{7,15},{8,0},{9,1},... | collective-permute-start | bytes 208904 | tf_op jit(solution)/shard_map/ppermute | solution.py:343
  12.9 5.8 %collective-permute-start.11 = (bf16[16,2048]{1,0:T(8,128)(2,1)S(1)}, bf16[16,2048]{1,0:T(8,128)(2,1)S(1)}, u32[]{:S(2)}, u32[]{:S(2)}) collective-permute-start(bf16[16,2048]{1,0:T(8,128)(2,1)S(1)} %get-tuple-element.52.refs_0_), channel_id=1, source_target_pairs={{0,14},{1,15},{2,12},{3,13},{4,10},{5,11},{6,8},{7,9},{8,22},{9,23... | collective-permute-start | bytes 196616 | tf_op jit(solution)/shard_map/ppermute | solution.py:343
  13.4 5.3 %collective-permute-start.10 = (bf16[16,2048]{1,0:T(8,128)(2,1)S(1)}, bf16[16,2048]{1,0:T(8,128)(2,1)S(1)}, u32[]{:S(2)}, u32[]{:S(2)}) collective-permute-start(bf16[16,2048]{1,0:T(8,128)(2,1)S(1)} %get-tuple-element.52.refs_0_), channel_id=1, source_target_pairs={{0,12},{1,13},{2,14},{3,15},{4,8},{5,9},{6,10},{7,11},{8,4},{9,5},... | collective-permute-start | bytes 196616 | tf_op jit(solution)/shard_map/ppermute | solution.py:343
  15.0 4.3 %collective-permute-start.9 = (bf16[16,2048]{1,0:T(8,128)(2,1)S(1)}, bf16[16,2048]{1,0:T(8,128)(2,1)S(1)}, u32[]{:S(2)}, u32[]{:S(2)}) collective-permute-start(bf16[16,2048]{1,0:T(8,128)(2,1)S(1)} %get-tuple-element.52.refs_0_), channel_id=1, source_target_pairs={{0,10},{1,11},{2,8},{3,9},{4,14},{5,15},{6,12},{7,13},{8,2},{9,3},... | collective-permute-start | bytes 196616 | tf_op jit(solution)/shard_map/ppermute | solution.py:343
  19.4 1.3 %collective-permute-start.12 = (bf16[16,2048]{1,0:T(8,128)(2,1)S(1)}, bf16[16,2048]{1,0:T(8,128)(2,1)S(1)}, u32[]{:S(2)}, u32[]{:S(2)}) collective-permute-start(bf16[16,2048]{1,0:T(8,128)(2,1)S(1)} %shard_map.80.half.refs_0_.refs_2_), channel_id=1, source_target_pairs={{0,1},{1,0},{2,3},{3,2},{4,5},{5,4},{6,7},{7,6},{8,9},{9,8},{10,11... | collective-permute-start | bytes 196616 | tf_op jit(solution)/shard_map/ppermute | solution.py:335
  22.1 11.3 %collective-permute-start.14 = (bf16[16,2176]{1,0:T(8,128)(2,1)S(1)}, bf16[16,2176]{1,0:T(8,128)(2,1)S(1)}, u32[]{:S(2)}, u32[]{:S(2)}) collective-permute-start(bf16[16,2176]{1,0:T(8,128)(2,1)S(1)} %get-tuple-element.58), channel_id=1, source_target_pairs={{0,0},{1,1},{2,2},{3,3},{4,4},{5,5},{6,6},{7,7},{8,16},{9,17},{10,... | collective-permute-start | bytes 208904 | tf_op jit(solution)/shard_map/ppermute | solution.py:343
  22.8 11.4 %collective-permute-start.17 = (bf16[16,2048]{1,0:T(8,128)(2,1)S(1)}, bf16[16,2048]{1,0:T(8,128)(2,1)S(1)}, u32[]{:S(2)}, u32[]{:S(2)}) collective-permute-start(bf16[16,2048]{1,0:T(8,128)(2,1)S(1)} %get-tuple-element.59.refs_1_), channel_id=1, source_target_pairs={{0,6},{1,7},{2,4},{3,5},{4,2},{5,3},{6,0},{7,1},{8,22},{9,23},{10,... | collective-permute-start | bytes 196616 | tf_op jit(solution)/shard_map/ppermute | solution.py:343
  31.4 4.3 %collective-permute-start.16 = (bf16[16,2048]{1,0:T(8,128)(2,1)S(1)}, bf16[16,2048]{1,0:T(8,128)(2,1)S(1)}, u32[]{:S(2)}, u32[]{:S(2)}) collective-permute-start(bf16[16,2048]{1,0:T(8,128)(2,1)S(1)} %get-tuple-element.59.refs_1_), channel_id=1, source_target_pairs={{0,4},{1,5},{2,6},{3,7},{4,0},{5,1},{6,2},{7,3},{8,20},{9,21},{10,... | collective-permute-start | bytes 196616 | tf_op jit(solution)/shard_map/ppermute | solution.py:343
  32.9 4.3 %collective-permute-start.15 = (bf16[16,2048]{1,0:T(8,128)(2,1)S(1)}, bf16[16,2048]{1,0:T(8,128)(2,1)S(1)}, u32[]{:S(2)}, u32[]{:S(2)}) collective-permute-start(bf16[16,2048]{1,0:T(8,128)(2,1)S(1)} %get-tuple-element.59.refs_1_), channel_id=1, source_target_pairs={{0,2},{1,3},{2,0},{3,1},{4,6},{5,7},{6,4},{7,5},{8,18},{9,19},{10,... | collective-permute-start | bytes 196616 | tf_op jit(solution)/shard_map/ppermute | solution.py:343
  37.4 1.3 %collective-permute-start.18 = (bf16[16,2048]{1,0:T(8,128)(2,1)S(1)}, bf16[16,2048]{1,0:T(8,128)(2,1)S(1)}, u32[]{:S(2)}, u32[]{:S(2)}) collective-permute-start(bf16[16,2048]{1,0:T(8,128)(2,1)S(1)} %shard_map.86.half.refs_0_.refs_2_), channel_id=1, source_target_pairs={{0,1},{1,0},{2,3},{3,2},{4,5},{5,4},{6,7},{7,6},{8,9},{9,8},{10,11... | collective-permute-start | bytes 196616 | tf_op jit(solution)/shard_map/ppermute | solution.py:335
  40.0 8.9 %collective-permute-start.20 = (bf16[16,2176]{1,0:T(8,128)(2,1)S(1)}, bf16[16,2176]{1,0:T(8,128)(2,1)S(1)}, u32[]{:S(2)}, u32[]{:S(2)}) collective-permute-start(bf16[16,2176]{1,0:T(8,128)(2,1)S(1)} %get-tuple-element.65), channel_id=1, source_target_pairs={{0,0},{1,1},{2,2},{3,3},{4,4},{5,5},{6,6},{7,7},{8,8},{9,9},{10,10... | collective-permute-start | bytes 208904 | tf_op jit(solution)/shard_map/ppermute | solution.py:343
  45.9 6.9 %collective-permute-start.23 = (bf16[16,2048]{1,0:T(8,128)(2,1)S(1)}, bf16[16,2048]{1,0:T(8,128)(2,1)S(1)}, u32[]{:S(2)}, u32[]{:S(2)}) collective-permute-start(bf16[16,2048]{1,0:T(8,128)(2,1)S(1)} %get-tuple-element.66.refs_2_), channel_id=1, source_target_pairs={{0,22},{1,23},{2,20},{3,21},{4,18},{5,19},{6,16},{7,17},{8,14},{9,... | collective-permute-start | bytes 196616 | tf_op jit(solution)/shard_map/ppermute | solution.py:343
  46.0 6.8 %collective-permute-start.22 = (bf16[16,2048]{1,0:T(8,128)(2,1)S(1)}, bf16[16,2048]{1,0:T(8,128)(2,1)S(1)}, u32[]{:S(2)}, u32[]{:S(2)}) collective-permute-start(bf16[16,2048]{1,0:T(8,128)(2,1)S(1)} %get-tuple-element.66.refs_2_), channel_id=1, source_target_pairs={{0,4},{1,5},{2,6},{3,7},{4,0},{5,1},{6,2},{7,3},{8,12},{9,13},{10,... | collective-permute-start | bytes 196616 | tf_op jit(solution)/shard_map/ppermute | solution.py:343
  48.9 5.2 %collective-permute-start.21 = (bf16[16,2048]{1,0:T(8,128)(2,1)S(1)}, bf16[16,2048]{1,0:T(8,128)(2,1)S(1)}, u32[]{:S(2)}, u32[]{:S(2)}) collective-permute-start(bf16[16,2048]{1,0:T(8,128)(2,1)S(1)} %get-tuple-element.66.refs_2_), channel_id=1, source_target_pairs={{0,2},{1,3},{2,0},{3,1},{4,6},{5,7},{6,4},{7,5},{8,10},{9,11},{10,... | collective-permute-start | bytes 196616 | tf_op jit(solution)/shard_map/ppermute | solution.py:343
  58.4 3.8 %collective-permute-start.27 = (bf16[2,4096]{1,0:T(2,128)(2,1)S(1)}, bf16[2,4096]{1,0:T(2,128)(2,1)S(1)}, u32[]{:S(2)}, u32[]{:S(2)}) collective-permute-start(bf16[2,4096]{1,0:T(2,128)(2,1)S(1)} %get-tuple-element.76), channel_id=1, source_target_pairs={{0,2},{1,3},{2,0},{3,1},{4,6},{5,7},{6,4},{7,5},{8,10},{9,11},{10,... | collective-permute-start | bytes 49160 | tf_op jit(solution)/shard_map/ppermute | solution.py:332
  59.9 3.9 %collective-permute-start.28 = (bf16[2,4096]{1,0:T(2,128)(2,1)S(1)}, bf16[2,4096]{1,0:T(2,128)(2,1)S(1)}, u32[]{:S(2)}, u32[]{:S(2)}) collective-permute-start(bf16[2,4096]{1,0:T(2,128)(2,1)S(1)} %get-tuple-element.77), channel_id=1, source_target_pairs={{0,4},{1,5},{2,6},{3,7},{4,0},{5,1},{6,2},{7,3},{8,12},{9,13},{10,... | collective-permute-start | bytes 49160 | tf_op jit(solution)/shard_map/ppermute | solution.py:332
  60.5 4.6 %collective-permute-start.29 = (bf16[2,4096]{1,0:T(2,128)(2,1)S(1)}, bf16[2,4096]{1,0:T(2,128)(2,1)S(1)}, u32[]{:S(2)}, u32[]{:S(2)}) collective-permute-start(bf16[2,4096]{1,0:T(2,128)(2,1)S(1)} %get-tuple-element.78), channel_id=1, source_target_pairs={{0,6},{1,7},{2,4},{3,5},{4,2},{5,3},{6,0},{7,1},{8,14},{9,15},{10,... | collective-permute-start | bytes 49160 | tf_op jit(solution)/shard_map/ppermute | solution.py:332
  (13 other events, 50.3 us)

commit v4 on v3

--- a/solution.py
+++ b/solution.py
@@ -334,23 +334,20 @@
     def within(value, m):
         return lax.ppermute(value, "expert", [(d, d ^ m) for d in range(peers)])
 
-    def onward(value, hops, i):
-        pairs = [
-            (s * peers + d, hops[s] * peers + (d // group ^ i) * group + d % group)
-            for s in range(sections)
-            for d in range(peers)
-        ]
-        return lax.ppermute(value, ("section", "expert"), pairs)
-
     def gather(value, marked, tick):
+        hops = list(range(sections))
+        ring = [tick, tick + 1, tick + 2 if tick + 2 < sections else 0]
+        for n, s in enumerate(ring):
+            hops[s] = ring[(n + 1) % 3]
+        pairs = [(s * peers + d, hops[s] * peers + d) for s in range(sections) for d in range(peers)]
         outs = []
         for i in range(EXPERTS):
-            hops = list(range(sections))
-            third = [tick + 2 if tick + 2 < sections else 0] if i == EXPERTS - 1 else []
-            ring = [tick, tick + 1] + third
-            for n, s in enumerate(ring):
-                hops[s] = ring[(n + 1) % len(ring)]
-            outs.append(onward(value if i else marked, hops, i))
+            if i:
+                pairs = [
+                    (tick * peers + d, (tick + 1) * peers + (d // group ^ i) * group + d % group)
+                    for d in range(peers)
+                ]
+            outs.append(lax.ppermute(value if i else marked, ("section", "expert"), pairs))
         return outs
 
     position = call(

time: 66.6 us -> 64.9 us (0.974)
  waiting for transfers between devices: 26.1 us -> 24.7 us
    ppermute x12, waiting for transfers between devices: 9.36 us -> 8.42 us  [within(): return lax.ppermute(value, 'expert', [(d, d ^ m) for d in range(peers)])]
    ppermute x12, waiting for transfers between devices: 9.62 us -> 8.9 us  [gather(): lax.ppermute(value if i else marked, ('section', 'expert'), pairs)]
  transfers between devices with their start and end apart: 30 -> 30, of which waited for: 22 -> 18; matrix products, arithmetic and copies ran while one was open for 0% -> 0% of each run, Pallas kernels for 3% -> 3%
where the time goes in v4:
time: 64.9 us; the launch traced here: 64.6 us
  starting transfers between devices  32.6 us (50%)
  waiting for transfers between devices  24.7 us (38%)
  Pallas kernels  5.55 us (9%)
  local copies, waits for them, and re-layouts  1.39 us (2%)
    ppermute x12, starting transfers between devices, gather(): lax.ppermute(value if i else marked, ('section', 'expert'), pairs)  23.9 us
    ppermute x12, waiting for transfers between devices, gather(): lax.ppermute(value if i else marked, ('section', 'expert'), pairs)  8.9 us
    ppermute x12, waiting for transfers between devices, within(): return lax.ppermute(value, 'expert', [(d, d ^ m) for d in range(peers)])  8.42 us
    ppermute x6, waiting for transfers between devices, across(): return lax.ppermute(value, 'expert', pairs)  7.34 us
    ppermute x6, starting transfers between devices, across(): return lax.ppermute(value, 'expert', pairs)  7.11 us
    pallas_call x25, Pallas kernels, call(): pl.pallas_call(kernel, out_shape=outs, in_specs=specs or [VMEM] * len(arg...  5.55 us
    ppermute x12, starting transfers between devices, within(): return lax.ppermute(value, 'expert', [(d, d ^ m) for d in range(peers)])  1.63 us
    unnamed x14, local copies, waits for them, and re-layouts  1.39 us
  transfers between devices with their start and end apart: 30, of which 18 were waited for; matrix products, arithmetic and copies ran while one was open for 0% of the time, Pallas kernels for 3%

profile of v4, /device:TPU:24, one launch (start us, length us, event | category | flops | bytes accessed | tf_op | source)
XLA Modules:
  0.0 64.6 jit_solution(3629645732917253048)
XLA Ops:
  1.7 1.6 %collective-permute-start = (bf16[2,4608]{1,0:T(2,128)(2,1)S(1)}, bf16[2,4608]{1,0:T(2,128)(2,1)S(1)}, u32[]{:S(2)}, u32[]{:S(2)}) collective-permute-start(bf16[2,4608]{1,0:T(2,128)(2,1)S(1)} %get-tuple-element.43), channel_id=1, source_target_pairs={{0,2},{1,3},{2,0},{3,1},{4,6},{5,7},{6,4},{7,5},{8,10},{9,11},{10,... | collective-permute-start | bytes 55304 | tf_op jit(solution)/shard_map/ppermute | solution.py:332
  3.2 1.5 %collective-permute-start.1 = (bf16[2,4608]{1,0:T(2,128)(2,1)S(1)}, bf16[2,4608]{1,0:T(2,128)(2,1)S(1)}, u32[]{:S(2)}, u32[]{:S(2)}) collective-permute-start(bf16[2,4608]{1,0:T(2,128)(2,1)S(1)} %get-tuple-element.44), channel_id=1, source_target_pairs={{0,4},{1,5},{2,6},{3,7},{4,0},{5,1},{6,2},{7,3},{8,12},{9,13},{10,... | collective-permute-start | bytes 55304 | tf_op jit(solution)/shard_map/ppermute | solution.py:332
  5.7 1.2 %collective-permute-done.1.refs_2_ = bf16[2,4608]{1,0:T(2,128)(2,1)S(1)} collective-permute-done((bf16[2,4608]{1,0:T(2,128)(2,1)S(1)}, bf16[2,4608]{1,0:T(2,128)(2,1)S(1)}, u32[]{:S(2)}, u32[]{:S(2)}) %collective-permute-start.1) | collective-permute-done | bytes 18464 | tf_op jit(solution)/shard_map/ppermute | solution.py:332
  7.0 2.4 %collective-permute-done.2.refs_3_ = bf16[2,4608]{1,0:T(2,128)(2,1)S(1)} collective-permute-done((bf16[2,4608]{1,0:T(2,128)(2,1)S(1)}, bf16[2,4608]{1,0:T(2,128)(2,1)S(1)}, u32[]{:S(2)}, u32[]{:S(2)}) %collective-permute-start.2) | collective-permute-done | bytes 18464 | tf_op jit(solution)/shard_map/ppermute | solution.py:332
  9.4 1.2 %collective-permute-done.6.refs_7_ = bf16[2,4608]{1,0:T(2,128)(2,1)S(1)} collective-permute-done((bf16[2,4608]{1,0:T(2,128)(2,1)S(1)}, bf16[2,4608]{1,0:T(2,128)(2,1)S(1)}, u32[]{:S(2)}, u32[]{:S(2)}) %collective-permute-start.6) | collective-permute-done | bytes 18464 | tf_op jit(solution)/shard_map/ppermute | solution.py:335
  11.0 1.1 %collective-permute-done.7.refs_1_ = bf16[16,2048]{1,0:T(8,128)(2,1)S(1)} collective-permute-done((bf16[16,2048]{1,0:T(8,128)(2,1)S(1)}, bf16[16,2048]{1,0:T(8,128)(2,1)S(1)}, u32[]{:S(2)}, u32[]{:S(2)}) %collective-permute-start.7) | collective-permute-done | bytes 65568 | tf_op jit(solution)/shard_map/ppermute | solution.py:335
  15.8 1.1 %collective-permute-done.12.refs_1_ = bf16[16,2048]{1,0:T(8,128)(2,1)S(1)} collective-permute-done((bf16[16,2048]{1,0:T(8,128)(2,1)S(1)}, bf16[16,2048]{1,0:T(8,128)(2,1)S(1)}, u32[]{:S(2)}, u32[]{:S(2)}) %collective-permute-start.12) | collective-permute-done | bytes 65568 | tf_op jit(solution)/shard_map/ppermute | solution.py:335
  17.0 1.1 %collective-permute-done.13.refs_1_ = bf16[16,2048]{1,0:T(8,128)(2,1)S(1)} collective-permute-done((bf16[16,2048]{1,0:T(8,128)(2,1)S(1)}, bf16[16,2048]{1,0:T(8,128)(2,1)S(1)}, u32[]{:S(2)}, u32[]{:S(2)}) %collective-permute-start.13) | collective-permute-done | bytes 65568 | tf_op jit(solution)/shard_map/ppermute | solution.py:335
  18.2 13.5 %collective-permute-start.14 = (bf16[16,2176]{1,0:T(8,128)(2,1)S(1)}, bf16[16,2176]{1,0:T(8,128)(2,1)S(1)}, u32[]{:S(2)}, u32[]{:S(2)}) collective-permute-start(bf16[16,2176]{1,0:T(8,128)(2,1)S(1)} %get-tuple-element.58), channel_id=1, source_target_pairs={{0,0},{1,1},{2,2},{3,3},{4,4},{5,5},{6,6},{7,7},{8,16},{9,17},{10,... | collective-permute-start | bytes 208904 | tf_op jit(solution)/shard_map/ppermute | solution.py:350
  34.5 1.2 %collective-permute-done.18.refs_1_ = bf16[16,2048]{1,0:T(8,128)(2,1)S(1)} collective-permute-done((bf16[16,2048]{1,0:T(8,128)(2,1)S(1)}, bf16[16,2048]{1,0:T(8,128)(2,1)S(1)}, u32[]{:S(2)}, u32[]{:S(2)}) %collective-permute-start.18) | collective-permute-done | bytes 65568 | tf_op jit(solution)/shard_map/ppermute | solution.py:335
  35.8 1.1 %collective-permute-done.19.refs_1_ = bf16[16,2048]{1,0:T(8,128)(2,1)S(1)} collective-permute-done((bf16[16,2048]{1,0:T(8,128)(2,1)S(1)}, bf16[16,2048]{1,0:T(8,128)(2,1)S(1)}, u32[]{:S(2)}, u32[]{:S(2)}) %collective-permute-start.19) | collective-permute-done | bytes 65568 | tf_op jit(solution)/shard_map/ppermute | solution.py:335
  37.0 1.9 %collective-permute-start.20 = (bf16[16,2176]{1,0:T(8,128)(2,1)S(1)}, bf16[16,2176]{1,0:T(8,128)(2,1)S(1)}, u32[]{:S(2)}, u32[]{:S(2)}) collective-permute-start(bf16[16,2176]{1,0:T(8,128)(2,1)S(1)} %get-tuple-element.65), channel_id=1, source_target_pairs={{0,16},{1,17},{2,18},{3,19},{4,20},{5,21},{6,22},{7,23},{8,8},{9,9... | collective-permute-start | bytes 208904 | tf_op jit(solution)/shard_map/ppermute | solution.py:350
  39.0 1.3 %collective-permute-start.23 = (bf16[16,2048]{1,0:T(8,128)(2,1)S(1)}, bf16[16,2048]{1,0:T(8,128)(2,1)S(1)}, u32[]{:S(2)}, u32[]{:S(2)}) collective-permute-start(bf16[16,2048]{1,0:T(8,128)(2,1)S(1)} %get-tuple-element.66.refs_2_), channel_id=1, source_target_pairs={{16,30},{17,31},{18,28},{19,29},{20,26},{21,27},{22,24},{23,25}} | collective-permute-start | bytes 196616 | tf_op jit(solution)/shard_map/ppermute | solution.py:350
  40.3 1.3 %collective-permute-start.22 = (bf16[16,2048]{1,0:T(8,128)(2,1)S(1)}, bf16[16,2048]{1,0:T(8,128)(2,1)S(1)}, u32[]{:S(2)}, u32[]{:S(2)}) collective-permute-start(bf16[16,2048]{1,0:T(8,128)(2,1)S(1)} %get-tuple-element.66.refs_2_), channel_id=1, source_target_pairs={{16,28},{17,29},{18,30},{19,31},{20,24},{21,25},{22,26},{23,27}} | collective-permute-start | bytes 196616 | tf_op jit(solution)/shard_map/ppermute | solution.py:350
  41.6 1.3 %collective-permute-start.21 = (bf16[16,2048]{1,0:T(8,128)(2,1)S(1)}, bf16[16,2048]{1,0:T(8,128)(2,1)S(1)}, u32[]{:S(2)}, u32[]{:S(2)}) collective-permute-start(bf16[16,2048]{1,0:T(8,128)(2,1)S(1)} %get-tuple-element.66.refs_2_), channel_id=1, source_target_pairs={{16,26},{17,27},{18,24},{19,25},{20,30},{21,31},{22,28},{23,29}} | collective-permute-start | bytes 196616 | tf_op jit(solution)/shard_map/ppermute | solution.py:350
  43.1 4.6 %collective-permute-done.20.before.refs_0_ = bf16[16,2176]{1,0:T(8,128)(2,1)S(1)} collective-permute-done((bf16[16,2176]{1,0:T(8,128)(2,1)S(1)}, bf16[16,2176]{1,0:T(8,128)(2,1)S(1)}, u32[]{:S(2)}, u32[]{:S(2)}) %collective-permute-start.20) | collective-permute-done | bytes 69664 | tf_op jit(solution)/shard_map/ppermute | solution.py:350
  48.1 3.5 %collective-permute-done.23.refs_3_ = bf16[16,2048]{1,0:T(8,128)(2,1)S(1)} collective-permute-done((bf16[16,2048]{1,0:T(8,128)(2,1)S(1)}, bf16[16,2048]{1,0:T(8,128)(2,1)S(1)}, u32[]{:S(2)}, u32[]{:S(2)}) %collective-permute-start.23) | collective-permute-done | bytes 65568 | tf_op jit(solution)/shard_map/ppermute | solution.py:350
  53.9 1.3 %shard_map.95 = (bf16[8,4096]{1,0:T(8,128)(2,1)S(1)}, bf16[8,4096]{1,0:T(8,128)(2,1)S(1)}, bf16[8,4096]{1,0:T(8,128)(2,1)S(1)}) custom-call(bf16[16,2048]{1,0:T(8,128)(2,1)S(1)} %shard_map.93.half.refs_0_, bf16[16,2048]{1,0:T(8,128)(2,1)S(1)} %collective-permute-done.25.refs_1_, f32[16,512]{1,0:T(8,128)S(1)} %get-tuple-element.69.refs_2_, ...), custom_call_target="tpu_custom_call" | custom-call | flops 100663296 | bytes 12804096 | tf_op jit(solution)/shard_map/pallas_call | solution.py:24
  55.5 1.1 %collective-permute-done.26.refs_1_ = bf16[8,4096]{1,0:T(8,128)(2,1)S(1)} collective-permute-done((bf16[8,4096]{1,0:T(8,128)(2,1)S(1)}, bf16[8,4096]{1,0:T(8,128)(2,1)S(1)}, u32[]{:S(2)}, u32[]{:S(2)}) %collective-permute-start.26) | collective-permute-done | bytes 65568 | tf_op jit(solution)/shard_map/ppermute | solution.py:335
  56.8 1.0 %collective-permute-start.27 = (bf16[2,4096]{1,0:T(2,128)(2,1)S(1)}, bf16[2,4096]{1,0:T(2,128)(2,1)S(1)}, u32[]{:S(2)}, u32[]{:S(2)}) collective-permute-start(bf16[2,4096]{1,0:T(2,128)(2,1)S(1)} %get-tuple-element.76), channel_id=1, source_target_pairs={{0,2},{1,3},{2,0},{3,1},{4,6},{5,7},{6,4},{7,5},{8,10},{9,11},{10,... | collective-permute-start | bytes 49160 | tf_op jit(solution)/shard_map/ppermute | solution.py:332
  57.7 1.4 %collective-permute-start.28 = (bf16[2,4096]{1,0:T(2,128)(2,1)S(1)}, bf16[2,4096]{1,0:T(2,128)(2,1)S(1)}, u32[]{:S(2)}, u32[]{:S(2)}) collective-permute-start(bf16[2,4096]{1,0:T(2,128)(2,1)S(1)} %get-tuple-element.77), channel_id=1, source_target_pairs={{0,4},{1,5},{2,6},{3,7},{4,0},{5,1},{6,2},{7,3},{8,12},{9,13},{10,... | collective-permute-start | bytes 49160 | tf_op jit(solution)/shard_map/ppermute | solution.py:332
  59.1 1.2 %collective-permute-start.29 = (bf16[2,4096]{1,0:T(2,128)(2,1)S(1)}, bf16[2,4096]{1,0:T(2,128)(2,1)S(1)}, u32[]{:S(2)}, u32[]{:S(2)}) collective-permute-start(bf16[2,4096]{1,0:T(2,128)(2,1)S(1)} %get-tuple-element.78), channel_id=1, source_target_pairs={{0,6},{1,7},{2,4},{3,5},{4,2},{5,3},{6,0},{7,1},{8,14},{9,15},{10,... | collective-permute-start | bytes 49160 | tf_op jit(solution)/shard_map/ppermute | solution.py:332
  60.6 0.9 %collective-permute-done.28.refs_2_ = bf16[2,4096]{1,0:T(2,128)(2,1)S(1)} collective-permute-done((bf16[2,4096]{1,0:T(2,128)(2,1)S(1)}, bf16[2,4096]{1,0:T(2,128)(2,1)S(1)}, u32[]{:S(2)}, u32[]{:S(2)}) %collective-permute-start.28) | collective-permute-done | bytes 16416 | tf_op jit(solution)/shard_map/ppermute | solution.py:332
  61.5 2.3 %collective-permute-done.29.refs_3_ = bf16[2,4096]{1,0:T(2,128)(2,1)S(1)} collective-permute-done((bf16[2,4096]{1,0:T(2,128)(2,1)S(1)}, bf16[2,4096]{1,0:T(2,128)(2,1)S(1)}, u32[]{:S(2)}, u32[]{:S(2)}) %collective-permute-start.29) | collective-permute-done | bytes 16416 | tf_op jit(solution)/shard_map/ppermute | solution.py:332
  (76 shorter events, 14.3 us)
Async XLA Ops:
  1.7 3.8 %collective-permute-start = (bf16[2,4608]{1,0:T(2,128)(2,1)S(1)}, bf16[2,4608]{1,0:T(2,128)(2,1)S(1)}, u32[]{:S(2)}, u32[]{:S(2)}) collective-permute-start(bf16[2,4608]{1,0:T(2,128)(2,1)S(1)} %get-tuple-element.43), channel_id=1, source_target_pairs={{0,2},{1,3},{2,0},{3,1},{4,6},{5,7},{6,4},{7,5},{8,10},{9,11},{10,... | collective-permute-start | bytes 55304 | tf_op jit(solution)/shard_map/ppermute | solution.py:332
  3.2 3.8 %collective-permute-start.1 = (bf16[2,4608]{1,0:T(2,128)(2,1)S(1)}, bf16[2,4608]{1,0:T(2,128)(2,1)S(1)}, u32[]{:S(2)}, u32[]{:S(2)}) collective-permute-start(bf16[2,4608]{1,0:T(2,128)(2,1)S(1)} %get-tuple-element.44), channel_id=1, source_target_pairs={{0,4},{1,5},{2,6},{3,7},{4,0},{5,1},{6,2},{7,3},{8,12},{9,13},{10,... | collective-permute-start | bytes 55304 | tf_op jit(solution)/shard_map/ppermute | solution.py:332
  4.8 4.7 %collective-permute-start.2 = (bf16[2,4608]{1,0:T(2,128)(2,1)S(1)}, bf16[2,4608]{1,0:T(2,128)(2,1)S(1)}, u32[]{:S(2)}, u32[]{:S(2)}) collective-permute-start(bf16[2,4608]{1,0:T(2,128)(2,1)S(1)} %get-tuple-element.45), channel_id=1, source_target_pairs={{0,6},{1,7},{2,4},{3,5},{4,2},{5,3},{6,0},{7,1},{8,14},{9,15},{10,... | collective-permute-start | bytes 55304 | tf_op jit(solution)/shard_map/ppermute | solution.py:332
  5.2 4.2 %collective-permute-start.3 = (bf16[2,4608]{1,0:T(2,128)(2,1)S(1)}, bf16[2,4608]{1,0:T(2,128)(2,1)S(1)}, u32[]{:S(2)}, u32[]{:S(2)}) collective-permute-start(bf16[2,4608]{1,0:T(2,128)(2,1)S(1)} %get-tuple-element.42.refs_0_), channel_id=1, source_target_pairs={{0,1},{1,0},{2,3},{3,2},{4,5},{5,4},{6,7},{7,6},{8,9},{9,8},{10,11... | collective-permute-start | bytes 55304 | tf_op jit(solution)/shard_map/ppermute | solution.py:335
  5.5 3.9 %collective-permute-start.4 = (bf16[2,4608]{1,0:T(2,128)(2,1)S(1)}, bf16[2,4608]{1,0:T(2,128)(2,1)S(1)}, u32[]{:S(2)}, u32[]{:S(2)}) collective-permute-start(bf16[2,4608]{1,0:T(2,128)(2,1)S(1)} %collective-permute-done.refs_1_), channel_id=1, source_target_pairs={{0,1},{1,0},{2,3},{3,2},{4,5},{5,4},{6,7},{7,6},{8,9},{9,8},{10,11... | collective-permute-start | bytes 55304 | tf_op jit(solution)/shard_map/ppermute | solution.py:335
  7.0 2.4 %collective-permute-start.5 = (bf16[2,4608]{1,0:T(2,128)(2,1)S(1)}, bf16[2,4608]{1,0:T(2,128)(2,1)S(1)}, u32[]{:S(2)}, u32[]{:S(2)}) collective-permute-start(bf16[2,4608]{1,0:T(2,128)(2,1)S(1)} %collective-permute-done.1.refs_2_), channel_id=1, source_target_pairs={{0,1},{1,0},{2,3},{3,2},{4,5},{5,4},{6,7},{7,6},{8,9},{9,8},{10,11... | collective-permute-start | bytes 55304 | tf_op jit(solution)/shard_map/ppermute | solution.py:335
  10.8 1.3 %collective-permute-start.7 = (bf16[16,2048]{1,0:T(8,128)(2,1)S(1)}, bf16[16,2048]{1,0:T(8,128)(2,1)S(1)}, u32[]{:S(2)}, u32[]{:S(2)}) collective-permute-start(bf16[16,2048]{1,0:T(8,128)(2,1)S(1)} %get-tuple-element.48), channel_id=1, source_target_pairs={{0,1},{1,0},{2,3},{3,2},{4,5},{5,4},{6,7},{7,6},{8,9},{9,8},{10,11... | collective-permute-start | bytes 196616 | tf_op jit(solution)/shard_map/ppermute | solution.py:335
  12.2 2.7 %collective-permute-start.8 = (bf16[16,2176]{1,0:T(8,128)(2,1)S(1)}, bf16[16,2176]{1,0:T(8,128)(2,1)S(1)}, u32[]{:S(2)}, u32[]{:S(2)}) collective-permute-start(bf16[16,2176]{1,0:T(8,128)(2,1)S(1)} %get-tuple-element.51), channel_id=1, source_target_pairs={{0,8},{1,9},{2,10},{3,11},{4,12},{5,13},{6,14},{7,15},{8,16},{9,17... | collective-permute-start | bytes 208904 | tf_op jit(solution)/shard_map/ppermute | solution.py:350
  12.9 2.4 %collective-permute-start.11 = (bf16[16,2048]{1,0:T(8,128)(2,1)S(1)}, bf16[16,2048]{1,0:T(8,128)(2,1)S(1)}, u32[]{:S(2)}, u32[]{:S(2)}) collective-permute-start(bf16[16,2048]{1,0:T(8,128)(2,1)S(1)} %get-tuple-element.52.refs_0_), channel_id=1, source_target_pairs={{0,14},{1,15},{2,12},{3,13},{4,10},{5,11},{6,8},{7,9}} | collective-permute-start | bytes 196616 | tf_op jit(solution)/shard_map/ppermute | solution.py:350
  13.6 1.7 %collective-permute-start.10 = (bf16[16,2048]{1,0:T(8,128)(2,1)S(1)}, bf16[16,2048]{1,0:T(8,128)(2,1)S(1)}, u32[]{:S(2)}, u32[]{:S(2)}) collective-permute-start(bf16[16,2048]{1,0:T(8,128)(2,1)S(1)} %get-tuple-element.52.refs_0_), channel_id=1, source_target_pairs={{0,12},{1,13},{2,14},{3,15},{4,8},{5,9},{6,10},{7,11}} | collective-permute-start | bytes 196616 | tf_op jit(solution)/shard_map/ppermute | solution.py:350
  15.5 1.3 %collective-permute-start.12 = (bf16[16,2048]{1,0:T(8,128)(2,1)S(1)}, bf16[16,2048]{1,0:T(8,128)(2,1)S(1)}, u32[]{:S(2)}, u32[]{:S(2)}) collective-permute-start(bf16[16,2048]{1,0:T(8,128)(2,1)S(1)} %shard_map.80.half.refs_0_.refs_2_), channel_id=1, source_target_pairs={{0,1},{1,0},{2,3},{3,2},{4,5},{5,4},{6,7},{7,6},{8,9},{9,8},{10,11... | collective-permute-start | bytes 196616 | tf_op jit(solution)/shard_map/ppermute | solution.py:335
  18.2 15.5 %collective-permute-start.14 = (bf16[16,2176]{1,0:T(8,128)(2,1)S(1)}, bf16[16,2176]{1,0:T(8,128)(2,1)S(1)}, u32[]{:S(2)}, u32[]{:S(2)}) collective-permute-start(bf16[16,2176]{1,0:T(8,128)(2,1)S(1)} %get-tuple-element.58), channel_id=1, source_target_pairs={{0,0},{1,1},{2,2},{3,3},{4,4},{5,5},{6,6},{7,7},{8,16},{9,17},{10,... | collective-permute-start | bytes 208904 | tf_op jit(solution)/shard_map/ppermute | solution.py:350
  31.7 2.4 %collective-permute-start.17 = (bf16[16,2048]{1,0:T(8,128)(2,1)S(1)}, bf16[16,2048]{1,0:T(8,128)(2,1)S(1)}, u32[]{:S(2)}, u32[]{:S(2)}) collective-permute-start(bf16[16,2048]{1,0:T(8,128)(2,1)S(1)} %get-tuple-element.59.refs_1_), channel_id=1, source_target_pairs={{8,22},{9,23},{10,20},{11,21},{12,18},{13,19},{14,16},{15,17}} | collective-permute-start | bytes 196616 | tf_op jit(solution)/shard_map/ppermute | solution.py:350
  32.4 1.7 %collective-permute-start.16 = (bf16[16,2048]{1,0:T(8,128)(2,1)S(1)}, bf16[16,2048]{1,0:T(8,128)(2,1)S(1)}, u32[]{:S(2)}, u32[]{:S(2)}) collective-permute-start(bf16[16,2048]{1,0:T(8,128)(2,1)S(1)} %get-tuple-element.59.refs_1_), channel_id=1, source_target_pairs={{8,20},{9,21},{10,22},{11,23},{12,16},{13,17},{14,18},{15,19}} | collective-permute-start | bytes 196616 | tf_op jit(solution)/shard_map/ppermute | solution.py:350
  34.3 1.3 %collective-permute-start.18 = (bf16[16,2048]{1,0:T(8,128)(2,1)S(1)}, bf16[16,2048]{1,0:T(8,128)(2,1)S(1)}, u32[]{:S(2)}, u32[]{:S(2)}) collective-permute-start(bf16[16,2048]{1,0:T(8,128)(2,1)S(1)} %shard_map.86.half.refs_0_.refs_2_), channel_id=1, source_target_pairs={{0,1},{1,0},{2,3},{3,2},{4,5},{5,4},{6,7},{7,6},{8,9},{9,8},{10,11... | collective-permute-start | bytes 196616 | tf_op jit(solution)/shard_map/ppermute | solution.py:335
  37.0 10.7 %collective-permute-start.20 = (bf16[16,2176]{1,0:T(8,128)(2,1)S(1)}, bf16[16,2176]{1,0:T(8,128)(2,1)S(1)}, u32[]{:S(2)}, u32[]{:S(2)}) collective-permute-start(bf16[16,2176]{1,0:T(8,128)(2,1)S(1)} %get-tuple-element.65), channel_id=1, source_target_pairs={{0,16},{1,17},{2,18},{3,19},{4,20},{5,21},{6,22},{7,23},{8,8},{9,9... | collective-permute-start | bytes 208904 | tf_op jit(solution)/shard_map/ppermute | solution.py:350
  39.0 12.7 %collective-permute-start.23 = (bf16[16,2048]{1,0:T(8,128)(2,1)S(1)}, bf16[16,2048]{1,0:T(8,128)(2,1)S(1)}, u32[]{:S(2)}, u32[]{:S(2)}) collective-permute-start(bf16[16,2048]{1,0:T(8,128)(2,1)S(1)} %get-tuple-element.66.refs_2_), channel_id=1, source_target_pairs={{16,30},{17,31},{18,28},{19,29},{20,26},{21,27},{22,24},{23,25}} | collective-permute-start | bytes 196616 | tf_op jit(solution)/shard_map/ppermute | solution.py:350
  40.3 11.7 %collective-permute-start.22 = (bf16[16,2048]{1,0:T(8,128)(2,1)S(1)}, bf16[16,2048]{1,0:T(8,128)(2,1)S(1)}, u32[]{:S(2)}, u32[]{:S(2)}) collective-permute-start(bf16[16,2048]{1,0:T(8,128)(2,1)S(1)} %get-tuple-element.66.refs_2_), channel_id=1, source_target_pairs={{16,28},{17,29},{18,30},{19,31},{20,24},{21,25},{22,26},{23,27}} | collective-permute-start | bytes 196616 | tf_op jit(solution)/shard_map/ppermute | solution.py:350
  41.6 10.8 %collective-permute-start.21 = (bf16[16,2048]{1,0:T(8,128)(2,1)S(1)}, bf16[16,2048]{1,0:T(8,128)(2,1)S(1)}, u32[]{:S(2)}, u32[]{:S(2)}) collective-permute-start(bf16[16,2048]{1,0:T(8,128)(2,1)S(1)} %get-tuple-element.66.refs_2_), channel_id=1, source_target_pairs={{16,26},{17,27},{18,24},{19,25},{20,30},{21,31},{22,28},{23,29}} | collective-permute-start | bytes 196616 | tf_op jit(solution)/shard_map/ppermute | solution.py:350
  42.9 5.2 %collective-permute-start.24 = (bf16[8,2048]{1,0:T(8,128)(2,1)S(1)}, bf16[8,2048]{1,0:T(8,128)(2,1)S(1)}, u32[]{:S(2)}, u32[]{:S(2)}) collective-permute-start(bf16[8,2048]{1,0:T(8,128)(2,1)S(1)} %get-tuple-element.68), channel_id=1, source_target_pairs={{0,1},{1,0},{2,3},{3,2},{4,5},{5,4},{6,7},{7,6},{8,9},{9,8},{10,11... | collective-permute-start | bytes 98312 | tf_op jit(solution)/shard_map/ppermute | solution.py:335
  52.6 1.3 %collective-permute-start.25 = (bf16[16,2048]{1,0:T(8,128)(2,1)S(1)}, bf16[16,2048]{1,0:T(8,128)(2,1)S(1)}, u32[]{:S(2)}, u32[]{:S(2)}) collective-permute-start(bf16[16,2048]{1,0:T(8,128)(2,1)S(1)} %shard_map.93.half.refs_0_), channel_id=1, source_target_pairs={{0,1},{1,0},{2,3},{3,2},{4,5},{5,4},{6,7},{7,6},{8,9},{9,8},{10,11... | collective-permute-start | bytes 196616 | tf_op jit(solution)/shard_map/ppermute | solution.py:335
  56.8 3.8 %collective-permute-start.27 = (bf16[2,4096]{1,0:T(2,128)(2,1)S(1)}, bf16[2,4096]{1,0:T(2,128)(2,1)S(1)}, u32[]{:S(2)}, u32[]{:S(2)}) collective-permute-start(bf16[2,4096]{1,0:T(2,128)(2,1)S(1)} %get-tuple-element.76), channel_id=1, source_target_pairs={{0,2},{1,3},{2,0},{3,1},{4,6},{5,7},{6,4},{7,5},{8,10},{9,11},{10,... | collective-permute-start | bytes 49160 | tf_op jit(solution)/shard_map/ppermute | solution.py:332
  57.7 3.7 %collective-permute-start.28 = (bf16[2,4096]{1,0:T(2,128)(2,1)S(1)}, bf16[2,4096]{1,0:T(2,128)(2,1)S(1)}, u32[]{:S(2)}, u32[]{:S(2)}) collective-permute-start(bf16[2,4096]{1,0:T(2,128)(2,1)S(1)} %get-tuple-element.77), channel_id=1, source_target_pairs={{0,4},{1,5},{2,6},{3,7},{4,0},{5,1},{6,2},{7,3},{8,12},{9,13},{10,... | collective-permute-start | bytes 49160 | tf_op jit(solution)/shard_map/ppermute | solution.py:332
  59.1 4.6 %collective-permute-start.29 = (bf16[2,4096]{1,0:T(2,128)(2,1)S(1)}, bf16[2,4096]{1,0:T(2,128)(2,1)S(1)}, u32[]{:S(2)}, u32[]{:S(2)}) collective-permute-start(bf16[2,4096]{1,0:T(2,128)(2,1)S(1)} %get-tuple-element.78), channel_id=1, source_target_pairs={{0,6},{1,7},{2,4},{3,5},{4,2},{5,3},{6,0},{7,1},{8,14},{9,15},{10,... | collective-permute-start | bytes 49160 | tf_op jit(solution)/shard_map/ppermute | solution.py:332
  (13 other events, 49.9 us)

commit v5 on v4

--- a/solution.py
+++ b/solution.py
@@ -45,26 +45,23 @@
     return lax.broadcasted_iota(jnp.int32, dims, axis)
 
 
-def rank_kernel(ids, out):
-    rows = ids.shape[1]
+def code_kernel(group, out):
+    expert, _ = place(group)
+    index = iota(out.shape, 0)
+    out[...] = ((expert ^ (index // CAP)) * CAP + lax.rem(index, CAP)).astype(F32)
+
+
+def slot_kernel(wanted, tokens, ids, scale, *outs):
+    rows = tokens.shape[0]
+    width = tokens.shape[1]
     ids_row = ids[...]
     ids_full = jnp.broadcast_to(ids_row, (rows, rows))
     diagonal = iota((rows, rows), 0) == iota((rows, rows), 1)
     ids_column = jnp.sum(jnp.where(diagonal, ids_full, 0), axis=1, keepdims=True)
     earlier = iota((rows, rows), 0) < iota((rows, rows), 1)
     rank = jnp.sum(jnp.where((ids_full == ids_column) & earlier, 1, 0), axis=0, keepdims=True)
-    out[...] = jnp.full(out.shape, -1.0, F32)
-    out[:, 0:rows] = jnp.broadcast_to((ids_row * CAP + rank).astype(F32), (out.shape[0], rows))
-
-
-def slot_kernel(group, position, tokens, scale, *outs):
-    expert, _ = place(group)
-    rows = tokens.shape[0]
-    width = tokens.shape[1]
-    codes = position[...]
-    index = iota(codes.shape, 0)
-    wanted = (expert ^ (index // CAP)) * CAP + lax.rem(index, CAP)
-    chosen = jnp.where(codes == wanted.astype(F32), 1.0, 0.0)[:, 0:rows].astype(BF16)
+    position = (ids_row * CAP + rank).astype(F32)
+    chosen = jnp.where(position == wanted[:, 0:rows], 1.0, 0.0).astype(BF16)
     body = jnp.dot(chosen, tokens[...], preferred_element_type=F32)
     value = scale[...]
     first = value.astype(BF16).astype(F32)
@@ -72,10 +69,9 @@
     third = value - first - second
     for i in range(EXPERTS):
         outs[i][:, 0:width] = body[i * CAP : (i + 1) * CAP, :].astype(BF16)
-        outs[i][:, width : width + LANES] = codes[0:CAP, :].astype(BF16)
-        outs[i][:, width + LANES :] = jnp.zeros((CAP, (BLOCKS - 1) * LANES), BF16)
-        for n, piece in enumerate((first, second, third)):
-            at = width + (n + 1) * LANES
+        outs[i][:, width:] = jnp.full((CAP, BLOCKS * LANES), -1.0, BF16)
+        for n, piece in enumerate((position, first, second, third)):
+            at = width + n * LANES
             outs[i][:, at : at + rows] = jnp.broadcast_to(piece, (CAP, rows)).astype(BF16)
 
 
@@ -335,28 +331,30 @@
         return lax.ppermute(value, "expert", [(d, d ^ m) for d in range(peers)])
 
     def gather(value, marked, tick):
-        hops = list(range(sections))
-        ring = [tick, tick + 1, tick + 2 if tick + 2 < sections else 0]
-        for n, s in enumerate(ring):
-            hops[s] = ring[(n + 1) % 3]
-        pairs = [(s * peers + d, hops[s] * peers + d) for s in range(sections) for d in range(peers)]
         outs = []
         for i in range(EXPERTS):
-            if i:
-                pairs = [
-                    (tick * peers + d, (tick + 1) * peers + (d // group ^ i) * group + d % group)
-                    for d in range(peers)
-                ]
+            ring = [tick, tick + 1]
+            if i == EXPERTS - 1 and sections > 2:
+                ring.append(tick - 1 if tick else 2)
+            pairs = []
+            for s in range(sections):
+                to, move = s, lambda d: d ^ 1
+                if s in ring:
+                    to = ring[(ring.index(s) + 1) % len(ring)]
+                    move = lambda d: d
+                if s == tick:
+                    move = lambda d: (d // group ^ i) * group + d % group
+                pairs += [(s * peers + d, to * peers + move(d)) for d in range(peers)]
             outs.append(lax.ppermute(value if i else marked, ("section", "expert"), pairs))
         return outs
 
-    position = call(
-        rank_kernel, shape((slots, LANES), F32), (expert_ids.reshape(1, count),), flops=START_FLOPS
+    wanted = call(
+        functools.partial(code_kernel, group), shape((slots, LANES), F32), (), flops=START_FLOPS
     )
     sent = call(
-        functools.partial(slot_kernel, group),
+        slot_kernel,
         [shape((CAP, wide))] * EXPERTS,
-        (position, tokens, gate_scale),
+        (wanted, tokens, expert_ids.reshape(1, count), gate_scale),
     )
     arrived = [across(sent[i], i) for i in range(EXPERTS)]
     pieces = list(arrived)

time: 64.9 us -> 59 us (0.909)
  waiting for transfers between devices: 24.7 us -> 21.5 us
  starting transfers between devices: 32.6 us -> 30.8 us
    ppermute x12, waiting for transfers between devices: 8.9 us -> 5.17 us  [gather(): lax.ppermute(value if i else marked, ('section', 'expert'), pairs)]
    ppermute x12, starting transfers between devices: 23.9 us -> 21.7 us  [gather(): lax.ppermute(value if i else marked, ('section', 'expert'), pairs)]
  transfers between devices with their start and end apart: 30 -> 30, of which waited for: 18 -> 25; matrix products, arithmetic and copies ran while one was open for 0% -> 0% of each run, Pallas kernels for 3% -> 3%
where the time goes in v5:
time: 59 us; the launch traced here: 58.9 us
  starting transfers between devices  30.8 us (52%)
  waiting for transfers between devices  21.5 us (36%)
  Pallas kernels  5.51 us (9%)
  local copies, waits for them, and re-layouts  0.82 us (1%)
    ppermute x12, starting transfers between devices, gather(): lax.ppermute(value if i else marked, ('section', 'expert'), pairs)  21.7 us
    ppermute x12, waiting for transfers between devices, within(): return lax.ppermute(value, 'expert', [(d, d ^ m) for d in range(peers)])  8.66 us
    ppermute x6, waiting for transfers between devices, across(): return lax.ppermute(value, 'expert', pairs)  7.66 us
    ppermute x6, starting transfers between devices, across(): return lax.ppermute(value, 'expert', pairs)  7.11 us
    pallas_call x25, Pallas kernels, call(): pl.pallas_call(kernel, out_shape=outs, in_specs=specs or [VMEM] * len(arg...  5.51 us
    ppermute x12, waiting for transfers between devices, gather(): lax.ppermute(value if i else marked, ('section', 'expert'), pairs)  5.17 us
    ppermute x12, starting transfers between devices, within(): return lax.ppermute(value, 'expert', [(d, d ^ m) for d in range(peers)])  2 us
  transfers between devices with their start and end apart: 30, of which 25 were waited for; matrix products, arithmetic and copies ran while one was open for 0% of the time, Pallas kernels for 3%

profile of v5, /device:TPU:24, one launch (start us, length us, event | category | flops | bytes accessed | tf_op | source)
XLA Modules:
  0.0 58.9 jit_solution(622638099740703104)
XLA Ops:
  1.1 1.6 %collective-permute-start = (bf16[2,4608]{1,0:T(2,128)(2,1)S(1)}, bf16[2,4608]{1,0:T(2,128)(2,1)S(1)}, u32[]{:S(2)}, u32[]{:S(2)}) collective-permute-start(bf16[2,4608]{1,0:T(2,128)(2,1)S(1)} %get-tuple-element.43), channel_id=1, source_target_pairs={{0,2},{1,3},{2,0},{3,1},{4,6},{5,7},{6,4},{7,5},{8,10},{9,11},{10,... | collective-permute-start | bytes 55304 | tf_op jit(solution)/shard_map/ppermute | solution.py:328
  2.7 1.5 %collective-permute-start.1 = (bf16[2,4608]{1,0:T(2,128)(2,1)S(1)}, bf16[2,4608]{1,0:T(2,128)(2,1)S(1)}, u32[]{:S(2)}, u32[]{:S(2)}) collective-permute-start(bf16[2,4608]{1,0:T(2,128)(2,1)S(1)} %get-tuple-element.44), channel_id=1, source_target_pairs={{0,4},{1,5},{2,6},{3,7},{4,0},{5,1},{6,2},{7,3},{8,12},{9,13},{10,... | collective-permute-start | bytes 55304 | tf_op jit(solution)/shard_map/ppermute | solution.py:328
  5.2 1.2 %collective-permute-done.1.refs_2_ = bf16[2,4608]{1,0:T(2,128)(2,1)S(1)} collective-permute-done((bf16[2,4608]{1,0:T(2,128)(2,1)S(1)}, bf16[2,4608]{1,0:T(2,128)(2,1)S(1)}, u32[]{:S(2)}, u32[]{:S(2)}) %collective-permute-start.1) | collective-permute-done | bytes 18464 | tf_op jit(solution)/shard_map/ppermute | solution.py:328
  6.5 2.4 %collective-permute-done.2.refs_3_ = bf16[2,4608]{1,0:T(2,128)(2,1)S(1)} collective-permute-done((bf16[2,4608]{1,0:T(2,128)(2,1)S(1)}, bf16[2,4608]{1,0:T(2,128)(2,1)S(1)}, u32[]{:S(2)}, u32[]{:S(2)}) %collective-permute-start.2) | collective-permute-done | bytes 18464 | tf_op jit(solution)/shard_map/ppermute | solution.py:328
  8.9 1.2 %collective-permute-done.6.refs_7_ = bf16[2,4608]{1,0:T(2,128)(2,1)S(1)} collective-permute-done((bf16[2,4608]{1,0:T(2,128)(2,1)S(1)}, bf16[2,4608]{1,0:T(2,128)(2,1)S(1)}, u32[]{:S(2)}, u32[]{:S(2)}) %collective-permute-start.6) | collective-permute-done | bytes 18464 | tf_op jit(solution)/shard_map/ppermute | solution.py:331
  10.5 1.1 %collective-permute-done.7.refs_1_ = bf16[16,2048]{1,0:T(8,128)(2,1)S(1)} collective-permute-done((bf16[16,2048]{1,0:T(8,128)(2,1)S(1)}, bf16[16,2048]{1,0:T(8,128)(2,1)S(1)}, u32[]{:S(2)}, u32[]{:S(2)}) %collective-permute-start.7) | collective-permute-done | bytes 65568 | tf_op jit(solution)/shard_map/ppermute | solution.py:331
  14.3 0.9 %collective-permute-done.12.refs_1_ = bf16[16,2048]{1,0:T(8,128)(2,1)S(1)} collective-permute-done((bf16[16,2048]{1,0:T(8,128)(2,1)S(1)}, bf16[16,2048]{1,0:T(8,128)(2,1)S(1)}, u32[]{:S(2)}, u32[]{:S(2)}) %collective-permute-start.12) | collective-permute-done | bytes 65568 | tf_op jit(solution)/shard_map/ppermute | solution.py:331
  15.6 0.9 %collective-permute-done.13.refs_1_ = bf16[16,2048]{1,0:T(8,128)(2,1)S(1)} collective-permute-done((bf16[16,2048]{1,0:T(8,128)(2,1)S(1)}, bf16[16,2048]{1,0:T(8,128)(2,1)S(1)}, u32[]{:S(2)}, u32[]{:S(2)}) %collective-permute-start.13) | collective-permute-done | bytes 65568 | tf_op jit(solution)/shard_map/ppermute | solution.py:331
  19.2 1.1 %collective-permute-done.18.refs_1_ = bf16[16,2048]{1,0:T(8,128)(2,1)S(1)} collective-permute-done((bf16[16,2048]{1,0:T(8,128)(2,1)S(1)}, bf16[16,2048]{1,0:T(8,128)(2,1)S(1)}, u32[]{:S(2)}, u32[]{:S(2)}) %collective-permute-start.18) | collective-permute-done | bytes 65568 | tf_op jit(solution)/shard_map/ppermute | solution.py:331
  20.5 1.1 %collective-permute-done.19.refs_1_ = bf16[16,2048]{1,0:T(8,128)(2,1)S(1)} collective-permute-done((bf16[16,2048]{1,0:T(8,128)(2,1)S(1)}, bf16[16,2048]{1,0:T(8,128)(2,1)S(1)}, u32[]{:S(2)}, u32[]{:S(2)}) %collective-permute-start.19) | collective-permute-done | bytes 65568 | tf_op jit(solution)/shard_map/ppermute | solution.py:331
  21.6 17.2 %collective-permute-start.20 = (bf16[16,2176]{1,0:T(8,128)(2,1)S(1)}, bf16[16,2176]{1,0:T(8,128)(2,1)S(1)}, u32[]{:S(2)}, u32[]{:S(2)}) collective-permute-start(bf16[16,2176]{1,0:T(8,128)(2,1)S(1)} %get-tuple-element.65), channel_id=1, source_target_pairs={{0,1},{1,0},{2,3},{3,2},{4,5},{5,4},{6,7},{7,6},{8,9},{9,8},{10,11... | collective-permute-start | bytes 208904 | tf_op jit(solution)/shard_map/ppermute | solution.py:348
  38.8 2.4 %collective-permute-start.22 = (bf16[16,2048]{1,0:T(8,128)(2,1)S(1)}, bf16[16,2048]{1,0:T(8,128)(2,1)S(1)}, u32[]{:S(2)}, u32[]{:S(2)}) collective-permute-start(bf16[16,2048]{1,0:T(8,128)(2,1)S(1)} %get-tuple-element.66.refs_2_), channel_id=1, source_target_pairs={{0,1},{1,0},{2,3},{3,2},{4,5},{5,4},{6,7},{7,6},{8,9},{9,8},{10,11... | collective-permute-start | bytes 196616 | tf_op jit(solution)/shard_map/ppermute | solution.py:348
  41.8 0.7 %collective-permute-done.24.refs_6_.refs_5_ = bf16[8,2048]{1,0:T(8,128)(2,1)S(1)} collective-permute-done((bf16[8,2048]{1,0:T(8,128)(2,1)S(1)}, bf16[8,2048]{1,0:T(8,128)(2,1)S(1)}, u32[]{:S(2)}, u32[]{:S(2)}) %collective-permute-start.24) | collective-permute-done | bytes 32800 | tf_op jit(solution)/shard_map/ppermute | solution.py:331
  42.5 3.0 %collective-permute-done.23.refs_3_ = bf16[16,2048]{1,0:T(8,128)(2,1)S(1)} collective-permute-done((bf16[16,2048]{1,0:T(8,128)(2,1)S(1)}, bf16[16,2048]{1,0:T(8,128)(2,1)S(1)}, u32[]{:S(2)}, u32[]{:S(2)}) %collective-permute-start.23) | collective-permute-done | bytes 65568 | tf_op jit(solution)/shard_map/ppermute | solution.py:348
  45.5 0.6 %collective-permute-done.22.refs_2_ = bf16[16,2048]{1,0:T(8,128)(2,1)S(1)} collective-permute-done((bf16[16,2048]{1,0:T(8,128)(2,1)S(1)}, bf16[16,2048]{1,0:T(8,128)(2,1)S(1)}, u32[]{:S(2)}, u32[]{:S(2)}) %collective-permute-start.22) | collective-permute-done | bytes 65568 | tf_op jit(solution)/shard_map/ppermute | solution.py:348
  46.6 0.7 %shard_map.94 = (f32[16,512]{1,0:T(8,128)S(1)}, f32[16,512]{1,0:T(8,128)S(1)}, f32[16,128]{1,0:T(8,128)S(1)}) custom-call(bf16[16,2048]{1,0:T(8,128)(2,1)S(1)} %shard_map.93.half.refs_0_, f32[1,4096]{1,0:T(1,128)S(1)} %copy-done.3, bf16[1,4096,512]{2,1,0:T(8,128)(2,1)S(1)} %copy-done, bf16[1,4096,512]{2,1,0:T(8,128)(2,1)S(1)} %copy-done.1), custom_call_target="tpu_custom_call" | custom-call | flops 67108864 | bytes 8470528 | tf_op jit(solution)/shard_map/pallas_call | solution.py:24
  47.9 1.3 %shard_map.95 = (bf16[8,4096]{1,0:T(8,128)(2,1)S(1)}, bf16[8,4096]{1,0:T(8,128)(2,1)S(1)}, bf16[8,4096]{1,0:T(8,128)(2,1)S(1)}) custom-call(bf16[16,2048]{1,0:T(8,128)(2,1)S(1)} %shard_map.93.half.refs_0_, bf16[16,2048]{1,0:T(8,128)(2,1)S(1)} %collective-permute-done.25.refs_1_, f32[16,512]{1,0:T(8,128)S(1)} %get-tuple-element.69.refs_2_, ...), custom_call_target="tpu_custom_call" | custom-call | flops 100663296 | bytes 12804096 | tf_op jit(solution)/shard_map/pallas_call | solution.py:24
  49.4 1.1 %collective-permute-done.26.refs_1_ = bf16[8,4096]{1,0:T(8,128)(2,1)S(1)} collective-permute-done((bf16[8,4096]{1,0:T(8,128)(2,1)S(1)}, bf16[8,4096]{1,0:T(8,128)(2,1)S(1)}, u32[]{:S(2)}, u32[]{:S(2)}) %collective-permute-start.26) | collective-permute-done | bytes 65568 | tf_op jit(solution)/shard_map/ppermute | solution.py:331
  50.7 1.1 %collective-permute-start.27 = (bf16[2,4096]{1,0:T(2,128)(2,1)S(1)}, bf16[2,4096]{1,0:T(2,128)(2,1)S(1)}, u32[]{:S(2)}, u32[]{:S(2)}) collective-permute-start(bf16[2,4096]{1,0:T(2,128)(2,1)S(1)} %get-tuple-element.76), channel_id=1, source_target_pairs={{0,2},{1,3},{2,0},{3,1},{4,6},{5,7},{6,4},{7,5},{8,10},{9,11},{10,... | collective-permute-start | bytes 49160 | tf_op jit(solution)/shard_map/ppermute | solution.py:328
  51.8 1.5 %collective-permute-start.28 = (bf16[2,4096]{1,0:T(2,128)(2,1)S(1)}, bf16[2,4096]{1,0:T(2,128)(2,1)S(1)}, u32[]{:S(2)}, u32[]{:S(2)}) collective-permute-start(bf16[2,4096]{1,0:T(2,128)(2,1)S(1)} %get-tuple-element.77), channel_id=1, source_target_pairs={{0,4},{1,5},{2,6},{3,7},{4,0},{5,1},{6,2},{7,3},{8,12},{9,13},{10,... | collective-permute-start | bytes 49160 | tf_op jit(solution)/shard_map/ppermute | solution.py:328
  53.4 0.9 %collective-permute-start.29 = (bf16[2,4096]{1,0:T(2,128)(2,1)S(1)}, bf16[2,4096]{1,0:T(2,128)(2,1)S(1)}, u32[]{:S(2)}, u32[]{:S(2)}) collective-permute-start(bf16[2,4096]{1,0:T(2,128)(2,1)S(1)} %get-tuple-element.78), channel_id=1, source_target_pairs={{0,6},{1,7},{2,4},{3,5},{4,2},{5,3},{6,0},{7,1},{8,14},{9,15},{10,... | collective-permute-start | bytes 49160 | tf_op jit(solution)/shard_map/ppermute | solution.py:328
  54.5 1.0 %collective-permute-done.28.refs_2_ = bf16[2,4096]{1,0:T(2,128)(2,1)S(1)} collective-permute-done((bf16[2,4096]{1,0:T(2,128)(2,1)S(1)}, bf16[2,4096]{1,0:T(2,128)(2,1)S(1)}, u32[]{:S(2)}, u32[]{:S(2)}) %collective-permute-start.28) | collective-permute-done | bytes 16416 | tf_op jit(solution)/shard_map/ppermute | solution.py:328
  55.6 2.4 %collective-permute-done.29.refs_3_ = bf16[2,4096]{1,0:T(2,128)(2,1)S(1)} collective-permute-done((bf16[2,4096]{1,0:T(2,128)(2,1)S(1)}, bf16[2,4096]{1,0:T(2,128)(2,1)S(1)}, u32[]{:S(2)}, u32[]{:S(2)}) %collective-permute-start.29) | collective-permute-done | bytes 16416 | tf_op jit(solution)/shard_map/ppermute | solution.py:328
  58.0 0.9 %shard_map.97 = bf16[1,6,4096]{2,1,0:T(8,128)(2,1)} custom-call(bf16[2,4096]{1,0:T(2,128)(2,1)S(1)} %get-tuple-element.75.refs_0_, bf16[2,4096]{1,0:T(2,128)(2,1)S(1)} %collective-permute-done.27.refs_1_, bf16[2,4096]{1,0:T(2,128)(2,1)S(1)} %collective-permute-done.28.refs_2_, bf16[2,4096]{1,0:T(2,128)(2,1)S(1)} %collective-permute-done.29.refs_3_, ...), custom_call_target="tpu_custom_call" | custom-call | flops 1000 | bytes 66048 | tf_op jit(solution)/shard_map/pallas_call | solution.py:24
  (76 shorter events, 10.9 us)
Async XLA Ops:
  1.1 3.8 %collective-permute-start = (bf16[2,4608]{1,0:T(2,128)(2,1)S(1)}, bf16[2,4608]{1,0:T(2,128)(2,1)S(1)}, u32[]{:S(2)}, u32[]{:S(2)}) collective-permute-start(bf16[2,4608]{1,0:T(2,128)(2,1)S(1)} %get-tuple-element.43), channel_id=1, source_target_pairs={{0,2},{1,3},{2,0},{3,1},{4,6},{5,7},{6,4},{7,5},{8,10},{9,11},{10,... | collective-permute-start | bytes 55304 | tf_op jit(solution)/shard_map/ppermute | solution.py:328
  2.7 3.8 %collective-permute-start.1 = (bf16[2,4608]{1,0:T(2,128)(2,1)S(1)}, bf16[2,4608]{1,0:T(2,128)(2,1)S(1)}, u32[]{:S(2)}, u32[]{:S(2)}) collective-permute-start(bf16[2,4608]{1,0:T(2,128)(2,1)S(1)} %get-tuple-element.44), channel_id=1, source_target_pairs={{0,4},{1,5},{2,6},{3,7},{4,0},{5,1},{6,2},{7,3},{8,12},{9,13},{10,... | collective-permute-start | bytes 55304 | tf_op jit(solution)/shard_map/ppermute | solution.py:328
  4.2 4.7 %collective-permute-start.2 = (bf16[2,4608]{1,0:T(2,128)(2,1)S(1)}, bf16[2,4608]{1,0:T(2,128)(2,1)S(1)}, u32[]{:S(2)}, u32[]{:S(2)}) collective-permute-start(bf16[2,4608]{1,0:T(2,128)(2,1)S(1)} %get-tuple-element.45), channel_id=1, source_target_pairs={{0,6},{1,7},{2,4},{3,5},{4,2},{5,3},{6,0},{7,1},{8,14},{9,15},{10,... | collective-permute-start | bytes 55304 | tf_op jit(solution)/shard_map/ppermute | solution.py:328
  4.7 4.2 %collective-permute-start.3 = (bf16[2,4608]{1,0:T(2,128)(2,1)S(1)}, bf16[2,4608]{1,0:T(2,128)(2,1)S(1)}, u32[]{:S(2)}, u32[]{:S(2)}) collective-permute-start(bf16[2,4608]{1,0:T(2,128)(2,1)S(1)} %get-tuple-element.42.refs_0_), channel_id=1, source_target_pairs={{0,1},{1,0},{2,3},{3,2},{4,5},{5,4},{6,7},{7,6},{8,9},{9,8},{10,11... | collective-permute-start | bytes 55304 | tf_op jit(solution)/shard_map/ppermute | solution.py:331
  5.0 3.9 %collective-permute-start.4 = (bf16[2,4608]{1,0:T(2,128)(2,1)S(1)}, bf16[2,4608]{1,0:T(2,128)(2,1)S(1)}, u32[]{:S(2)}, u32[]{:S(2)}) collective-permute-start(bf16[2,4608]{1,0:T(2,128)(2,1)S(1)} %collective-permute-done.refs_1_), channel_id=1, source_target_pairs={{0,1},{1,0},{2,3},{3,2},{4,5},{5,4},{6,7},{7,6},{8,9},{9,8},{10,11... | collective-permute-start | bytes 55304 | tf_op jit(solution)/shard_map/ppermute | solution.py:331
  6.5 2.4 %collective-permute-start.5 = (bf16[2,4608]{1,0:T(2,128)(2,1)S(1)}, bf16[2,4608]{1,0:T(2,128)(2,1)S(1)}, u32[]{:S(2)}, u32[]{:S(2)}) collective-permute-start(bf16[2,4608]{1,0:T(2,128)(2,1)S(1)} %collective-permute-done.1.refs_2_), channel_id=1, source_target_pairs={{0,1},{1,0},{2,3},{3,2},{4,5},{5,4},{6,7},{7,6},{8,9},{9,8},{10,11... | collective-permute-start | bytes 55304 | tf_op jit(solution)/shard_map/ppermute | solution.py:331
  10.3 1.3 %collective-permute-start.7 = (bf16[16,2048]{1,0:T(8,128)(2,1)S(1)}, bf16[16,2048]{1,0:T(8,128)(2,1)S(1)}, u32[]{:S(2)}, u32[]{:S(2)}) collective-permute-start(bf16[16,2048]{1,0:T(8,128)(2,1)S(1)} %get-tuple-element.48), channel_id=1, source_target_pairs={{0,1},{1,0},{2,3},{3,2},{4,5},{5,4},{6,7},{7,6},{8,9},{9,8},{10,11... | collective-permute-start | bytes 196616 | tf_op jit(solution)/shard_map/ppermute | solution.py:331
  11.7 1.3 %collective-permute-start.8 = (bf16[16,2176]{1,0:T(8,128)(2,1)S(1)}, bf16[16,2176]{1,0:T(8,128)(2,1)S(1)}, u32[]{:S(2)}, u32[]{:S(2)}) collective-permute-start(bf16[16,2176]{1,0:T(8,128)(2,1)S(1)} %get-tuple-element.51), channel_id=1, source_target_pairs={{0,8},{1,9},{2,10},{3,11},{4,12},{5,13},{6,14},{7,15},{8,0},{9,1},... | collective-permute-start | bytes 208904 | tf_op jit(solution)/shard_map/ppermute | solution.py:348
  11.9 1.5 %collective-permute-start.11 = (bf16[16,2048]{1,0:T(8,128)(2,1)S(1)}, bf16[16,2048]{1,0:T(8,128)(2,1)S(1)}, u32[]{:S(2)}, u32[]{:S(2)}) collective-permute-start(bf16[16,2048]{1,0:T(8,128)(2,1)S(1)} %get-tuple-element.52.refs_0_), channel_id=1, source_target_pairs={{0,14},{1,15},{2,12},{3,13},{4,10},{5,11},{6,8},{7,9},{8,16},{9,17... | collective-permute-start | bytes 196616 | tf_op jit(solution)/shard_map/ppermute | solution.py:348
  12.3 1.3 %collective-permute-start.10 = (bf16[16,2048]{1,0:T(8,128)(2,1)S(1)}, bf16[16,2048]{1,0:T(8,128)(2,1)S(1)}, u32[]{:S(2)}, u32[]{:S(2)}) collective-permute-start(bf16[16,2048]{1,0:T(8,128)(2,1)S(1)} %get-tuple-element.52.refs_0_), channel_id=1, source_target_pairs={{0,12},{1,13},{2,14},{3,15},{4,8},{5,9},{6,10},{7,11},{8,0},{9,1},... | collective-permute-start | bytes 196616 | tf_op jit(solution)/shard_map/ppermute | solution.py:348
  13.9 1.3 %collective-permute-start.12 = (bf16[16,2048]{1,0:T(8,128)(2,1)S(1)}, bf16[16,2048]{1,0:T(8,128)(2,1)S(1)}, u32[]{:S(2)}, u32[]{:S(2)}) collective-permute-start(bf16[16,2048]{1,0:T(8,128)(2,1)S(1)} %shard_map.80.half.refs_0_.refs_2_), channel_id=1, source_target_pairs={{0,1},{1,0},{2,3},{3,2},{4,5},{5,4},{6,7},{7,6},{8,9},{9,8},{10,11... | collective-permute-start | bytes 196616 | tf_op jit(solution)/shard_map/ppermute | solution.py:331
  16.6 1.3 %collective-permute-start.14 = (bf16[16,2176]{1,0:T(8,128)(2,1)S(1)}, bf16[16,2176]{1,0:T(8,128)(2,1)S(1)}, u32[]{:S(2)}, u32[]{:S(2)}) collective-permute-start(bf16[16,2176]{1,0:T(8,128)(2,1)S(1)} %get-tuple-element.58), channel_id=1, source_target_pairs={{0,1},{1,0},{2,3},{3,2},{4,5},{5,4},{6,7},{7,6},{8,16},{9,17},{10,... | collective-permute-start | bytes 208904 | tf_op jit(solution)/shard_map/ppermute | solution.py:348
  17.0 1.3 %collective-permute-start.17 = (bf16[16,2048]{1,0:T(8,128)(2,1)S(1)}, bf16[16,2048]{1,0:T(8,128)(2,1)S(1)}, u32[]{:S(2)}, u32[]{:S(2)}) collective-permute-start(bf16[16,2048]{1,0:T(8,128)(2,1)S(1)} %get-tuple-element.59.refs_1_), channel_id=1, source_target_pairs={{0,8},{1,9},{2,10},{3,11},{4,12},{5,13},{6,14},{7,15},{8,22},{9,23... | collective-permute-start | bytes 196616 | tf_op jit(solution)/shard_map/ppermute | solution.py:348
  19.0 1.3 %collective-permute-start.18 = (bf16[16,2048]{1,0:T(8,128)(2,1)S(1)}, bf16[16,2048]{1,0:T(8,128)(2,1)S(1)}, u32[]{:S(2)}, u32[]{:S(2)}) collective-permute-start(bf16[16,2048]{1,0:T(8,128)(2,1)S(1)} %shard_map.86.half.refs_0_.refs_2_), channel_id=1, source_target_pairs={{0,1},{1,0},{2,3},{3,2},{4,5},{5,4},{6,7},{7,6},{8,9},{9,8},{10,11... | collective-permute-start | bytes 196616 | tf_op jit(solution)/shard_map/ppermute | solution.py:331
  21.6 19.7 %collective-permute-start.20 = (bf16[16,2176]{1,0:T(8,128)(2,1)S(1)}, bf16[16,2176]{1,0:T(8,128)(2,1)S(1)}, u32[]{:S(2)}, u32[]{:S(2)}) collective-permute-start(bf16[16,2176]{1,0:T(8,128)(2,1)S(1)} %get-tuple-element.65), channel_id=1, source_target_pairs={{0,1},{1,0},{2,3},{3,2},{4,5},{5,4},{6,7},{7,6},{8,9},{9,8},{10,11... | collective-permute-start | bytes 208904 | tf_op jit(solution)/shard_map/ppermute | solution.py:348
  38.8 6.7 %collective-permute-start.23 = (bf16[16,2048]{1,0:T(8,128)(2,1)S(1)}, bf16[16,2048]{1,0:T(8,128)(2,1)S(1)}, u32[]{:S(2)}, u32[]{:S(2)}) collective-permute-start(bf16[16,2048]{1,0:T(8,128)(2,1)S(1)} %get-tuple-element.66.refs_2_), channel_id=1, source_target_pairs={{0,1},{1,0},{2,3},{3,2},{4,5},{5,4},{6,7},{7,6},{8,16},{9,17},{10,... | collective-permute-start | bytes 196616 | tf_op jit(solution)/shard_map/ppermute | solution.py:348
  38.8 7.3 %collective-permute-start.22 = (bf16[16,2048]{1,0:T(8,128)(2,1)S(1)}, bf16[16,2048]{1,0:T(8,128)(2,1)S(1)}, u32[]{:S(2)}, u32[]{:S(2)}) collective-permute-start(bf16[16,2048]{1,0:T(8,128)(2,1)S(1)} %get-tuple-element.66.refs_2_), channel_id=1, source_target_pairs={{0,1},{1,0},{2,3},{3,2},{4,5},{5,4},{6,7},{7,6},{8,9},{9,8},{10,11... | collective-permute-start | bytes 196616 | tf_op jit(solution)/shard_map/ppermute | solution.py:348
  41.2 5.2 %collective-permute-start.21 = (bf16[16,2048]{1,0:T(8,128)(2,1)S(1)}, bf16[16,2048]{1,0:T(8,128)(2,1)S(1)}, u32[]{:S(2)}, u32[]{:S(2)}) collective-permute-start(bf16[16,2048]{1,0:T(8,128)(2,1)S(1)} %get-tuple-element.66.refs_2_), channel_id=1, source_target_pairs={{0,1},{1,0},{2,3},{3,2},{4,5},{5,4},{6,7},{7,6},{8,9},{9,8},{10,11... | collective-permute-start | bytes 196616 | tf_op jit(solution)/shard_map/ppermute | solution.py:348
  41.2 1.3 %collective-permute-start.24 = (bf16[8,2048]{1,0:T(8,128)(2,1)S(1)}, bf16[8,2048]{1,0:T(8,128)(2,1)S(1)}, u32[]{:S(2)}, u32[]{:S(2)}) collective-permute-start(bf16[8,2048]{1,0:T(8,128)(2,1)S(1)} %get-tuple-element.68), channel_id=1, source_target_pairs={{0,1},{1,0},{2,3},{3,2},{4,5},{5,4},{6,7},{7,6},{8,9},{9,8},{10,11... | collective-permute-start | bytes 98312 | tf_op jit(solution)/shard_map/ppermute | solution.py:331
  46.6 1.3 %collective-permute-start.25 = (bf16[16,2048]{1,0:T(8,128)(2,1)S(1)}, bf16[16,2048]{1,0:T(8,128)(2,1)S(1)}, u32[]{:S(2)}, u32[]{:S(2)}) collective-permute-start(bf16[16,2048]{1,0:T(8,128)(2,1)S(1)} %shard_map.93.half.refs_0_), channel_id=1, source_target_pairs={{0,1},{1,0},{2,3},{3,2},{4,5},{5,4},{6,7},{7,6},{8,9},{9,8},{10,11... | collective-permute-start | bytes 196616 | tf_op jit(solution)/shard_map/ppermute | solution.py:331
  49.2 1.3 %collective-permute-start.26 = (bf16[8,4096]{1,0:T(8,128)(2,1)S(1)}, bf16[8,4096]{1,0:T(8,128)(2,1)S(1)}, u32[]{:S(2)}, u32[]{:S(2)}) collective-permute-start(bf16[8,4096]{1,0:T(8,128)(2,1)S(1)} %get-tuple-element.73), channel_id=1, source_target_pairs={{0,1},{1,0},{2,3},{3,2},{4,5},{5,4},{6,7},{7,6},{8,9},{9,8},{10,11... | collective-permute-start | bytes 196616 | tf_op jit(solution)/shard_map/ppermute | solution.py:331
  50.7 3.8 %collective-permute-start.27 = (bf16[2,4096]{1,0:T(2,128)(2,1)S(1)}, bf16[2,4096]{1,0:T(2,128)(2,1)S(1)}, u32[]{:S(2)}, u32[]{:S(2)}) collective-permute-start(bf16[2,4096]{1,0:T(2,128)(2,1)S(1)} %get-tuple-element.76), channel_id=1, source_target_pairs={{0,2},{1,3},{2,0},{3,1},{4,6},{5,7},{6,4},{7,5},{8,10},{9,11},{10,... | collective-permute-start | bytes 49160 | tf_op jit(solution)/shard_map/ppermute | solution.py:328
  51.8 3.7 %collective-permute-start.28 = (bf16[2,4096]{1,0:T(2,128)(2,1)S(1)}, bf16[2,4096]{1,0:T(2,128)(2,1)S(1)}, u32[]{:S(2)}, u32[]{:S(2)}) collective-permute-start(bf16[2,4096]{1,0:T(2,128)(2,1)S(1)} %get-tuple-element.77), channel_id=1, source_target_pairs={{0,4},{1,5},{2,6},{3,7},{4,0},{5,1},{6,2},{7,3},{8,12},{9,13},{10,... | collective-permute-start | bytes 49160 | tf_op jit(solution)/shard_map/ppermute | solution.py:328
  53.4 4.6 %collective-permute-start.29 = (bf16[2,4096]{1,0:T(2,128)(2,1)S(1)}, bf16[2,4096]{1,0:T(2,128)(2,1)S(1)}, u32[]{:S(2)}, u32[]{:S(2)}) collective-permute-start(bf16[2,4096]{1,0:T(2,128)(2,1)S(1)} %get-tuple-element.78), channel_id=1, source_target_pairs={{0,6},{1,7},{2,4},{3,5},{4,2},{5,3},{6,0},{7,1},{8,14},{9,15},{10,... | collective-permute-start | bytes 49160 | tf_op jit(solution)/shard_map/ppermute | solution.py:328
  (13 other events, 50.4 us)

commit v6 on v5

--- a/solution.py
+++ b/solution.py
@@ -101,16 +101,17 @@
 
 def join_kernel(group, width, *refs):
     count = group * EXPERTS
-    whole, half, table = refs[count : count + 3]
-    block, rows = refs[count + 3 :]
-    _, own = place(group)
+    whole, half, table, scale = refs[count : count + 4]
+    block, rows = refs[count + 4 :]
+    expert, own = place(group)
     slots = EXPERTS * CAP
     for m in range(group):
         for i in range(EXPERTS):
             block[i * CAP : (i + 1) * CAP, :] = refs[m * EXPERTS + i][...].astype(F32)
         at = pl.multiple_of((own ^ m) * slots, slots)
         rows[pl.ds(at, slots), :] = block[...]
-    table[...] = rows[:, width:].astype(BF16)
+    table[...] = rows[:, width : width + LANES].astype(BF16)
+    scale[...] = scales(expert, rows[:, width:])
     at = pl.multiple_of(own * half.shape[1], half.shape[1])
     half[...] = rows[:, pl.ds(at, half.shape[1])].astype(BF16)
     whole[...] = rows[:, 0:width].astype(BF16)
@@ -199,10 +200,10 @@
 
 def scales(expert, table):
     rows = table.shape[0]
-    position = table[:, 0:LANES].astype(F32)
-    mine = position == slot_codes(expert, (rows, LANES)).astype(F32)
-    scale = sum(table[:, n * LANES : (n + 1) * LANES].astype(F32) for n in range(1, BLOCKS))
-    return jnp.sum(jnp.where(mine, scale, 0.0), axis=1, keepdims=True)
+    mine = table[:, 0:LANES] == slot_codes(expert, (rows, LANES)).astype(F32)
+    scale = sum(table[:, n * LANES : (n + 1) * LANES] for n in range(1, BLOCKS))
+    scale = jnp.sum(jnp.where(mine, scale, 0.0), axis=1, keepdims=True)
+    return jnp.broadcast_to(scale, (rows, LANES))
 
 
 def updated(pieces, before, scale):
@@ -213,13 +214,12 @@
 
 
 def update_kernel(group, *refs):
-    half, table, out, marked = refs[group : group + 4]
-    expert, _ = place(group)
+    half, table, scale, out, marked = refs[group : group + 5]
     width = out.shape[1]
-    result = updated(refs[:group], half, scales(expert, table)).astype(BF16)
+    result = updated(refs[:group], half, scale[:, 0:1]).astype(BF16)
     out[...] = result
     marked[:, 0:width] = result
-    marked[:, width:] = table[:, 0:LANES]
+    marked[:, width:] = table[...]
 
 
 def keep_kernel(group, saved, *refs):
@@ -236,21 +236,19 @@
 
 
 def leave_kernel(group, *refs):
-    before, table = refs[group : group + 2]
+    before, scale = refs[group : group + 2]
     kept = refs[group + 2 : 2 * group + 2]
     outs = refs[2 * group + 2 : 2 * group + 2 + EXPERTS]
-    column, rows = refs[-2:]
+    rows = refs[-1]
     slots = EXPERTS * CAP
     final = lax.axis_size("section") - 1
     section = lax.axis_index("section")
-    expert, own = place(group)
+    _, own = place(group)
 
     @pl.when(section == final)
     def _():
-        column[...] = jnp.broadcast_to(scales(expert, table), column.shape)
         at = pl.multiple_of(own * slots, slots)
-        scale = column[pl.ds(at, slots), :][:, 0:1]
-        rows[...] = updated(refs[:group], before, scale)
+        rows[...] = updated(refs[:group], before, scale[pl.ds(at, slots), :][:, 0:1])
 
     @pl.when(section != final)
     def _():
@@ -267,7 +265,7 @@
     expert, _ = place(group)
     rows = current.shape[0]
     span = EXPERTS * CAP
-    here = current[:, 0:LANES].astype(F32)
+    here = current[...].astype(F32)
     there = before[:, before.shape[1] - LANES :].astype(F32)
     mine = jnp.where(here == slot_codes(expert, here.shape).astype(F32), 1.0, 0.0).astype(BF16)
     a, b = iota((rows, rows), 0), iota((rows, rows), 1)
@@ -283,12 +281,18 @@
         out[i] = jnp.dot(both, order, preferred_element_type=F32).astype(BF16)
 
 
-def pick_kernel(*refs):
-    choice, out = refs[EXPERTS], refs[-1]
+def early_kernel(turns, *refs):
+    choice, out = refs[-2], refs[-1]
     width = out.shape[1]
-    total = jnp.dot(choice[0], refs[0][:, 0:width], preferred_element_type=F32)
-    for i in range(1, EXPERTS):
-        total = total + jnp.dot(choice[i], refs[i][...], preferred_element_type=F32)
+    total = 0.0
+    for n, i in enumerate(turns):
+        total = total + jnp.dot(choice[i], refs[n][:, 0:width], preferred_element_type=F32)
+    out[...] = total
+
+
+def pick_kernel(i, *refs):
+    sofar, last, choice, out = refs[0], refs[1], refs[2], refs[-1]
+    total = sofar[...] + jnp.dot(choice[i], last[...], preferred_element_type=F32)
     out[...] = total.astype(BF16)
 
 
@@ -349,7 +353,10 @@
         return outs
 
     wanted = call(
-        functools.partial(code_kernel, group), shape((slots, LANES), F32), (), flops=START_FLOPS
+        functools.partial(code_kernel, group),
+        shape((slots, LANES), F32),
+        (),
+        flops=START_FLOPS,
     )
     sent = call(
         slot_kernel,
@@ -359,11 +366,17 @@
     arrived = [across(sent[i], i) for i in range(EXPERTS)]
     pieces = list(arrived)
     for m in range(1, group):
-        pieces += [within(piece, m) for piece in arrived]
+        for piece in arrived:
+            pieces.append(within(piece, m))
     flops = 6 * rows * width * w_gate.shape[2]
-    whole, half, table = call(
+    whole, half, table, scale = call(
         functools.partial(join_kernel, group, width),
-        [shape((rows, width)), shape((rows, chunk)), shape((rows, BLOCKS * LANES))],
+        [
+            shape((rows, width)),
+            shape((rows, chunk)),
+            shape((rows, LANES)),
+            shape((rows, LANES), F32),
+        ],
         tuple(pieces),
         scratch=[pltpu.VMEM((slots, wide), F32), pltpu.VMEM((rows, wide), F32)],
     )
@@ -387,7 +400,18 @@
                     scratch=[pltpu.VMEM((rows, chunk), F32)],
                 )
                 kept = [kept[0]] + [within(kept[m], m) for m in range(1, group)]
-            half = call(pick_kernel, shape((rows, chunk)), (*gathered, choice, *kept))
+            turns = [EXPERTS - 1, *range(EXPERTS - 2)]
+            sofar = call(
+                functools.partial(early_kernel, turns),
+                shape((rows, chunk), F32),
+                (*[gathered[i] for i in turns], choice),
+                flops=2 * rows * rows * EXPERTS * chunk,
+            )
+            half = call(
+                functools.partial(pick_kernel, EXPERTS - 2),
+                shape((rows, chunk)),
+                (sofar, gathered[EXPERTS - 2], choice, *kept),
+            )
             halves = [half] + [within(half, m) for m in range(1, group)]
             begun = call(
                 functools.partial(half_kernel, group, tick),
@@ -429,14 +453,14 @@
             latest, marked = call(
                 functools.partial(update_kernel, group),
                 [shape((rows, chunk)), shape((rows, chunk + LANES))],
-                (*terms, half, table),
+                (*terms, half, table, scale),
             )
             saved.append(latest)
     leaving = call(
         functools.partial(leave_kernel, group),
         [shape((CAP, width))] * EXPERTS,
-        (*terms, outs[group], table, *kept),
-        scratch=[pltpu.VMEM((rows, LANES), F32), pltpu.VMEM((slots, width), F32)],
+        (*terms, outs[group], scale, *kept),
+        scratch=[pltpu.VMEM((slots, width), F32)],
     )
     back = [across(leaving[i], i) for i in range(EXPERTS)]
     return call(

time: 59 us -> 58.2 us (0.986)
  waiting for transfers between devices: 21.5 us -> 20.1 us
    ppermute x6, waiting for transfers between devices: 7.66 us -> 6.8 us  [across(): return lax.ppermute(value, 'expert', pairs)]
    ppermute x12, waiting for transfers between devices: 8.66 us -> 7.93 us  [within(): return lax.ppermute(value, 'expert', [(d, d ^ m) for d in range(peers)])]
    pallas_call x25 -> x28, Pallas kernels: 5.51 us -> 5.73 us  [call(): pl.pallas_call(kernel, out_shape=outs, in_specs=specs or [VMEM] * len(arg...]
  transfers between devices with their start and end apart: 30 -> 30, of which waited for: 25 -> 22; matrix products, arithmetic and copies ran while one was open for 0% -> 0% of each run, Pallas kernels for 3% -> 4%
where the time goes in v6:
time: 58.2 us; the launch traced here: 58.1 us
  starting transfers between devices  31.2 us (54%)
  waiting for transfers between devices  20.1 us (35%)
  Pallas kernels  5.73 us (10%)
  local copies, waits for them, and re-layouts  0.81 us (1%)
    ppermute x12, starting transfers between devices, gather(): lax.ppermute(value if i else marked, ('section', 'expert'), pairs)  22.1 us
    ppermute x12, waiting for transfers between devices, within(): return lax.ppermute(value, 'expert', [(d, d ^ m) for d in range(peers)])  7.93 us
    ppermute x6, starting transfers between devices, across(): return lax.ppermute(value, 'expert', pairs)  7.11 us
    ppermute x6, waiting for transfers between devices, across(): return lax.ppermute(value, 'expert', pairs)  6.8 us
    pallas_call x28, Pallas kernels, call(): pl.pallas_call(kernel, out_shape=outs, in_specs=specs or [VMEM] * len(arg...  5.73 us
    ppermute x12, waiting for transfers between devices, gather(): lax.ppermute(value if i else marked, ('section', 'expert'), pairs)  5.35 us
    ppermute x12, starting transfers between devices, within(): return lax.ppermute(value, 'expert', [(d, d ^ m) for d in range(peers)])  2 us
  transfers between devices with their start and end apart: 30, of which 22 were waited for; matrix products, arithmetic and copies ran while one was open for 0% of the time, Pallas kernels for 4%

profile of v6, /device:TPU:24, one launch (start us, length us, event | category | flops | bytes accessed | tf_op | source)
XLA Modules:
  0.0 58.1 jit_solution(6574531227027177892)
XLA Ops:
  1.1 1.6 %collective-permute-start = (bf16[2,4608]{1,0:T(2,128)(2,1)S(1)}, bf16[2,4608]{1,0:T(2,128)(2,1)S(1)}, u32[]{:S(2)}, u32[]{:S(2)}) collective-permute-start(bf16[2,4608]{1,0:T(2,128)(2,1)S(1)} %get-tuple-element.44), channel_id=1, source_target_pairs={{0,2},{1,3},{2,0},{3,1},{4,6},{5,7},{6,4},{7,5},{8,10},{9,11},{10,... | collective-permute-start | bytes 55304 | tf_op jit(solution)/shard_map/ppermute | solution.py:332
  2.7 1.5 %collective-permute-start.1 = (bf16[2,4608]{1,0:T(2,128)(2,1)S(1)}, bf16[2,4608]{1,0:T(2,128)(2,1)S(1)}, u32[]{:S(2)}, u32[]{:S(2)}) collective-permute-start(bf16[2,4608]{1,0:T(2,128)(2,1)S(1)} %get-tuple-element.45), channel_id=1, source_target_pairs={{0,4},{1,5},{2,6},{3,7},{4,0},{5,1},{6,2},{7,3},{8,12},{9,13},{10,... | collective-permute-start | bytes 55304 | tf_op jit(solution)/shard_map/ppermute | solution.py:332
  5.2 1.3 %collective-permute-done.1.refs_2_ = bf16[2,4608]{1,0:T(2,128)(2,1)S(1)} collective-permute-done((bf16[2,4608]{1,0:T(2,128)(2,1)S(1)}, bf16[2,4608]{1,0:T(2,128)(2,1)S(1)}, u32[]{:S(2)}, u32[]{:S(2)}) %collective-permute-start.1) | collective-permute-done | bytes 18464 | tf_op jit(solution)/shard_map/ppermute | solution.py:332
  6.4 2.4 %collective-permute-done.2.refs_3_ = bf16[2,4608]{1,0:T(2,128)(2,1)S(1)} collective-permute-done((bf16[2,4608]{1,0:T(2,128)(2,1)S(1)}, bf16[2,4608]{1,0:T(2,128)(2,1)S(1)}, u32[]{:S(2)}, u32[]{:S(2)}) %collective-permute-start.2) | collective-permute-done | bytes 18464 | tf_op jit(solution)/shard_map/ppermute | solution.py:332
  8.9 1.2 %collective-permute-done.6.refs_7_ = bf16[2,4608]{1,0:T(2,128)(2,1)S(1)} collective-permute-done((bf16[2,4608]{1,0:T(2,128)(2,1)S(1)}, bf16[2,4608]{1,0:T(2,128)(2,1)S(1)}, u32[]{:S(2)}, u32[]{:S(2)}) %collective-permute-start.6) | collective-permute-done | bytes 18464 | tf_op jit(solution)/shard_map/ppermute | solution.py:335
  10.5 1.1 %collective-permute-done.7.refs_1_ = bf16[16,2048]{1,0:T(8,128)(2,1)S(1)} collective-permute-done((bf16[16,2048]{1,0:T(8,128)(2,1)S(1)}, bf16[16,2048]{1,0:T(8,128)(2,1)S(1)}, u32[]{:S(2)}, u32[]{:S(2)}) %collective-permute-start.7) | collective-permute-done | bytes 65568 | tf_op jit(solution)/shard_map/ppermute | solution.py:335
  14.2 0.9 %collective-permute-done.12.refs_1_ = bf16[16,2048]{1,0:T(8,128)(2,1)S(1)} collective-permute-done((bf16[16,2048]{1,0:T(8,128)(2,1)S(1)}, bf16[16,2048]{1,0:T(8,128)(2,1)S(1)}, u32[]{:S(2)}, u32[]{:S(2)}) %collective-permute-start.12) | collective-permute-done | bytes 65568 | tf_op jit(solution)/shard_map/ppermute | solution.py:335
  15.5 0.9 %collective-permute-done.13.refs_1_ = bf16[16,2048]{1,0:T(8,128)(2,1)S(1)} collective-permute-done((bf16[16,2048]{1,0:T(8,128)(2,1)S(1)}, bf16[16,2048]{1,0:T(8,128)(2,1)S(1)}, u32[]{:S(2)}, u32[]{:S(2)}) %collective-permute-start.13) | collective-permute-done | bytes 65568 | tf_op jit(solution)/shard_map/ppermute | solution.py:335
  19.1 1.1 %collective-permute-done.18.refs_1_ = bf16[16,2048]{1,0:T(8,128)(2,1)S(1)} collective-permute-done((bf16[16,2048]{1,0:T(8,128)(2,1)S(1)}, bf16[16,2048]{1,0:T(8,128)(2,1)S(1)}, u32[]{:S(2)}, u32[]{:S(2)}) %collective-permute-start.18) | collective-permute-done | bytes 65568 | tf_op jit(solution)/shard_map/ppermute | solution.py:335
  20.3 1.1 %collective-permute-done.19.refs_1_ = bf16[16,2048]{1,0:T(8,128)(2,1)S(1)} collective-permute-done((bf16[16,2048]{1,0:T(8,128)(2,1)S(1)}, bf16[16,2048]{1,0:T(8,128)(2,1)S(1)}, u32[]{:S(2)}, u32[]{:S(2)}) %collective-permute-start.19) | collective-permute-done | bytes 65568 | tf_op jit(solution)/shard_map/ppermute | solution.py:335
  21.5 16.7 %collective-permute-start.21 = (bf16[16,2176]{1,0:T(8,128)(2,1)S(1)}, bf16[16,2176]{1,0:T(8,128)(2,1)S(1)}, u32[]{:S(2)}, u32[]{:S(2)}) collective-permute-start(bf16[16,2176]{1,0:T(8,128)(2,1)S(1)} %get-tuple-element.68), channel_id=1, source_target_pairs={{0,1},{1,0},{2,3},{3,2},{4,5},{5,4},{6,7},{7,6},{8,9},{9,8},{10,11... | collective-permute-start | bytes 208904 | tf_op jit(solution)/shard_map/ppermute | solution.py:352
  38.2 3.2 %collective-permute-start.22 = (bf16[16,2048]{1,0:T(8,128)(2,1)S(1)}, bf16[16,2048]{1,0:T(8,128)(2,1)S(1)}, u32[]{:S(2)}, u32[]{:S(2)}) collective-permute-start(bf16[16,2048]{1,0:T(8,128)(2,1)S(1)} %get-tuple-element.67.refs_2_), channel_id=1, source_target_pairs={{0,1},{1,0},{2,3},{3,2},{4,5},{5,4},{6,7},{7,6},{8,9},{9,8},{10,11... | collective-permute-start | bytes 196616 | tf_op jit(solution)/shard_map/ppermute | solution.py:352
  41.9 2.9 %collective-permute-done.20.refs_0_ = bf16[16,2048]{1,0:T(8,128)(2,1)S(1)} collective-permute-done((bf16[16,2048]{1,0:T(8,128)(2,1)S(1)}, bf16[16,2048]{1,0:T(8,128)(2,1)S(1)}, u32[]{:S(2)}, u32[]{:S(2)}) %collective-permute-start.20) | collective-permute-done | bytes 65568 | tf_op jit(solution)/shard_map/ppermute | solution.py:352
  44.8 0.6 %collective-permute-done.22.refs_2_ = bf16[16,2048]{1,0:T(8,128)(2,1)S(1)} collective-permute-done((bf16[16,2048]{1,0:T(8,128)(2,1)S(1)}, bf16[16,2048]{1,0:T(8,128)(2,1)S(1)}, u32[]{:S(2)}, u32[]{:S(2)}) %collective-permute-start.22) | collective-permute-done | bytes 65568 | tf_op jit(solution)/shard_map/ppermute | solution.py:352
  45.6 0.9 %collective-permute-done.23.refs_1_ = bf16[16,2048]{1,0:T(8,128)(2,1)S(1)} collective-permute-done((bf16[16,2048]{1,0:T(8,128)(2,1)S(1)}, bf16[16,2048]{1,0:T(8,128)(2,1)S(1)}, u32[]{:S(2)}, u32[]{:S(2)}) %collective-permute-start.23) | collective-permute-done | bytes 65568 | tf_op jit(solution)/shard_map/ppermute | solution.py:352
  46.8 0.7 %shard_map.97 = (f32[16,512]{1,0:T(8,128)S(1)}, f32[16,512]{1,0:T(8,128)S(1)}, f32[16,128]{1,0:T(8,128)S(1)}) custom-call(bf16[16,2048]{1,0:T(8,128)(2,1)S(1)} %shard_map.96.half.refs_0_, f32[1,4096]{1,0:T(1,128)S(1)} %copy-done.3, bf16[1,4096,512]{2,1,0:T(8,128)(2,1)S(1)} %copy-done, bf16[1,4096,512]{2,1,0:T(8,128)(2,1)S(1)} %copy-done.1), custom_call_target="tpu_custom_call" | custom-call | flops 67108864 | bytes 8470528 | tf_op jit(solution)/shard_map/pallas_call | solution.py:24
  48.0 1.3 %shard_map.98 = (bf16[8,4096]{1,0:T(8,128)(2,1)S(1)}, bf16[8,4096]{1,0:T(8,128)(2,1)S(1)}, bf16[8,4096]{1,0:T(8,128)(2,1)S(1)}) custom-call(bf16[16,2048]{1,0:T(8,128)(2,1)S(1)} %shard_map.96.half.refs_0_, bf16[16,2048]{1,0:T(8,128)(2,1)S(1)} %collective-permute-done.25.refs_1_, f32[16,512]{1,0:T(8,128)S(1)} %get-tuple-element.71.refs_2_, ...), custom_call_target="tpu_custom_call" | custom-call | flops 100663296 | bytes 12804096 | tf_op jit(solution)/shard_map/pallas_call | solution.py:24
  49.6 1.1 %collective-permute-done.26.refs_1_ = bf16[8,4096]{1,0:T(8,128)(2,1)S(1)} collective-permute-done((bf16[8,4096]{1,0:T(8,128)(2,1)S(1)}, bf16[8,4096]{1,0:T(8,128)(2,1)S(1)}, u32[]{:S(2)}, u32[]{:S(2)}) %collective-permute-start.26) | collective-permute-done | bytes 65568 | tf_op jit(solution)/shard_map/ppermute | solution.py:335
  50.8 0.7 %collective-permute-start.27 = (bf16[2,4096]{1,0:T(2,128)(2,1)S(1)}, bf16[2,4096]{1,0:T(2,128)(2,1)S(1)}, u32[]{:S(2)}, u32[]{:S(2)}) collective-permute-start(bf16[2,4096]{1,0:T(2,128)(2,1)S(1)} %get-tuple-element.78), channel_id=1, source_target_pairs={{0,2},{1,3},{2,0},{3,1},{4,6},{5,7},{6,4},{7,5},{8,10},{9,11},{10,... | collective-permute-start | bytes 49160 | tf_op jit(solution)/shard_map/ppermute | solution.py:332
  51.5 1.1 %collective-permute-start.28 = (bf16[2,4096]{1,0:T(2,128)(2,1)S(1)}, bf16[2,4096]{1,0:T(2,128)(2,1)S(1)}, u32[]{:S(2)}, u32[]{:S(2)}) collective-permute-start(bf16[2,4096]{1,0:T(2,128)(2,1)S(1)} %get-tuple-element.79), channel_id=1, source_target_pairs={{0,4},{1,5},{2,6},{3,7},{4,0},{5,1},{6,2},{7,3},{8,12},{9,13},{10,... | collective-permute-start | bytes 49160 | tf_op jit(solution)/shard_map/ppermute | solution.py:332
  52.6 1.8 %collective-permute-start.29 = (bf16[2,4096]{1,0:T(2,128)(2,1)S(1)}, bf16[2,4096]{1,0:T(2,128)(2,1)S(1)}, u32[]{:S(2)}, u32[]{:S(2)}) collective-permute-start(bf16[2,4096]{1,0:T(2,128)(2,1)S(1)} %get-tuple-element.80), channel_id=1, source_target_pairs={{0,6},{1,7},{2,4},{3,5},{4,2},{5,3},{6,0},{7,1},{8,14},{9,15},{10,... | collective-permute-start | bytes 49160 | tf_op jit(solution)/shard_map/ppermute | solution.py:332
  54.6 0.6 %collective-permute-done.28.refs_2_ = bf16[2,4096]{1,0:T(2,128)(2,1)S(1)} collective-permute-done((bf16[2,4096]{1,0:T(2,128)(2,1)S(1)}, bf16[2,4096]{1,0:T(2,128)(2,1)S(1)}, u32[]{:S(2)}, u32[]{:S(2)}) %collective-permute-start.28) | collective-permute-done | bytes 16416 | tf_op jit(solution)/shard_map/ppermute | solution.py:332
  55.2 2.0 %collective-permute-done.29.refs_3_ = bf16[2,4096]{1,0:T(2,128)(2,1)S(1)} collective-permute-done((bf16[2,4096]{1,0:T(2,128)(2,1)S(1)}, bf16[2,4096]{1,0:T(2,128)(2,1)S(1)}, u32[]{:S(2)}, u32[]{:S(2)}) %collective-permute-start.29) | collective-permute-done | bytes 16416 | tf_op jit(solution)/shard_map/ppermute | solution.py:332
  57.2 0.9 %shard_map.100 = bf16[1,6,4096]{2,1,0:T(8,128)(2,1)} custom-call(bf16[2,4096]{1,0:T(2,128)(2,1)S(1)} %get-tuple-element.77.refs_0_, bf16[2,4096]{1,0:T(2,128)(2,1)S(1)} %collective-permute-done.27.refs_1_, bf16[2,4096]{1,0:T(2,128)(2,1)S(1)} %collective-permute-done.28.refs_2_, bf16[2,4096]{1,0:T(2,128)(2,1)S(1)} %collective-permute-done.29.refs_3_, ...), custom_call_target="tpu_custom_call" | custom-call | flops 1000 | bytes 66048 | tf_op jit(solution)/shard_map/pallas_call | solution.py:24
  (79 shorter events, 10.4 us)
Async XLA Ops:
  1.1 3.8 %collective-permute-start = (bf16[2,4608]{1,0:T(2,128)(2,1)S(1)}, bf16[2,4608]{1,0:T(2,128)(2,1)S(1)}, u32[]{:S(2)}, u32[]{:S(2)}) collective-permute-start(bf16[2,4608]{1,0:T(2,128)(2,1)S(1)} %get-tuple-element.44), channel_id=1, source_target_pairs={{0,2},{1,3},{2,0},{3,1},{4,6},{5,7},{6,4},{7,5},{8,10},{9,11},{10,... | collective-permute-start | bytes 55304 | tf_op jit(solution)/shard_map/ppermute | solution.py:332
  2.7 3.8 %collective-permute-start.1 = (bf16[2,4608]{1,0:T(2,128)(2,1)S(1)}, bf16[2,4608]{1,0:T(2,128)(2,1)S(1)}, u32[]{:S(2)}, u32[]{:S(2)}) collective-permute-start(bf16[2,4608]{1,0:T(2,128)(2,1)S(1)} %get-tuple-element.45), channel_id=1, source_target_pairs={{0,4},{1,5},{2,6},{3,7},{4,0},{5,1},{6,2},{7,3},{8,12},{9,13},{10,... | collective-permute-start | bytes 55304 | tf_op jit(solution)/shard_map/ppermute | solution.py:332
  4.2 4.7 %collective-permute-start.2 = (bf16[2,4608]{1,0:T(2,128)(2,1)S(1)}, bf16[2,4608]{1,0:T(2,128)(2,1)S(1)}, u32[]{:S(2)}, u32[]{:S(2)}) collective-permute-start(bf16[2,4608]{1,0:T(2,128)(2,1)S(1)} %get-tuple-element.46), channel_id=1, source_target_pairs={{0,6},{1,7},{2,4},{3,5},{4,2},{5,3},{6,0},{7,1},{8,14},{9,15},{10,... | collective-permute-start | bytes 55304 | tf_op jit(solution)/shard_map/ppermute | solution.py:332
  4.7 4.2 %collective-permute-start.3 = (bf16[2,4608]{1,0:T(2,128)(2,1)S(1)}, bf16[2,4608]{1,0:T(2,128)(2,1)S(1)}, u32[]{:S(2)}, u32[]{:S(2)}) collective-permute-start(bf16[2,4608]{1,0:T(2,128)(2,1)S(1)} %get-tuple-element.43.refs_0_), channel_id=1, source_target_pairs={{0,1},{1,0},{2,3},{3,2},{4,5},{5,4},{6,7},{7,6},{8,9},{9,8},{10,11... | collective-permute-start | bytes 55304 | tf_op jit(solution)/shard_map/ppermute | solution.py:335
  4.9 3.9 %collective-permute-start.4 = (bf16[2,4608]{1,0:T(2,128)(2,1)S(1)}, bf16[2,4608]{1,0:T(2,128)(2,1)S(1)}, u32[]{:S(2)}, u32[]{:S(2)}) collective-permute-start(bf16[2,4608]{1,0:T(2,128)(2,1)S(1)} %collective-permute-done.refs_1_), channel_id=1, source_target_pairs={{0,1},{1,0},{2,3},{3,2},{4,5},{5,4},{6,7},{7,6},{8,9},{9,8},{10,11... | collective-permute-start | bytes 55304 | tf_op jit(solution)/shard_map/ppermute | solution.py:335
  6.4 2.4 %collective-permute-start.5 = (bf16[2,4608]{1,0:T(2,128)(2,1)S(1)}, bf16[2,4608]{1,0:T(2,128)(2,1)S(1)}, u32[]{:S(2)}, u32[]{:S(2)}) collective-permute-start(bf16[2,4608]{1,0:T(2,128)(2,1)S(1)} %collective-permute-done.1.refs_2_), channel_id=1, source_target_pairs={{0,1},{1,0},{2,3},{3,2},{4,5},{5,4},{6,7},{7,6},{8,9},{9,8},{10,11... | collective-permute-start | bytes 55304 | tf_op jit(solution)/shard_map/ppermute | solution.py:335
  10.3 1.3 %collective-permute-start.7 = (bf16[16,2048]{1,0:T(8,128)(2,1)S(1)}, bf16[16,2048]{1,0:T(8,128)(2,1)S(1)}, u32[]{:S(2)}, u32[]{:S(2)}) collective-permute-start(bf16[16,2048]{1,0:T(8,128)(2,1)S(1)} %get-tuple-element.49), channel_id=1, source_target_pairs={{0,1},{1,0},{2,3},{3,2},{4,5},{5,4},{6,7},{7,6},{8,9},{9,8},{10,11... | collective-permute-start | bytes 196616 | tf_op jit(solution)/shard_map/ppermute | solution.py:335
  11.7 1.3 %collective-permute-start.9 = (bf16[16,2176]{1,0:T(8,128)(2,1)S(1)}, bf16[16,2176]{1,0:T(8,128)(2,1)S(1)}, u32[]{:S(2)}, u32[]{:S(2)}) collective-permute-start(bf16[16,2176]{1,0:T(8,128)(2,1)S(1)} %get-tuple-element.54), channel_id=1, source_target_pairs={{0,8},{1,9},{2,10},{3,11},{4,12},{5,13},{6,14},{7,15},{8,0},{9,1},... | collective-permute-start | bytes 208904 | tf_op jit(solution)/shard_map/ppermute | solution.py:352
  11.9 1.5 %collective-permute-start.10 = (bf16[16,2048]{1,0:T(8,128)(2,1)S(1)}, bf16[16,2048]{1,0:T(8,128)(2,1)S(1)}, u32[]{:S(2)}, u32[]{:S(2)}) collective-permute-start(bf16[16,2048]{1,0:T(8,128)(2,1)S(1)} %get-tuple-element.53.refs_0_), channel_id=1, source_target_pairs={{0,10},{1,11},{2,8},{3,9},{4,14},{5,15},{6,12},{7,13},{8,0},{9,1},... | collective-permute-start | bytes 196616 | tf_op jit(solution)/shard_map/ppermute | solution.py:352
  12.4 1.3 %collective-permute-start.11 = (bf16[16,2048]{1,0:T(8,128)(2,1)S(1)}, bf16[16,2048]{1,0:T(8,128)(2,1)S(1)}, u32[]{:S(2)}, u32[]{:S(2)}) collective-permute-start(bf16[16,2048]{1,0:T(8,128)(2,1)S(1)} %get-tuple-element.53.refs_0_), channel_id=1, source_target_pairs={{0,12},{1,13},{2,14},{3,15},{4,8},{5,9},{6,10},{7,11},{8,0},{9,1},... | collective-permute-start | bytes 196616 | tf_op jit(solution)/shard_map/ppermute | solution.py:352
  13.9 1.3 %collective-permute-start.12 = (bf16[16,2048]{1,0:T(8,128)(2,1)S(1)}, bf16[16,2048]{1,0:T(8,128)(2,1)S(1)}, u32[]{:S(2)}, u32[]{:S(2)}) collective-permute-start(bf16[16,2048]{1,0:T(8,128)(2,1)S(1)} %shard_map.81.half.refs_0_.refs_2_), channel_id=1, source_target_pairs={{0,1},{1,0},{2,3},{3,2},{4,5},{5,4},{6,7},{7,6},{8,9},{9,8},{10,11... | collective-permute-start | bytes 196616 | tf_op jit(solution)/shard_map/ppermute | solution.py:335
  16.5 1.3 %collective-permute-start.15 = (bf16[16,2176]{1,0:T(8,128)(2,1)S(1)}, bf16[16,2176]{1,0:T(8,128)(2,1)S(1)}, u32[]{:S(2)}, u32[]{:S(2)}) collective-permute-start(bf16[16,2176]{1,0:T(8,128)(2,1)S(1)} %get-tuple-element.61), channel_id=1, source_target_pairs={{0,1},{1,0},{2,3},{3,2},{4,5},{5,4},{6,7},{7,6},{8,16},{9,17},{10,... | collective-permute-start | bytes 208904 | tf_op jit(solution)/shard_map/ppermute | solution.py:352
  16.9 1.3 %collective-permute-start.14 = (bf16[16,2048]{1,0:T(8,128)(2,1)S(1)}, bf16[16,2048]{1,0:T(8,128)(2,1)S(1)}, u32[]{:S(2)}, u32[]{:S(2)}) collective-permute-start(bf16[16,2048]{1,0:T(8,128)(2,1)S(1)} %get-tuple-element.60.refs_1_), channel_id=1, source_target_pairs={{0,8},{1,9},{2,10},{3,11},{4,12},{5,13},{6,14},{7,15},{8,22},{9,23... | collective-permute-start | bytes 196616 | tf_op jit(solution)/shard_map/ppermute | solution.py:352
  18.8 1.3 %collective-permute-start.18 = (bf16[16,2048]{1,0:T(8,128)(2,1)S(1)}, bf16[16,2048]{1,0:T(8,128)(2,1)S(1)}, u32[]{:S(2)}, u32[]{:S(2)}) collective-permute-start(bf16[16,2048]{1,0:T(8,128)(2,1)S(1)} %shard_map.88.half.refs_0_.refs_2_), channel_id=1, source_target_pairs={{0,1},{1,0},{2,3},{3,2},{4,5},{5,4},{6,7},{7,6},{8,9},{9,8},{10,11... | collective-permute-start | bytes 196616 | tf_op jit(solution)/shard_map/ppermute | solution.py:335
  21.5 20.0 %collective-permute-start.21 = (bf16[16,2176]{1,0:T(8,128)(2,1)S(1)}, bf16[16,2176]{1,0:T(8,128)(2,1)S(1)}, u32[]{:S(2)}, u32[]{:S(2)}) collective-permute-start(bf16[16,2176]{1,0:T(8,128)(2,1)S(1)} %get-tuple-element.68), channel_id=1, source_target_pairs={{0,1},{1,0},{2,3},{3,2},{4,5},{5,4},{6,7},{7,6},{8,9},{9,8},{10,11... | collective-permute-start | bytes 208904 | tf_op jit(solution)/shard_map/ppermute | solution.py:352
  38.2 6.7 %collective-permute-start.20 = (bf16[16,2048]{1,0:T(8,128)(2,1)S(1)}, bf16[16,2048]{1,0:T(8,128)(2,1)S(1)}, u32[]{:S(2)}, u32[]{:S(2)}) collective-permute-start(bf16[16,2048]{1,0:T(8,128)(2,1)S(1)} %get-tuple-element.67.refs_2_), channel_id=1, source_target_pairs={{0,1},{1,0},{2,3},{3,2},{4,5},{5,4},{6,7},{7,6},{8,16},{9,17},{10,... | collective-permute-start | bytes 196616 | tf_op jit(solution)/shard_map/ppermute | solution.py:352
  38.2 7.3 %collective-permute-start.22 = (bf16[16,2048]{1,0:T(8,128)(2,1)S(1)}, bf16[16,2048]{1,0:T(8,128)(2,1)S(1)}, u32[]{:S(2)}, u32[]{:S(2)}) collective-permute-start(bf16[16,2048]{1,0:T(8,128)(2,1)S(1)} %get-tuple-element.67.refs_2_), channel_id=1, source_target_pairs={{0,1},{1,0},{2,3},{3,2},{4,5},{5,4},{6,7},{7,6},{8,9},{9,8},{10,11... | collective-permute-start | bytes 196616 | tf_op jit(solution)/shard_map/ppermute | solution.py:352
  41.4 5.2 %collective-permute-start.23 = (bf16[16,2048]{1,0:T(8,128)(2,1)S(1)}, bf16[16,2048]{1,0:T(8,128)(2,1)S(1)}, u32[]{:S(2)}, u32[]{:S(2)}) collective-permute-start(bf16[16,2048]{1,0:T(8,128)(2,1)S(1)} %get-tuple-element.67.refs_2_), channel_id=1, source_target_pairs={{0,1},{1,0},{2,3},{3,2},{4,5},{5,4},{6,7},{7,6},{8,9},{9,8},{10,11... | collective-permute-start | bytes 196616 | tf_op jit(solution)/shard_map/ppermute | solution.py:352
  41.4 4.2 %collective-permute-start.24 = (bf16[8,2048]{1,0:T(8,128)(2,1)S(1)}, bf16[8,2048]{1,0:T(8,128)(2,1)S(1)}, u32[]{:S(2)}, u32[]{:S(2)}) collective-permute-start(bf16[8,2048]{1,0:T(8,128)(2,1)S(1)} %get-tuple-element.70), channel_id=1, source_target_pairs={{0,1},{1,0},{2,3},{3,2},{4,5},{5,4},{6,7},{7,6},{8,9},{9,8},{10,11... | collective-permute-start | bytes 98312 | tf_op jit(solution)/shard_map/ppermute | solution.py:335
  46.7 1.3 %collective-permute-start.25 = (bf16[16,2048]{1,0:T(8,128)(2,1)S(1)}, bf16[16,2048]{1,0:T(8,128)(2,1)S(1)}, u32[]{:S(2)}, u32[]{:S(2)}) collective-permute-start(bf16[16,2048]{1,0:T(8,128)(2,1)S(1)} %shard_map.96.half.refs_0_), channel_id=1, source_target_pairs={{0,1},{1,0},{2,3},{3,2},{4,5},{5,4},{6,7},{7,6},{8,9},{9,8},{10,11... | collective-permute-start | bytes 196616 | tf_op jit(solution)/shard_map/ppermute | solution.py:335
  49.3 1.3 %collective-permute-start.26 = (bf16[8,4096]{1,0:T(8,128)(2,1)S(1)}, bf16[8,4096]{1,0:T(8,128)(2,1)S(1)}, u32[]{:S(2)}, u32[]{:S(2)}) collective-permute-start(bf16[8,4096]{1,0:T(8,128)(2,1)S(1)} %get-tuple-element.75), channel_id=1, source_target_pairs={{0,1},{1,0},{2,3},{3,2},{4,5},{5,4},{6,7},{7,6},{8,9},{9,8},{10,11... | collective-permute-start | bytes 196616 | tf_op jit(solution)/shard_map/ppermute | solution.py:335
  50.8 3.8 %collective-permute-start.27 = (bf16[2,4096]{1,0:T(2,128)(2,1)S(1)}, bf16[2,4096]{1,0:T(2,128)(2,1)S(1)}, u32[]{:S(2)}, u32[]{:S(2)}) collective-permute-start(bf16[2,4096]{1,0:T(2,128)(2,1)S(1)} %get-tuple-element.78), channel_id=1, source_target_pairs={{0,2},{1,3},{2,0},{3,1},{4,6},{5,7},{6,4},{7,5},{8,10},{9,11},{10,... | collective-permute-start | bytes 49160 | tf_op jit(solution)/shard_map/ppermute | solution.py:332
  51.5 3.7 %collective-permute-start.28 = (bf16[2,4096]{1,0:T(2,128)(2,1)S(1)}, bf16[2,4096]{1,0:T(2,128)(2,1)S(1)}, u32[]{:S(2)}, u32[]{:S(2)}) collective-permute-start(bf16[2,4096]{1,0:T(2,128)(2,1)S(1)} %get-tuple-element.79), channel_id=1, source_target_pairs={{0,4},{1,5},{2,6},{3,7},{4,0},{5,1},{6,2},{7,3},{8,12},{9,13},{10,... | collective-permute-start | bytes 49160 | tf_op jit(solution)/shard_map/ppermute | solution.py:332
  52.6 4.6 %collective-permute-start.29 = (bf16[2,4096]{1,0:T(2,128)(2,1)S(1)}, bf16[2,4096]{1,0:T(2,128)(2,1)S(1)}, u32[]{:S(2)}, u32[]{:S(2)}) collective-permute-start(bf16[2,4096]{1,0:T(2,128)(2,1)S(1)} %get-tuple-element.80), channel_id=1, source_target_pairs={{0,6},{1,7},{2,4},{3,5},{4,2},{5,3},{6,0},{7,1},{8,14},{9,15},{10,... | collective-permute-start | bytes 49160 | tf_op jit(solution)/shard_map/ppermute | solution.py:332
  (13 other events, 50.7 us)

commit v7 on v6

--- a/solution.py
+++ b/solution.py
@@ -12,6 +12,7 @@
 CAP = 2
 LANES = 128
 BLOCKS = 4
+RELAYED = (0,)
 START_FLOPS = 10_000_000_000
 F32 = jnp.float32
 BF16 = jnp.bfloat16
@@ -292,7 +293,8 @@
 
 def pick_kernel(i, *refs):
     sofar, last, choice, out = refs[0], refs[1], refs[2], refs[-1]
-    total = sofar[...] + jnp.dot(choice[i], last[...], preferred_element_type=F32)
+    piece = last[:, 0 : out.shape[1]]
+    total = sofar[...] + jnp.dot(choice[i], piece, preferred_element_type=F32)
     out[...] = total.astype(BF16)
 
 
@@ -335,11 +337,12 @@
         return lax.ppermute(value, "expert", [(d, d ^ m) for d in range(peers)])
 
     def gather(value, marked, tick):
-        outs = []
-        for i in range(EXPERTS):
+        outs = {}
+        turns = gather_turns(tick)
+        for i in turns:
             ring = [tick, tick + 1]
-            if i == EXPERTS - 1 and sections > 2:
-                ring.append(tick - 1 if tick else 2)
+            if i == turns[0] and sections > 2:
+                ring.append((tick + 2) % sections if tick else min(3, sections - 1))
             pairs = []
             for s in range(sections):
                 to, move = s, lambda d: d ^ 1
@@ -349,8 +352,11 @@
                 if s == tick:
                     move = lambda d: (d // group ^ i) * group + d % group
                 pairs += [(s * peers + d, to * peers + move(d)) for d in range(peers)]
-            outs.append(lax.ppermute(value if i else marked, ("section", "expert"), pairs))
-        return outs
+            outs[i] = lax.ppermute(value if i else marked, ("section", "expert"), pairs)
+        if 1 not in outs:
+            outs[1] = across(outs[0], 1)
+            turns = [*turns, 1]
+        return outs, turns
 
     wanted = call(
         functools.partial(code_kernel, group),
@@ -385,7 +391,7 @@
     for tick in range(sections):
         last = tick == sections - 1
         if tick:
-            gathered = gather(saved[-1], marked, tick - 1)
+            gathered, turns = gather(saved[-1], marked, tick - 1)
             choice = call(
                 functools.partial(choice_kernel, group),
                 shape((EXPERTS, rows, rows)),
@@ -400,17 +406,16 @@
                     scratch=[pltpu.VMEM((rows, chunk), F32)],
                 )
                 kept = [kept[0]] + [within(kept[m], m) for m in range(1, group)]
-            turns = [EXPERTS - 1, *range(EXPERTS - 2)]
             sofar = call(
-                functools.partial(early_kernel, turns),
+                functools.partial(early_kernel, turns[:-1]),
                 shape((rows, chunk), F32),
-                (*[gathered[i] for i in turns], choice),
+                (*[gathered[i] for i in turns[:-1]], choice),
                 flops=2 * rows * rows * EXPERTS * chunk,
             )
             half = call(
-                functools.partial(pick_kernel, EXPERTS - 2),
+                functools.partial(pick_kernel, turns[-1]),
                 shape((rows, chunk)),
-                (sofar, gathered[EXPERTS - 2], choice, *kept),
+                (sofar, gathered[turns[-1]], choice, *kept),
             )
             halves = [half] + [within(half, m) for m in range(1, group)]
             begun = call(
@@ -469,6 +474,11 @@
         (*back, sent[0][:, width : width + LANES]),
         scratch=[pltpu.VMEM((slots, width), F32)],
     )
+
+
+def gather_turns(tick):
+    far = EXPERTS - 1
+    return [0, far, *range(2, far)] if tick in RELAYED else [far, *range(far)]
 
 
 def solution(mesh):

time: 58.2 us -> 63.9 us (1.098)
  waiting for transfers between devices: 20.1 us -> 28.5 us
  starting transfers between devices: 31.2 us -> 28.4 us
    ppermute x12 -> x11, waiting for transfers between devices: 5.35 us -> 10.3 us  [gather(): outs[i] = lax.ppermute(value if i else marked, ('section', 'expert'), pairs)]
    ppermute x6 -> x7, waiting for transfers between devices: 6.8 us -> 9.72 us  [across(): return lax.ppermute(value, 'expert', pairs)]
    ppermute x12 -> x11, starting transfers between devices: 22.1 us -> 19.4 us  [gather(): outs[i] = lax.ppermute(value if i else marked, ('section', 'expert'), pairs)]
    ppermute x12, starting transfers between devices: 2 us -> 1.31 us  [within(): return lax.ppermute(value, 'expert', [(d, d ^ m) for d in range(peers)])]
    ppermute x6 -> x7, starting transfers between devices: 7.11 us -> 7.64 us  [across(): return lax.ppermute(value, 'expert', pairs)]
where the time goes in v7:
time: 63.9 us; the launch traced here: 63.8 us
  waiting for transfers between devices  28.5 us (45%)
  starting transfers between devices  28.4 us (44%)
  Pallas kernels  5.75 us (9%)
  local copies, waits for them, and re-layouts  0.81 us (1%)
    ppermute x11, starting transfers between devices, gather(): outs[i] = lax.ppermute(value if i else marked, ('section', 'expert'), pairs)  19.4 us
    ppermute x11, waiting for transfers between devices, gather(): outs[i] = lax.ppermute(value if i else marked, ('section', 'expert'), pairs)  10.3 us
    ppermute x7, waiting for transfers between devices, across(): return lax.ppermute(value, 'expert', pairs)  9.72 us
    ppermute x12, waiting for transfers between devices, within(): return lax.ppermute(value, 'expert', [(d, d ^ m) for d in range(peers)])  8.56 us
    ppermute x7, starting transfers between devices, across(): return lax.ppermute(value, 'expert', pairs)  7.64 us
    pallas_call x28, Pallas kernels, call(): pl.pallas_call(kernel, out_shape=outs, in_specs=specs or [VMEM] * len(arg...  5.75 us
    ppermute x12, starting transfers between devices, within(): return lax.ppermute(value, 'expert', [(d, d ^ m) for d in range(peers)])  1.31 us
  transfers between devices with their start and end apart: 30, of which 22 were waited for; matrix products, arithmetic and copies ran while one was open for 0% of the time, Pallas kernels for 4%

profile of v7, /device:TPU:24, one launch (start us, length us, event | category | flops | bytes accessed | tf_op | source)
XLA Modules:
  0.0 63.8 jit_solution(3480710543257345286)
XLA Ops:
  1.1 1.6 %collective-permute-start = (bf16[2,4608]{1,0:T(2,128)(2,1)S(1)}, bf16[2,4608]{1,0:T(2,128)(2,1)S(1)}, u32[]{:S(2)}, u32[]{:S(2)}) collective-permute-start(bf16[2,4608]{1,0:T(2,128)(2,1)S(1)} %get-tuple-element.44), channel_id=1, source_target_pairs={{0,2},{1,3},{2,0},{3,1},{4,6},{5,7},{6,4},{7,5},{8,10},{9,11},{10,... | collective-permute-start | bytes 55304 | tf_op jit(solution)/shard_map/ppermute | solution.py:334
  2.7 1.5 %collective-permute-start.1 = (bf16[2,4608]{1,0:T(2,128)(2,1)S(1)}, bf16[2,4608]{1,0:T(2,128)(2,1)S(1)}, u32[]{:S(2)}, u32[]{:S(2)}) collective-permute-start(bf16[2,4608]{1,0:T(2,128)(2,1)S(1)} %get-tuple-element.45), channel_id=1, source_target_pairs={{0,4},{1,5},{2,6},{3,7},{4,0},{5,1},{6,2},{7,3},{8,12},{9,13},{10,... | collective-permute-start | bytes 55304 | tf_op jit(solution)/shard_map/ppermute | solution.py:334
  5.2 1.3 %collective-permute-done.1.refs_2_ = bf16[2,4608]{1,0:T(2,128)(2,1)S(1)} collective-permute-done((bf16[2,4608]{1,0:T(2,128)(2,1)S(1)}, bf16[2,4608]{1,0:T(2,128)(2,1)S(1)}, u32[]{:S(2)}, u32[]{:S(2)}) %collective-permute-start.1) | collective-permute-done | bytes 18464 | tf_op jit(solution)/shard_map/ppermute | solution.py:334
  6.4 2.4 %collective-permute-done.2.refs_3_ = bf16[2,4608]{1,0:T(2,128)(2,1)S(1)} collective-permute-done((bf16[2,4608]{1,0:T(2,128)(2,1)S(1)}, bf16[2,4608]{1,0:T(2,128)(2,1)S(1)}, u32[]{:S(2)}, u32[]{:S(2)}) %collective-permute-start.2) | collective-permute-done | bytes 18464 | tf_op jit(solution)/shard_map/ppermute | solution.py:334
  8.9 1.2 %collective-permute-done.6.refs_7_ = bf16[2,4608]{1,0:T(2,128)(2,1)S(1)} collective-permute-done((bf16[2,4608]{1,0:T(2,128)(2,1)S(1)}, bf16[2,4608]{1,0:T(2,128)(2,1)S(1)}, u32[]{:S(2)}, u32[]{:S(2)}) %collective-permute-start.6) | collective-permute-done | bytes 18464 | tf_op jit(solution)/shard_map/ppermute | solution.py:337
  10.5 1.1 %collective-permute-done.7.refs_1_ = bf16[16,2048]{1,0:T(8,128)(2,1)S(1)} collective-permute-done((bf16[16,2048]{1,0:T(8,128)(2,1)S(1)}, bf16[16,2048]{1,0:T(8,128)(2,1)S(1)}, u32[]{:S(2)}, u32[]{:S(2)}) %collective-permute-start.7) | collective-permute-done | bytes 65568 | tf_op jit(solution)/shard_map/ppermute | solution.py:337
  11.7 1.8 %collective-permute-start.8 = (bf16[16,2176]{1,0:T(8,128)(2,1)S(1)}, bf16[16,2176]{1,0:T(8,128)(2,1)S(1)}, u32[]{:S(2)}, u32[]{:S(2)}) collective-permute-start(bf16[16,2176]{1,0:T(8,128)(2,1)S(1)} %get-tuple-element.53), channel_id=1, source_target_pairs={{0,8},{1,9},{2,10},{3,11},{4,12},{5,13},{6,14},{7,15},{8,24},{9,25... | collective-permute-start | bytes 208904 | tf_op jit(solution)/shard_map/ppermute | solution.py:355
  13.5 3.4 %collective-permute-done.8.before.refs_0_ = bf16[16,2176]{1,0:T(8,128)(2,1)S(1)} collective-permute-done((bf16[16,2176]{1,0:T(8,128)(2,1)S(1)}, bf16[16,2176]{1,0:T(8,128)(2,1)S(1)}, u32[]{:S(2)}, u32[]{:S(2)}) %collective-permute-start.8) | collective-permute-done | bytes 69664 | tf_op jit(solution)/shard_map/ppermute | solution.py:355
  19.1 2.2 %collective-permute-done.11.refs_1_ = bf16[16,2176]{1,0:T(8,128)(2,1)S(1)} collective-permute-done((bf16[16,2176]{1,0:T(8,128)(2,1)S(1)}, bf16[16,2176]{1,0:T(8,128)(2,1)S(1)}, u32[]{:S(2)}, u32[]{:S(2)}) %collective-permute-start.11) | collective-permute-done | bytes 69664 | tf_op jit(solution)/shard_map/ppermute | solution.py:334
  21.5 1.2 %collective-permute-done.12.refs_1_ = bf16[16,2048]{1,0:T(8,128)(2,1)S(1)} collective-permute-done((bf16[16,2048]{1,0:T(8,128)(2,1)S(1)}, bf16[16,2048]{1,0:T(8,128)(2,1)S(1)}, u32[]{:S(2)}, u32[]{:S(2)}) %collective-permute-start.12) | collective-permute-done | bytes 65568 | tf_op jit(solution)/shard_map/ppermute | solution.py:337
  22.9 1.1 %collective-permute-done.13.refs_1_ = bf16[16,2048]{1,0:T(8,128)(2,1)S(1)} collective-permute-done((bf16[16,2048]{1,0:T(8,128)(2,1)S(1)}, bf16[16,2048]{1,0:T(8,128)(2,1)S(1)}, u32[]{:S(2)}, u32[]{:S(2)}) %collective-permute-start.13) | collective-permute-done | bytes 65568 | tf_op jit(solution)/shard_map/ppermute | solution.py:337
  24.3 6.7 %collective-permute-start.14 = (bf16[16,2048]{1,0:T(8,128)(2,1)S(1)}, bf16[16,2048]{1,0:T(8,128)(2,1)S(1)}, u32[]{:S(2)}, u32[]{:S(2)}) collective-permute-start(bf16[16,2048]{1,0:T(8,128)(2,1)S(1)} %get-tuple-element.60.refs_1_), channel_id=1, source_target_pairs={{0,1},{1,0},{2,3},{3,2},{4,5},{5,4},{6,7},{7,6},{8,22},{9,23},{10,... | collective-permute-start | bytes 196616 | tf_op jit(solution)/shard_map/ppermute | solution.py:355
  31.8 1.9 %collective-permute-done.14.refs_0_ = bf16[16,2048]{1,0:T(8,128)(2,1)S(1)} collective-permute-done((bf16[16,2048]{1,0:T(8,128)(2,1)S(1)}, bf16[16,2048]{1,0:T(8,128)(2,1)S(1)}, u32[]{:S(2)}, u32[]{:S(2)}) %collective-permute-start.14) | collective-permute-done | bytes 65568 | tf_op jit(solution)/shard_map/ppermute | solution.py:355
  34.1 1.2 %collective-permute-done.18.refs_1_ = bf16[16,2048]{1,0:T(8,128)(2,1)S(1)} collective-permute-done((bf16[16,2048]{1,0:T(8,128)(2,1)S(1)}, bf16[16,2048]{1,0:T(8,128)(2,1)S(1)}, u32[]{:S(2)}, u32[]{:S(2)}) %collective-permute-start.18) | collective-permute-done | bytes 65568 | tf_op jit(solution)/shard_map/ppermute | solution.py:337
  35.5 1.1 %collective-permute-done.19.refs_1_ = bf16[16,2048]{1,0:T(8,128)(2,1)S(1)} collective-permute-done((bf16[16,2048]{1,0:T(8,128)(2,1)S(1)}, bf16[16,2048]{1,0:T(8,128)(2,1)S(1)}, u32[]{:S(2)}, u32[]{:S(2)}) %collective-permute-start.19) | collective-permute-done | bytes 65568 | tf_op jit(solution)/shard_map/ppermute | solution.py:337
  36.7 7.2 %collective-permute-start.21 = (bf16[16,2176]{1,0:T(8,128)(2,1)S(1)}, bf16[16,2176]{1,0:T(8,128)(2,1)S(1)}, u32[]{:S(2)}, u32[]{:S(2)}) collective-permute-start(bf16[16,2176]{1,0:T(8,128)(2,1)S(1)} %get-tuple-element.68), channel_id=1, source_target_pairs={{0,1},{1,0},{2,3},{3,2},{4,5},{5,4},{6,7},{7,6},{8,9},{9,8},{10,11... | collective-permute-start | bytes 208904 | tf_op jit(solution)/shard_map/ppermute | solution.py:355
  43.9 2.5 %collective-permute-start.22 = (bf16[16,2048]{1,0:T(8,128)(2,1)S(1)}, bf16[16,2048]{1,0:T(8,128)(2,1)S(1)}, u32[]{:S(2)}, u32[]{:S(2)}) collective-permute-start(bf16[16,2048]{1,0:T(8,128)(2,1)S(1)} %get-tuple-element.67.refs_2_), channel_id=1, source_target_pairs={{0,1},{1,0},{2,3},{3,2},{4,5},{5,4},{6,7},{7,6},{8,9},{9,8},{10,11... | collective-permute-start | bytes 196616 | tf_op jit(solution)/shard_map/ppermute | solution.py:355
  46.9 3.6 %collective-permute-done.20.refs_0_ = bf16[16,2048]{1,0:T(8,128)(2,1)S(1)} collective-permute-done((bf16[16,2048]{1,0:T(8,128)(2,1)S(1)}, bf16[16,2048]{1,0:T(8,128)(2,1)S(1)}, u32[]{:S(2)}, u32[]{:S(2)}) %collective-permute-start.20) | collective-permute-done | bytes 65568 | tf_op jit(solution)/shard_map/ppermute | solution.py:355
  53.0 1.3 %shard_map.98 = (bf16[8,4096]{1,0:T(8,128)(2,1)S(1)}, bf16[8,4096]{1,0:T(8,128)(2,1)S(1)}, bf16[8,4096]{1,0:T(8,128)(2,1)S(1)}) custom-call(bf16[16,2048]{1,0:T(8,128)(2,1)S(1)} %shard_map.96.half.refs_0_, bf16[16,2048]{1,0:T(8,128)(2,1)S(1)} %collective-permute-done.25.refs_1_, f32[16,512]{1,0:T(8,128)S(1)} %get-tuple-element.71.refs_2_, ...), custom_call_target="tpu_custom_call" | custom-call | flops 100663296 | bytes 12804096 | tf_op jit(solution)/shard_map/pallas_call | solution.py:25
  54.5 1.1 %collective-permute-done.26.refs_1_ = bf16[8,4096]{1,0:T(8,128)(2,1)S(1)} collective-permute-done((bf16[8,4096]{1,0:T(8,128)(2,1)S(1)}, bf16[8,4096]{1,0:T(8,128)(2,1)S(1)}, u32[]{:S(2)}, u32[]{:S(2)}) %collective-permute-start.26) | collective-permute-done | bytes 65568 | tf_op jit(solution)/shard_map/ppermute | solution.py:337
  55.7 1.6 %collective-permute-start.27 = (bf16[2,4096]{1,0:T(2,128)(2,1)S(1)}, bf16[2,4096]{1,0:T(2,128)(2,1)S(1)}, u32[]{:S(2)}, u32[]{:S(2)}) collective-permute-start(bf16[2,4096]{1,0:T(2,128)(2,1)S(1)} %get-tuple-element.78), channel_id=1, source_target_pairs={{0,2},{1,3},{2,0},{3,1},{4,6},{5,7},{6,4},{7,5},{8,10},{9,11},{10,... | collective-permute-start | bytes 49160 | tf_op jit(solution)/shard_map/ppermute | solution.py:334
  58.2 1.0 %collective-permute-start.29 = (bf16[2,4096]{1,0:T(2,128)(2,1)S(1)}, bf16[2,4096]{1,0:T(2,128)(2,1)S(1)}, u32[]{:S(2)}, u32[]{:S(2)}) collective-permute-start(bf16[2,4096]{1,0:T(2,128)(2,1)S(1)} %get-tuple-element.80), channel_id=1, source_target_pairs={{0,6},{1,7},{2,4},{3,5},{4,2},{5,3},{6,0},{7,1},{8,14},{9,15},{10,... | collective-permute-start | bytes 49160 | tf_op jit(solution)/shard_map/ppermute | solution.py:334
  59.5 1.5 %collective-permute-done.28.refs_2_ = bf16[2,4096]{1,0:T(2,128)(2,1)S(1)} collective-permute-done((bf16[2,4096]{1,0:T(2,128)(2,1)S(1)}, bf16[2,4096]{1,0:T(2,128)(2,1)S(1)}, u32[]{:S(2)}, u32[]{:S(2)}) %collective-permute-start.28) | collective-permute-done | bytes 16416 | tf_op jit(solution)/shard_map/ppermute | solution.py:334
  61.0 1.9 %collective-permute-done.29.refs_3_ = bf16[2,4096]{1,0:T(2,128)(2,1)S(1)} collective-permute-done((bf16[2,4096]{1,0:T(2,128)(2,1)S(1)}, bf16[2,4096]{1,0:T(2,128)(2,1)S(1)}, u32[]{:S(2)}, u32[]{:S(2)}) %collective-permute-start.29) | collective-permute-done | bytes 16416 | tf_op jit(solution)/shard_map/ppermute | solution.py:334
  (79 shorter events, 12.3 us)
Async XLA Ops:
  1.1 3.8 %collective-permute-start = (bf16[2,4608]{1,0:T(2,128)(2,1)S(1)}, bf16[2,4608]{1,0:T(2,128)(2,1)S(1)}, u32[]{:S(2)}, u32[]{:S(2)}) collective-permute-start(bf16[2,4608]{1,0:T(2,128)(2,1)S(1)} %get-tuple-element.44), channel_id=1, source_target_pairs={{0,2},{1,3},{2,0},{3,1},{4,6},{5,7},{6,4},{7,5},{8,10},{9,11},{10,... | collective-permute-start | bytes 55304 | tf_op jit(solution)/shard_map/ppermute | solution.py:334
  2.7 3.8 %collective-permute-start.1 = (bf16[2,4608]{1,0:T(2,128)(2,1)S(1)}, bf16[2,4608]{1,0:T(2,128)(2,1)S(1)}, u32[]{:S(2)}, u32[]{:S(2)}) collective-permute-start(bf16[2,4608]{1,0:T(2,128)(2,1)S(1)} %get-tuple-element.45), channel_id=1, source_target_pairs={{0,4},{1,5},{2,6},{3,7},{4,0},{5,1},{6,2},{7,3},{8,12},{9,13},{10,... | collective-permute-start | bytes 55304 | tf_op jit(solution)/shard_map/ppermute | solution.py:334
  4.2 4.7 %collective-permute-start.2 = (bf16[2,4608]{1,0:T(2,128)(2,1)S(1)}, bf16[2,4608]{1,0:T(2,128)(2,1)S(1)}, u32[]{:S(2)}, u32[]{:S(2)}) collective-permute-start(bf16[2,4608]{1,0:T(2,128)(2,1)S(1)} %get-tuple-element.46), channel_id=1, source_target_pairs={{0,6},{1,7},{2,4},{3,5},{4,2},{5,3},{6,0},{7,1},{8,14},{9,15},{10,... | collective-permute-start | bytes 55304 | tf_op jit(solution)/shard_map/ppermute | solution.py:334
  4.7 4.2 %collective-permute-start.3 = (bf16[2,4608]{1,0:T(2,128)(2,1)S(1)}, bf16[2,4608]{1,0:T(2,128)(2,1)S(1)}, u32[]{:S(2)}, u32[]{:S(2)}) collective-permute-start(bf16[2,4608]{1,0:T(2,128)(2,1)S(1)} %get-tuple-element.43.refs_0_), channel_id=1, source_target_pairs={{0,1},{1,0},{2,3},{3,2},{4,5},{5,4},{6,7},{7,6},{8,9},{9,8},{10,11... | collective-permute-start | bytes 55304 | tf_op jit(solution)/shard_map/ppermute | solution.py:337
  4.9 3.9 %collective-permute-start.4 = (bf16[2,4608]{1,0:T(2,128)(2,1)S(1)}, bf16[2,4608]{1,0:T(2,128)(2,1)S(1)}, u32[]{:S(2)}, u32[]{:S(2)}) collective-permute-start(bf16[2,4608]{1,0:T(2,128)(2,1)S(1)} %collective-permute-done.refs_1_), channel_id=1, source_target_pairs={{0,1},{1,0},{2,3},{3,2},{4,5},{5,4},{6,7},{7,6},{8,9},{9,8},{10,11... | collective-permute-start | bytes 55304 | tf_op jit(solution)/shard_map/ppermute | solution.py:337
  6.4 2.4 %collective-permute-start.5 = (bf16[2,4608]{1,0:T(2,128)(2,1)S(1)}, bf16[2,4608]{1,0:T(2,128)(2,1)S(1)}, u32[]{:S(2)}, u32[]{:S(2)}) collective-permute-start(bf16[2,4608]{1,0:T(2,128)(2,1)S(1)} %collective-permute-done.1.refs_2_), channel_id=1, source_target_pairs={{0,1},{1,0},{2,3},{3,2},{4,5},{5,4},{6,7},{7,6},{8,9},{9,8},{10,11... | collective-permute-start | bytes 55304 | tf_op jit(solution)/shard_map/ppermute | solution.py:337
  10.3 1.3 %collective-permute-start.7 = (bf16[16,2048]{1,0:T(8,128)(2,1)S(1)}, bf16[16,2048]{1,0:T(8,128)(2,1)S(1)}, u32[]{:S(2)}, u32[]{:S(2)}) collective-permute-start(bf16[16,2048]{1,0:T(8,128)(2,1)S(1)} %get-tuple-element.49), channel_id=1, source_target_pairs={{0,1},{1,0},{2,3},{3,2},{4,5},{5,4},{6,7},{7,6},{8,9},{9,8},{10,11... | collective-permute-start | bytes 196616 | tf_op jit(solution)/shard_map/ppermute | solution.py:337
  11.7 5.3 %collective-permute-start.8 = (bf16[16,2176]{1,0:T(8,128)(2,1)S(1)}, bf16[16,2176]{1,0:T(8,128)(2,1)S(1)}, u32[]{:S(2)}, u32[]{:S(2)}) collective-permute-start(bf16[16,2176]{1,0:T(8,128)(2,1)S(1)} %get-tuple-element.53), channel_id=1, source_target_pairs={{0,8},{1,9},{2,10},{3,11},{4,12},{5,13},{6,14},{7,15},{8,24},{9,25... | collective-permute-start | bytes 208904 | tf_op jit(solution)/shard_map/ppermute | solution.py:355
  17.0 4.3 %collective-permute-start.11 = (bf16[16,2176]{1,0:T(8,128)(2,1)S(1)}, bf16[16,2176]{1,0:T(8,128)(2,1)S(1)}, u32[]{:S(2)}, u32[]{:S(2)}) collective-permute-start(bf16[16,2176]{1,0:T(8,128)(2,1)S(1)} %collective-permute-done.8.before.refs_0_), channel_id=1, source_target_pairs={{0,2},{1,3},{2,0},{3,1},{4,6},{5,7},{6,4},{7,5},{8,10},{9,11},{10,... | collective-permute-start | bytes 208904 | tf_op jit(solution)/shard_map/ppermute | solution.py:334
  17.5 1.4 %collective-permute-start.9 = (bf16[16,2048]{1,0:T(8,128)(2,1)S(1)}, bf16[16,2048]{1,0:T(8,128)(2,1)S(1)}, u32[]{:S(2)}, u32[]{:S(2)}) collective-permute-start(bf16[16,2048]{1,0:T(8,128)(2,1)S(1)} %get-tuple-element.54.refs_0_), channel_id=1, source_target_pairs={{0,14},{1,15},{2,12},{3,13},{4,10},{5,11},{6,8},{7,9},{8,0},{9,1},... | collective-permute-start | bytes 196616 | tf_op jit(solution)/shard_map/ppermute | solution.py:355
  21.4 1.3 %collective-permute-start.12 = (bf16[16,2048]{1,0:T(8,128)(2,1)S(1)}, bf16[16,2048]{1,0:T(8,128)(2,1)S(1)}, u32[]{:S(2)}, u32[]{:S(2)}) collective-permute-start(bf16[16,2048]{1,0:T(8,128)(2,1)S(1)} %shard_map.81.half.refs_0_.refs_2_), channel_id=1, source_target_pairs={{0,1},{1,0},{2,3},{3,2},{4,5},{5,4},{6,7},{7,6},{8,9},{9,8},{10,11... | collective-permute-start | bytes 196616 | tf_op jit(solution)/shard_map/ppermute | solution.py:337
  24.1 7.4 %collective-permute-start.15 = (bf16[16,2176]{1,0:T(8,128)(2,1)S(1)}, bf16[16,2176]{1,0:T(8,128)(2,1)S(1)}, u32[]{:S(2)}, u32[]{:S(2)}) collective-permute-start(bf16[16,2176]{1,0:T(8,128)(2,1)S(1)} %get-tuple-element.61), channel_id=1, source_target_pairs={{0,1},{1,0},{2,3},{3,2},{4,5},{5,4},{6,7},{7,6},{8,16},{9,17},{10,... | collective-permute-start | bytes 208904 | tf_op jit(solution)/shard_map/ppermute | solution.py:355
  24.3 9.4 %collective-permute-start.14 = (bf16[16,2048]{1,0:T(8,128)(2,1)S(1)}, bf16[16,2048]{1,0:T(8,128)(2,1)S(1)}, u32[]{:S(2)}, u32[]{:S(2)}) collective-permute-start(bf16[16,2048]{1,0:T(8,128)(2,1)S(1)} %get-tuple-element.60.refs_1_), channel_id=1, source_target_pairs={{0,1},{1,0},{2,3},{3,2},{4,5},{5,4},{6,7},{7,6},{8,22},{9,23},{10,... | collective-permute-start | bytes 196616 | tf_op jit(solution)/shard_map/ppermute | solution.py:355
  31.0 2.7 %collective-permute-start.16 = (bf16[16,2048]{1,0:T(8,128)(2,1)S(1)}, bf16[16,2048]{1,0:T(8,128)(2,1)S(1)}, u32[]{:S(2)}, u32[]{:S(2)}) collective-permute-start(bf16[16,2048]{1,0:T(8,128)(2,1)S(1)} %get-tuple-element.60.refs_1_), channel_id=1, source_target_pairs={{0,1},{1,0},{2,3},{3,2},{4,5},{5,4},{6,7},{7,6},{8,18},{9,19},{10,... | collective-permute-start | bytes 196616 | tf_op jit(solution)/shard_map/ppermute | solution.py:355
  31.0 2.9 %collective-permute-start.17 = (bf16[16,2048]{1,0:T(8,128)(2,1)S(1)}, bf16[16,2048]{1,0:T(8,128)(2,1)S(1)}, u32[]{:S(2)}, u32[]{:S(2)}) collective-permute-start(bf16[16,2048]{1,0:T(8,128)(2,1)S(1)} %get-tuple-element.60.refs_1_), channel_id=1, source_target_pairs={{0,1},{1,0},{2,3},{3,2},{4,5},{5,4},{6,7},{7,6},{8,20},{9,21},{10,... | collective-permute-start | bytes 196616 | tf_op jit(solution)/shard_map/ppermute | solution.py:355
  34.0 1.3 %collective-permute-start.18 = (bf16[16,2048]{1,0:T(8,128)(2,1)S(1)}, bf16[16,2048]{1,0:T(8,128)(2,1)S(1)}, u32[]{:S(2)}, u32[]{:S(2)}) collective-permute-start(bf16[16,2048]{1,0:T(8,128)(2,1)S(1)} %shard_map.88.half.refs_0_.refs_2_), channel_id=1, source_target_pairs={{0,1},{1,0},{2,3},{3,2},{4,5},{5,4},{6,7},{7,6},{8,9},{9,8},{10,11... | collective-permute-start | bytes 196616 | tf_op jit(solution)/shard_map/ppermute | solution.py:337
  36.7 9.8 %collective-permute-start.21 = (bf16[16,2176]{1,0:T(8,128)(2,1)S(1)}, bf16[16,2176]{1,0:T(8,128)(2,1)S(1)}, u32[]{:S(2)}, u32[]{:S(2)}) collective-permute-start(bf16[16,2176]{1,0:T(8,128)(2,1)S(1)} %get-tuple-element.68), channel_id=1, source_target_pairs={{0,1},{1,0},{2,3},{3,2},{4,5},{5,4},{6,7},{7,6},{8,9},{9,8},{10,11... | collective-permute-start | bytes 208904 | tf_op jit(solution)/shard_map/ppermute | solution.py:355
  43.9 6.6 %collective-permute-start.20 = (bf16[16,2048]{1,0:T(8,128)(2,1)S(1)}, bf16[16,2048]{1,0:T(8,128)(2,1)S(1)}, u32[]{:S(2)}, u32[]{:S(2)}) collective-permute-start(bf16[16,2048]{1,0:T(8,128)(2,1)S(1)} %get-tuple-element.67.refs_2_), channel_id=1, source_target_pairs={{0,16},{1,17},{2,18},{3,19},{4,20},{5,21},{6,22},{7,23},{8,9},{9,8... | collective-permute-start | bytes 196616 | tf_op jit(solution)/shard_map/ppermute | solution.py:355
  43.9 7.4 %collective-permute-start.22 = (bf16[16,2048]{1,0:T(8,128)(2,1)S(1)}, bf16[16,2048]{1,0:T(8,128)(2,1)S(1)}, u32[]{:S(2)}, u32[]{:S(2)}) collective-permute-start(bf16[16,2048]{1,0:T(8,128)(2,1)S(1)} %get-tuple-element.67.refs_2_), channel_id=1, source_target_pairs={{0,1},{1,0},{2,3},{3,2},{4,5},{5,4},{6,7},{7,6},{8,9},{9,8},{10,11... | collective-permute-start | bytes 196616 | tf_op jit(solution)/shard_map/ppermute | solution.py:355
  46.4 5.2 %collective-permute-start.23 = (bf16[16,2048]{1,0:T(8,128)(2,1)S(1)}, bf16[16,2048]{1,0:T(8,128)(2,1)S(1)}, u32[]{:S(2)}, u32[]{:S(2)}) collective-permute-start(bf16[16,2048]{1,0:T(8,128)(2,1)S(1)} %get-tuple-element.67.refs_2_), channel_id=1, source_target_pairs={{0,1},{1,0},{2,3},{3,2},{4,5},{5,4},{6,7},{7,6},{8,9},{9,8},{10,11... | collective-permute-start | bytes 196616 | tf_op jit(solution)/shard_map/ppermute | solution.py:355
  46.4 5.0 %collective-permute-start.24 = (bf16[8,2048]{1,0:T(8,128)(2,1)S(1)}, bf16[8,2048]{1,0:T(8,128)(2,1)S(1)}, u32[]{:S(2)}, u32[]{:S(2)}) collective-permute-start(bf16[8,2048]{1,0:T(8,128)(2,1)S(1)} %get-tuple-element.70), channel_id=1, source_target_pairs={{0,1},{1,0},{2,3},{3,2},{4,5},{5,4},{6,7},{7,6},{8,9},{9,8},{10,11... | collective-permute-start | bytes 98312 | tf_op jit(solution)/shard_map/ppermute | solution.py:337
  55.7 3.8 %collective-permute-start.27 = (bf16[2,4096]{1,0:T(2,128)(2,1)S(1)}, bf16[2,4096]{1,0:T(2,128)(2,1)S(1)}, u32[]{:S(2)}, u32[]{:S(2)}) collective-permute-start(bf16[2,4096]{1,0:T(2,128)(2,1)S(1)} %get-tuple-element.78), channel_id=1, source_target_pairs={{0,2},{1,3},{2,0},{3,1},{4,6},{5,7},{6,4},{7,5},{8,10},{9,11},{10,... | collective-permute-start | bytes 49160 | tf_op jit(solution)/shard_map/ppermute | solution.py:334
  57.3 3.7 %collective-permute-start.28 = (bf16[2,4096]{1,0:T(2,128)(2,1)S(1)}, bf16[2,4096]{1,0:T(2,128)(2,1)S(1)}, u32[]{:S(2)}, u32[]{:S(2)}) collective-permute-start(bf16[2,4096]{1,0:T(2,128)(2,1)S(1)} %get-tuple-element.79), channel_id=1, source_target_pairs={{0,4},{1,5},{2,6},{3,7},{4,0},{5,1},{6,2},{7,3},{8,12},{9,13},{10,... | collective-permute-start | bytes 49160 | tf_op jit(solution)/shard_map/ppermute | solution.py:334
  58.2 4.6 %collective-permute-start.29 = (bf16[2,4096]{1,0:T(2,128)(2,1)S(1)}, bf16[2,4096]{1,0:T(2,128)(2,1)S(1)}, u32[]{:S(2)}, u32[]{:S(2)}) collective-permute-start(bf16[2,4096]{1,0:T(2,128)(2,1)S(1)} %get-tuple-element.80), channel_id=1, source_target_pairs={{0,6},{1,7},{2,4},{3,5},{4,2},{5,3},{6,0},{7,1},{8,14},{9,15},{10,... | collective-permute-start | bytes 49160 | tf_op jit(solution)/shard_map/ppermute | solution.py:334
  (13 other events, 50.8 us)

commit v8 on v7

--- a/solution.py
+++ b/solution.py
@@ -342,7 +342,7 @@
         for i in turns:
             ring = [tick, tick + 1]
             if i == turns[0] and sections > 2:
-                ring.append((tick + 2) % sections if tick else min(3, sections - 1))
+                ring.append((tick + 2) % sections)
             pairs = []
             for s in range(sections):
                 to, move = s, lambda d: d ^ 1
@@ -354,15 +354,17 @@
                 pairs += [(s * peers + d, to * peers + move(d)) for d in range(peers)]
             outs[i] = lax.ppermute(value if i else marked, ("section", "expert"), pairs)
         if 1 not in outs:
-            outs[1] = across(outs[0], 1)
+            pairs = [
+                (s * peers + d, s * peers + ((d // group ^ 1) * group + d % group if s == tick + 1 else d ^ 1))
+                for s in range(sections)
+                for d in range(peers)
+            ]
+            outs[1] = lax.ppermute(outs[0], ("section", "expert"), pairs)
             turns = [*turns, 1]
         return outs, turns
 
     wanted = call(
-        functools.partial(code_kernel, group),
-        shape((slots, LANES), F32),
-        (),
-        flops=START_FLOPS,
+        functools.partial(code_kernel, group), shape((slots, LANES), F32), (), flops=START_FLOPS
     )
     sent = call(
         slot_kernel,

time: 63.9 us -> 62.2 us (0.973); the launches traced: 63.8 us -> 61.4 us
  waiting for transfers between devices: 28.5 us -> 23.2 us
  starting transfers between devices: 28.4 us -> 31.4 us
    ppermute x11, starting transfers between devices: 19.4 us -> 22.7 us  [gather(): outs[i] = lax.ppermute(value if i else marked, ('section', 'expert'), pairs)]
    ppermute x7 -> x6, waiting for transfers between devices: 9.72 us -> 6.57 us  [across(): return lax.ppermute(value, 'expert', pairs)]
    ppermute x11, waiting for transfers between devices: 10.3 us -> 8.15 us  [gather(): outs[i] = lax.ppermute(value if i else marked, ('section', 'expert'), pairs)]
    ppermute x7 -> x6, starting transfers between devices: 7.64 us -> 7.11 us  [across(): return lax.ppermute(value, 'expert', pairs)]
  transfers between devices with their start and end apart: 30 -> 30, of which waited for: 22 -> 21; matrix products, arithmetic and copies ran while one was open for 0% -> 0% of each run, Pallas kernels for 4% -> 4%
where the time goes in v8:
time: 62.2 us; the launch traced here: 61.4 us
  starting transfers between devices  31.4 us (50%)
  waiting for transfers between devices  23.2 us (37%)
  Pallas kernels  5.74 us (9%)
  local copies, waits for them, and re-layouts  0.81 us (1%)
    ppermute x11, starting transfers between devices, gather(): outs[i] = lax.ppermute(value if i else marked, ('section', 'expert'), pairs)  22.7 us
    ppermute x12, waiting for transfers between devices, within(): return lax.ppermute(value, 'expert', [(d, d ^ m) for d in range(peers)])  8.42 us
    ppermute x11, waiting for transfers between devices, gather(): outs[i] = lax.ppermute(value if i else marked, ('section', 'expert'), pairs)  8.15 us
    ppermute x6, starting transfers between devices, across(): return lax.ppermute(value, 'expert', pairs)  7.11 us
    ppermute x6, waiting for transfers between devices, across(): return lax.ppermute(value, 'expert', pairs)  6.57 us
    pallas_call x28, Pallas kernels, call(): pl.pallas_call(kernel, out_shape=outs, in_specs=specs or [VMEM] * len(arg...  5.74 us
    ppermute x12, starting transfers between devices, within(): return lax.ppermute(value, 'expert', [(d, d ^ m) for d in range(peers)])  1.47 us
  transfers between devices with their start and end apart: 30, of which 21 were waited for; matrix products, arithmetic and copies ran while one was open for 0% of the time, Pallas kernels for 4%

profile of v8, /device:TPU:24, one launch (start us, length us, event | category | flops | bytes accessed | tf_op | source)
XLA Modules:
  0.0 61.4 jit_solution(11127228303744018948)
XLA Ops:
  1.1 1.6 %collective-permute-start = (bf16[2,4608]{1,0:T(2,128)(2,1)S(1)}, bf16[2,4608]{1,0:T(2,128)(2,1)S(1)}, u32[]{:S(2)}, u32[]{:S(2)}) collective-permute-start(bf16[2,4608]{1,0:T(2,128)(2,1)S(1)} %get-tuple-element.44), channel_id=1, source_target_pairs={{0,2},{1,3},{2,0},{3,1},{4,6},{5,7},{6,4},{7,5},{8,10},{9,11},{10,... | collective-permute-start | bytes 55304 | tf_op jit(solution)/shard_map/ppermute | solution.py:334
  2.7 1.5 %collective-permute-start.1 = (bf16[2,4608]{1,0:T(2,128)(2,1)S(1)}, bf16[2,4608]{1,0:T(2,128)(2,1)S(1)}, u32[]{:S(2)}, u32[]{:S(2)}) collective-permute-start(bf16[2,4608]{1,0:T(2,128)(2,1)S(1)} %get-tuple-element.45), channel_id=1, source_target_pairs={{0,4},{1,5},{2,6},{3,7},{4,0},{5,1},{6,2},{7,3},{8,12},{9,13},{10,... | collective-permute-start | bytes 55304 | tf_op jit(solution)/shard_map/ppermute | solution.py:334
  5.2 1.3 %collective-permute-done.1.refs_2_ = bf16[2,4608]{1,0:T(2,128)(2,1)S(1)} collective-permute-done((bf16[2,4608]{1,0:T(2,128)(2,1)S(1)}, bf16[2,4608]{1,0:T(2,128)(2,1)S(1)}, u32[]{:S(2)}, u32[]{:S(2)}) %collective-permute-start.1) | collective-permute-done | bytes 18464 | tf_op jit(solution)/shard_map/ppermute | solution.py:334
  6.4 2.4 %collective-permute-done.2.refs_3_ = bf16[2,4608]{1,0:T(2,128)(2,1)S(1)} collective-permute-done((bf16[2,4608]{1,0:T(2,128)(2,1)S(1)}, bf16[2,4608]{1,0:T(2,128)(2,1)S(1)}, u32[]{:S(2)}, u32[]{:S(2)}) %collective-permute-start.2) | collective-permute-done | bytes 18464 | tf_op jit(solution)/shard_map/ppermute | solution.py:334
  8.9 1.2 %collective-permute-done.6.refs_7_ = bf16[2,4608]{1,0:T(2,128)(2,1)S(1)} collective-permute-done((bf16[2,4608]{1,0:T(2,128)(2,1)S(1)}, bf16[2,4608]{1,0:T(2,128)(2,1)S(1)}, u32[]{:S(2)}, u32[]{:S(2)}) %collective-permute-start.6) | collective-permute-done | bytes 18464 | tf_op jit(solution)/shard_map/ppermute | solution.py:337
  10.5 1.1 %collective-permute-done.7.refs_1_ = bf16[16,2048]{1,0:T(8,128)(2,1)S(1)} collective-permute-done((bf16[16,2048]{1,0:T(8,128)(2,1)S(1)}, bf16[16,2048]{1,0:T(8,128)(2,1)S(1)}, u32[]{:S(2)}, u32[]{:S(2)}) %collective-permute-start.7) | collective-permute-done | bytes 65568 | tf_op jit(solution)/shard_map/ppermute | solution.py:337
  11.9 1.1 %collective-permute-done.8.before.refs_0_ = bf16[16,2176]{1,0:T(8,128)(2,1)S(1)} collective-permute-done((bf16[16,2176]{1,0:T(8,128)(2,1)S(1)}, bf16[16,2176]{1,0:T(8,128)(2,1)S(1)}, u32[]{:S(2)}, u32[]{:S(2)}) %collective-permute-start.8) | collective-permute-done | bytes 69664 | tf_op jit(solution)/shard_map/ppermute | solution.py:355
  15.3 1.1 %collective-permute-done.12.refs_1_ = bf16[16,2048]{1,0:T(8,128)(2,1)S(1)} collective-permute-done((bf16[16,2048]{1,0:T(8,128)(2,1)S(1)}, bf16[16,2048]{1,0:T(8,128)(2,1)S(1)}, u32[]{:S(2)}, u32[]{:S(2)}) %collective-permute-start.12) | collective-permute-done | bytes 65568 | tf_op jit(solution)/shard_map/ppermute | solution.py:337
  16.6 1.1 %collective-permute-done.13.refs_1_ = bf16[16,2048]{1,0:T(8,128)(2,1)S(1)} collective-permute-done((bf16[16,2048]{1,0:T(8,128)(2,1)S(1)}, bf16[16,2048]{1,0:T(8,128)(2,1)S(1)}, u32[]{:S(2)}, u32[]{:S(2)}) %collective-permute-start.13) | collective-permute-done | bytes 65568 | tf_op jit(solution)/shard_map/ppermute | solution.py:337
  18.0 11.5 %collective-permute-start.14 = (bf16[16,2048]{1,0:T(8,128)(2,1)S(1)}, bf16[16,2048]{1,0:T(8,128)(2,1)S(1)}, u32[]{:S(2)}, u32[]{:S(2)}) collective-permute-start(bf16[16,2048]{1,0:T(8,128)(2,1)S(1)} %get-tuple-element.60.refs_1_), channel_id=1, source_target_pairs={{0,1},{1,0},{2,3},{3,2},{4,5},{5,4},{6,7},{7,6},{8,22},{9,23},{10,... | collective-permute-start | bytes 196616 | tf_op jit(solution)/shard_map/ppermute | solution.py:355
  30.4 1.9 %collective-permute-done.14.refs_0_ = bf16[16,2048]{1,0:T(8,128)(2,1)S(1)} collective-permute-done((bf16[16,2048]{1,0:T(8,128)(2,1)S(1)}, bf16[16,2048]{1,0:T(8,128)(2,1)S(1)}, u32[]{:S(2)}, u32[]{:S(2)}) %collective-permute-start.14) | collective-permute-done | bytes 65568 | tf_op jit(solution)/shard_map/ppermute | solution.py:355
  32.7 1.2 %collective-permute-done.18.refs_1_ = bf16[16,2048]{1,0:T(8,128)(2,1)S(1)} collective-permute-done((bf16[16,2048]{1,0:T(8,128)(2,1)S(1)}, bf16[16,2048]{1,0:T(8,128)(2,1)S(1)}, u32[]{:S(2)}, u32[]{:S(2)}) %collective-permute-start.18) | collective-permute-done | bytes 65568 | tf_op jit(solution)/shard_map/ppermute | solution.py:337
  34.1 1.1 %collective-permute-done.19.refs_1_ = bf16[16,2048]{1,0:T(8,128)(2,1)S(1)} collective-permute-done((bf16[16,2048]{1,0:T(8,128)(2,1)S(1)}, bf16[16,2048]{1,0:T(8,128)(2,1)S(1)}, u32[]{:S(2)}, u32[]{:S(2)}) %collective-permute-start.19) | collective-permute-done | bytes 65568 | tf_op jit(solution)/shard_map/ppermute | solution.py:337
  35.3 6.2 %collective-permute-start.21 = (bf16[16,2176]{1,0:T(8,128)(2,1)S(1)}, bf16[16,2176]{1,0:T(8,128)(2,1)S(1)}, u32[]{:S(2)}, u32[]{:S(2)}) collective-permute-start(bf16[16,2176]{1,0:T(8,128)(2,1)S(1)} %get-tuple-element.68), channel_id=1, source_target_pairs={{0,1},{1,0},{2,3},{3,2},{4,5},{5,4},{6,7},{7,6},{8,9},{9,8},{10,11... | collective-permute-start | bytes 208904 | tf_op jit(solution)/shard_map/ppermute | solution.py:355
  41.5 3.5 %collective-permute-start.22 = (bf16[16,2048]{1,0:T(8,128)(2,1)S(1)}, bf16[16,2048]{1,0:T(8,128)(2,1)S(1)}, u32[]{:S(2)}, u32[]{:S(2)}) collective-permute-start(bf16[16,2048]{1,0:T(8,128)(2,1)S(1)} %get-tuple-element.67.refs_2_), channel_id=1, source_target_pairs={{0,1},{1,0},{2,3},{3,2},{4,5},{5,4},{6,7},{7,6},{8,9},{9,8},{10,11... | collective-permute-start | bytes 196616 | tf_op jit(solution)/shard_map/ppermute | solution.py:355
  45.4 2.5 %collective-permute-done.20.refs_0_ = bf16[16,2048]{1,0:T(8,128)(2,1)S(1)} collective-permute-done((bf16[16,2048]{1,0:T(8,128)(2,1)S(1)}, bf16[16,2048]{1,0:T(8,128)(2,1)S(1)}, u32[]{:S(2)}, u32[]{:S(2)}) %collective-permute-start.20) | collective-permute-done | bytes 65568 | tf_op jit(solution)/shard_map/ppermute | solution.py:355
  48.0 0.9 %collective-permute-done.22.refs_2_ = bf16[16,2048]{1,0:T(8,128)(2,1)S(1)} collective-permute-done((bf16[16,2048]{1,0:T(8,128)(2,1)S(1)}, bf16[16,2048]{1,0:T(8,128)(2,1)S(1)}, u32[]{:S(2)}, u32[]{:S(2)}) %collective-permute-start.22) | collective-permute-done | bytes 65568 | tf_op jit(solution)/shard_map/ppermute | solution.py:355
  49.0 1.0 %collective-permute-done.23.refs_1_ = bf16[16,2048]{1,0:T(8,128)(2,1)S(1)} collective-permute-done((bf16[16,2048]{1,0:T(8,128)(2,1)S(1)}, bf16[16,2048]{1,0:T(8,128)(2,1)S(1)}, u32[]{:S(2)}, u32[]{:S(2)}) %collective-permute-start.23) | collective-permute-done | bytes 65568 | tf_op jit(solution)/shard_map/ppermute | solution.py:355
  51.5 1.3 %shard_map.98 = (bf16[8,4096]{1,0:T(8,128)(2,1)S(1)}, bf16[8,4096]{1,0:T(8,128)(2,1)S(1)}, bf16[8,4096]{1,0:T(8,128)(2,1)S(1)}) custom-call(bf16[16,2048]{1,0:T(8,128)(2,1)S(1)} %shard_map.96.half.refs_0_, bf16[16,2048]{1,0:T(8,128)(2,1)S(1)} %collective-permute-done.25.refs_1_, f32[16,512]{1,0:T(8,128)S(1)} %get-tuple-element.71.refs_2_, ...), custom_call_target="tpu_custom_call" | custom-call | flops 100663296 | bytes 12804096 | tf_op jit(solution)/shard_map/pallas_call | solution.py:25
  53.1 1.1 %collective-permute-done.26.refs_1_ = bf16[8,4096]{1,0:T(8,128)(2,1)S(1)} collective-permute-done((bf16[8,4096]{1,0:T(8,128)(2,1)S(1)}, bf16[8,4096]{1,0:T(8,128)(2,1)S(1)}, u32[]{:S(2)}, u32[]{:S(2)}) %collective-permute-start.26) | collective-permute-done | bytes 65568 | tf_op jit(solution)/shard_map/ppermute | solution.py:337
  54.9 1.0 %collective-permute-start.28 = (bf16[2,4096]{1,0:T(2,128)(2,1)S(1)}, bf16[2,4096]{1,0:T(2,128)(2,1)S(1)}, u32[]{:S(2)}, u32[]{:S(2)}) collective-permute-start(bf16[2,4096]{1,0:T(2,128)(2,1)S(1)} %get-tuple-element.79), channel_id=1, source_target_pairs={{0,4},{1,5},{2,6},{3,7},{4,0},{5,1},{6,2},{7,3},{8,12},{9,13},{10,... | collective-permute-start | bytes 49160 | tf_op jit(solution)/shard_map/ppermute | solution.py:334
  55.9 2.0 %collective-permute-start.29 = (bf16[2,4096]{1,0:T(2,128)(2,1)S(1)}, bf16[2,4096]{1,0:T(2,128)(2,1)S(1)}, u32[]{:S(2)}, u32[]{:S(2)}) collective-permute-start(bf16[2,4096]{1,0:T(2,128)(2,1)S(1)} %get-tuple-element.80), channel_id=1, source_target_pairs={{0,6},{1,7},{2,4},{3,5},{4,2},{5,3},{6,0},{7,1},{8,14},{9,15},{10,... | collective-permute-start | bytes 49160 | tf_op jit(solution)/shard_map/ppermute | solution.py:334
  58.6 1.9 %collective-permute-done.29.refs_3_ = bf16[2,4096]{1,0:T(2,128)(2,1)S(1)} collective-permute-done((bf16[2,4096]{1,0:T(2,128)(2,1)S(1)}, bf16[2,4096]{1,0:T(2,128)(2,1)S(1)}, u32[]{:S(2)}, u32[]{:S(2)}) %collective-permute-start.29) | collective-permute-done | bytes 16416 | tf_op jit(solution)/shard_map/ppermute | solution.py:334
  60.5 0.9 %shard_map.100 = bf16[1,6,4096]{2,1,0:T(8,128)(2,1)} custom-call(bf16[2,4096]{1,0:T(2,128)(2,1)S(1)} %get-tuple-element.77.refs_0_, bf16[2,4096]{1,0:T(2,128)(2,1)S(1)} %collective-permute-done.27.refs_1_, bf16[2,4096]{1,0:T(2,128)(2,1)S(1)} %collective-permute-done.28.refs_2_, bf16[2,4096]{1,0:T(2,128)(2,1)S(1)} %collective-permute-done.29.refs_3_, ...), custom_call_target="tpu_custom_call" | custom-call | flops 1000 | bytes 66048 | tf_op jit(solution)/shard_map/pallas_call | solution.py:25
  (79 shorter events, 11.0 us)
Async XLA Ops:
  1.1 3.8 %collective-permute-start = (bf16[2,4608]{1,0:T(2,128)(2,1)S(1)}, bf16[2,4608]{1,0:T(2,128)(2,1)S(1)}, u32[]{:S(2)}, u32[]{:S(2)}) collective-permute-start(bf16[2,4608]{1,0:T(2,128)(2,1)S(1)} %get-tuple-element.44), channel_id=1, source_target_pairs={{0,2},{1,3},{2,0},{3,1},{4,6},{5,7},{6,4},{7,5},{8,10},{9,11},{10,... | collective-permute-start | bytes 55304 | tf_op jit(solution)/shard_map/ppermute | solution.py:334
  2.7 3.8 %collective-permute-start.1 = (bf16[2,4608]{1,0:T(2,128)(2,1)S(1)}, bf16[2,4608]{1,0:T(2,128)(2,1)S(1)}, u32[]{:S(2)}, u32[]{:S(2)}) collective-permute-start(bf16[2,4608]{1,0:T(2,128)(2,1)S(1)} %get-tuple-element.45), channel_id=1, source_target_pairs={{0,4},{1,5},{2,6},{3,7},{4,0},{5,1},{6,2},{7,3},{8,12},{9,13},{10,... | collective-permute-start | bytes 55304 | tf_op jit(solution)/shard_map/ppermute | solution.py:334
  4.2 4.7 %collective-permute-start.2 = (bf16[2,4608]{1,0:T(2,128)(2,1)S(1)}, bf16[2,4608]{1,0:T(2,128)(2,1)S(1)}, u32[]{:S(2)}, u32[]{:S(2)}) collective-permute-start(bf16[2,4608]{1,0:T(2,128)(2,1)S(1)} %get-tuple-element.46), channel_id=1, source_target_pairs={{0,6},{1,7},{2,4},{3,5},{4,2},{5,3},{6,0},{7,1},{8,14},{9,15},{10,... | collective-permute-start | bytes 55304 | tf_op jit(solution)/shard_map/ppermute | solution.py:334
  4.7 4.2 %collective-permute-start.3 = (bf16[2,4608]{1,0:T(2,128)(2,1)S(1)}, bf16[2,4608]{1,0:T(2,128)(2,1)S(1)}, u32[]{:S(2)}, u32[]{:S(2)}) collective-permute-start(bf16[2,4608]{1,0:T(2,128)(2,1)S(1)} %get-tuple-element.43.refs_0_), channel_id=1, source_target_pairs={{0,1},{1,0},{2,3},{3,2},{4,5},{5,4},{6,7},{7,6},{8,9},{9,8},{10,11... | collective-permute-start | bytes 55304 | tf_op jit(solution)/shard_map/ppermute | solution.py:337
  4.9 3.9 %collective-permute-start.4 = (bf16[2,4608]{1,0:T(2,128)(2,1)S(1)}, bf16[2,4608]{1,0:T(2,128)(2,1)S(1)}, u32[]{:S(2)}, u32[]{:S(2)}) collective-permute-start(bf16[2,4608]{1,0:T(2,128)(2,1)S(1)} %collective-permute-done.refs_1_), channel_id=1, source_target_pairs={{0,1},{1,0},{2,3},{3,2},{4,5},{5,4},{6,7},{7,6},{8,9},{9,8},{10,11... | collective-permute-start | bytes 55304 | tf_op jit(solution)/shard_map/ppermute | solution.py:337
  6.4 2.4 %collective-permute-start.5 = (bf16[2,4608]{1,0:T(2,128)(2,1)S(1)}, bf16[2,4608]{1,0:T(2,128)(2,1)S(1)}, u32[]{:S(2)}, u32[]{:S(2)}) collective-permute-start(bf16[2,4608]{1,0:T(2,128)(2,1)S(1)} %collective-permute-done.1.refs_2_), channel_id=1, source_target_pairs={{0,1},{1,0},{2,3},{3,2},{4,5},{5,4},{6,7},{7,6},{8,9},{9,8},{10,11... | collective-permute-start | bytes 55304 | tf_op jit(solution)/shard_map/ppermute | solution.py:337
  10.3 1.3 %collective-permute-start.7 = (bf16[16,2048]{1,0:T(8,128)(2,1)S(1)}, bf16[16,2048]{1,0:T(8,128)(2,1)S(1)}, u32[]{:S(2)}, u32[]{:S(2)}) collective-permute-start(bf16[16,2048]{1,0:T(8,128)(2,1)S(1)} %get-tuple-element.49), channel_id=1, source_target_pairs={{0,1},{1,0},{2,3},{3,2},{4,5},{5,4},{6,7},{7,6},{8,9},{9,8},{10,11... | collective-permute-start | bytes 196616 | tf_op jit(solution)/shard_map/ppermute | solution.py:337
  13.0 1.9 %collective-permute-start.11 = (bf16[16,2176]{1,0:T(8,128)(2,1)S(1)}, bf16[16,2176]{1,0:T(8,128)(2,1)S(1)}, u32[]{:S(2)}, u32[]{:S(2)}) collective-permute-start(bf16[16,2176]{1,0:T(8,128)(2,1)S(1)} %collective-permute-done.8.before.refs_0_), channel_id=1, source_target_pairs={{0,1},{1,0},{2,3},{3,2},{4,5},{5,4},{6,7},{7,6},{8,10},{9,11},{10,... | collective-permute-start | bytes 208904 | tf_op jit(solution)/shard_map/ppermute | solution.py:362
  15.1 1.3 %collective-permute-start.12 = (bf16[16,2048]{1,0:T(8,128)(2,1)S(1)}, bf16[16,2048]{1,0:T(8,128)(2,1)S(1)}, u32[]{:S(2)}, u32[]{:S(2)}) collective-permute-start(bf16[16,2048]{1,0:T(8,128)(2,1)S(1)} %shard_map.81.half.refs_0_.refs_2_), channel_id=1, source_target_pairs={{0,1},{1,0},{2,3},{3,2},{4,5},{5,4},{6,7},{7,6},{8,9},{9,8},{10,11... | collective-permute-start | bytes 196616 | tf_op jit(solution)/shard_map/ppermute | solution.py:337
  17.8 12.3 %collective-permute-start.15 = (bf16[16,2176]{1,0:T(8,128)(2,1)S(1)}, bf16[16,2176]{1,0:T(8,128)(2,1)S(1)}, u32[]{:S(2)}, u32[]{:S(2)}) collective-permute-start(bf16[16,2176]{1,0:T(8,128)(2,1)S(1)} %get-tuple-element.61), channel_id=1, source_target_pairs={{0,1},{1,0},{2,3},{3,2},{4,5},{5,4},{6,7},{7,6},{8,16},{9,17},{10,... | collective-permute-start | bytes 208904 | tf_op jit(solution)/shard_map/ppermute | solution.py:355
  18.0 14.3 %collective-permute-start.14 = (bf16[16,2048]{1,0:T(8,128)(2,1)S(1)}, bf16[16,2048]{1,0:T(8,128)(2,1)S(1)}, u32[]{:S(2)}, u32[]{:S(2)}) collective-permute-start(bf16[16,2048]{1,0:T(8,128)(2,1)S(1)} %get-tuple-element.60.refs_1_), channel_id=1, source_target_pairs={{0,1},{1,0},{2,3},{3,2},{4,5},{5,4},{6,7},{7,6},{8,22},{9,23},{10,... | collective-permute-start | bytes 196616 | tf_op jit(solution)/shard_map/ppermute | solution.py:355
  29.5 2.7 %collective-permute-start.16 = (bf16[16,2048]{1,0:T(8,128)(2,1)S(1)}, bf16[16,2048]{1,0:T(8,128)(2,1)S(1)}, u32[]{:S(2)}, u32[]{:S(2)}) collective-permute-start(bf16[16,2048]{1,0:T(8,128)(2,1)S(1)} %get-tuple-element.60.refs_1_), channel_id=1, source_target_pairs={{0,1},{1,0},{2,3},{3,2},{4,5},{5,4},{6,7},{7,6},{8,18},{9,19},{10,... | collective-permute-start | bytes 196616 | tf_op jit(solution)/shard_map/ppermute | solution.py:355
  29.5 2.9 %collective-permute-start.17 = (bf16[16,2048]{1,0:T(8,128)(2,1)S(1)}, bf16[16,2048]{1,0:T(8,128)(2,1)S(1)}, u32[]{:S(2)}, u32[]{:S(2)}) collective-permute-start(bf16[16,2048]{1,0:T(8,128)(2,1)S(1)} %get-tuple-element.60.refs_1_), channel_id=1, source_target_pairs={{0,1},{1,0},{2,3},{3,2},{4,5},{5,4},{6,7},{7,6},{8,20},{9,21},{10,... | collective-permute-start | bytes 196616 | tf_op jit(solution)/shard_map/ppermute | solution.py:355
  32.6 1.3 %collective-permute-start.18 = (bf16[16,2048]{1,0:T(8,128)(2,1)S(1)}, bf16[16,2048]{1,0:T(8,128)(2,1)S(1)}, u32[]{:S(2)}, u32[]{:S(2)}) collective-permute-start(bf16[16,2048]{1,0:T(8,128)(2,1)S(1)} %shard_map.88.half.refs_0_.refs_2_), channel_id=1, source_target_pairs={{0,1},{1,0},{2,3},{3,2},{4,5},{5,4},{6,7},{7,6},{8,9},{9,8},{10,11... | collective-permute-start | bytes 196616 | tf_op jit(solution)/shard_map/ppermute | solution.py:337
  35.3 9.8 %collective-permute-start.21 = (bf16[16,2176]{1,0:T(8,128)(2,1)S(1)}, bf16[16,2176]{1,0:T(8,128)(2,1)S(1)}, u32[]{:S(2)}, u32[]{:S(2)}) collective-permute-start(bf16[16,2176]{1,0:T(8,128)(2,1)S(1)} %get-tuple-element.68), channel_id=1, source_target_pairs={{0,1},{1,0},{2,3},{3,2},{4,5},{5,4},{6,7},{7,6},{8,9},{9,8},{10,11... | collective-permute-start | bytes 208904 | tf_op jit(solution)/shard_map/ppermute | solution.py:355
  41.5 6.5 %collective-permute-start.20 = (bf16[16,2048]{1,0:T(8,128)(2,1)S(1)}, bf16[16,2048]{1,0:T(8,128)(2,1)S(1)}, u32[]{:S(2)}, u32[]{:S(2)}) collective-permute-start(bf16[16,2048]{1,0:T(8,128)(2,1)S(1)} %get-tuple-element.67.refs_2_), channel_id=1, source_target_pairs={{0,16},{1,17},{2,18},{3,19},{4,20},{5,21},{6,22},{7,23},{8,9},{9,8... | collective-permute-start | bytes 196616 | tf_op jit(solution)/shard_map/ppermute | solution.py:355
  41.5 7.4 %collective-permute-start.22 = (bf16[16,2048]{1,0:T(8,128)(2,1)S(1)}, bf16[16,2048]{1,0:T(8,128)(2,1)S(1)}, u32[]{:S(2)}, u32[]{:S(2)}) collective-permute-start(bf16[16,2048]{1,0:T(8,128)(2,1)S(1)} %get-tuple-element.67.refs_2_), channel_id=1, source_target_pairs={{0,1},{1,0},{2,3},{3,2},{4,5},{5,4},{6,7},{7,6},{8,9},{9,8},{10,11... | collective-permute-start | bytes 196616 | tf_op jit(solution)/shard_map/ppermute | solution.py:355
  44.9 5.2 %collective-permute-start.23 = (bf16[16,2048]{1,0:T(8,128)(2,1)S(1)}, bf16[16,2048]{1,0:T(8,128)(2,1)S(1)}, u32[]{:S(2)}, u32[]{:S(2)}) collective-permute-start(bf16[16,2048]{1,0:T(8,128)(2,1)S(1)} %get-tuple-element.67.refs_2_), channel_id=1, source_target_pairs={{0,1},{1,0},{2,3},{3,2},{4,5},{5,4},{6,7},{7,6},{8,9},{9,8},{10,11... | collective-permute-start | bytes 196616 | tf_op jit(solution)/shard_map/ppermute | solution.py:355
  45.0 4.1 %collective-permute-start.24 = (bf16[8,2048]{1,0:T(8,128)(2,1)S(1)}, bf16[8,2048]{1,0:T(8,128)(2,1)S(1)}, u32[]{:S(2)}, u32[]{:S(2)}) collective-permute-start(bf16[8,2048]{1,0:T(8,128)(2,1)S(1)} %get-tuple-element.70), channel_id=1, source_target_pairs={{0,1},{1,0},{2,3},{3,2},{4,5},{5,4},{6,7},{7,6},{8,9},{9,8},{10,11... | collective-permute-start | bytes 98312 | tf_op jit(solution)/shard_map/ppermute | solution.py:337
  50.2 1.3 %collective-permute-start.25 = (bf16[16,2048]{1,0:T(8,128)(2,1)S(1)}, bf16[16,2048]{1,0:T(8,128)(2,1)S(1)}, u32[]{:S(2)}, u32[]{:S(2)}) collective-permute-start(bf16[16,2048]{1,0:T(8,128)(2,1)S(1)} %shard_map.96.half.refs_0_), channel_id=1, source_target_pairs={{0,1},{1,0},{2,3},{3,2},{4,5},{5,4},{6,7},{7,6},{8,9},{9,8},{10,11... | collective-permute-start | bytes 196616 | tf_op jit(solution)/shard_map/ppermute | solution.py:337
  52.9 1.3 %collective-permute-start.26 = (bf16[8,4096]{1,0:T(8,128)(2,1)S(1)}, bf16[8,4096]{1,0:T(8,128)(2,1)S(1)}, u32[]{:S(2)}, u32[]{:S(2)}) collective-permute-start(bf16[8,4096]{1,0:T(8,128)(2,1)S(1)} %get-tuple-element.75), channel_id=1, source_target_pairs={{0,1},{1,0},{2,3},{3,2},{4,5},{5,4},{6,7},{7,6},{8,9},{9,8},{10,11... | collective-permute-start | bytes 196616 | tf_op jit(solution)/shard_map/ppermute | solution.py:337
  54.3 3.8 %collective-permute-start.27 = (bf16[2,4096]{1,0:T(2,128)(2,1)S(1)}, bf16[2,4096]{1,0:T(2,128)(2,1)S(1)}, u32[]{:S(2)}, u32[]{:S(2)}) collective-permute-start(bf16[2,4096]{1,0:T(2,128)(2,1)S(1)} %get-tuple-element.78), channel_id=1, source_target_pairs={{0,2},{1,3},{2,0},{3,1},{4,6},{5,7},{6,4},{7,5},{8,10},{9,11},{10,... | collective-permute-start | bytes 49160 | tf_op jit(solution)/shard_map/ppermute | solution.py:334
  54.9 3.7 %collective-permute-start.28 = (bf16[2,4096]{1,0:T(2,128)(2,1)S(1)}, bf16[2,4096]{1,0:T(2,128)(2,1)S(1)}, u32[]{:S(2)}, u32[]{:S(2)}) collective-permute-start(bf16[2,4096]{1,0:T(2,128)(2,1)S(1)} %get-tuple-element.79), channel_id=1, source_target_pairs={{0,4},{1,5},{2,6},{3,7},{4,0},{5,1},{6,2},{7,3},{8,12},{9,13},{10,... | collective-permute-start | bytes 49160 | tf_op jit(solution)/shard_map/ppermute | solution.py:334
  55.9 4.6 %collective-permute-start.29 = (bf16[2,4096]{1,0:T(2,128)(2,1)S(1)}, bf16[2,4096]{1,0:T(2,128)(2,1)S(1)}, u32[]{:S(2)}, u32[]{:S(2)}) collective-permute-start(bf16[2,4096]{1,0:T(2,128)(2,1)S(1)} %get-tuple-element.80), channel_id=1, source_target_pairs={{0,6},{1,7},{2,4},{3,5},{4,2},{5,3},{6,0},{7,1},{8,14},{9,15},{10,... | collective-permute-start | bytes 49160 | tf_op jit(solution)/shard_map/ppermute | solution.py:334
  (13 other events, 50.8 us)

commit v9 on v8

--- a/solution.py
+++ b/solution.py
@@ -374,8 +374,14 @@
     arrived = [across(sent[i], i) for i in range(EXPERTS)]
     pieces = list(arrived)
     for m in range(1, group):
-        for piece in arrived:
-            pieces.append(within(piece, m))
+        for i, piece in enumerate(arrived):
+            if i == EXPERTS - 2:
+                pairs = [
+                    (d, (d // group ^ i) * group + (d % group ^ m)) for d in range(peers)
+                ]
+                pieces.append(lax.ppermute(sent[i], "expert", pairs))
+            else:
+                pieces.append(within(piece, m))
     flops = 6 * rows * width * w_gate.shape[2]
     whole, half, table, scale = call(
         functools.partial(join_kernel, group, width),

time: 62.2 us -> 61 us (0.981)
  waiting for transfers between devices: 23.2 us -> 20.7 us
  starting transfers between devices: 31.4 us -> 33.3 us
    ppermute x6, waiting for transfers between devices: 6.57 us -> 4.79 us  [across(): return lax.ppermute(value, 'expert', pairs)]
    ppermute x12 -> x11, starting transfers between devices: 1.47 us -> 2.75 us  [within(): return lax.ppermute(value, 'expert', [(d, d ^ m) for d in range(peers)])]
    ppermute x12 -> x11, waiting for transfers between devices: 8.42 us -> 7.72 us  [within(): return lax.ppermute(value, 'expert', [(d, d ^ m) for d in range(peers)])]
  transfers between devices with their start and end apart: 30 -> 30, of which waited for: 21 -> 20; matrix products, arithmetic and copies ran while one was open for 0% -> 0% of each run, Pallas kernels for 4% -> 4%
where the time goes in v9:
time: 61 us; the launch traced here: 60.7 us
  starting transfers between devices  33.3 us (55%)
  waiting for transfers between devices  20.7 us (34%)
  Pallas kernels  5.74 us (9%)
  local copies, waits for them, and re-layouts  0.81 us (1%)
    ppermute x11, starting transfers between devices, gather(): outs[i] = lax.ppermute(value if i else marked, ('section', 'expert'), pairs)  23.1 us
    ppermute x11, waiting for transfers between devices, gather(): outs[i] = lax.ppermute(value if i else marked, ('section', 'expert'), pairs)  8.15 us
    ppermute x11, waiting for transfers between devices, within(): return lax.ppermute(value, 'expert', [(d, d ^ m) for d in range(peers)])  7.72 us
    ppermute x6, starting transfers between devices, across(): return lax.ppermute(value, 'expert', pairs)  7.11 us
    pallas_call x28, Pallas kernels, call(): pl.pallas_call(kernel, out_shape=outs, in_specs=specs or [VMEM] * len(arg...  5.74 us
    ppermute x6, waiting for transfers between devices, across(): return lax.ppermute(value, 'expert', pairs)  4.79 us
    ppermute x11, starting transfers between devices, within(): return lax.ppermute(value, 'expert', [(d, d ^ m) for d in range(peers)])  2.75 us
  transfers between devices with their start and end apart: 30, of which 20 were waited for; matrix products, arithmetic and copies ran while one was open for 0% of the time, Pallas kernels for 4%

profile of v9, /device:TPU:24, one launch (start us, length us, event | category | flops | bytes accessed | tf_op | source)
XLA Modules:
  0.0 60.7 jit_solution(7141331439093397602)
XLA Ops:
  1.1 1.6 %collective-permute-start = (bf16[2,4608]{1,0:T(2,128)(2,1)S(1)}, bf16[2,4608]{1,0:T(2,128)(2,1)S(1)}, u32[]{:S(2)}, u32[]{:S(2)}) collective-permute-start(bf16[2,4608]{1,0:T(2,128)(2,1)S(1)} %get-tuple-element.44), channel_id=1, source_target_pairs={{0,2},{1,3},{2,0},{3,1},{4,6},{5,7},{6,4},{7,5},{8,10},{9,11},{10,... | collective-permute-start | bytes 55304 | tf_op jit(solution)/shard_map/ppermute | solution.py:334
  2.7 1.5 %collective-permute-start.2 = (bf16[2,4608]{1,0:T(2,128)(2,1)S(1)}, bf16[2,4608]{1,0:T(2,128)(2,1)S(1)}, u32[]{:S(2)}, u32[]{:S(2)}) collective-permute-start(bf16[2,4608]{1,0:T(2,128)(2,1)S(1)} %get-tuple-element.46), channel_id=1, source_target_pairs={{0,6},{1,7},{2,4},{3,5},{4,2},{5,3},{6,0},{7,1},{8,14},{9,15},{10,... | collective-permute-start | bytes 55304 | tf_op jit(solution)/shard_map/ppermute | solution.py:334
  4.8 1.5 %collective-permute-start.3 = (bf16[2,4608]{1,0:T(2,128)(2,1)S(1)}, bf16[2,4608]{1,0:T(2,128)(2,1)S(1)}, u32[]{:S(2)}, u32[]{:S(2)}) collective-permute-start(bf16[2,4608]{1,0:T(2,128)(2,1)S(1)} %get-tuple-element.43.refs_0_), channel_id=1, source_target_pairs={{0,1},{1,0},{2,3},{3,2},{4,5},{5,4},{6,7},{7,6},{8,9},{9,8},{10,11... | collective-permute-start | bytes 55304 | tf_op jit(solution)/shard_map/ppermute | solution.py:337
  6.3 1.0 %collective-permute-done.2.refs_3_ = bf16[2,4608]{1,0:T(2,128)(2,1)S(1)} collective-permute-done((bf16[2,4608]{1,0:T(2,128)(2,1)S(1)}, bf16[2,4608]{1,0:T(2,128)(2,1)S(1)}, u32[]{:S(2)}, u32[]{:S(2)}) %collective-permute-start.2) | collective-permute-done | bytes 18464 | tf_op jit(solution)/shard_map/ppermute | solution.py:334
  9.0 1.1 %collective-permute-done.7.refs_1_ = bf16[16,2048]{1,0:T(8,128)(2,1)S(1)} collective-permute-done((bf16[16,2048]{1,0:T(8,128)(2,1)S(1)}, bf16[16,2048]{1,0:T(8,128)(2,1)S(1)}, u32[]{:S(2)}, u32[]{:S(2)}) %collective-permute-start.7) | collective-permute-done | bytes 65568 | tf_op jit(solution)/shard_map/ppermute | solution.py:337
  10.4 1.1 %collective-permute-done.8.before.refs_0_ = bf16[16,2176]{1,0:T(8,128)(2,1)S(1)} collective-permute-done((bf16[16,2176]{1,0:T(8,128)(2,1)S(1)}, bf16[16,2176]{1,0:T(8,128)(2,1)S(1)}, u32[]{:S(2)}, u32[]{:S(2)}) %collective-permute-start.8) | collective-permute-done | bytes 69664 | tf_op jit(solution)/shard_map/ppermute | solution.py:355
  13.8 1.1 %collective-permute-done.12.refs_1_ = bf16[16,2048]{1,0:T(8,128)(2,1)S(1)} collective-permute-done((bf16[16,2048]{1,0:T(8,128)(2,1)S(1)}, bf16[16,2048]{1,0:T(8,128)(2,1)S(1)}, u32[]{:S(2)}, u32[]{:S(2)}) %collective-permute-start.12) | collective-permute-done | bytes 65568 | tf_op jit(solution)/shard_map/ppermute | solution.py:337
  15.1 1.1 %collective-permute-done.13.refs_1_ = bf16[16,2048]{1,0:T(8,128)(2,1)S(1)} collective-permute-done((bf16[16,2048]{1,0:T(8,128)(2,1)S(1)}, bf16[16,2048]{1,0:T(8,128)(2,1)S(1)}, u32[]{:S(2)}, u32[]{:S(2)}) %collective-permute-start.13) | collective-permute-done | bytes 65568 | tf_op jit(solution)/shard_map/ppermute | solution.py:337
  16.5 11.5 %collective-permute-start.14 = (bf16[16,2048]{1,0:T(8,128)(2,1)S(1)}, bf16[16,2048]{1,0:T(8,128)(2,1)S(1)}, u32[]{:S(2)}, u32[]{:S(2)}) collective-permute-start(bf16[16,2048]{1,0:T(8,128)(2,1)S(1)} %get-tuple-element.60.refs_1_), channel_id=1, source_target_pairs={{0,1},{1,0},{2,3},{3,2},{4,5},{5,4},{6,7},{7,6},{8,22},{9,23},{10,... | collective-permute-start | bytes 196616 | tf_op jit(solution)/shard_map/ppermute | solution.py:355
  28.9 1.9 %collective-permute-done.14.refs_0_ = bf16[16,2048]{1,0:T(8,128)(2,1)S(1)} collective-permute-done((bf16[16,2048]{1,0:T(8,128)(2,1)S(1)}, bf16[16,2048]{1,0:T(8,128)(2,1)S(1)}, u32[]{:S(2)}, u32[]{:S(2)}) %collective-permute-start.14) | collective-permute-done | bytes 65568 | tf_op jit(solution)/shard_map/ppermute | solution.py:355
  31.2 1.2 %collective-permute-done.18.refs_1_ = bf16[16,2048]{1,0:T(8,128)(2,1)S(1)} collective-permute-done((bf16[16,2048]{1,0:T(8,128)(2,1)S(1)}, bf16[16,2048]{1,0:T(8,128)(2,1)S(1)}, u32[]{:S(2)}, u32[]{:S(2)}) %collective-permute-start.18) | collective-permute-done | bytes 65568 | tf_op jit(solution)/shard_map/ppermute | solution.py:337
  32.6 1.1 %collective-permute-done.19.refs_1_ = bf16[16,2048]{1,0:T(8,128)(2,1)S(1)} collective-permute-done((bf16[16,2048]{1,0:T(8,128)(2,1)S(1)}, bf16[16,2048]{1,0:T(8,128)(2,1)S(1)}, u32[]{:S(2)}, u32[]{:S(2)}) %collective-permute-start.19) | collective-permute-done | bytes 65568 | tf_op jit(solution)/shard_map/ppermute | solution.py:337
  33.8 7.1 %collective-permute-start.21 = (bf16[16,2176]{1,0:T(8,128)(2,1)S(1)}, bf16[16,2176]{1,0:T(8,128)(2,1)S(1)}, u32[]{:S(2)}, u32[]{:S(2)}) collective-permute-start(bf16[16,2176]{1,0:T(8,128)(2,1)S(1)} %get-tuple-element.68), channel_id=1, source_target_pairs={{0,1},{1,0},{2,3},{3,2},{4,5},{5,4},{6,7},{7,6},{8,9},{9,8},{10,11... | collective-permute-start | bytes 208904 | tf_op jit(solution)/shard_map/ppermute | solution.py:355
  40.8 3.0 %collective-permute-start.22 = (bf16[16,2048]{1,0:T(8,128)(2,1)S(1)}, bf16[16,2048]{1,0:T(8,128)(2,1)S(1)}, u32[]{:S(2)}, u32[]{:S(2)}) collective-permute-start(bf16[16,2048]{1,0:T(8,128)(2,1)S(1)} %get-tuple-element.67.refs_2_), channel_id=1, source_target_pairs={{0,1},{1,0},{2,3},{3,2},{4,5},{5,4},{6,7},{7,6},{8,9},{9,8},{10,11... | collective-permute-start | bytes 196616 | tf_op jit(solution)/shard_map/ppermute | solution.py:355
  44.4 3.2 %collective-permute-done.20.refs_0_ = bf16[16,2048]{1,0:T(8,128)(2,1)S(1)} collective-permute-done((bf16[16,2048]{1,0:T(8,128)(2,1)S(1)}, bf16[16,2048]{1,0:T(8,128)(2,1)S(1)}, u32[]{:S(2)}, u32[]{:S(2)}) %collective-permute-start.20) | collective-permute-done | bytes 65568 | tf_op jit(solution)/shard_map/ppermute | solution.py:355
  48.3 0.7 %collective-permute-done.23.refs_1_ = bf16[16,2048]{1,0:T(8,128)(2,1)S(1)} collective-permute-done((bf16[16,2048]{1,0:T(8,128)(2,1)S(1)}, bf16[16,2048]{1,0:T(8,128)(2,1)S(1)}, u32[]{:S(2)}, u32[]{:S(2)}) %collective-permute-start.23) | collective-permute-done | bytes 65568 | tf_op jit(solution)/shard_map/ppermute | solution.py:355
  50.5 1.3 %shard_map.98 = (bf16[8,4096]{1,0:T(8,128)(2,1)S(1)}, bf16[8,4096]{1,0:T(8,128)(2,1)S(1)}, bf16[8,4096]{1,0:T(8,128)(2,1)S(1)}) custom-call(bf16[16,2048]{1,0:T(8,128)(2,1)S(1)} %shard_map.96.half.refs_0_, bf16[16,2048]{1,0:T(8,128)(2,1)S(1)} %collective-permute-done.25.refs_1_, f32[16,512]{1,0:T(8,128)S(1)} %get-tuple-element.71.refs_2_, ...), custom_call_target="tpu_custom_call" | custom-call | flops 100663296 | bytes 12804096 | tf_op jit(solution)/shard_map/pallas_call | solution.py:25
  52.0 1.1 %collective-permute-done.26.refs_1_ = bf16[8,4096]{1,0:T(8,128)(2,1)S(1)} collective-permute-done((bf16[8,4096]{1,0:T(8,128)(2,1)S(1)}, bf16[8,4096]{1,0:T(8,128)(2,1)S(1)}, u32[]{:S(2)}, u32[]{:S(2)}) %collective-permute-start.26) | collective-permute-done | bytes 65568 | tf_op jit(solution)/shard_map/ppermute | solution.py:337
  53.2 0.9 %collective-permute-start.27 = (bf16[2,4096]{1,0:T(2,128)(2,1)S(1)}, bf16[2,4096]{1,0:T(2,128)(2,1)S(1)}, u32[]{:S(2)}, u32[]{:S(2)}) collective-permute-start(bf16[2,4096]{1,0:T(2,128)(2,1)S(1)} %get-tuple-element.78), channel_id=1, source_target_pairs={{0,2},{1,3},{2,0},{3,1},{4,6},{5,7},{6,4},{7,5},{8,10},{9,11},{10,... | collective-permute-start | bytes 49160 | tf_op jit(solution)/shard_map/ppermute | solution.py:334
  54.1 1.1 %collective-permute-start.28 = (bf16[2,4096]{1,0:T(2,128)(2,1)S(1)}, bf16[2,4096]{1,0:T(2,128)(2,1)S(1)}, u32[]{:S(2)}, u32[]{:S(2)}) collective-permute-start(bf16[2,4096]{1,0:T(2,128)(2,1)S(1)} %get-tuple-element.79), channel_id=1, source_target_pairs={{0,4},{1,5},{2,6},{3,7},{4,0},{5,1},{6,2},{7,3},{8,12},{9,13},{10,... | collective-permute-start | bytes 49160 | tf_op jit(solution)/shard_map/ppermute | solution.py:334
  55.2 1.6 %collective-permute-start.29 = (bf16[2,4096]{1,0:T(2,128)(2,1)S(1)}, bf16[2,4096]{1,0:T(2,128)(2,1)S(1)}, u32[]{:S(2)}, u32[]{:S(2)}) collective-permute-start(bf16[2,4096]{1,0:T(2,128)(2,1)S(1)} %get-tuple-element.80), channel_id=1, source_target_pairs={{0,6},{1,7},{2,4},{3,5},{4,2},{5,3},{6,0},{7,1},{8,14},{9,15},{10,... | collective-permute-start | bytes 49160 | tf_op jit(solution)/shard_map/ppermute | solution.py:334
  57.0 0.8 %collective-permute-done.28.refs_2_ = bf16[2,4096]{1,0:T(2,128)(2,1)S(1)} collective-permute-done((bf16[2,4096]{1,0:T(2,128)(2,1)S(1)}, bf16[2,4096]{1,0:T(2,128)(2,1)S(1)}, u32[]{:S(2)}, u32[]{:S(2)}) %collective-permute-start.28) | collective-permute-done | bytes 16416 | tf_op jit(solution)/shard_map/ppermute | solution.py:334
  57.9 2.0 %collective-permute-done.29.refs_3_ = bf16[2,4096]{1,0:T(2,128)(2,1)S(1)} collective-permute-done((bf16[2,4096]{1,0:T(2,128)(2,1)S(1)}, bf16[2,4096]{1,0:T(2,128)(2,1)S(1)}, u32[]{:S(2)}, u32[]{:S(2)}) %collective-permute-start.29) | collective-permute-done | bytes 16416 | tf_op jit(solution)/shard_map/ppermute | solution.py:334
  59.9 0.9 %shard_map.100 = bf16[1,6,4096]{2,1,0:T(8,128)(2,1)} custom-call(bf16[2,4096]{1,0:T(2,128)(2,1)S(1)} %get-tuple-element.77.refs_0_, bf16[2,4096]{1,0:T(2,128)(2,1)S(1)} %collective-permute-done.27.refs_1_, bf16[2,4096]{1,0:T(2,128)(2,1)S(1)} %collective-permute-done.28.refs_2_, bf16[2,4096]{1,0:T(2,128)(2,1)S(1)} %collective-permute-done.29.refs_3_, ...), custom_call_target="tpu_custom_call" | custom-call | flops 1000 | bytes 66048 | tf_op jit(solution)/shard_map/pallas_call | solution.py:25
  (79 shorter events, 11.2 us)
Async XLA Ops:
  1.1 5.2 %collective-permute-start = (bf16[2,4608]{1,0:T(2,128)(2,1)S(1)}, bf16[2,4608]{1,0:T(2,128)(2,1)S(1)}, u32[]{:S(2)}, u32[]{:S(2)}) collective-permute-start(bf16[2,4608]{1,0:T(2,128)(2,1)S(1)} %get-tuple-element.44), channel_id=1, source_target_pairs={{0,2},{1,3},{2,0},{3,1},{4,6},{5,7},{6,4},{7,5},{8,10},{9,11},{10,... | collective-permute-start | bytes 55304 | tf_op jit(solution)/shard_map/ppermute | solution.py:334
  2.7 4.7 %collective-permute-start.2 = (bf16[2,4608]{1,0:T(2,128)(2,1)S(1)}, bf16[2,4608]{1,0:T(2,128)(2,1)S(1)}, u32[]{:S(2)}, u32[]{:S(2)}) collective-permute-start(bf16[2,4608]{1,0:T(2,128)(2,1)S(1)} %get-tuple-element.46), channel_id=1, source_target_pairs={{0,6},{1,7},{2,4},{3,5},{4,2},{5,3},{6,0},{7,1},{8,14},{9,15},{10,... | collective-permute-start | bytes 55304 | tf_op jit(solution)/shard_map/ppermute | solution.py:334
  4.2 3.9 %collective-permute-start.1 = (bf16[2,4608]{1,0:T(2,128)(2,1)S(1)}, bf16[2,4608]{1,0:T(2,128)(2,1)S(1)}, u32[]{:S(2)}, u32[]{:S(2)}) collective-permute-start(bf16[2,4608]{1,0:T(2,128)(2,1)S(1)} %get-tuple-element.45), channel_id=1, source_target_pairs={{0,4},{1,5},{2,6},{3,7},{4,0},{5,1},{6,2},{7,3},{8,12},{9,13},{10,... | collective-permute-start | bytes 55304 | tf_op jit(solution)/shard_map/ppermute | solution.py:334
  4.7 3.4 %collective-permute-start.5 = (bf16[2,4608]{1,0:T(2,128)(2,1)S(1)}, bf16[2,4608]{1,0:T(2,128)(2,1)S(1)}, u32[]{:S(2)}, u32[]{:S(2)}) collective-permute-start(bf16[2,4608]{1,0:T(2,128)(2,1)S(1)} %get-tuple-element.45), channel_id=1, source_target_pairs={{0,5},{1,4},{2,7},{3,6},{4,1},{5,0},{6,3},{7,2},{8,13},{9,12},{10,... | collective-permute-start | bytes 55304 | tf_op jit(solution)/shard_map/ppermute | solution.py:382
  4.8 2.6 %collective-permute-start.3 = (bf16[2,4608]{1,0:T(2,128)(2,1)S(1)}, bf16[2,4608]{1,0:T(2,128)(2,1)S(1)}, u32[]{:S(2)}, u32[]{:S(2)}) collective-permute-start(bf16[2,4608]{1,0:T(2,128)(2,1)S(1)} %get-tuple-element.43.refs_0_), channel_id=1, source_target_pairs={{0,1},{1,0},{2,3},{3,2},{4,5},{5,4},{6,7},{7,6},{8,9},{9,8},{10,11... | collective-permute-start | bytes 55304 | tf_op jit(solution)/shard_map/ppermute | solution.py:337
  6.3 1.7 %collective-permute-start.4 = (bf16[2,4608]{1,0:T(2,128)(2,1)S(1)}, bf16[2,4608]{1,0:T(2,128)(2,1)S(1)}, u32[]{:S(2)}, u32[]{:S(2)}) collective-permute-start(bf16[2,4608]{1,0:T(2,128)(2,1)S(1)} %collective-permute-done.refs_1_), channel_id=1, source_target_pairs={{0,1},{1,0},{2,3},{3,2},{4,5},{5,4},{6,7},{7,6},{8,9},{9,8},{10,11... | collective-permute-start | bytes 55304 | tf_op jit(solution)/shard_map/ppermute | solution.py:337
  8.8 1.3 %collective-permute-start.7 = (bf16[16,2048]{1,0:T(8,128)(2,1)S(1)}, bf16[16,2048]{1,0:T(8,128)(2,1)S(1)}, u32[]{:S(2)}, u32[]{:S(2)}) collective-permute-start(bf16[16,2048]{1,0:T(8,128)(2,1)S(1)} %get-tuple-element.49), channel_id=1, source_target_pairs={{0,1},{1,0},{2,3},{3,2},{4,5},{5,4},{6,7},{7,6},{8,9},{9,8},{10,11... | collective-permute-start | bytes 196616 | tf_op jit(solution)/shard_map/ppermute | solution.py:337
  11.5 1.9 %collective-permute-start.11 = (bf16[16,2176]{1,0:T(8,128)(2,1)S(1)}, bf16[16,2176]{1,0:T(8,128)(2,1)S(1)}, u32[]{:S(2)}, u32[]{:S(2)}) collective-permute-start(bf16[16,2176]{1,0:T(8,128)(2,1)S(1)} %collective-permute-done.8.before.refs_0_), channel_id=1, source_target_pairs={{0,1},{1,0},{2,3},{3,2},{4,5},{5,4},{6,7},{7,6},{8,10},{9,11},{10,... | collective-permute-start | bytes 208904 | tf_op jit(solution)/shard_map/ppermute | solution.py:362
  13.6 1.3 %collective-permute-start.12 = (bf16[16,2048]{1,0:T(8,128)(2,1)S(1)}, bf16[16,2048]{1,0:T(8,128)(2,1)S(1)}, u32[]{:S(2)}, u32[]{:S(2)}) collective-permute-start(bf16[16,2048]{1,0:T(8,128)(2,1)S(1)} %shard_map.81.half.refs_0_.refs_2_), channel_id=1, source_target_pairs={{0,1},{1,0},{2,3},{3,2},{4,5},{5,4},{6,7},{7,6},{8,9},{9,8},{10,11... | collective-permute-start | bytes 196616 | tf_op jit(solution)/shard_map/ppermute | solution.py:337
  16.3 12.3 %collective-permute-start.15 = (bf16[16,2176]{1,0:T(8,128)(2,1)S(1)}, bf16[16,2176]{1,0:T(8,128)(2,1)S(1)}, u32[]{:S(2)}, u32[]{:S(2)}) collective-permute-start(bf16[16,2176]{1,0:T(8,128)(2,1)S(1)} %get-tuple-element.61), channel_id=1, source_target_pairs={{0,1},{1,0},{2,3},{3,2},{4,5},{5,4},{6,7},{7,6},{8,16},{9,17},{10,... | collective-permute-start | bytes 208904 | tf_op jit(solution)/shard_map/ppermute | solution.py:355
  16.5 14.3 %collective-permute-start.14 = (bf16[16,2048]{1,0:T(8,128)(2,1)S(1)}, bf16[16,2048]{1,0:T(8,128)(2,1)S(1)}, u32[]{:S(2)}, u32[]{:S(2)}) collective-permute-start(bf16[16,2048]{1,0:T(8,128)(2,1)S(1)} %get-tuple-element.60.refs_1_), channel_id=1, source_target_pairs={{0,1},{1,0},{2,3},{3,2},{4,5},{5,4},{6,7},{7,6},{8,22},{9,23},{10,... | collective-permute-start | bytes 196616 | tf_op jit(solution)/shard_map/ppermute | solution.py:355
  28.0 2.7 %collective-permute-start.16 = (bf16[16,2048]{1,0:T(8,128)(2,1)S(1)}, bf16[16,2048]{1,0:T(8,128)(2,1)S(1)}, u32[]{:S(2)}, u32[]{:S(2)}) collective-permute-start(bf16[16,2048]{1,0:T(8,128)(2,1)S(1)} %get-tuple-element.60.refs_1_), channel_id=1, source_target_pairs={{0,1},{1,0},{2,3},{3,2},{4,5},{5,4},{6,7},{7,6},{8,18},{9,19},{10,... | collective-permute-start | bytes 196616 | tf_op jit(solution)/shard_map/ppermute | solution.py:355
  28.0 2.9 %collective-permute-start.17 = (bf16[16,2048]{1,0:T(8,128)(2,1)S(1)}, bf16[16,2048]{1,0:T(8,128)(2,1)S(1)}, u32[]{:S(2)}, u32[]{:S(2)}) collective-permute-start(bf16[16,2048]{1,0:T(8,128)(2,1)S(1)} %get-tuple-element.60.refs_1_), channel_id=1, source_target_pairs={{0,1},{1,0},{2,3},{3,2},{4,5},{5,4},{6,7},{7,6},{8,20},{9,21},{10,... | collective-permute-start | bytes 196616 | tf_op jit(solution)/shard_map/ppermute | solution.py:355
  31.1 1.3 %collective-permute-start.18 = (bf16[16,2048]{1,0:T(8,128)(2,1)S(1)}, bf16[16,2048]{1,0:T(8,128)(2,1)S(1)}, u32[]{:S(2)}, u32[]{:S(2)}) collective-permute-start(bf16[16,2048]{1,0:T(8,128)(2,1)S(1)} %shard_map.88.half.refs_0_.refs_2_), channel_id=1, source_target_pairs={{0,1},{1,0},{2,3},{3,2},{4,5},{5,4},{6,7},{7,6},{8,9},{9,8},{10,11... | collective-permute-start | bytes 196616 | tf_op jit(solution)/shard_map/ppermute | solution.py:337
  33.8 10.2 %collective-permute-start.21 = (bf16[16,2176]{1,0:T(8,128)(2,1)S(1)}, bf16[16,2176]{1,0:T(8,128)(2,1)S(1)}, u32[]{:S(2)}, u32[]{:S(2)}) collective-permute-start(bf16[16,2176]{1,0:T(8,128)(2,1)S(1)} %get-tuple-element.68), channel_id=1, source_target_pairs={{0,1},{1,0},{2,3},{3,2},{4,5},{5,4},{6,7},{7,6},{8,9},{9,8},{10,11... | collective-permute-start | bytes 208904 | tf_op jit(solution)/shard_map/ppermute | solution.py:355
  40.8 6.7 %collective-permute-start.20 = (bf16[16,2048]{1,0:T(8,128)(2,1)S(1)}, bf16[16,2048]{1,0:T(8,128)(2,1)S(1)}, u32[]{:S(2)}, u32[]{:S(2)}) collective-permute-start(bf16[16,2048]{1,0:T(8,128)(2,1)S(1)} %get-tuple-element.67.refs_2_), channel_id=1, source_target_pairs={{0,16},{1,17},{2,18},{3,19},{4,20},{5,21},{6,22},{7,23},{8,9},{9,8... | collective-permute-start | bytes 196616 | tf_op jit(solution)/shard_map/ppermute | solution.py:355
  40.8 7.3 %collective-permute-start.22 = (bf16[16,2048]{1,0:T(8,128)(2,1)S(1)}, bf16[16,2048]{1,0:T(8,128)(2,1)S(1)}, u32[]{:S(2)}, u32[]{:S(2)}) collective-permute-start(bf16[16,2048]{1,0:T(8,128)(2,1)S(1)} %get-tuple-element.67.refs_2_), channel_id=1, source_target_pairs={{0,1},{1,0},{2,3},{3,2},{4,5},{5,4},{6,7},{7,6},{8,9},{9,8},{10,11... | collective-permute-start | bytes 196616 | tf_op jit(solution)/shard_map/ppermute | solution.py:355
  43.9 5.2 %collective-permute-start.23 = (bf16[16,2048]{1,0:T(8,128)(2,1)S(1)}, bf16[16,2048]{1,0:T(8,128)(2,1)S(1)}, u32[]{:S(2)}, u32[]{:S(2)}) collective-permute-start(bf16[16,2048]{1,0:T(8,128)(2,1)S(1)} %get-tuple-element.67.refs_2_), channel_id=1, source_target_pairs={{0,1},{1,0},{2,3},{3,2},{4,5},{5,4},{6,7},{7,6},{8,9},{9,8},{10,11... | collective-permute-start | bytes 196616 | tf_op jit(solution)/shard_map/ppermute | solution.py:355
  43.9 4.4 %collective-permute-start.24 = (bf16[8,2048]{1,0:T(8,128)(2,1)S(1)}, bf16[8,2048]{1,0:T(8,128)(2,1)S(1)}, u32[]{:S(2)}, u32[]{:S(2)}) collective-permute-start(bf16[8,2048]{1,0:T(8,128)(2,1)S(1)} %get-tuple-element.70), channel_id=1, source_target_pairs={{0,1},{1,0},{2,3},{3,2},{4,5},{5,4},{6,7},{7,6},{8,9},{9,8},{10,11... | collective-permute-start | bytes 98312 | tf_op jit(solution)/shard_map/ppermute | solution.py:337
  49.2 1.3 %collective-permute-start.25 = (bf16[16,2048]{1,0:T(8,128)(2,1)S(1)}, bf16[16,2048]{1,0:T(8,128)(2,1)S(1)}, u32[]{:S(2)}, u32[]{:S(2)}) collective-permute-start(bf16[16,2048]{1,0:T(8,128)(2,1)S(1)} %shard_map.96.half.refs_0_), channel_id=1, source_target_pairs={{0,1},{1,0},{2,3},{3,2},{4,5},{5,4},{6,7},{7,6},{8,9},{9,8},{10,11... | collective-permute-start | bytes 196616 | tf_op jit(solution)/shard_map/ppermute | solution.py:337
  51.8 1.3 %collective-permute-start.26 = (bf16[8,4096]{1,0:T(8,128)(2,1)S(1)}, bf16[8,4096]{1,0:T(8,128)(2,1)S(1)}, u32[]{:S(2)}, u32[]{:S(2)}) collective-permute-start(bf16[8,4096]{1,0:T(8,128)(2,1)S(1)} %get-tuple-element.75), channel_id=1, source_target_pairs={{0,1},{1,0},{2,3},{3,2},{4,5},{5,4},{6,7},{7,6},{8,9},{9,8},{10,11... | collective-permute-start | bytes 196616 | tf_op jit(solution)/shard_map/ppermute | solution.py:337
  53.2 3.8 %collective-permute-start.27 = (bf16[2,4096]{1,0:T(2,128)(2,1)S(1)}, bf16[2,4096]{1,0:T(2,128)(2,1)S(1)}, u32[]{:S(2)}, u32[]{:S(2)}) collective-permute-start(bf16[2,4096]{1,0:T(2,128)(2,1)S(1)} %get-tuple-element.78), channel_id=1, source_target_pairs={{0,2},{1,3},{2,0},{3,1},{4,6},{5,7},{6,4},{7,5},{8,10},{9,11},{10,... | collective-permute-start | bytes 49160 | tf_op jit(solution)/shard_map/ppermute | solution.py:334
  54.1 3.7 %collective-permute-start.28 = (bf16[2,4096]{1,0:T(2,128)(2,1)S(1)}, bf16[2,4096]{1,0:T(2,128)(2,1)S(1)}, u32[]{:S(2)}, u32[]{:S(2)}) collective-permute-start(bf16[2,4096]{1,0:T(2,128)(2,1)S(1)} %get-tuple-element.79), channel_id=1, source_target_pairs={{0,4},{1,5},{2,6},{3,7},{4,0},{5,1},{6,2},{7,3},{8,12},{9,13},{10,... | collective-permute-start | bytes 49160 | tf_op jit(solution)/shard_map/ppermute | solution.py:334
  55.2 4.6 %collective-permute-start.29 = (bf16[2,4096]{1,0:T(2,128)(2,1)S(1)}, bf16[2,4096]{1,0:T(2,128)(2,1)S(1)}, u32[]{:S(2)}, u32[]{:S(2)}) collective-permute-start(bf16[2,4096]{1,0:T(2,128)(2,1)S(1)} %get-tuple-element.80), channel_id=1, source_target_pairs={{0,6},{1,7},{2,4},{3,5},{4,2},{5,3},{6,0},{7,1},{8,14},{9,15},{10,... | collective-permute-start | bytes 49160 | tf_op jit(solution)/shard_map/ppermute | solution.py:334
  (13 other events, 44.7 us)

commit v10 on v9

--- a/solution.py
+++ b/solution.py
@@ -100,30 +100,40 @@
         blocks[m][...] = source[pl.ds(at, slots), :].astype(BF16)
 
 
-def join_kernel(group, width, *refs):
-    count = group * EXPERTS
-    whole, half, table, scale = refs[count : count + 4]
-    block, rows = refs[count + 4 :]
-    expert, own = place(group)
+def assemble(group, pieces, block, rows, width):
+    _, own = place(group)
     slots = EXPERTS * CAP
     for m in range(group):
         for i in range(EXPERTS):
-            block[i * CAP : (i + 1) * CAP, :] = refs[m * EXPERTS + i][...].astype(F32)
+            piece = pieces[m * EXPERTS + i]
+            block[i * CAP : (i + 1) * CAP, :] = piece[:, 0:width].astype(F32)
         at = pl.multiple_of((own ^ m) * slots, slots)
         rows[pl.ds(at, slots), :] = block[...]
+
+
+def join_kernel(group, width, *refs):
+    count = group * EXPERTS
+    half, table, scale = refs[count : count + 3]
+    block, rows = refs[count + 3 :]
+    expert, own = place(group)
+    assemble(group, refs[:count], block, rows, rows.shape[1])
     table[...] = rows[:, width : width + LANES].astype(BF16)
     scale[...] = scales(expert, rows[:, width:])
     at = pl.multiple_of(own * half.shape[1], half.shape[1])
     half[...] = rows[:, pl.ds(at, half.shape[1])].astype(BF16)
-    whole[...] = rows[:, 0:width].astype(BF16)
-
-
-def whole_kernel(group, tick, rows, gain, w_gate, w_up, w_down, *outs):
+
+
+def whole_kernel(group, tick, *refs):
+    count = group * EXPERTS
+    gain, w_gate, w_up, w_down = refs[count : count + 4]
+    outs = refs[count + 4 : -2]
+    block, rows = refs[-2:]
     _, own = place(group)
 
     @active(tick)
     def _():
-        values = rows[...].astype(F32)
+        assemble(group, refs[:count], block, rows, rows.shape[1])
+        values = rows[...]
         inverse = lax.rsqrt(jnp.mean(values * values, axis=-1, keepdims=True) + 1e-06)
         normed = (values * inverse * gain[...]).astype(BF16)
         gate = jnp.dot(normed, w_gate[0], preferred_element_type=F32)
@@ -383,14 +393,9 @@
             else:
                 pieces.append(within(piece, m))
     flops = 6 * rows * width * w_gate.shape[2]
-    whole, half, table, scale = call(
+    half, table, scale = call(
         functools.partial(join_kernel, group, width),
-        [
-            shape((rows, width)),
-            shape((rows, chunk)),
-            shape((rows, LANES)),
-            shape((rows, LANES), F32),
-        ],
+        [shape((rows, chunk)), shape((rows, LANES)), shape((rows, LANES), F32)],
         tuple(pieces),
         scratch=[pltpu.VMEM((slots, wide), F32), pltpu.VMEM((rows, wide), F32)],
     )
@@ -448,7 +453,8 @@
             outs = call(
                 functools.partial(whole_kernel, group, tick),
                 [shape((rows, inner))] + [shape((rows, chunk))] * (group - 1),
-                (whole, *weights),
+                (*pieces, *weights),
+                scratch=[pltpu.VMEM((slots, width), F32), pltpu.VMEM((rows, width), F32)],
                 flops=flops * 5 // 6,
             )
         terms = [within(outs[m], m) for m in range(1, group)]

time: 61 us -> 60.9 us (level)
  no operation moved by 1% of the time
where the time goes in v10:
time: 60.9 us; the launch traced here: 60.6 us
  starting transfers between devices  33.3 us (55%)
  waiting for transfers between devices  20.5 us (34%)
  Pallas kernels  5.75 us (9%)
  local copies, waits for them, and re-layouts  0.81 us (1%)
    ppermute x11, starting transfers between devices, gather(): outs[i] = lax.ppermute(value if i else marked, ('section', 'expert'), pairs)  23.2 us
    ppermute x11, waiting for transfers between devices, gather(): outs[i] = lax.ppermute(value if i else marked, ('section', 'expert'), pairs)  8.16 us
    ppermute x11, waiting for transfers between devices, within(): return lax.ppermute(value, 'expert', [(d, d ^ m) for d in range(peers)])  7.55 us
    ppermute x6, starting transfers between devices, across(): return lax.ppermute(value, 'expert', pairs)  7.11 us
    pallas_call x28, Pallas kernels, call(): pl.pallas_call(kernel, out_shape=outs, in_specs=specs or [VMEM] * len(arg...  5.75 us
    ppermute x6, waiting for transfers between devices, across(): return lax.ppermute(value, 'expert', pairs)  4.8 us
    ppermute x11, starting transfers between devices, within(): return lax.ppermute(value, 'expert', [(d, d ^ m) for d in range(peers)])  2.72 us
  transfers between devices with their start and end apart: 30, of which 20 were waited for; matrix products, arithmetic and copies ran while one was open for 0% of the time, Pallas kernels for 4%

profile of v10, /device:TPU:24, one launch (start us, length us, event | category | flops | bytes accessed | tf_op | source)
XLA Modules:
  0.0 60.6 jit_solution(14001851515772630497)
XLA Ops:
  1.1 1.6 %collective-permute-start = (bf16[2,4608]{1,0:T(2,128)(2,1)S(1)}, bf16[2,4608]{1,0:T(2,128)(2,1)S(1)}, u32[]{:S(2)}, u32[]{:S(2)}) collective-permute-start(bf16[2,4608]{1,0:T(2,128)(2,1)S(1)} %get-tuple-element.43), channel_id=1, source_target_pairs={{0,2},{1,3},{2,0},{3,1},{4,6},{5,7},{6,4},{7,5},{8,10},{9,11},{10,... | collective-permute-start | bytes 55304 | tf_op jit(solution)/shard_map/ppermute | solution.py:344
  2.7 1.5 %collective-permute-start.2 = (bf16[2,4608]{1,0:T(2,128)(2,1)S(1)}, bf16[2,4608]{1,0:T(2,128)(2,1)S(1)}, u32[]{:S(2)}, u32[]{:S(2)}) collective-permute-start(bf16[2,4608]{1,0:T(2,128)(2,1)S(1)} %get-tuple-element.45), channel_id=1, source_target_pairs={{0,6},{1,7},{2,4},{3,5},{4,2},{5,3},{6,0},{7,1},{8,14},{9,15},{10,... | collective-permute-start | bytes 55304 | tf_op jit(solution)/shard_map/ppermute | solution.py:344
  4.8 1.5 %collective-permute-start.3 = (bf16[2,4608]{1,0:T(2,128)(2,1)S(1)}, bf16[2,4608]{1,0:T(2,128)(2,1)S(1)}, u32[]{:S(2)}, u32[]{:S(2)}) collective-permute-start(bf16[2,4608]{1,0:T(2,128)(2,1)S(1)} %get-tuple-element.42.refs_0_), channel_id=1, source_target_pairs={{0,1},{1,0},{2,3},{3,2},{4,5},{5,4},{6,7},{7,6},{8,9},{9,8},{10,11... | collective-permute-start | bytes 55304 | tf_op jit(solution)/shard_map/ppermute | solution.py:347
  6.3 1.0 %collective-permute-done.2.refs_3_ = bf16[2,4608]{1,0:T(2,128)(2,1)S(1)} collective-permute-done((bf16[2,4608]{1,0:T(2,128)(2,1)S(1)}, bf16[2,4608]{1,0:T(2,128)(2,1)S(1)}, u32[]{:S(2)}, u32[]{:S(2)}) %collective-permute-start.2) | collective-permute-done | bytes 18464 | tf_op jit(solution)/shard_map/ppermute | solution.py:344
  9.0 0.9 %collective-permute-done.7.refs_1_ = bf16[16,2048]{1,0:T(8,128)(2,1)S(1)} collective-permute-done((bf16[16,2048]{1,0:T(8,128)(2,1)S(1)}, bf16[16,2048]{1,0:T(8,128)(2,1)S(1)}, u32[]{:S(2)}, u32[]{:S(2)}) %collective-permute-start.7) | collective-permute-done | bytes 65568 | tf_op jit(solution)/shard_map/ppermute | solution.py:347
  10.2 1.1 %collective-permute-done.8.before.refs_0_ = bf16[16,2176]{1,0:T(8,128)(2,1)S(1)} collective-permute-done((bf16[16,2176]{1,0:T(8,128)(2,1)S(1)}, bf16[16,2176]{1,0:T(8,128)(2,1)S(1)}, u32[]{:S(2)}, u32[]{:S(2)}) %collective-permute-start.8) | collective-permute-done | bytes 69664 | tf_op jit(solution)/shard_map/ppermute | solution.py:365
  13.6 1.1 %collective-permute-done.12.refs_1_ = bf16[16,2048]{1,0:T(8,128)(2,1)S(1)} collective-permute-done((bf16[16,2048]{1,0:T(8,128)(2,1)S(1)}, bf16[16,2048]{1,0:T(8,128)(2,1)S(1)}, u32[]{:S(2)}, u32[]{:S(2)}) %collective-permute-start.12) | collective-permute-done | bytes 65568 | tf_op jit(solution)/shard_map/ppermute | solution.py:347
  14.9 1.1 %collective-permute-done.13.refs_1_ = bf16[16,2048]{1,0:T(8,128)(2,1)S(1)} collective-permute-done((bf16[16,2048]{1,0:T(8,128)(2,1)S(1)}, bf16[16,2048]{1,0:T(8,128)(2,1)S(1)}, u32[]{:S(2)}, u32[]{:S(2)}) %collective-permute-start.13) | collective-permute-done | bytes 65568 | tf_op jit(solution)/shard_map/ppermute | solution.py:347
  16.3 11.6 %collective-permute-start.14 = (bf16[16,2048]{1,0:T(8,128)(2,1)S(1)}, bf16[16,2048]{1,0:T(8,128)(2,1)S(1)}, u32[]{:S(2)}, u32[]{:S(2)}) collective-permute-start(bf16[16,2048]{1,0:T(8,128)(2,1)S(1)} %get-tuple-element.58.refs_1_), channel_id=1, source_target_pairs={{0,1},{1,0},{2,3},{3,2},{4,5},{5,4},{6,7},{7,6},{8,22},{9,23},{10,... | collective-permute-start | bytes 196616 | tf_op jit(solution)/shard_map/ppermute | solution.py:365
  28.8 1.9 %collective-permute-done.14.refs_0_ = bf16[16,2048]{1,0:T(8,128)(2,1)S(1)} collective-permute-done((bf16[16,2048]{1,0:T(8,128)(2,1)S(1)}, bf16[16,2048]{1,0:T(8,128)(2,1)S(1)}, u32[]{:S(2)}, u32[]{:S(2)}) %collective-permute-start.14) | collective-permute-done | bytes 65568 | tf_op jit(solution)/shard_map/ppermute | solution.py:365
  31.1 1.2 %collective-permute-done.18.refs_1_ = bf16[16,2048]{1,0:T(8,128)(2,1)S(1)} collective-permute-done((bf16[16,2048]{1,0:T(8,128)(2,1)S(1)}, bf16[16,2048]{1,0:T(8,128)(2,1)S(1)}, u32[]{:S(2)}, u32[]{:S(2)}) %collective-permute-start.18) | collective-permute-done | bytes 65568 | tf_op jit(solution)/shard_map/ppermute | solution.py:347
  32.5 1.1 %collective-permute-done.19.refs_1_ = bf16[16,2048]{1,0:T(8,128)(2,1)S(1)} collective-permute-done((bf16[16,2048]{1,0:T(8,128)(2,1)S(1)}, bf16[16,2048]{1,0:T(8,128)(2,1)S(1)}, u32[]{:S(2)}, u32[]{:S(2)}) %collective-permute-start.19) | collective-permute-done | bytes 65568 | tf_op jit(solution)/shard_map/ppermute | solution.py:347
  33.7 7.1 %collective-permute-start.21 = (bf16[16,2176]{1,0:T(8,128)(2,1)S(1)}, bf16[16,2176]{1,0:T(8,128)(2,1)S(1)}, u32[]{:S(2)}, u32[]{:S(2)}) collective-permute-start(bf16[16,2176]{1,0:T(8,128)(2,1)S(1)} %get-tuple-element.66), channel_id=1, source_target_pairs={{0,1},{1,0},{2,3},{3,2},{4,5},{5,4},{6,7},{7,6},{8,9},{9,8},{10,11... | collective-permute-start | bytes 208904 | tf_op jit(solution)/shard_map/ppermute | solution.py:365
  40.7 3.0 %collective-permute-start.22 = (bf16[16,2048]{1,0:T(8,128)(2,1)S(1)}, bf16[16,2048]{1,0:T(8,128)(2,1)S(1)}, u32[]{:S(2)}, u32[]{:S(2)}) collective-permute-start(bf16[16,2048]{1,0:T(8,128)(2,1)S(1)} %get-tuple-element.65.refs_2_), channel_id=1, source_target_pairs={{0,1},{1,0},{2,3},{3,2},{4,5},{5,4},{6,7},{7,6},{8,9},{9,8},{10,11... | collective-permute-start | bytes 196616 | tf_op jit(solution)/shard_map/ppermute | solution.py:365
  44.3 3.2 %collective-permute-done.20.refs_0_ = bf16[16,2048]{1,0:T(8,128)(2,1)S(1)} collective-permute-done((bf16[16,2048]{1,0:T(8,128)(2,1)S(1)}, bf16[16,2048]{1,0:T(8,128)(2,1)S(1)}, u32[]{:S(2)}, u32[]{:S(2)}) %collective-permute-start.20) | collective-permute-done | bytes 65568 | tf_op jit(solution)/shard_map/ppermute | solution.py:365
  48.2 0.7 %collective-permute-done.23.refs_1_ = bf16[16,2048]{1,0:T(8,128)(2,1)S(1)} collective-permute-done((bf16[16,2048]{1,0:T(8,128)(2,1)S(1)}, bf16[16,2048]{1,0:T(8,128)(2,1)S(1)}, u32[]{:S(2)}, u32[]{:S(2)}) %collective-permute-start.23) | collective-permute-done | bytes 65568 | tf_op jit(solution)/shard_map/ppermute | solution.py:365
  50.4 1.3 %shard_map.98 = (bf16[8,4096]{1,0:T(8,128)(2,1)S(1)}, bf16[8,4096]{1,0:T(8,128)(2,1)S(1)}, bf16[8,4096]{1,0:T(8,128)(2,1)S(1)}) custom-call(bf16[16,2048]{1,0:T(8,128)(2,1)S(1)} %shard_map.96.half.refs_0_, bf16[16,2048]{1,0:T(8,128)(2,1)S(1)} %collective-permute-done.25.refs_1_, f32[16,512]{1,0:T(8,128)S(1)} %get-tuple-element.69.refs_2_, ...), custom_call_target="tpu_custom_call" | custom-call | flops 100663296 | bytes 12804096 | tf_op jit(solution)/shard_map/pallas_call | solution.py:25
  51.9 1.1 %collective-permute-done.26.refs_1_ = bf16[8,4096]{1,0:T(8,128)(2,1)S(1)} collective-permute-done((bf16[8,4096]{1,0:T(8,128)(2,1)S(1)}, bf16[8,4096]{1,0:T(8,128)(2,1)S(1)}, u32[]{:S(2)}, u32[]{:S(2)}) %collective-permute-start.26) | collective-permute-done | bytes 65568 | tf_op jit(solution)/shard_map/ppermute | solution.py:347
  53.1 0.9 %collective-permute-start.27 = (bf16[2,4096]{1,0:T(2,128)(2,1)S(1)}, bf16[2,4096]{1,0:T(2,128)(2,1)S(1)}, u32[]{:S(2)}, u32[]{:S(2)}) collective-permute-start(bf16[2,4096]{1,0:T(2,128)(2,1)S(1)} %get-tuple-element.76), channel_id=1, source_target_pairs={{0,2},{1,3},{2,0},{3,1},{4,6},{5,7},{6,4},{7,5},{8,10},{9,11},{10,... | collective-permute-start | bytes 49160 | tf_op jit(solution)/shard_map/ppermute | solution.py:344
  54.1 1.1 %collective-permute-start.28 = (bf16[2,4096]{1,0:T(2,128)(2,1)S(1)}, bf16[2,4096]{1,0:T(2,128)(2,1)S(1)}, u32[]{:S(2)}, u32[]{:S(2)}) collective-permute-start(bf16[2,4096]{1,0:T(2,128)(2,1)S(1)} %get-tuple-element.77), channel_id=1, source_target_pairs={{0,4},{1,5},{2,6},{3,7},{4,0},{5,1},{6,2},{7,3},{8,12},{9,13},{10,... | collective-permute-start | bytes 49160 | tf_op jit(solution)/shard_map/ppermute | solution.py:344
  55.1 1.6 %collective-permute-start.29 = (bf16[2,4096]{1,0:T(2,128)(2,1)S(1)}, bf16[2,4096]{1,0:T(2,128)(2,1)S(1)}, u32[]{:S(2)}, u32[]{:S(2)}) collective-permute-start(bf16[2,4096]{1,0:T(2,128)(2,1)S(1)} %get-tuple-element.78), channel_id=1, source_target_pairs={{0,6},{1,7},{2,4},{3,5},{4,2},{5,3},{6,0},{7,1},{8,14},{9,15},{10,... | collective-permute-start | bytes 49160 | tf_op jit(solution)/shard_map/ppermute | solution.py:344
  57.0 0.8 %collective-permute-done.28.refs_2_ = bf16[2,4096]{1,0:T(2,128)(2,1)S(1)} collective-permute-done((bf16[2,4096]{1,0:T(2,128)(2,1)S(1)}, bf16[2,4096]{1,0:T(2,128)(2,1)S(1)}, u32[]{:S(2)}, u32[]{:S(2)}) %collective-permute-start.28) | collective-permute-done | bytes 16416 | tf_op jit(solution)/shard_map/ppermute | solution.py:344
  57.8 2.0 %collective-permute-done.29.refs_3_ = bf16[2,4096]{1,0:T(2,128)(2,1)S(1)} collective-permute-done((bf16[2,4096]{1,0:T(2,128)(2,1)S(1)}, bf16[2,4096]{1,0:T(2,128)(2,1)S(1)}, u32[]{:S(2)}, u32[]{:S(2)}) %collective-permute-start.29) | collective-permute-done | bytes 16416 | tf_op jit(solution)/shard_map/ppermute | solution.py:344
  59.8 0.9 %shard_map.100 = bf16[1,6,4096]{2,1,0:T(8,128)(2,1)} custom-call(bf16[2,4096]{1,0:T(2,128)(2,1)S(1)} %get-tuple-element.75.refs_0_, bf16[2,4096]{1,0:T(2,128)(2,1)S(1)} %collective-permute-done.27.refs_1_, bf16[2,4096]{1,0:T(2,128)(2,1)S(1)} %collective-permute-done.28.refs_2_, bf16[2,4096]{1,0:T(2,128)(2,1)S(1)} %collective-permute-done.29.refs_3_, ...), custom_call_target="tpu_custom_call" | custom-call | flops 1000 | bytes 66048 | tf_op jit(solution)/shard_map/pallas_call | solution.py:25
  (79 shorter events, 11.2 us)
Async XLA Ops:
  1.1 5.2 %collective-permute-start = (bf16[2,4608]{1,0:T(2,128)(2,1)S(1)}, bf16[2,4608]{1,0:T(2,128)(2,1)S(1)}, u32[]{:S(2)}, u32[]{:S(2)}) collective-permute-start(bf16[2,4608]{1,0:T(2,128)(2,1)S(1)} %get-tuple-element.43), channel_id=1, source_target_pairs={{0,2},{1,3},{2,0},{3,1},{4,6},{5,7},{6,4},{7,5},{8,10},{9,11},{10,... | collective-permute-start | bytes 55304 | tf_op jit(solution)/shard_map/ppermute | solution.py:344
  2.7 4.7 %collective-permute-start.2 = (bf16[2,4608]{1,0:T(2,128)(2,1)S(1)}, bf16[2,4608]{1,0:T(2,128)(2,1)S(1)}, u32[]{:S(2)}, u32[]{:S(2)}) collective-permute-start(bf16[2,4608]{1,0:T(2,128)(2,1)S(1)} %get-tuple-element.45), channel_id=1, source_target_pairs={{0,6},{1,7},{2,4},{3,5},{4,2},{5,3},{6,0},{7,1},{8,14},{9,15},{10,... | collective-permute-start | bytes 55304 | tf_op jit(solution)/shard_map/ppermute | solution.py:344
  4.2 3.9 %collective-permute-start.1 = (bf16[2,4608]{1,0:T(2,128)(2,1)S(1)}, bf16[2,4608]{1,0:T(2,128)(2,1)S(1)}, u32[]{:S(2)}, u32[]{:S(2)}) collective-permute-start(bf16[2,4608]{1,0:T(2,128)(2,1)S(1)} %get-tuple-element.44), channel_id=1, source_target_pairs={{0,4},{1,5},{2,6},{3,7},{4,0},{5,1},{6,2},{7,3},{8,12},{9,13},{10,... | collective-permute-start | bytes 55304 | tf_op jit(solution)/shard_map/ppermute | solution.py:344
  4.7 3.4 %collective-permute-start.5 = (bf16[2,4608]{1,0:T(2,128)(2,1)S(1)}, bf16[2,4608]{1,0:T(2,128)(2,1)S(1)}, u32[]{:S(2)}, u32[]{:S(2)}) collective-permute-start(bf16[2,4608]{1,0:T(2,128)(2,1)S(1)} %get-tuple-element.44), channel_id=1, source_target_pairs={{0,5},{1,4},{2,7},{3,6},{4,1},{5,0},{6,3},{7,2},{8,13},{9,12},{10,... | collective-permute-start | bytes 55304 | tf_op jit(solution)/shard_map/ppermute | solution.py:392
  4.8 2.6 %collective-permute-start.3 = (bf16[2,4608]{1,0:T(2,128)(2,1)S(1)}, bf16[2,4608]{1,0:T(2,128)(2,1)S(1)}, u32[]{:S(2)}, u32[]{:S(2)}) collective-permute-start(bf16[2,4608]{1,0:T(2,128)(2,1)S(1)} %get-tuple-element.42.refs_0_), channel_id=1, source_target_pairs={{0,1},{1,0},{2,3},{3,2},{4,5},{5,4},{6,7},{7,6},{8,9},{9,8},{10,11... | collective-permute-start | bytes 55304 | tf_op jit(solution)/shard_map/ppermute | solution.py:347
  6.3 1.7 %collective-permute-start.4 = (bf16[2,4608]{1,0:T(2,128)(2,1)S(1)}, bf16[2,4608]{1,0:T(2,128)(2,1)S(1)}, u32[]{:S(2)}, u32[]{:S(2)}) collective-permute-start(bf16[2,4608]{1,0:T(2,128)(2,1)S(1)} %collective-permute-done.refs_1_), channel_id=1, source_target_pairs={{0,1},{1,0},{2,3},{3,2},{4,5},{5,4},{6,7},{7,6},{8,9},{9,8},{10,11... | collective-permute-start | bytes 55304 | tf_op jit(solution)/shard_map/ppermute | solution.py:347
  8.6 1.3 %collective-permute-start.7 = (bf16[16,2048]{1,0:T(8,128)(2,1)S(1)}, bf16[16,2048]{1,0:T(8,128)(2,1)S(1)}, u32[]{:S(2)}, u32[]{:S(2)}) collective-permute-start(bf16[16,2048]{1,0:T(8,128)(2,1)S(1)} %get-tuple-element.47), channel_id=1, source_target_pairs={{0,1},{1,0},{2,3},{3,2},{4,5},{5,4},{6,7},{7,6},{8,9},{9,8},{10,11... | collective-permute-start | bytes 196616 | tf_op jit(solution)/shard_map/ppermute | solution.py:347
  11.3 1.9 %collective-permute-start.11 = (bf16[16,2176]{1,0:T(8,128)(2,1)S(1)}, bf16[16,2176]{1,0:T(8,128)(2,1)S(1)}, u32[]{:S(2)}, u32[]{:S(2)}) collective-permute-start(bf16[16,2176]{1,0:T(8,128)(2,1)S(1)} %collective-permute-done.8.before.refs_0_), channel_id=1, source_target_pairs={{0,1},{1,0},{2,3},{3,2},{4,5},{5,4},{6,7},{7,6},{8,10},{9,11},{10,... | collective-permute-start | bytes 208904 | tf_op jit(solution)/shard_map/ppermute | solution.py:372
  13.4 1.3 %collective-permute-start.12 = (bf16[16,2048]{1,0:T(8,128)(2,1)S(1)}, bf16[16,2048]{1,0:T(8,128)(2,1)S(1)}, u32[]{:S(2)}, u32[]{:S(2)}) collective-permute-start(bf16[16,2048]{1,0:T(8,128)(2,1)S(1)} %shard_map.81.half.refs_0_.refs_2_), channel_id=1, source_target_pairs={{0,1},{1,0},{2,3},{3,2},{4,5},{5,4},{6,7},{7,6},{8,9},{9,8},{10,11... | collective-permute-start | bytes 196616 | tf_op jit(solution)/shard_map/ppermute | solution.py:347
  16.1 12.4 %collective-permute-start.15 = (bf16[16,2176]{1,0:T(8,128)(2,1)S(1)}, bf16[16,2176]{1,0:T(8,128)(2,1)S(1)}, u32[]{:S(2)}, u32[]{:S(2)}) collective-permute-start(bf16[16,2176]{1,0:T(8,128)(2,1)S(1)} %get-tuple-element.59), channel_id=1, source_target_pairs={{0,1},{1,0},{2,3},{3,2},{4,5},{5,4},{6,7},{7,6},{8,16},{9,17},{10,... | collective-permute-start | bytes 208904 | tf_op jit(solution)/shard_map/ppermute | solution.py:365
  16.3 14.4 %collective-permute-start.14 = (bf16[16,2048]{1,0:T(8,128)(2,1)S(1)}, bf16[16,2048]{1,0:T(8,128)(2,1)S(1)}, u32[]{:S(2)}, u32[]{:S(2)}) collective-permute-start(bf16[16,2048]{1,0:T(8,128)(2,1)S(1)} %get-tuple-element.58.refs_1_), channel_id=1, source_target_pairs={{0,1},{1,0},{2,3},{3,2},{4,5},{5,4},{6,7},{7,6},{8,22},{9,23},{10,... | collective-permute-start | bytes 196616 | tf_op jit(solution)/shard_map/ppermute | solution.py:365
  27.9 2.7 %collective-permute-start.16 = (bf16[16,2048]{1,0:T(8,128)(2,1)S(1)}, bf16[16,2048]{1,0:T(8,128)(2,1)S(1)}, u32[]{:S(2)}, u32[]{:S(2)}) collective-permute-start(bf16[16,2048]{1,0:T(8,128)(2,1)S(1)} %get-tuple-element.58.refs_1_), channel_id=1, source_target_pairs={{0,1},{1,0},{2,3},{3,2},{4,5},{5,4},{6,7},{7,6},{8,18},{9,19},{10,... | collective-permute-start | bytes 196616 | tf_op jit(solution)/shard_map/ppermute | solution.py:365
  27.9 2.9 %collective-permute-start.17 = (bf16[16,2048]{1,0:T(8,128)(2,1)S(1)}, bf16[16,2048]{1,0:T(8,128)(2,1)S(1)}, u32[]{:S(2)}, u32[]{:S(2)}) collective-permute-start(bf16[16,2048]{1,0:T(8,128)(2,1)S(1)} %get-tuple-element.58.refs_1_), channel_id=1, source_target_pairs={{0,1},{1,0},{2,3},{3,2},{4,5},{5,4},{6,7},{7,6},{8,20},{9,21},{10,... | collective-permute-start | bytes 196616 | tf_op jit(solution)/shard_map/ppermute | solution.py:365
  31.0 1.3 %collective-permute-start.18 = (bf16[16,2048]{1,0:T(8,128)(2,1)S(1)}, bf16[16,2048]{1,0:T(8,128)(2,1)S(1)}, u32[]{:S(2)}, u32[]{:S(2)}) collective-permute-start(bf16[16,2048]{1,0:T(8,128)(2,1)S(1)} %shard_map.88.half.refs_0_.refs_2_), channel_id=1, source_target_pairs={{0,1},{1,0},{2,3},{3,2},{4,5},{5,4},{6,7},{7,6},{8,9},{9,8},{10,11... | collective-permute-start | bytes 196616 | tf_op jit(solution)/shard_map/ppermute | solution.py:347
  33.7 10.2 %collective-permute-start.21 = (bf16[16,2176]{1,0:T(8,128)(2,1)S(1)}, bf16[16,2176]{1,0:T(8,128)(2,1)S(1)}, u32[]{:S(2)}, u32[]{:S(2)}) collective-permute-start(bf16[16,2176]{1,0:T(8,128)(2,1)S(1)} %get-tuple-element.66), channel_id=1, source_target_pairs={{0,1},{1,0},{2,3},{3,2},{4,5},{5,4},{6,7},{7,6},{8,9},{9,8},{10,11... | collective-permute-start | bytes 208904 | tf_op jit(solution)/shard_map/ppermute | solution.py:365
  40.7 6.7 %collective-permute-start.20 = (bf16[16,2048]{1,0:T(8,128)(2,1)S(1)}, bf16[16,2048]{1,0:T(8,128)(2,1)S(1)}, u32[]{:S(2)}, u32[]{:S(2)}) collective-permute-start(bf16[16,2048]{1,0:T(8,128)(2,1)S(1)} %get-tuple-element.65.refs_2_), channel_id=1, source_target_pairs={{0,16},{1,17},{2,18},{3,19},{4,20},{5,21},{6,22},{7,23},{8,9},{9,8... | collective-permute-start | bytes 196616 | tf_op jit(solution)/shard_map/ppermute | solution.py:365
  40.7 7.3 %collective-permute-start.22 = (bf16[16,2048]{1,0:T(8,128)(2,1)S(1)}, bf16[16,2048]{1,0:T(8,128)(2,1)S(1)}, u32[]{:S(2)}, u32[]{:S(2)}) collective-permute-start(bf16[16,2048]{1,0:T(8,128)(2,1)S(1)} %get-tuple-element.65.refs_2_), channel_id=1, source_target_pairs={{0,1},{1,0},{2,3},{3,2},{4,5},{5,4},{6,7},{7,6},{8,9},{9,8},{10,11... | collective-permute-start | bytes 196616 | tf_op jit(solution)/shard_map/ppermute | solution.py:365
  43.8 5.2 %collective-permute-start.23 = (bf16[16,2048]{1,0:T(8,128)(2,1)S(1)}, bf16[16,2048]{1,0:T(8,128)(2,1)S(1)}, u32[]{:S(2)}, u32[]{:S(2)}) collective-permute-start(bf16[16,2048]{1,0:T(8,128)(2,1)S(1)} %get-tuple-element.65.refs_2_), channel_id=1, source_target_pairs={{0,1},{1,0},{2,3},{3,2},{4,5},{5,4},{6,7},{7,6},{8,9},{9,8},{10,11... | collective-permute-start | bytes 196616 | tf_op jit(solution)/shard_map/ppermute | solution.py:365
  43.8 4.4 %collective-permute-start.24 = (bf16[8,2048]{1,0:T(8,128)(2,1)S(1)}, bf16[8,2048]{1,0:T(8,128)(2,1)S(1)}, u32[]{:S(2)}, u32[]{:S(2)}) collective-permute-start(bf16[8,2048]{1,0:T(8,128)(2,1)S(1)} %get-tuple-element.68), channel_id=1, source_target_pairs={{0,1},{1,0},{2,3},{3,2},{4,5},{5,4},{6,7},{7,6},{8,9},{9,8},{10,11... | collective-permute-start | bytes 98312 | tf_op jit(solution)/shard_map/ppermute | solution.py:347
  49.1 1.3 %collective-permute-start.25 = (bf16[16,2048]{1,0:T(8,128)(2,1)S(1)}, bf16[16,2048]{1,0:T(8,128)(2,1)S(1)}, u32[]{:S(2)}, u32[]{:S(2)}) collective-permute-start(bf16[16,2048]{1,0:T(8,128)(2,1)S(1)} %shard_map.96.half.refs_0_), channel_id=1, source_target_pairs={{0,1},{1,0},{2,3},{3,2},{4,5},{5,4},{6,7},{7,6},{8,9},{9,8},{10,11... | collective-permute-start | bytes 196616 | tf_op jit(solution)/shard_map/ppermute | solution.py:347
  51.7 1.3 %collective-permute-start.26 = (bf16[8,4096]{1,0:T(8,128)(2,1)S(1)}, bf16[8,4096]{1,0:T(8,128)(2,1)S(1)}, u32[]{:S(2)}, u32[]{:S(2)}) collective-permute-start(bf16[8,4096]{1,0:T(8,128)(2,1)S(1)} %get-tuple-element.73), channel_id=1, source_target_pairs={{0,1},{1,0},{2,3},{3,2},{4,5},{5,4},{6,7},{7,6},{8,9},{9,8},{10,11... | collective-permute-start | bytes 196616 | tf_op jit(solution)/shard_map/ppermute | solution.py:347
  53.1 3.8 %collective-permute-start.27 = (bf16[2,4096]{1,0:T(2,128)(2,1)S(1)}, bf16[2,4096]{1,0:T(2,128)(2,1)S(1)}, u32[]{:S(2)}, u32[]{:S(2)}) collective-permute-start(bf16[2,4096]{1,0:T(2,128)(2,1)S(1)} %get-tuple-element.76), channel_id=1, source_target_pairs={{0,2},{1,3},{2,0},{3,1},{4,6},{5,7},{6,4},{7,5},{8,10},{9,11},{10,... | collective-permute-start | bytes 49160 | tf_op jit(solution)/shard_map/ppermute | solution.py:344
  54.1 3.7 %collective-permute-start.28 = (bf16[2,4096]{1,0:T(2,128)(2,1)S(1)}, bf16[2,4096]{1,0:T(2,128)(2,1)S(1)}, u32[]{:S(2)}, u32[]{:S(2)}) collective-permute-start(bf16[2,4096]{1,0:T(2,128)(2,1)S(1)} %get-tuple-element.77), channel_id=1, source_target_pairs={{0,4},{1,5},{2,6},{3,7},{4,0},{5,1},{6,2},{7,3},{8,12},{9,13},{10,... | collective-permute-start | bytes 49160 | tf_op jit(solution)/shard_map/ppermute | solution.py:344
  55.1 4.6 %collective-permute-start.29 = (bf16[2,4096]{1,0:T(2,128)(2,1)S(1)}, bf16[2,4096]{1,0:T(2,128)(2,1)S(1)}, u32[]{:S(2)}, u32[]{:S(2)}) collective-permute-start(bf16[2,4096]{1,0:T(2,128)(2,1)S(1)} %get-tuple-element.78), channel_id=1, source_target_pairs={{0,6},{1,7},{2,4},{3,5},{4,2},{5,3},{6,0},{7,1},{8,14},{9,15},{10,... | collective-permute-start | bytes 49160 | tf_op jit(solution)/shard_map/ppermute | solution.py:344
  (13 other events, 43.9 us)
